TPU v7x, 32 devices: a whole 2x2x4 slice. The times are simulated.
32 devices in a mesh: space: 8 (over z, x), freq: 4 (over y, core).
Axes of the slice: x: 2, y: 2, z: 4, core: 2. Of those that a mesh axis runs over, the one named last changes fastest.
Arguments:
- u_velocity: bfloat16 [2176, 16, 512], P(None, 'space', 'freq'), may hold values from -6 to 6
- v_velocity: bfloat16 [2176, 16, 512], P(None, 'space', 'freq'), may hold values from -6 to 6
- cell_weights: float32 [16, 512], P('space', 'freq'), may hold values from 0.25 to 4
- block_offsets: int32 [16], replicated, may hold values from 0 to 1920
- triads: int32 [64, 2], replicated, may hold values from 0 to 63
Outputs:
- eigen_values: float32 [64, 2], replicated
- mode_fields: float32 [64, 2, 16, 512], P(None, None, 'space', 'freq')
Inputs may be any that keep to these rules, and one draw needn't show every extreme that they name: `triads`: k and l are each below 64, so k + l is below 128.
All inputs are finite; a program needn't handle non-finite values.
Results may differ from a plain program's by a relative error of at most 0.012.
Values may be sent and summed in bfloat16 or wider, within the bound.
No kernel may reach another device: no remote copies, remote signals or barrier semaphores. Data moves between devices by JAX's collectives and lax.ppermute only.
A program may use at most 64 MiB of HBM per device.

v0:
```python
import math

import jax
import jax.numpy as jnp
from jax import lax
from jax.sharding import PartitionSpec as P

NFFT = 256
POW = 4


def with_halo(cells, sides, width):
    for axis, dim in sides:
        count = lax.axis_size(axis)
        ends = count - 1
        head = lax.slice_in_dim(cells, 0, width, axis=dim)
        tail = lax.slice_in_dim(cells, cells.shape[dim] - width, cells.shape[dim], axis=dim)
        cells = jnp.concatenate(
            [
                lax.ppermute(tail, axis, [(i, (i + 1) % count) for i in range(ends)]),
                cells,
                lax.ppermute(head, axis, [((i + 1) % count, i) for i in range(ends)]),
            ],
            axis=dim,
        )
    return cells


def make_table(length):
    half_len = length // 2
    times_idx = jnp.arange(length, dtype=jnp.int32)
    freq_idx = jnp.arange(half_len, dtype=jnp.int32)
    phases = freq_idx[:, None] * times_idx[None, :] % length
    angles = phases.astype(jnp.float32) * (2.0 * math.pi / length)
    window = 0.5 - 0.5 * jnp.cos(times_idx.astype(jnp.float32) * (2.0 * math.pi / length))
    scaling = 1.0 / jnp.sqrt(jnp.sum(window * window))
    transform = jnp.concatenate([jnp.cos(angles) * scaling, -jnp.sin(angles) * scaling], axis=0)
    return (window, transform.astype(jnp.bfloat16))


def spectra(vorticity, offsets):
    window, transform = make_table(NFFT)
    fluct = vorticity - jnp.mean(vorticity, axis=0, keepdims=True)
    blocks = jax.vmap(lambda start: lax.dynamic_slice_in_dim(fluct, start, NFFT, 0))(offsets)
    windowed = (blocks * window[None, :, None, None]).astype(jnp.bfloat16)
    return jnp.einsum("ft,btxy->bfxy", transform, windowed, preferred_element_type=jnp.float32)


def cross_terms(spectrum, weights, triads):
    half_len = spectrum.shape[1] // 2
    real_part = spectrum[:, :half_len]
    imag_part = spectrum[:, half_len:]
    target = triads[:, 0] + triads[:, 1]
    first_re = jnp.take(real_part, triads[:, 0], axis=1)
    first_im = jnp.take(imag_part, triads[:, 0], axis=1)
    second_re = jnp.take(real_part, triads[:, 1], axis=1)
    second_im = jnp.take(imag_part, triads[:, 1], axis=1)
    target_re = jnp.take(real_part, target, axis=1)
    target_im = jnp.take(imag_part, target, axis=1)
    prod_re = (first_re * second_re - first_im * second_im) * weights
    prod_im = (first_re * second_im + first_im * second_re) * weights
    high = lax.Precision.HIGHEST
    cross_re = jnp.einsum("btxy,ctxy->tbc", prod_re, target_re, precision=high) + jnp.einsum(
        "btxy,ctxy->tbc", prod_im, target_im, precision=high
    )
    cross_im = jnp.einsum("btxy,ctxy->tbc", prod_re, target_im, precision=high) - jnp.einsum(
        "btxy,ctxy->tbc", prod_im, target_re, precision=high
    )
    return (jnp.stack([cross_re, cross_im], axis=1), target_re, target_im)


def leading(matrices):
    high = lax.Precision.HIGHEST
    mat_re = matrices[:, 0]
    mat_im = matrices[:, 1]
    vec_re = jnp.full(mat_re.shape[:2], 1.0 / math.sqrt(mat_re.shape[1]), jnp.float32)
    vec_im = jnp.zeros(mat_re.shape[:2], jnp.float32)

    def apply(part_re, part_im):
        out_re = jnp.einsum("tbc,tc->tb", mat_re, part_re, precision=high) - jnp.einsum(
            "tbc,tc->tb", mat_im, part_im, precision=high
        )
        out_im = jnp.einsum("tbc,tc->tb", mat_re, part_im, precision=high) + jnp.einsum(
            "tbc,tc->tb", mat_im, part_re, precision=high
        )
        return (out_re, out_im)

    for repeat in range(POW):
        out_re, out_im = apply(vec_re, vec_im)
        length = jnp.sqrt(jnp.sum(out_re * out_re + out_im * out_im, axis=1, keepdims=True))
        vec_re = out_re / length
        vec_im = out_im / length
    out_re, out_im = apply(vec_re, vec_im)
    value_re = jnp.sum(vec_re * out_re + vec_im * out_im, axis=1)
    value_im = jnp.sum(vec_re * out_im - vec_im * out_re, axis=1)
    return (jnp.stack([vec_re, vec_im], axis=1), jnp.stack([value_re, value_im], axis=1))


def on_device(u_velocity, v_velocity, cell_weights, block_offsets, triads):
    u_part = with_halo(u_velocity, (("freq", 2),), 1).astype(jnp.float32)
    v_part = with_halo(v_velocity, (("space", 1),), 1).astype(jnp.float32)
    vorticity = 0.5 * (v_part[:, 2:, :] - v_part[:, :-2, :]) - 0.5 * (
        u_part[:, :, 2:] - u_part[:, :, :-2]
    )
    spectrum = spectra(vorticity, block_offsets)
    partial_value, target_re, target_im = cross_terms(spectrum, cell_weights, triads)
    cells = vorticity.shape[1] * vorticity.shape[2] * lax.axis_size("space") * lax.axis_size("freq")
    scaling = 1.0 / (partial_value.shape[2] * math.sqrt(cells))
    mine = lax.psum_scatter(partial_value, "freq", scatter_dimension=0, tiled=True)
    mine = lax.psum(mine, "space") * scaling
    own_vectors, own_values = leading(mine)
    vectors, values = (
        lax.all_gather(own_vectors, "freq", axis=0, tiled=True),
        lax.all_gather(own_values, "freq", axis=0, tiled=True),
    )
    high = lax.Precision.HIGHEST
    vec_re = vectors[:, 0]
    vec_im = vectors[:, 1]
    mode_re = jnp.einsum("tb,btxy->txy", vec_re, target_re, precision=high) - jnp.einsum(
        "tb,btxy->txy", vec_im, target_im, precision=high
    )
    mode_im = jnp.einsum("tb,btxy->txy", vec_re, target_im, precision=high) + jnp.einsum(
        "tb,btxy->txy", vec_im, target_re, precision=high
    )
    return (values, jnp.stack([mode_re, mode_im], axis=1))


def solution(mesh):
    return jax.shard_map(
        on_device,
        mesh=mesh,
        in_specs=(P(None, "space", "freq"), P(None, "space", "freq"), P("space", "freq"), P(), P()),
        out_specs=(P(), P(None, None, "space", "freq")),
        check_vma=False,
    )
```

profile of v0, /device:TPU:0, one launch (start us, length us, event | category | flops | bytes accessed | tf_op | source)
XLA Modules:
  0.0 192.5 jit_solution(13298839978467539383)
XLA Ops:
  7.2 3.7 %fusion.92 = (bf16[2176,1,128]{2,1,0:T(2,128)(2,1)S(1)}, bf16[2176,1,128]{2,1,0:T(2,128)(2,1)S(1)}) fusion(bf16[2176,2,128]{2,1,0:T(2,128)(2,1)} %param.8), kind=kLoop, calls=%fused_computation.155 | loop fusion | bytes 2228224 | tf_op jit(solution)/shard_map/slice | solution.py:17
  11.8 5.7 %collective-permute-start = (bf16[2176,1,128]{2,0,1:T(8,128)(2,1)}, bf16[2176,1,128]{2,0,1:T(8,128)(2,1)}, u32[]{:S(2)}, u32[]{:S(2)}) collective-permute-start(bf16[2176,1,128]{2,0,1:T(8,128)(2,1)} %copy.121), channel_id=1, source_target_pairs={{0,4},{4,8},{8,12},{12,16},{16,20},{20,24},{24,28},{1,5},{5,9},{9,... | collective-permute-start | bytes 1671176 | tf_op jit(solution)/shard_map/ppermute | solution.py:20
  18.4 1.3 collective-permute-start.1
  19.7 2.1 %fusion.93 = (bf16[2176,2,1]{2,1,0:T(2,128)(2,1)S(1)}, bf16[2176,2,1]{2,1,0:T(2,128)(2,1)S(1)}) fusion(bf16[2176,2,128]{2,1,0:T(2,128)(2,1)S(1)} %copy-done.2), kind=kLoop, calls=%fused_computation.156 | loop fusion | bytes 34816 | tf_op jit(solution)/shard_map/slice | solution.py:17
  21.8 1.3 copy.123
  23.1 1.5 collective-permute-start.2
  24.6 1.3 copy.124
  25.9 1.5 collective-permute-start.3
  29.4 1.6 copy.66
  31.0 1.6 copy.67
  32.7 6.0 %maximum_convert_fusion.1 = f32[2176,2,130]{2,1,0:T(2,128)S(1)} fusion(bf16[2176,2,1]{2,1,0:T(2,128)(2,1)S(1)} %copy.67, bf16[2176,2,128]{2,1,0:T(2,128)(2,1)S(1)} %copy-done.2, bf16[2176,2,1]{2,1,0:T(2,128)(2,1)S(1)} %copy.66), kind=kLoop, calls=%fused_computation.15 | loop fusion | flops 3394560 | bytes 3394560 | tf_op jit(solution)/shard_map/convert_element_type | solution.py:100
  38.7 2.1 %collective-permute-done = bf16[2176,1,128]{2,0,1:T(8,128)(2,1)} collective-permute-done((bf16[2176,1,128]{2,0,1:T(8,128)(2,1)}, bf16[2176,1,128]{2,0,1:T(8,128)(2,1)}, u32[]{:S(2)}, u32[]{:S(2)}) %collective-permute-start) | collective-permute-done | bytes 557088 | tf_op jit(solution)/shard_map/ppermute | solution.py:20
  40.8 5.6 %copy.62 = bf16[2176,1,128]{2,1,0:T(2,128)(2,1)S(1)} copy(bf16[2176,1,128]{2,0,1:T(8,128)(2,1)} %collective-permute-done) | data formatting | bytes 1114112 | tf_op jit(solution)/shard_map/ppermute | solution.py:20
  46.4 5.6 %copy.63 = bf16[2176,1,128]{2,1,0:T(2,128)(2,1)S(1)} copy(bf16[2176,1,128]{2,0,1:T(8,128)(2,1)} %collective-permute-done.1) | data formatting | bytes 1114112 | tf_op jit(solution)/shard_map/ppermute | solution.py:22
  52.0 3.5 %maximum_convert_fusion = f32[2176,4,128]{2,1,0:T(4,128)S(1)} fusion(bf16[2176,1,128]{2,1,0:T(2,128)(2,1)S(1)} %copy.63, bf16[2176,2,128]{2,1,0:T(2,128)(2,1)S(1)} %copy-done.3, bf16[2176,1,128]{2,1,0:T(2,128)(2,1)S(1)} %copy.62), kind=kLoop, calls=%fused_computation.14 | loop fusion | flops 6684672 | bytes 6684672 | tf_op jit(solution)/shard_map/convert_element_type | solution.py:101
  55.6 3.1 %fusion.89 = (f32[2,128]{1,0:T(2,128)S(1)}, f32[2176,2,128]{2,1,0:T(2,128)S(1)}) fusion(f32[2176,2,130]{2,1,0:T(2,128)S(1)} %maximum_convert_fusion.1, f32[2176,4,128]{2,1,0:T(4,128)S(1)} %maximum_convert_fusion), kind=kLoop, calls=%fused_computation.153 | loop fusion | flops 3342080 | bytes 11142144 | tf_op jit(solution)/shard_map/reduce_sum | solution.py:43
  58.9 6.5 %gather_fusion = f32[16,256,2,128]{3,2,1,0:T(2,128)} fusion(f32[2176,2,128]{2,1,0:T(2,128)S(1)} %bitcast.240, s32[16]{0:T(128)S(1)} %fusion.79), kind=kCustom, calls=%fused_computation.6 | custom fusion | bytes 8388800 | tf_op jit(solution)/shard_map/vmap()/gather | solution.py:44
  65.3 3.0 %convolution_bitcast_fusion = f32[16,256,2,128]{1,3,2,0:T(8,128)S(1)} fusion(f32[16,256,2,128]{3,2,1,0:T(2,128)} %gather_fusion, f32[256]{0:T(256)S(1)} %multiply_subtract_fusion, bf16[128,256]{1,0:T(8,128)(2,1)S(1)} %get-tuple-element.47, bf16[128,256]{1,0:T(8,128)(2,1)S(1)} %get-tuple-element.48), kind=kOutput, calls=%fused_computation.16 | convolution fusion | flops 539230208 | bytes 8520704 | tf_op jit(solution)/shard_map/ft,btxy->bfxy/dot_general | solution.py:46
  68.4 2.5 %fusion.91 = (f32[16,128,2,128]{1,3,2,0:T(8,128)}, f32[16,128,2,128]{1,3,2,0:T(8,128)}) fusion(f32[16,256,2,128]{1,3,2,0:T(8,128)S(1)} %convolution_bitcast_fusion), kind=kLoop, calls=%fused_computation.154 | loop fusion | bytes 8388608 | tf_op jit(solution)/shard_map/slice | solution.py:51
  70.9 2.4 %copy.70 = f32[16,128,2,128]{3,0,2,1:T(8,128)S(1)} copy(f32[16,128,2,128]{1,3,2,0:T(8,128)} %get-tuple-element.27) | data formatting | bytes 4194304 | tf_op jit(solution)/shard_map/slice | solution.py:51
  73.3 3.9 %copy.72 = f32[16,128,2,128]{3,0,2,1:T(8,128)} copy(f32[16,128,2,128]{1,3,2,0:T(8,128)} %get-tuple-element.28) | data formatting | bytes 4194304 | tf_op jit(solution)/shard_map/slice | solution.py:52
  77.1 1.6 gather_fusion.2
  78.8 3.2 %gather_fusion.4 = f32[64,16,2,128]{3,1,2,0:T(8,128)} fusion(f32[16,128,2,128]{3,0,2,1:T(8,128)} %copy.72, s32[1024]{0:T(1024)S(1)} %get-tuple-element.50), kind=kCustom, calls=%fused_computation.3.clone | custom fusion | bytes 2097408 | tf_op jit(solution)/shard_map/jit(_take)/gather | solution.py:57
  82.0 1.6 gather_fusion.1
  83.6 3.3 %gather_fusion.3 = f32[64,16,2,128]{3,1,2,0:T(8,128)} fusion(f32[16,128,2,128]{3,0,2,1:T(8,128)} %copy.72, s32[1024]{0:T(1024)S(1)} %pad_clamp_fusion.2), kind=kCustom, calls=%fused_computation.2.clone | custom fusion | bytes 2097408 | tf_op jit(solution)/shard_map/jit(_take)/gather | solution.py:55
  87.6 2.3 %gather_fusion.5 = f32[64,16,2,128]{3,1,2,0:T(8,128)S(1)} fusion(f32[16,128,2,128]{3,0,2,1:T(8,128)} %copy-done, s32[1024]{0:T(1024)S(1)} %get-tuple-element.49), kind=kCustom, calls=%fused_computation.4.clone | custom fusion | bytes 2097408 | tf_op jit(solution)/shard_map/jit(_take)/gather | solution.py:58
  89.9 2.4 %fusion.23 = (f32[16,64,2,128]{3,0,2,1:T(8,128)S(1)}, f32[16,64,2,128]{3,0,2,1:T(8,128)S(1)}) fusion(f32[64,16,2,128]{3,1,2,0:T(8,128)} %gather_fusion.4, f32[64,16,2,128]{3,1,2,0:T(8,128)} %gather_fusion.3, f32[64,16,2,128]{3,1,2,0:T(8,128)S(1)} %copy-done.4, f32[64,16,2,128]{3,1,2,0:T(8,128)} %gather_fusion.1, f32[2,128]{1,0:T(2,128)S(1)} %copy-done.5, ...), kind=kLoop, calls=%fused_computation.43 | loop fusion | flops 3145728 | bytes 6292608 | tf_op jit(solution)/shard_map/mul | solution.py:60
  97.2 1.3 reshape.159
  98.5 22.9 %reduce-scatter.4.cloned.1.call-done = f32[16,512]{1,0:T(8,128)} async-done(((f32[64,512]{1,0:T(8,128)}), f32[16,512]{1,0:T(8,128)}) %reduce-scatter.4.cloned.1.call-update) | async-done | bytes 32784
  122.4 40.6 %psum.7 = f32[16,2,16,16]{3,2,0,1:T(8,128)S(1)} all-reduce(f32[16,2,16,16]{3,2,0,1:T(8,128)S(1)} %copy.120), channel_id=1, replica_groups=mesh['space'=8,'freq'=4] {'space'}, use_global_device_ids=true, to_apply=%region_3.5 | all-reduce | flops 8192 | bytes 65536 | tf_op jit(solution)/shard_map/psum | solution.py:110
  169.2 5.2 %all_gather.7 = f32[64,2,16]{2,0,1:T(8,128)S(1)} all-gather(f32[16,2,16]{2,0,1:T(8,128)S(1)} %pad_maximum_fusion.2), channel_id=1, replica_groups=mesh['space'=8,'freq'=4] {'freq'}, dimensions={0}, use_global_device_ids=true | all-gather | bytes 10240 | tf_op jit(solution)/shard_map/all_gather | solution.py:113
  179.1 5.1 %all-gather = f32[4,16,2]{1,2,0:T(2,128)S(1)} all-gather(f32[1,16,2]{1,2,0:T(2,128)S(1)} %maximum_bitcast_fusion.2), channel_id=1, replica_groups=mesh['space'=8,'freq'=4] {'freq'}, dimensions={0}, use_global_device_ids=true | all-gather | bytes 640 | tf_op jit(solution)/shard_map/all_gather | solution.py:114
  (90 shorter events, 21.9 us)
Async XLA Ops:
  7.2 114.3 %reduce-scatter.4.cloned.1.call-start = ((), (), s32[]{:S(2)}) async-start(), calls=%async_computation.1 | async-start | bytes 163840
  10.9 8.8 %copy-start.2 = (bf16[2176,2,128]{2,1,0:T(2,128)(2,1)S(1)}, bf16[2176,2,128]{2,1,0:T(2,128)(2,1)}, u32[]{:S(2)}) copy-start(bf16[2176,2,128]{2,1,0:T(2,128)(2,1)} %param.7) | copy-start | bytes 3342340
  11.8 29.0 %collective-permute-start = (bf16[2176,1,128]{2,0,1:T(8,128)(2,1)}, bf16[2176,1,128]{2,0,1:T(8,128)(2,1)}, u32[]{:S(2)}, u32[]{:S(2)}) collective-permute-start(bf16[2176,1,128]{2,0,1:T(8,128)(2,1)} %copy.121), channel_id=1, source_target_pairs={{0,4},{4,8},{8,12},{12,16},{16,20},{20,24},{24,28},{1,5},{5,9},{9,... | collective-permute-start | bytes 1671176 | tf_op jit(solution)/shard_map/ppermute | solution.py:20
  18.4 28.0 %collective-permute-start.1 = (bf16[2176,1,128]{2,0,1:T(8,128)(2,1)}, bf16[2176,1,128]{2,0,1:T(8,128)(2,1)}, u32[]{:S(2)}, u32[]{:S(2)}) collective-permute-start(bf16[2176,1,128]{2,0,1:T(8,128)(2,1)} %copy.122), channel_id=1, source_target_pairs={{4,0},{8,4},{12,8},{16,12},{20,16},{24,20},{28,24},{5,1},{9,5},{13... | collective-permute-start | bytes 1671176 | tf_op jit(solution)/shard_map/ppermute | solution.py:22
  21.8 6.3 %copy-start.7 = (s32[16]{0:T(128)S(1)}, s32[16]{0:T(128)}, u32[]{:S(2)}) copy-start(s32[16]{0:T(128)} %param.10) | copy-start | bytes 196
  21.8 7.5 %copy-start.6 = (s32[64,2]{0,1:T(2,128)S(1)}, s32[64,2]{0,1:T(2,128)}, u32[]{:S(2)}) copy-start(s32[64,2]{0,1:T(2,128)} %param.11) | copy-start | bytes 1540
  23.1 6.3 %collective-permute-start.2 = (bf16[2176,2,1]{0,1,2:T(2,128)(2,1)S(1)}, bf16[2176,2,1]{0,1,2:T(2,128)(2,1)S(1)}, u32[]{:S(2)}, u32[]{:S(2)}) collective-permute-start(bf16[2176,2,1]{0,1,2:T(2,128)(2,1)S(1)} %copy.123), channel_id=1, source_target_pairs={{0,1},{1,2},{2,3},{4,5},{5,6},{6,7},{8,9},{9,10},{10,11},{12,13},{... | collective-permute-start | bytes 26120 | tf_op jit(solution)/shard_map/ppermute | solution.py:20
  25.9 5.1 %collective-permute-start.3 = (bf16[2176,2,1]{0,1,2:T(2,128)(2,1)S(1)}, bf16[2176,2,1]{0,1,2:T(2,128)(2,1)S(1)}, u32[]{:S(2)}, u32[]{:S(2)}) collective-permute-start(bf16[2176,2,1]{0,1,2:T(2,128)(2,1)S(1)} %copy.124), channel_id=1, source_target_pairs={{1,0},{2,1},{3,2},{5,4},{6,5},{7,6},{9,8},{10,9},{11,10},{13,12},{... | collective-permute-start | bytes 26120 | tf_op jit(solution)/shard_map/ppermute | solution.py:22
  38.7 13.3 %copy-start.3 = (bf16[2176,2,128]{2,1,0:T(2,128)(2,1)S(1)}, bf16[2176,2,128]{2,1,0:T(2,128)(2,1)}, u32[]{:S(2)}) copy-start(bf16[2176,2,128]{2,1,0:T(2,128)(2,1)} %param.8) | copy-start | bytes 3342340
  73.3 8.7 %copy-start = (f32[16,128,2,128]{3,0,2,1:T(8,128)}, f32[16,128,2,128]{3,0,2,1:T(8,128)S(1)}, u32[]{:S(2)}) copy-start(f32[16,128,2,128]{3,0,2,1:T(8,128)S(1)} %copy.70) | copy-start | bytes 6291460
  83.6 3.4 %copy-start.1 = (f32[16,128,2,128]{3,0,2,1:T(8,128)S(1)}, f32[16,128,2,128]{3,0,2,1:T(8,128)}, u32[]{:S(2)}) copy-start(f32[16,128,2,128]{3,0,2,1:T(8,128)} %copy.72) | copy-start | bytes 6291460
  86.9 3.0 %copy-start.5 = (f32[2,128]{1,0:T(2,128)S(1)}, f32[2,128]{1,0:T(2,128)}, u32[]{:S(2)}) copy-start(f32[2,128]{1,0:T(2,128)} %param.9) | copy-start | bytes 3076
  87.6 2.3 %copy-start.4 = (f32[64,16,2,128]{3,1,2,0:T(8,128)S(1)}, f32[64,16,2,128]{3,1,2,0:T(8,128)}, u32[]{:S(2)}) copy-start(f32[64,16,2,128]{3,1,2,0:T(8,128)} %gather_fusion.2) | copy-start | bytes 3145732
Sparse Core Ops, SparseCore 0:
  98.6 22.7 reduce-scatter.3
where the time goes:
time: 193 us
  local copies, waits for them, and re-layouts  55.6 us (29%)
  blocking collectives  50.9 us (26%)
  waiting for transfers between devices  25.1 us (13%)
  other arithmetic  18.2 us (9%)
  matrix products  17.5 us (9%)
  between operations  15.3 us (8%)
  starting transfers between devices  9.92 us (5%)
    psum x1, blocking collectives, on_device(): mine = lax.psum(mine, 'space') * scaling  40.6 us
    unnamed x2, waiting for transfers between devices  23 us
    unnamed x26, local copies, waits for them, and re-layouts  7.42 us
    ppermute x2, local copies, waits for them, and re-layouts, with_halo(): lax.ppermute(head, axis, [((i + 1) % count, i) for i in range(ends)])  7.22 us
    ppermute x2, local copies, waits for them, and re-layouts, with_halo(): lax.ppermute(tail, axis, [(i, (i + 1) % count) for i in range(ends)])  7.22 us
    ppermute x2, starting transfers between devices, with_halo(): lax.ppermute(tail, axis, [(i, (i + 1) % count) for i in range(ends)])  7.13 us
    gather x1, local copies, waits for them, and re-layouts, spectra(): lax.dynamic_slice_in_dim(fluct, start, NFFT, 0)  6.47 us
    convert_element_type x1, other arithmetic, on_device(): u_part = with_halo(u_velocity, (('freq', 2),), 1).astype(jnp.float32)  5.99 us
  transfers between devices with their start and end apart: 5, of which 2 were waited for; matrix products, arithmetic and copies ran while one was open for 11% of the time, Pallas kernels for 0%

commit v1 on v0

v1 whole, which is shorter than its diff:
```python
import functools
import math

import jax
import jax.numpy as jnp
import numpy as np
from jax import lax
from jax.experimental import pallas as pl
from jax.experimental.pallas import tpu as pltpu
from jax.sharding import PartitionSpec as P

NFFT = 256
POW = 4
LANES = 128
F32 = jnp.float32
BF16 = jnp.bfloat16
VMEM = pl.BlockSpec(memory_space=pltpu.VMEM)
SMEM = pl.BlockSpec(memory_space=pltpu.SMEM)


def make_table(length):
    half_len = length // 2
    times_idx = np.arange(length)
    phases = np.arange(half_len)[:, None] * times_idx[None, :] % length
    angles = phases * (2.0 * math.pi / length)
    window = 0.5 - 0.5 * np.cos(times_idx * (2.0 * math.pi / length))
    scaling = 1.0 / np.sqrt(np.sum(window * window))
    transform = np.concatenate([np.cos(angles) * scaling, -np.sin(angles) * scaling], axis=0)
    return window.astype(np.float32), transform.astype(np.float32)


def edge_columns(rows, pieces):
    picks = np.zeros((pieces, 2 * pieces, LANES), np.float32)
    places = np.zeros((pieces, 2 * pieces, LANES), np.float32)
    for m in range(pieces):
        picks[m, m, 0] = 1.0
        picks[m, pieces + m, LANES - 1] = 1.0
        places[m, m, 0] = 0.5
        places[m, pieces + m, LANES - 1] = -0.5
    return picks, places


def pack_kernel(sx, pieces, v_ref, u_ref, picks_ref, first_ref, last_ref, cols_ref, plain):
    rows = v_ref.shape[0]
    times = rows // sx
    plain[...] = v_ref[...].astype(F32)
    first_ref[...] = plain[pl.ds(0, times, stride=sx), :].astype(BF16)
    last_ref[...] = plain[pl.ds(sx - 1, times, stride=sx), :].astype(BF16)
    part = rows // pieces
    cols = jnp.zeros((2 * pieces, part), F32)
    for m in range(pieces):
        cols += lax.dot_general(
            picks_ref[m], u_ref[m * part : (m + 1) * part, :], (((1,), (1,)), ((), ())), preferred_element_type=F32
        )
    cols_ref[...] = cols.astype(BF16)


def pack(v, u, picks, sx):
    rows = v.shape[0]
    pieces = picks.shape[0]
    times = rows // sx
    return pl.pallas_call(
        functools.partial(pack_kernel, sx, pieces),
        out_shape=(
            jax.ShapeDtypeStruct((times, LANES), BF16),
            jax.ShapeDtypeStruct((times, LANES), BF16),
            jax.ShapeDtypeStruct((2 * pieces, rows // pieces), BF16),
        ),
        in_specs=[VMEM] * 3,
        out_specs=(VMEM,) * 3,
        scratch_shapes=[pltpu.VMEM((rows, LANES), F32)],
        name="pack",
    )(v, u, picks)


def local_kernel(sx, pieces, v_ref, u_ref, shift_ref, cols_ref, places_ref, z_ref, sum_ref, plain, slope):
    rows = v_ref.shape[0]
    times = rows // sx
    part = rows // pieces
    plain[...] = 0.5 * v_ref[...].astype(F32)
    for m in range(pieces):
        inner = jnp.dot(u_ref[m * part : (m + 1) * part, :], shift_ref[...], preferred_element_type=F32)
        outer = lax.dot_general(
            cols_ref[...], places_ref[m], (((0,), (0,)), ((), ())), preferred_element_type=F32
        )
        slope[m * part : (m + 1) * part, :] = inner + outer
    for row in range(sx):
        z = slope[pl.ds(row, times, stride=sx), :]
        if row + 1 < sx:
            z += plain[pl.ds(row + 1, times, stride=sx), :]
        if row > 0:
            z -= plain[pl.ds(row - 1, times, stride=sx), :]
        z_ref[row] = z
        sum_ref[row] = jnp.sum(z.reshape(times // 8, 8, LANES), axis=0)


def local_part(v, u, shift, cols, places, sx):
    rows = v.shape[0]
    pieces = places.shape[0]
    times = rows // sx
    return pl.pallas_call(
        functools.partial(local_kernel, sx, pieces),
        out_shape=(
            jax.ShapeDtypeStruct((sx, times, LANES), F32),
            jax.ShapeDtypeStruct((sx, 8, LANES), F32),
        ),
        in_specs=[VMEM] * 5,
        out_specs=(VMEM,) * 2,
        scratch_shapes=[pltpu.VMEM((rows, LANES), F32), pltpu.VMEM((rows, LANES), F32)],
        cost_estimate=pl.CostEstimate(flops=1000000000, bytes_accessed=8000000, transcendentals=0),
        name="local",
    )(v, u, shift, cols, places)


def cross_kernel(
    offsets_ref, triads_ref, z_ref, sum_ref, left_ref, right_ref, weights_ref, window_ref, transform_ref,
    cross_ref, target_ref, full, spec, prod, packed,
):
    sx, times, _ = z_ref.shape
    blocks = offsets_ref.shape[0]
    ntri = triads_ref.shape[0]
    half = NFFT // 2
    groups = LANES // blocks
    per = ntri // groups
    wide = 2 * blocks

    chunk = times // 8
    totals = [sum_ref[row] for row in range(sx)]

    def add_halo(step, carry):
        at = pl.ds(pl.multiple_of(step * chunk, 8), chunk)
        low = 0.5 * left_ref[at, :].astype(F32)
        high = 0.5 * right_ref[at, :].astype(F32)
        for row in range(sx):
            z = z_ref[row, at, :]
            if row == 0:
                z -= low
            if row == sx - 1:
                z += high
            full[row, at, :] = z
        return (
            carry[0] + jnp.sum(low.reshape(chunk // 8, 8, LANES), axis=0),
            carry[1] + jnp.sum(high.reshape(chunk // 8, 8, LANES), axis=0),
        )

    zero = jnp.zeros((8, LANES), F32)
    low_sum, high_sum = lax.fori_loop(0, 8, add_halo, (zero, zero))
    totals[0] = totals[0] - low_sum
    totals[sx - 1] = totals[sx - 1] + high_sum
    means = [jnp.sum(total, axis=0, keepdims=True) * (1.0 / times) for total in totals]

    def one_block(b, carry):
        at = pl.ds(offsets_ref[b], NFFT)
        window = window_ref[...]
        for row in range(sx):
            windowed = ((full[row, at, :] - means[row]) * window).astype(BF16)
            out = jnp.dot(transform_ref[...], windowed, preferred_element_type=F32)
            spec[row, pl.ds(b, NFFT, stride=blocks), :] = out
        return carry

    lax.fori_loop(0, blocks, one_block, 0, unroll=2)

    def one_triad(j, carry):
        k = triads_ref[j, 0]
        l = triads_ref[j, 1]

        def take(f, row):
            re = spec[row, pl.ds(pl.multiple_of(f * blocks, 8), blocks), :]
            im = spec[row, pl.ds(pl.multiple_of((f + half) * blocks, 8), blocks), :]
            return re, im

        base = pl.multiple_of(j * wide, 8)
        for row in range(sx):
            lanes = slice(row * LANES, (row + 1) * LANES)
            first_re, first_im = take(k, row)
            second_re, second_im = take(l, row)
            target_re, target_im = take(k + l, row)
            weight = weights_ref[row : row + 1, :]
            prod[pl.ds(base, wide), lanes] = jnp.concatenate(
                [
                    (first_re * second_re - first_im * second_im) * weight,
                    (first_re * second_im + first_im * second_re) * weight,
                ],
                axis=0,
            ).astype(BF16)
            target_ref[pl.ds(base, wide), lanes] = jnp.concatenate([target_re, target_im], axis=0).astype(BF16)
        return carry

    lax.fori_loop(0, ntri, one_triad, 0, unroll=4)

    tall = per * wide
    lane = lax.broadcasted_iota(jnp.int32, (wide, tall), 1)
    owner = lane // wide
    is_re = (lax.broadcasted_iota(jnp.int32, (blocks, tall), 1) % wide) < blocks

    def one_group(g, carry):
        at = pl.ds(pl.multiple_of(g * tall, 8), tall)
        every = lax.dot_general(
            prod[at, :], target_ref[at, :], (((1,), (1,)), ((), ())), preferred_element_type=F32
        )
        kept = every[0:wide]
        for i in range(1, per):
            kept = jnp.where(owner == i, every[i * wide : (i + 1) * wide], kept)
        by_re = kept[0:blocks]
        by_im = kept[blocks:wide]
        ahead = pltpu.roll(by_im, tall - blocks, 1)
        behind = pltpu.roll(by_im, blocks, 1)
        packed[pl.ds(pl.multiple_of(g * blocks, 8), blocks), :] = by_re + jnp.where(is_re, ahead, -behind)
        return carry

    lax.fori_loop(0, groups, one_group, 0, unroll=2)
    cross_ref[...] = packed[...].T


def cross_part(offsets, triads, z, sums, left, right, weights, window, transform):
    sx, times, _ = z.shape
    blocks = offsets.shape[0]
    ntri = triads.shape[0]
    groups = LANES // blocks
    wide = 2 * blocks
    tall = ntri // groups * wide
    return pl.pallas_call(
        cross_kernel,
        out_shape=(
            jax.ShapeDtypeStruct((tall, LANES), F32),
            jax.ShapeDtypeStruct((ntri * wide, sx * LANES), BF16),
        ),
        in_specs=[SMEM, SMEM] + [VMEM] * 7,
        out_specs=(VMEM,) * 2,
        scratch_shapes=[
            pltpu.VMEM((sx, times, LANES), F32),
            pltpu.VMEM((sx, NFFT * blocks, LANES), F32),
            pltpu.VMEM((ntri * wide, sx * LANES), BF16),
            pltpu.VMEM((LANES, tall), F32),
        ],
        name="cross",
    )(offsets, triads, z, sums, left, right, weights, window, transform)


def swap(x, axis, bit):
    count = lax.axis_size(axis)
    return lax.ppermute(x, axis, [(i, i ^ bit) for i in range(count)])


def sum_over(x, axes):
    for axis in axes:
        count = lax.axis_size(axis)
        if count & (count - 1):
            x = lax.psum(x, axis)
            continue
        bit = 1
        while bit < count:
            x = x + swap(x, axis, bit)
            bit *= 2
    return x


def sum_all(x):
    return sum_over(x, ("freq", "space"))


def modes_kernel(blocks, scaling, cross_ref, target_ref, values_ref, modes_ref):
    tall = cross_ref.shape[0]
    wide = 2 * blocks
    per = tall // wide
    groups = LANES // blocks
    sx = target_ref.shape[1] // LANES
    lane = lax.broadcasted_iota(jnp.int32, (per, LANES), 1)
    start = lane - lane % blocks

    mat_re = [cross_ref[pl.ds(c, per, stride=wide), :] * scaling for c in range(blocks)]
    mat_im = [cross_ref[pl.ds(blocks + c, per, stride=wide), :] * scaling for c in range(blocks)]

    def pick(x, index):
        return jnp.take_along_axis(x, index, axis=1)

    spots = [start + c for c in range(blocks)]

    def apply(part_re, part_im):
        sums = []
        for parity in range(2):
            out_re = jnp.zeros((per, LANES), F32)
            out_im = jnp.zeros((per, LANES), F32)
            for c in range(parity, blocks, 2):
                re = pick(part_re, spots[c])
                im = pick(part_im, spots[c])
                out_re += mat_re[c] * re - mat_im[c] * im
                out_im += mat_re[c] * im + mat_im[c] * re
            sums.append((out_re, out_im))
        return sums[0][0] + sums[1][0], sums[0][1] + sums[1][1]

    def over_blocks(x):
        bit = 1
        while bit < blocks:
            x = x + pick(x, lane ^ bit)
            bit *= 2
        return x

    vec_re = jnp.full((per, LANES), 1.0 / math.sqrt(blocks), F32)
    vec_im = jnp.zeros((per, LANES), F32)
    for _ in range(POW):
        out_re, out_im = apply(vec_re, vec_im)
        length = jnp.sqrt(over_blocks(out_re * out_re + out_im * out_im))
        vec_re = out_re / length
        vec_im = out_im / length
    out_re, out_im = apply(vec_re, vec_im)
    value_re = over_blocks(vec_re * out_re + vec_im * out_im)
    value_im = over_blocks(vec_re * out_im - vec_im * out_re)

    source = jnp.minimum(lane // per * blocks, LANES - 1)
    mine = lax.broadcasted_iota(jnp.int32, (per, LANES), 0) == lane % per
    for part, value in enumerate((value_re, value_im)):
        row = jnp.sum(jnp.where(mine, pick(value, source), 0.0), axis=0, keepdims=True)
        values_ref[part : part + 1, :] = row[:, : values_ref.shape[1]]

    tall_re = vec_re.T
    tall_im = vec_im.T
    for g in range(groups):
        for i in range(per):
            j = g * per + i
            col_re = jnp.broadcast_to(tall_re[g * blocks : (g + 1) * blocks, i : i + 1], (blocks, LANES))
            col_im = jnp.broadcast_to(tall_im[g * blocks : (g + 1) * blocks, i : i + 1], (blocks, LANES))
            for row in range(sx):
                lanes = slice(row * LANES, (row + 1) * LANES)
                re = target_ref[j * wide : j * wide + blocks, lanes].astype(F32)
                im = target_ref[j * wide + blocks : (j + 1) * wide, lanes].astype(F32)
                at = 2 * j * sx + row
                modes_ref[at : at + 1, :] = jnp.sum(col_re * re - col_im * im, axis=0, keepdims=True)
                modes_ref[at + sx : at + sx + 1, :] = jnp.sum(col_re * im + col_im * re, axis=0, keepdims=True)


def modes_part(cross, target, blocks, ntri, scaling):
    sx = target.shape[1] // LANES
    return pl.pallas_call(
        functools.partial(modes_kernel, blocks, scaling),
        out_shape=(
            jax.ShapeDtypeStruct((2, ntri), F32),
            jax.ShapeDtypeStruct((ntri * 2 * sx, LANES), F32),
        ),
        in_specs=[VMEM] * 2,
        out_specs=(VMEM,) * 2,
        name="modes",
    )(cross, target)


def neighbours(low, high, axis):
    ends = lax.axis_size(axis) - 1
    return (
        lax.ppermute(high, axis, [(i, i + 1) for i in range(ends)]),
        lax.ppermute(low, axis, [(i + 1, i) for i in range(ends)]),
    )


def on_device(u_velocity, v_velocity, cell_weights, block_offsets, triads):
    times, sx, columns = u_velocity.shape
    blocks = block_offsets.shape[0]
    ntri = triads.shape[0]
    cells = sx * columns * lax.axis_size("space") * lax.axis_size("freq")
    scaling = 1.0 / (blocks * math.sqrt(cells))
    pieces = 8
    window, transform = make_table(NFFT)
    picks, places = edge_columns(times * sx, pieces)
    shift = 0.5 * (np.eye(LANES, k=1, dtype=np.float32) - np.eye(LANES, k=-1, dtype=np.float32))
    v = v_velocity.reshape(times * sx, columns)
    u = u_velocity.reshape(times * sx, columns)

    first, last, cols = pack(v, u, jnp.asarray(picks, BF16), sx)
    left, right = neighbours(first, last, "space")
    col_left, col_right = neighbours(cols[:pieces], cols[pieces:], "freq")
    z, sums = local_part(
        v, u, jnp.asarray(shift, BF16), jnp.concatenate([col_left, col_right], axis=0), jnp.asarray(places, BF16), sx
    )
    share, target = cross_part(
        block_offsets, triads, z, sums, left, right, cell_weights,
        jnp.asarray(np.broadcast_to(window[:, None], (NFFT, LANES))), jnp.asarray(transform, BF16),
    )
    cross = sum_all(share)
    values, modes = modes_part(cross, target, blocks, ntri, scaling)
    return (values.T, modes.reshape(ntri, 2, sx, columns))


def solution(mesh):
    return jax.shard_map(
        on_device,
        mesh=mesh,
        in_specs=(P(None, "space", "freq"), P(None, "space", "freq"), P("space", "freq"), P(), P()),
        out_specs=(P(), P(None, None, "space", "freq")),
        check_vma=False,
    )
```

time: 193 us -> 75.8 us (0.39)
  local copies, waits for them, and re-layouts: 55.6 us -> 2.45 us
  blocking collectives: 50.9 us -> 0 us
  Pallas kernels: 0 us -> 20.8 us
  matrix products: 17.5 us -> 0 us
  other arithmetic: 18.2 us -> 2.25 us
  between operations: 15.3 us -> 0.7 us
  starting transfers between devices: 9.92 us -> 19.4 us
  waiting for transfers between devices: 25.1 us -> 29.9 us
    psum x1 -> x0, blocking collectives: 40.6 us -> none  [on_device(): mine = lax.psum(mine, 'space') * scaling]
    ppermute x4 -> x9, waiting for transfers between devices: 2.14 us -> 29.9 us  [the longest x5 15.8 us: swap(): return lax.ppermute(x, axis, [(i, i ^ bit) for i in range(count)])]
    unnamed x2 -> x0, waiting for transfers between devices: 23 us -> none
    pallas_call x0 -> x4, Pallas kernels: none -> 20.8 us  [the longest x1 9.03 us: cross_part(): pl.pallas_call(cross_kernel, out_shape=(jax.ShapeDtypeStruct((tall, LANES...]
    gather x7 -> x0, local copies, waits for them, and re-layouts: 19.2 us -> none  [the longest x1 6.47 us: spectra(): lax.dynamic_slice_in_dim(fluct, start, NFFT, 0)]
    dot_general x29 -> x0, matrix products: 17.5 us -> none  [the longest x1 3.03 us: spectra(): jnp.einsum('ft,btxy->bfxy', transform, windowed, preferred_element_type=j...]
    ppermute x4 -> x0, local copies, waits for them, and re-layouts: 14.4 us -> none  [the longest x2 7.22 us: with_halo(): lax.ppermute(head, axis, [((i + 1) % count, i) for i in range(ends)])]
    slice x6 -> x1, local copies, waits for them, and re-layouts: 14.6 us -> 0.73 us  [on_device(): col_left, col_right = neighbours(cols[:pieces], cols[pieces:], 'freq')]
  transfers between devices with their start and end apart: 5 -> 9, of which waited for: 2 -> 7; matrix products, arithmetic and copies ran while one was open for 11% -> 3% of each run, Pallas kernels for 0% -> 5%
where the time goes in v1:
time: 75.8 us; the launch traced here: 75.5 us
  waiting for transfers between devices  29.9 us (39%)
  Pallas kernels  20.8 us (27%)
  starting transfers between devices  19.4 us (26%)
  local copies, waits for them, and re-layouts  2.45 us (3%)
  other arithmetic  2.25 us (3%)
    ppermute x5, waiting for transfers between devices, swap(): return lax.ppermute(x, axis, [(i, i ^ bit) for i in range(count)])  15.8 us
    ppermute x2, waiting for transfers between devices, neighbours(): lax.ppermute(high, axis, [(i, i + 1) for i in range(ends)])  11.4 us
    ppermute x5, starting transfers between devices, swap(): return lax.ppermute(x, axis, [(i, i ^ bit) for i in range(count)])  10.4 us
    pallas_call x1, Pallas kernels, cross_part(): pl.pallas_call(cross_kernel, out_shape=(jax.ShapeDtypeStruct((tall, LANES...  9.03 us
    ppermute x2, starting transfers between devices, neighbours(): lax.ppermute(high, axis, [(i, i + 1) for i in range(ends)])  6.34 us
    pallas_call x1, Pallas kernels, modes_part(): pl.pallas_call(functools.partial(modes_kernel, blocks, scaling), out_shap...  4.76 us
    pallas_call x1, Pallas kernels, local_part(): pl.pallas_call(functools.partial(local_kernel, sx, pieces), out_shape=(ja...  3.94 us
    pallas_call x1, Pallas kernels, pack(): pl.pallas_call(functools.partial(pack_kernel, sx, pieces), out_shape=(jax...  3.07 us
  transfers between devices with their start and end apart: 9, of which 7 were waited for; matrix products, arithmetic and copies ran while one was open for 3% of the time, Pallas kernels for 5%

profile of v1, /device:TPU:0, one launch (start us, length us, event | category | flops | bytes accessed | tf_op | source)
XLA Modules:
  0.0 75.5 jit_solution(16753298763074561331)
XLA Ops:
  0.6 0.0 copy-start.3
  0.6 3.1 %pack.1 = (bf16[2176,128]{1,0:T(8,128)(2,1)}, bf16[2176,128]{1,0:T(8,128)(2,1)}, bf16[16,544]{1,0:T(8,128)(2,1)}) custom-call(bf16[4352,128]{1,0:T(8,128)(2,1)} %bitcast.4, bf16[4352,128]{1,0:T(8,128)(2,1)} %bitcast.6, bf16[8,16,128]{2,1,0:T(8,128)(2,1)} %constant.10.clone.picks_ref), custom_call_target="tpu_custom_call" | custom-call | tf_op jit(solution)/shard_map/pack/pallas_call | solution.py:62
  3.7 4.9 %collective-permute-start.2 = (bf16[2176,128]{1,0:T(8,128)(2,1)}, bf16[2176,128]{1,0:T(8,128)(2,1)S(1)}, u32[]{:S(2)}, u32[]{:S(2)}) collective-permute-start(bf16[2176,128]{1,0:T(8,128)(2,1)} %get-tuple-element.14), channel_id=1, source_target_pairs={{0,4},{4,8},{8,12},{12,16},{16,20},{20,24},{24,28},{1,5},{5,9},{9,... | collective-permute-start | bytes 1671176 | tf_op jit(solution)/shard_map/ppermute | solution.py:349
  8.6 1.3 %collective-permute-start.3 = (bf16[2176,128]{1,0:T(8,128)(2,1)}, bf16[2176,128]{1,0:T(8,128)(2,1)S(1)}, u32[]{:S(2)}, u32[]{:S(2)}) collective-permute-start(bf16[2176,128]{1,0:T(8,128)(2,1)} %get-tuple-element.15), channel_id=1, source_target_pairs={{4,0},{8,4},{12,8},{16,12},{20,16},{24,20},{28,24},{5,1},{9,5},{13... | collective-permute-start | bytes 1671176 | tf_op jit(solution)/shard_map/ppermute | solution.py:350
  9.9 0.7 fusion
  10.6 1.4 %collective-permute-start = (bf16[8,544]{1,0:T(8,128)(2,1)S(1)}, bf16[8,544]{1,0:T(8,128)(2,1)S(1)}, u32[]{:S(2)}, u32[]{:S(2)}) collective-permute-start(bf16[8,544]{1,0:T(8,128)(2,1)S(1)} %get-tuple-element.20), channel_id=1, source_target_pairs={{0,1},{1,2},{2,3},{4,5},{5,6},{6,7},{8,9},{9,10},{10,11},{12,13},{... | collective-permute-start | bytes 26120 | tf_op jit(solution)/shard_map/ppermute | solution.py:349
  12.1 1.3 %collective-permute-start.1 = (bf16[8,544]{1,0:T(8,128)(2,1)S(1)}, bf16[8,544]{1,0:T(8,128)(2,1)S(1)}, u32[]{:S(2)}, u32[]{:S(2)}) collective-permute-start(bf16[8,544]{1,0:T(8,128)(2,1)S(1)} %get-tuple-element.21), channel_id=1, source_target_pairs={{1,0},{2,1},{3,2},{5,4},{6,5},{7,6},{9,8},{10,9},{11,10},{13,12},{... | collective-permute-start | bytes 26120 | tf_op jit(solution)/shard_map/ppermute | solution.py:350
  13.4 0.0 copy-done.3
  13.4 0.7 copy.12.triads_ref
  14.1 0.0 collective-permute-done
  14.1 2.6 %collective-permute-done.1 = bf16[8,544]{1,0:T(8,128)(2,1)S(1)} collective-permute-done((bf16[8,544]{1,0:T(8,128)(2,1)S(1)}, bf16[8,544]{1,0:T(8,128)(2,1)S(1)}, u32[]{:S(2)}, u32[]{:S(2)}) %collective-permute-start.1) | collective-permute-done | bytes 8736 | tf_op jit(solution)/shard_map/ppermute | solution.py:350
  16.7 0.6 pad_maximum_fusion.cols_ref
  17.4 3.9 %local.1 = (f32[2,2176,128]{2,1,0:T(8,128)}, f32[2,8,128]{2,1,0:T(8,128)}) custom-call(bf16[4352,128]{1,0:T(8,128)(2,1)} %bitcast.5, bf16[4352,128]{1,0:T(8,128)(2,1)} %bitcast.7, bf16[128,128]{1,0:T(8,128)(2,1)} %constant.11.clone.shift_ref, bf16[16,544]{1,0:T(8,128)(2,1)} %pad_maximum_fusion.cols_ref, bf16[8,16,128]{2,1,0:T(8,128)(2,1)} %constant.12.clone.places_ref), custom_call_target="tpu_custom_call" | custom-call | flops 1000000000 | bytes 8000000 | tf_op jit(solution)/shard_map/local/pallas_call | solution.py:101
  21.3 11.4 %collective-permute-done.2.left_ref = bf16[2176,128]{1,0:T(8,128)(2,1)S(1)} collective-permute-done((bf16[2176,128]{1,0:T(8,128)(2,1)}, bf16[2176,128]{1,0:T(8,128)(2,1)S(1)}, u32[]{:S(2)}, u32[]{:S(2)}) %collective-permute-start.2) | collective-permute-done | bytes 557088 | tf_op jit(solution)/shard_map/ppermute | solution.py:349
  32.7 0.0 collective-permute-done.3.right_ref
  32.7 0.9 %jit_solution_.3.window_ref = f32[256,128]{1,0:T(8,128)} broadcast(f32[256]{0:T(256)S(1)} %copy-done.2), dimensions={0} | broadcast | bytes 132096 | tf_op jit(solution)
  33.6 0.0 copy-done
  33.6 0.1 copy-done.1
  33.7 9.0 %cross.1 = (f32[256,128]{1,0:T(8,128)}, bf16[2048,256]{1,0:T(8,128)(2,1)}) custom-call(s32[16]{0:T(128)} %offsets_ref.1, s32[64,2]{1,0:T(8,128)} %copy.12.triads_ref, f32[2,2176,128]{2,1,0:T(8,128)} %get-tuple-element.12.z_ref, f32[2,8,128]{2,1,0:T(8,128)} %get-tuple-element.13.sum_ref, bf16[2176,128]{1,0:T(8,128)(2,1)} %copy-done, ...), custom_call_target="tpu_custom_call" | custom-call | tf_op jit(solution)/shard_map/cross/pallas_call | solution.py:222
  42.7 0.0 collective-permute-start.4
  42.8 1.6 %collective-permute-done.4 = f32[256,128]{1,0:T(8,128)S(1)} collective-permute-done((f32[256,128]{1,0:T(8,128)}, f32[256,128]{1,0:T(8,128)S(1)}, u32[]{:S(2)}, u32[]{:S(2)}) %collective-permute-start.4) | collective-permute-done | bytes 131104 | tf_op jit(solution)/shard_map/ppermute | solution.py:242
  44.3 0.9 %add.15 = f32[256,128]{1,0:T(8,128)S(1)} add(f32[256,128]{1,0:T(8,128)} %get-tuple-element.16, f32[256,128]{1,0:T(8,128)S(1)} %collective-permute-done.4) | non-fusion elementwise | flops 32768 | bytes 393216 | tf_op jit(solution)/shard_map/add | solution.py:253
  45.2 1.6 %collective-permute-start.5 = (f32[256,128]{1,0:T(8,128)S(1)}, f32[256,128]{1,0:T(8,128)S(1)}, u32[]{:S(2)}, u32[]{:S(2)}) collective-permute-start(f32[256,128]{1,0:T(8,128)S(1)} %add.15), channel_id=1, source_target_pairs={{0,2},{1,3},{2,0},{3,1},{4,6},{5,7},{6,4},{7,5},{8,10},{9,11},{10,... | collective-permute-start | bytes 393224 | tf_op jit(solution)/shard_map/ppermute | solution.py:242
  46.8 4.0 %collective-permute-done.5 = f32[256,128]{1,0:T(8,128)S(1)} collective-permute-done((f32[256,128]{1,0:T(8,128)S(1)}, f32[256,128]{1,0:T(8,128)S(1)}, u32[]{:S(2)}, u32[]{:S(2)}) %collective-permute-start.5) | collective-permute-done | bytes 131104 | tf_op jit(solution)/shard_map/ppermute | solution.py:242
  50.9 2.4 %collective-permute-start.6 = (f32[256,128]{1,0:T(8,128)S(1)}, f32[256,128]{1,0:T(8,128)S(1)}, u32[]{:S(2)}, u32[]{:S(2)}) collective-permute-start(f32[256,128]{1,0:T(8,128)S(1)} %add.16), channel_id=1, source_target_pairs={{0,4},{4,0},{8,12},{12,8},{16,20},{20,16},{24,28},{28,24},{1,5},{5... | collective-permute-start | bytes 393224 | tf_op jit(solution)/shard_map/ppermute | solution.py:242
  53.3 3.0 %collective-permute-done.6 = f32[256,128]{1,0:T(8,128)S(1)} collective-permute-done((f32[256,128]{1,0:T(8,128)S(1)}, f32[256,128]{1,0:T(8,128)S(1)}, u32[]{:S(2)}, u32[]{:S(2)}) %collective-permute-start.6) | collective-permute-done | bytes 131104 | tf_op jit(solution)/shard_map/ppermute | solution.py:242
  56.3 2.9 %collective-permute-start.7 = (f32[256,128]{1,0:T(8,128)S(1)}, f32[256,128]{1,0:T(8,128)S(1)}, u32[]{:S(2)}, u32[]{:S(2)}) collective-permute-start(f32[256,128]{1,0:T(8,128)S(1)} %add.17), channel_id=1, source_target_pairs={{0,8},{4,12},{8,0},{12,4},{16,24},{20,28},{24,16},{28,20},{1,9},{5... | collective-permute-start | bytes 393224 | tf_op jit(solution)/shard_map/ppermute | solution.py:242
  59.2 2.9 %collective-permute-done.7 = f32[256,128]{1,0:T(8,128)S(1)} collective-permute-done((f32[256,128]{1,0:T(8,128)S(1)}, f32[256,128]{1,0:T(8,128)S(1)}, u32[]{:S(2)}, u32[]{:S(2)}) %collective-permute-start.7) | collective-permute-done | bytes 131104 | tf_op jit(solution)/shard_map/ppermute | solution.py:242
  62.1 3.5 %collective-permute-start.8 = (f32[256,128]{1,0:T(8,128)S(1)}, f32[256,128]{1,0:T(8,128)S(1)}, u32[]{:S(2)}, u32[]{:S(2)}) collective-permute-start(f32[256,128]{1,0:T(8,128)S(1)} %add.18), channel_id=1, source_target_pairs={{0,16},{4,20},{8,24},{12,28},{16,0},{20,4},{24,8},{28,12},{1,17},{... | collective-permute-start | bytes 393224 | tf_op jit(solution)/shard_map/ppermute | solution.py:242
  65.7 4.4 %collective-permute-done.8 = f32[256,128]{1,0:T(8,128)S(1)} collective-permute-done((f32[256,128]{1,0:T(8,128)S(1)}, f32[256,128]{1,0:T(8,128)S(1)}, u32[]{:S(2)}, u32[]{:S(2)}) %collective-permute-start.8) | collective-permute-done | bytes 131104 | tf_op jit(solution)/shard_map/ppermute | solution.py:242
  70.0 0.7 add.19.cross_ref
  70.7 4.8 %modes.1 = (f32[2,64]{1,0:T(2,128)}, f32[256,128]{1,0:T(8,128)}) custom-call(f32[256,128]{1,0:T(8,128)} %add.19.cross_ref, bf16[2048,256]{1,0:T(8,128)(2,1)} %get-tuple-element.17.target_ref), custom_call_target="tpu_custom_call" | custom-call | tf_op jit(solution)/shard_map/modes/pallas_call | solution.py:334
  (7 shorter events, 0.1 us)
Async XLA Ops:
  0.6 12.8 %copy-start.3 = (s32[64,2]{0,1:T(2,128)S(1)}, s32[64,2]{0,1:T(2,128)}, u32[]{:S(2)}) copy-start(s32[64,2]{0,1:T(2,128)} %param.14) | copy-start | bytes 1540
  3.7 29.0 %collective-permute-start.2 = (bf16[2176,128]{1,0:T(8,128)(2,1)}, bf16[2176,128]{1,0:T(8,128)(2,1)S(1)}, u32[]{:S(2)}, u32[]{:S(2)}) collective-permute-start(bf16[2176,128]{1,0:T(8,128)(2,1)} %get-tuple-element.14), channel_id=1, source_target_pairs={{0,4},{4,8},{8,12},{12,16},{16,20},{20,24},{24,28},{1,5},{5,9},{9,... | collective-permute-start | bytes 1671176 | tf_op jit(solution)/shard_map/ppermute | solution.py:349
  8.6 24.1 %collective-permute-start.3 = (bf16[2176,128]{1,0:T(8,128)(2,1)}, bf16[2176,128]{1,0:T(8,128)(2,1)S(1)}, u32[]{:S(2)}, u32[]{:S(2)}) collective-permute-start(bf16[2176,128]{1,0:T(8,128)(2,1)} %get-tuple-element.15), channel_id=1, source_target_pairs={{4,0},{8,4},{12,8},{16,12},{20,16},{24,20},{28,24},{5,1},{9,5},{13... | collective-permute-start | bytes 1671176 | tf_op jit(solution)/shard_map/ppermute | solution.py:350
  10.6 3.5 %collective-permute-start = (bf16[8,544]{1,0:T(8,128)(2,1)S(1)}, bf16[8,544]{1,0:T(8,128)(2,1)S(1)}, u32[]{:S(2)}, u32[]{:S(2)}) collective-permute-start(bf16[8,544]{1,0:T(8,128)(2,1)S(1)} %get-tuple-element.20), channel_id=1, source_target_pairs={{0,1},{1,2},{2,3},{4,5},{5,6},{6,7},{8,9},{9,10},{10,11},{12,13},{... | collective-permute-start | bytes 26120 | tf_op jit(solution)/shard_map/ppermute | solution.py:349
  12.1 4.7 %collective-permute-start.1 = (bf16[8,544]{1,0:T(8,128)(2,1)S(1)}, bf16[8,544]{1,0:T(8,128)(2,1)S(1)}, u32[]{:S(2)}, u32[]{:S(2)}) collective-permute-start(bf16[8,544]{1,0:T(8,128)(2,1)S(1)} %get-tuple-element.21), channel_id=1, source_target_pairs={{1,0},{2,1},{3,2},{5,4},{6,5},{7,6},{9,8},{10,9},{11,10},{13,12},{... | collective-permute-start | bytes 26120 | tf_op jit(solution)/shard_map/ppermute | solution.py:350
  17.4 15.3 %copy-start.2 = (f32[256]{0:T(256)S(1)}, f32[256]{0:T(256)}, u32[]{:S(2)}) copy-start(f32[256]{0:T(256)} %constant.13.clone) | copy-start | bytes 3076
  32.7 0.9 %copy-start = (bf16[2176,128]{1,0:T(8,128)(2,1)}, bf16[2176,128]{1,0:T(8,128)(2,1)S(1)}, u32[]{:S(2)}) copy-start(bf16[2176,128]{1,0:T(8,128)(2,1)S(1)} %collective-permute-done.2.left_ref) | copy-start | bytes 1671172
  32.7 1.0 %copy-start.1 = (bf16[2176,128]{1,0:T(8,128)(2,1)}, bf16[2176,128]{1,0:T(8,128)(2,1)S(1)}, u32[]{:S(2)}) copy-start(bf16[2176,128]{1,0:T(8,128)(2,1)S(1)} %collective-permute-done.3.right_ref) | copy-start | bytes 1671172
  42.7 1.6 %collective-permute-start.4 = (f32[256,128]{1,0:T(8,128)}, f32[256,128]{1,0:T(8,128)S(1)}, u32[]{:S(2)}, u32[]{:S(2)}) collective-permute-start(f32[256,128]{1,0:T(8,128)} %get-tuple-element.16), channel_id=1, source_target_pairs={{0,1},{1,0},{2,3},{3,2},{4,5},{5,4},{6,7},{7,6},{8,9},{9,8},{10,11... | collective-permute-start | bytes 393224 | tf_op jit(solution)/shard_map/ppermute | solution.py:242
  45.2 5.6 %collective-permute-start.5 = (f32[256,128]{1,0:T(8,128)S(1)}, f32[256,128]{1,0:T(8,128)S(1)}, u32[]{:S(2)}, u32[]{:S(2)}) collective-permute-start(f32[256,128]{1,0:T(8,128)S(1)} %add.15), channel_id=1, source_target_pairs={{0,2},{1,3},{2,0},{3,1},{4,6},{5,7},{6,4},{7,5},{8,10},{9,11},{10,... | collective-permute-start | bytes 393224 | tf_op jit(solution)/shard_map/ppermute | solution.py:242
  50.9 5.4 %collective-permute-start.6 = (f32[256,128]{1,0:T(8,128)S(1)}, f32[256,128]{1,0:T(8,128)S(1)}, u32[]{:S(2)}, u32[]{:S(2)}) collective-permute-start(f32[256,128]{1,0:T(8,128)S(1)} %add.16), channel_id=1, source_target_pairs={{0,4},{4,0},{8,12},{12,8},{16,20},{20,16},{24,28},{28,24},{1,5},{5... | collective-permute-start | bytes 393224 | tf_op jit(solution)/shard_map/ppermute | solution.py:242
  56.3 5.8 %collective-permute-start.7 = (f32[256,128]{1,0:T(8,128)S(1)}, f32[256,128]{1,0:T(8,128)S(1)}, u32[]{:S(2)}, u32[]{:S(2)}) collective-permute-start(f32[256,128]{1,0:T(8,128)S(1)} %add.17), channel_id=1, source_target_pairs={{0,8},{4,12},{8,0},{12,4},{16,24},{20,28},{24,16},{28,20},{1,9},{5... | collective-permute-start | bytes 393224 | tf_op jit(solution)/shard_map/ppermute | solution.py:242
  62.1 7.9 %collective-permute-start.8 = (f32[256,128]{1,0:T(8,128)S(1)}, f32[256,128]{1,0:T(8,128)S(1)}, u32[]{:S(2)}, u32[]{:S(2)}) collective-permute-start(f32[256,128]{1,0:T(8,128)S(1)} %add.18), channel_id=1, source_target_pairs={{0,16},{4,20},{8,24},{12,28},{16,0},{20,4},{24,8},{28,12},{1,17},{... | collective-permute-start | bytes 393224 | tf_op jit(solution)/shard_map/ppermute | solution.py:242

commit v2 on v1

v2 whole, which is shorter than its diff:
```python
import functools
import math

import jax
import jax.numpy as jnp
import numpy as np
from jax import lax
from jax.experimental import pallas as pl
from jax.experimental.pallas import tpu as pltpu
from jax.sharding import PartitionSpec as P

NFFT = 256
POW = 4
NEAR_STEPS = 2
LANES = 128
F32 = jnp.float32
BF16 = jnp.bfloat16
MIB = 2**20
VMEM = pl.BlockSpec(memory_space=pltpu.VMEM)
SMEM = pl.BlockSpec(memory_space=pltpu.SMEM)


def make_table(length):
    half_len = length // 2
    times_idx = np.arange(length)
    phases = np.arange(half_len)[:, None] * times_idx[None, :] % length
    angles = phases * (2.0 * math.pi / length)
    window = 0.5 - 0.5 * np.cos(times_idx * (2.0 * math.pi / length))
    scaling = 1.0 / np.sqrt(np.sum(window * window))
    transform = np.concatenate([np.cos(angles) * scaling, -np.sin(angles) * scaling], axis=0)
    return window.astype(np.float32), transform.astype(np.float32)


def edge_columns(rows, pieces):
    picks = np.zeros((pieces, 2 * pieces, LANES), np.float32)
    places = np.zeros((pieces, 2 * pieces, LANES), np.float32)
    for m in range(pieces):
        picks[m, m, 0] = 1.0
        picks[m, pieces + m, LANES - 1] = 1.0
        places[m, m, 0] = 0.5
        places[m, pieces + m, LANES - 1] = -0.5
    return picks, places


def is_odd():
    return lax.axis_index("space") % 2


def row_at(position, sx, odd):
    return jnp.where(odd == 1, position, sx - 1 - position)


def limit(mib):
    return pltpu.CompilerParams(vmem_limit_bytes=mib * MIB)


def near_kernel(sx, odd_ref, v_ref, near_ref, plain):
    times = near_ref.shape[0]
    plain[...] = v_ref[...].astype(F32)
    near_ref[...] = plain[pl.ds(row_at(0, sx, odd_ref[0]), times, stride=sx), :].astype(BF16)


def near_edge(odd, v, sx):
    rows = v.shape[0]
    steps = NEAR_STEPS
    return pl.pallas_call(
        functools.partial(near_kernel, sx),
        grid=(steps,),
        out_shape=jax.ShapeDtypeStruct((rows // sx, LANES), BF16),
        in_specs=[SMEM, pl.BlockSpec((rows // steps, LANES), lambda i: (i, 0))],
        out_specs=pl.BlockSpec((rows // sx // steps, LANES), lambda i: (i, 0)),
        scratch_shapes=[pltpu.VMEM((rows // steps, LANES), F32)],
        compiler_params=limit(8),
        name="near",
    )(odd, v)


def far_kernel(sx, pieces, odd_ref, v_ref, u_ref, picks_ref, far_ref, low_ref, high_ref, plain):
    rows = v_ref.shape[0]
    times = rows // sx
    plain[...] = v_ref[...].astype(F32)
    far_ref[...] = plain[pl.ds(row_at(sx - 1, sx, odd_ref[0]), times, stride=sx), :].astype(BF16)
    part = rows // pieces
    cols = jnp.zeros((2 * pieces, part), F32)
    for m in range(pieces):
        cols += lax.dot_general(
            picks_ref[m], u_ref[m * part : (m + 1) * part, :], (((1,), (1,)), ((), ())), preferred_element_type=F32
        )
    low_ref[...] = cols[:pieces].astype(BF16)
    high_ref[...] = cols[pieces:].astype(BF16)


def far_edge(odd, v, u, picks, sx):
    rows = v.shape[0]
    pieces = picks.shape[0]
    times = rows // sx
    return pl.pallas_call(
        functools.partial(far_kernel, sx, pieces),
        out_shape=(
            jax.ShapeDtypeStruct((times, LANES), BF16),
            jax.ShapeDtypeStruct((pieces, rows // pieces), BF16),
            jax.ShapeDtypeStruct((pieces, rows // pieces), BF16),
        ),
        in_specs=[SMEM] + [VMEM] * 3,
        out_specs=(VMEM,) * 3,
        scratch_shapes=[pltpu.VMEM((rows, LANES), F32)],
        compiler_params=limit(12),
        cost_estimate=pl.CostEstimate(flops=200000000, bytes_accessed=4000000, transcendentals=0),
        name="far",
    )(odd, v, u, picks)


def local_kernel(
    sx, pieces, odd_ref, v_ref, u_ref, shift_ref, low_ref, high_ref, places_ref, z_ref, sum_ref, plain, slope
):
    rows = v_ref.shape[0]
    times = rows // sx
    part = rows // pieces
    odd = odd_ref[0]
    sign = jnp.where(odd == 1, 0.5, -0.5)
    plain[...] = sign * v_ref[...].astype(F32)
    cols = jnp.concatenate([low_ref[...], high_ref[...]], axis=0)
    for m in range(pieces):
        inner = jnp.dot(u_ref[m * part : (m + 1) * part, :], shift_ref[...], preferred_element_type=F32)
        outer = lax.dot_general(cols, places_ref[m], (((0,), (0,)), ((), ())), preferred_element_type=F32)
        slope[m * part : (m + 1) * part, :] = inner + outer
    for position in range(sx):
        z = slope[pl.ds(row_at(position, sx, odd), times, stride=sx), :]
        if position + 1 < sx:
            z += plain[pl.ds(row_at(position + 1, sx, odd), times, stride=sx), :]
        if position > 0:
            z -= plain[pl.ds(row_at(position - 1, sx, odd), times, stride=sx), :]
        z_ref[position] = z
        sum_ref[position] = jnp.sum(z.reshape(times // 8, 8, LANES), axis=0)


def local_part(odd, v, u, shift, low, high, places, sx):
    rows = v.shape[0]
    pieces = places.shape[0]
    times = rows // sx
    return pl.pallas_call(
        functools.partial(local_kernel, sx, pieces),
        out_shape=(
            jax.ShapeDtypeStruct((sx, times, LANES), F32),
            jax.ShapeDtypeStruct((sx, 8, LANES), F32),
        ),
        in_specs=[SMEM] + [VMEM] * 6,
        out_specs=(VMEM,) * 2,
        scratch_shapes=[pltpu.VMEM((rows, LANES), F32), pltpu.VMEM((rows, LANES), F32)],
        compiler_params=limit(20),
        cost_estimate=pl.CostEstimate(flops=1000000000, bytes_accessed=8000000, transcendentals=0),
        name="local",
    )(odd, v, u, shift, low, high, places)


def cross_kernel(
    sx, begin, odd_ref, offsets_ref, triads_ref, z_ref, sum_ref, halo_ref, weights_ref, window_ref, transform_ref,
    *rest,
):
    far = begin > 0
    if far:
        before_ref, cross_ref, target_ref, full, spec, prod, packed = rest
    else:
        cross_ref, target_ref, full, spec, prod, packed = rest
    count, times, _ = full.shape
    blocks = offsets_ref.shape[0]
    ntri = triads_ref.shape[0]
    half = NFFT // 2
    groups = LANES // blocks
    per = ntri // groups
    wide = 2 * blocks
    pitch = blocks + 1
    odd = odd_ref[0]
    sign = jnp.where(odd == 1, 0.5, -0.5)
    if not far:
        sign = -sign
    touched = count - 1 if far else 0

    chunk = times // 8

    def add_halo(step, carry):
        at = pl.ds(pl.multiple_of(step * chunk, 8), chunk)
        halo = sign * halo_ref[at, :].astype(F32)
        for row in range(count):
            z = z_ref[begin + row, at, :]
            full[row, at, :] = z + halo if row == touched else z
        return carry + jnp.sum(halo.reshape(chunk // 8, 8, LANES), axis=0)

    halo_sum = lax.fori_loop(0, 8, add_halo, jnp.zeros((8, LANES), F32))
    means = []
    for row in range(count):
        total = sum_ref[begin + row]
        if row == touched:
            total = total + halo_sum
        means.append(jnp.sum(total, axis=0, keepdims=True) * (1.0 / times))

    def one_block(b, carry):
        at = pl.ds(offsets_ref[b], NFFT)
        window = window_ref[...]
        for row in range(count):
            windowed = ((full[row, at, :] - means[row]) * window).astype(BF16)
            out = jnp.dot(transform_ref[...], windowed, preferred_element_type=F32)
            spec[row, pl.ds(b, NFFT, stride=pitch), :] = out
        return carry

    lax.fori_loop(0, blocks, one_block, 0, unroll=True)
    weights = [weights_ref[pl.ds(row_at(begin + row, sx, odd), 1), :] for row in range(count)]

    def one_triad(j, carry):
        k = triads_ref[j, 0]
        l = triads_ref[j, 1]

        def take(f, row):
            re = spec[row, pl.ds(f * pitch, blocks), :]
            im = spec[row, pl.ds((f + half) * pitch, blocks), :]
            return re, im

        base = pl.multiple_of(j * wide, 8)
        for row in range(count):
            lanes = slice(row * LANES, (row + 1) * LANES)
            first_re, first_im = take(k, row)
            second_re, second_im = take(l, row)
            target_re, target_im = take(k + l, row)
            weight = weights[row]
            prod[pl.ds(base, wide), lanes] = jnp.concatenate(
                [
                    (first_re * second_re - first_im * second_im) * weight,
                    (first_re * second_im + first_im * second_re) * weight,
                ],
                axis=0,
            ).astype(BF16)
            target_ref[pl.ds(base, wide), lanes] = jnp.concatenate([target_re, target_im], axis=0).astype(BF16)
        return carry

    lax.fori_loop(0, ntri, one_triad, 0, unroll=4)

    tall = per * wide
    lane = lax.broadcasted_iota(jnp.int32, (wide, tall), 1)
    owner = lane // wide
    is_re = (lax.broadcasted_iota(jnp.int32, (blocks, tall), 1) % wide) < blocks

    def one_group(g, carry):
        at = pl.ds(pl.multiple_of(g * tall, 8), tall)
        every = lax.dot_general(
            prod[at, :], target_ref[at, :], (((1,), (1,)), ((), ())), preferred_element_type=F32
        )
        kept = every[0:wide]
        for i in range(1, per):
            kept = jnp.where(owner == i, every[i * wide : (i + 1) * wide], kept)
        by_re = kept[0:blocks]
        by_im = kept[blocks:wide]
        ahead = pltpu.roll(by_im, tall - blocks, 1)
        behind = pltpu.roll(by_im, blocks, 1)
        packed[pl.ds(pl.multiple_of(g * blocks, 8), blocks), :] = by_re + jnp.where(is_re, ahead, -behind)
        return carry

    lax.fori_loop(0, groups, one_group, 0, unroll=True)
    share = packed[...].T
    if far:
        share = share + before_ref[...]
    cross_ref[...] = share


def cross_part(begin, count, odd, offsets, triads, z, sums, halo, weights, window, transform, before=None):
    sx, times, _ = z.shape
    blocks = offsets.shape[0]
    ntri = triads.shape[0]
    groups = LANES // blocks
    wide = 2 * blocks
    tall = ntri // groups * wide
    more = [] if before is None else [before]
    return pl.pallas_call(
        functools.partial(cross_kernel, sx, begin),
        out_shape=(
            jax.ShapeDtypeStruct((tall, LANES), F32),
            jax.ShapeDtypeStruct((ntri * wide, count * LANES), BF16),
        ),
        in_specs=[SMEM] * 3 + [VMEM] * (6 + len(more)),
        out_specs=(VMEM,) * 2,
        scratch_shapes=[
            pltpu.VMEM((count, times, LANES), F32),
            pltpu.VMEM((count, NFFT * (blocks + 1), LANES), F32),
            pltpu.VMEM((ntri * wide, count * LANES), BF16),
            pltpu.VMEM((LANES, tall), F32),
        ],
        compiler_params=limit(26),
        cost_estimate=pl.CostEstimate(flops=2000000000, bytes_accessed=4000000, transcendentals=0),
        name="cross",
    )(odd, offsets, triads, z, sums, halo, weights, window, transform, *more)


def swap(x, axis, bit):
    count = lax.axis_size(axis)
    return lax.ppermute(x, axis, [(i, i ^ bit) for i in range(count)])


def sum_over(x, axis, bit):
    count = lax.axis_size(axis)
    while bit < count:
        x = x + swap(x, axis, bit)
        bit *= 2
    return x


def modes_kernel(sx, blocks, scaling, odd_ref, core_ref, mine_ref, other_ref, near_ref, far_ref, values_ref, modes_ref, cross):
    tall = cross.shape[0]
    wide = 2 * blocks
    per = tall // wide
    groups = LANES // blocks
    odd = odd_ref[0]
    core = core_ref[0]
    half = tall // 2
    cross[pl.ds(pl.multiple_of(core * half, 8), half), :] = mine_ref[...] * scaling
    cross[pl.ds(pl.multiple_of((1 - core) * half, 8), half), :] = other_ref[...] * scaling
    lane = lax.broadcasted_iota(jnp.int32, (per, LANES), 1)
    start = lane - lane % blocks

    mat_re = [cross[pl.ds(c, per, stride=wide), :] for c in range(blocks)]
    mat_im = [cross[pl.ds(blocks + c, per, stride=wide), :] for c in range(blocks)]

    def pick(x, index):
        return jnp.take_along_axis(x, index, axis=1)

    spots = [start + c for c in range(blocks)]

    def apply(part_re, part_im):
        sums = []
        for parity in range(2):
            out_re = jnp.zeros((per, LANES), F32)
            out_im = jnp.zeros((per, LANES), F32)
            for c in range(parity, blocks, 2):
                re = pick(part_re, spots[c])
                im = pick(part_im, spots[c])
                out_re += mat_re[c] * re - mat_im[c] * im
                out_im += mat_re[c] * im + mat_im[c] * re
            sums.append((out_re, out_im))
        return sums[0][0] + sums[1][0], sums[0][1] + sums[1][1]

    def over_blocks(x):
        bit = 1
        while bit < blocks:
            x = x + pick(x, lane ^ bit)
            bit *= 2
        return x

    vec_re = jnp.full((per, LANES), 1.0 / math.sqrt(blocks), F32)
    vec_im = jnp.zeros((per, LANES), F32)
    for _ in range(POW):
        out_re, out_im = apply(vec_re, vec_im)
        length = jnp.sqrt(over_blocks(out_re * out_re + out_im * out_im))
        vec_re = out_re / length
        vec_im = out_im / length
    out_re, out_im = apply(vec_re, vec_im)
    value_re = over_blocks(vec_re * out_re + vec_im * out_im)
    value_im = over_blocks(vec_re * out_im - vec_im * out_re)

    source = jnp.minimum(lane // per * blocks, LANES - 1)
    mine = lax.broadcasted_iota(jnp.int32, (per, LANES), 0) == lane % per
    for part, value in enumerate((value_re, value_im)):
        row = jnp.sum(jnp.where(mine, pick(value, source), 0.0), axis=0, keepdims=True)
        values_ref[part : part + 1, :] = row[:, : values_ref.shape[1]]

    own = lax.broadcasted_iota(jnp.int32, (per, tall), 1) // wide == lax.broadcasted_iota(jnp.int32, (per, tall), 0)
    is_re = lax.broadcasted_iota(jnp.int32, (per, tall), 1) % wide < blocks
    for g in range(groups):
        spot = g * blocks + lane % blocks
        re = jnp.concatenate([pick(vec_re, spot)] * (tall // LANES), axis=1)
        im = jnp.concatenate([pick(vec_im, spot)] * (tall // LANES), axis=1)
        rows = jnp.concatenate(
            [
                jnp.where(own, jnp.where(is_re, re, -im), 0.0),
                jnp.where(own, jnp.where(is_re, im, re), 0.0),
            ],
            axis=0,
        )
        high = rows.astype(BF16)
        both = jnp.concatenate([high, (rows - high.astype(F32)).astype(BF16)], axis=0)
        at = slice(g * tall, (g + 1) * tall)
        for position in range(sx):
            if position + 1 < sx:
                target = near_ref[at, position * LANES : (position + 1) * LANES]
            else:
                target = far_ref[at, :]
            out = jnp.dot(both, target, preferred_element_type=F32)
            out = out[: 2 * per] + out[2 * per :]
            row = row_at(position, sx, odd)
            for part in range(2):
                first = g * per * 2 * sx + part * sx
                modes_ref[pl.ds(first + row, per, stride=2 * sx), :] = out[part * per : (part + 1) * per]


def modes_part(odd, core, mine, other, near, far, blocks, ntri, sx, scaling):
    return pl.pallas_call(
        functools.partial(modes_kernel, sx, blocks, scaling),
        out_shape=(
            jax.ShapeDtypeStruct((2, ntri), F32),
            jax.ShapeDtypeStruct((ntri * 2 * sx, LANES), F32),
        ),
        in_specs=[SMEM] * 2 + [VMEM] * 4,
        out_specs=(VMEM,) * 2,
        scratch_shapes=[pltpu.VMEM((2 * mine.shape[0], LANES), F32)],
        compiler_params=limit(12),
        name="modes",
    )(odd, core, mine, other, near, far)


def on_device(u_velocity, v_velocity, cell_weights, block_offsets, triads):
    times, sx, columns = u_velocity.shape
    blocks = block_offsets.shape[0]
    ntri = triads.shape[0]
    slabs = lax.axis_size("space")
    cells = sx * columns * slabs * lax.axis_size("freq")
    scaling = 1.0 / (blocks * math.sqrt(cells))
    pieces = 8
    window, transform = make_table(NFFT)
    picks, places = edge_columns(times * sx, pieces)
    shift = 0.5 * (np.eye(LANES, k=1, dtype=np.float32) - np.eye(LANES, k=-1, dtype=np.float32))
    v = v_velocity.reshape(times * sx, columns)
    u = u_velocity.reshape(times * sx, columns)
    odd = is_odd()[None]
    core = (lax.axis_index("freq") % 2)[None]

    near = lax.ppermute(near_edge(odd, v, sx), "space", [(i, i ^ 1) for i in range(slabs)])
    far, low, high = far_edge(odd, v, u, jnp.asarray(picks, BF16), sx)
    inner = [(i, i + 1) for i in range(1, slabs - 1, 2)]
    far = lax.ppermute(far, "space", inner + [(b, a) for a, b in inner])
    ends = lax.axis_size("freq") - 1
    col_low = lax.ppermute(high, "freq", [(i, i + 1) for i in range(ends)])
    col_high = lax.ppermute(low, "freq", [(i + 1, i) for i in range(ends)])
    z, sums = local_part(odd, v, u, jnp.asarray(shift, BF16), col_low, col_high, jnp.asarray(places, BF16), sx)
    window = jnp.asarray(np.ascontiguousarray(np.broadcast_to(window[:, None], (NFFT, LANES))))
    transform = jnp.asarray(transform, BF16)
    share, near_target = cross_part(
        0, sx - 1, odd, block_offsets, triads, z, sums, near, cell_weights, window, transform
    )
    share, far_target = cross_part(
        sx - 1, 1, odd, block_offsets, triads, z, sums, far, cell_weights, window, transform, share
    )
    half = share.shape[0] // 2
    mine = lax.dynamic_slice_in_dim(share, core[0] * half, half, 0)
    other = lax.dynamic_slice_in_dim(share, (1 - core[0]) * half, half, 0)
    mine = mine + swap(other, "freq", 1)
    mine = sum_over(sum_over(mine, "freq", 2), "space", 1)
    other = swap(mine, "freq", 1)
    values, modes = modes_part(odd, core, mine, other, near_target, far_target, blocks, ntri, sx, scaling)
    return (values.T, modes.reshape(ntri, 2, sx, columns))


def solution(mesh):
    return jax.shard_map(
        on_device,
        mesh=mesh,
        in_specs=(P(None, "space", "freq"), P(None, "space", "freq"), P("space", "freq"), P(), P()),
        out_specs=(P(), P(None, None, "space", "freq")),
        check_vma=False,
    )
```

time: 75.8 us -> 60.8 us (0.80)
  Pallas kernels: 20.8 us -> 11.8 us
  starting transfers between devices: 19.4 us -> 16.8 us
  other arithmetic: 2.25 us -> 0.05 us
  waiting for transfers between devices: 29.9 us -> 28.4 us
    pallas_call x3 -> x5, Pallas kernels: 16.9 us -> 10.7 us  [the longest x2 6.24 us: cross_part(): pl.pallas_call(functools.partial(cross_kernel, sx, begin), out_shape=(jax...]
    ppermute x5 -> x6, waiting for transfers between devices: 15.8 us -> 12 us  [swap(): return lax.ppermute(x, axis, [(i, i ^ bit) for i in range(count)])]
    pallas_call x1, Pallas kernels: 3.94 us -> 1.15 us  [local_part(): pl.pallas_call(functools.partial(local_kernel, sx, pieces), out_shape=(ja...]
    ppermute x4, starting transfers between devices: 8.93 us -> 6.47 us  [the longest x1 3.03 us: on_device(): lax.ppermute(near_edge(odd, v, sx), 'space', [(i, i ^ 1) for i in range(s...]
    ppermute x4, waiting for transfers between devices: 14 us -> 16.4 us  [the longest x1 13.2 us: on_device(): lax.ppermute(near_edge(odd, v, sx), 'space', [(i, i ^ 1) for i in range(s...]
    unnamed x9 -> x25, local copies, waits for them, and re-layouts: 0.83 us -> 2.63 us
    add x5 -> x4, other arithmetic: 1.64 us -> 0.04 us  [sum_over(): x = x + swap(x, axis, bit)]
    another operation x1 -> x0, local copies, waits for them, and re-layouts: 0.89 us -> none
  transfers between devices with their start and end apart: 9 -> 10, of which waited for: 7 -> 8; matrix products, arithmetic and copies ran while one was open for 3% -> 0% of each run, Pallas kernels for 5% -> 9%
where the time goes in v2:
time: 60.8 us; the launch traced here: 60.5 us
  waiting for transfers between devices  28.4 us (47%)
  starting transfers between devices  16.8 us (28%)
  Pallas kernels  11.8 us (19%)
  local copies, waits for them, and re-layouts  2.65 us (4%)
  between operations  0.83 us (1%)
    ppermute x1, waiting for transfers between devices, on_device(): lax.ppermute(near_edge(odd, v, sx), 'space', [(i, i ^ 1) for i in range(s...  13.2 us
    ppermute x6, waiting for transfers between devices, swap(): return lax.ppermute(x, axis, [(i, i ^ bit) for i in range(count)])  12 us
    ppermute x6, starting transfers between devices, swap(): return lax.ppermute(x, axis, [(i, i ^ bit) for i in range(count)])  10.3 us
    pallas_call x2, Pallas kernels, cross_part(): pl.pallas_call(functools.partial(cross_kernel, sx, begin), out_shape=(jax...  6.24 us
    ppermute x1, waiting for transfers between devices, on_device(): col_high = lax.ppermute(low, 'freq', [(i + 1, i) for i in range(ends)])  3.19 us
    ppermute x1, starting transfers between devices, on_device(): lax.ppermute(near_edge(odd, v, sx), 'space', [(i, i ^ 1) for i in range(s...  3.03 us
    pallas_call x1, Pallas kernels, modes_part(): pl.pallas_call(functools.partial(modes_kernel, sx, blocks, scaling), out_...  2.82 us
    unnamed x25, local copies, waits for them, and re-layouts  2.63 us
  transfers between devices with their start and end apart: 10, of which 8 were waited for; matrix products, arithmetic and copies ran while one was open for 0% of the time, Pallas kernels for 9%

profile of v2, /device:TPU:0, one launch (start us, length us, event | category | flops | bytes accessed | tf_op | source)
XLA Modules:
  0.0 60.5 jit_solution(4948307604521131524)
XLA Ops:
  0.6 0.0 copy-start.4
  0.7 1.2 %copy-done = bf16[2176,2,128]{2,1,0:T(2,128)(2,1)S(1)} copy-done((bf16[2176,2,128]{2,1,0:T(2,128)(2,1)S(1)}, bf16[2176,2,128]{2,1,0:T(2,128)(2,1)}, u32[]{:S(2)}) %copy-start) | copy-done | bytes 1114136
  1.9 0.3 near.1
  2.2 3.0 %collective-permute-start.3 = (bf16[2176,128]{1,0:T(8,128)(2,1)S(1)}, bf16[2176,128]{1,0:T(8,128)(2,1)}, u32[]{:S(2)}, u32[]{:S(2)}) collective-permute-start(bf16[2176,128]{1,0:T(8,128)(2,1)S(1)} %near.1), channel_id=1, source_target_pairs={{0,4},{4,0},{8,12},{12,8},{16,20},{20,16},{24,28},{28,24},{1,5},{5... | collective-permute-start | bytes 1671176 | tf_op jit(solution)/shard_map/ppermute | solution.py:423
  5.2 1.2 %copy-done.2 = bf16[2176,2,128]{2,1,0:T(2,128)(2,1)S(1)} copy-done((bf16[2176,2,128]{2,1,0:T(2,128)(2,1)S(1)}, bf16[2176,2,128]{2,1,0:T(2,128)(2,1)}, u32[]{:S(2)}) %copy-start.2) | copy-done | bytes 1114136
  6.5 1.3 %far.1 = (bf16[2176,128]{1,0:T(8,128)(2,1)}, bf16[8,544]{1,0:T(8,128)(2,1)S(1)}, bf16[8,544]{1,0:T(8,128)(2,1)S(1)}) custom-call(s32[1]{0:T(128)} %bitcast.odd_ref, bf16[4352,128]{1,0:T(8,128)(2,1)S(1)} %bitcast.7, bf16[4352,128]{1,0:T(8,128)(2,1)S(1)} %bitcast.9, bf16[8,16,128]{2,1,0:T(8,128)(2,1)S(1)} %copy-done.4), custom_call_target="tpu_custom_call" | custom-call | flops 200000000 | bytes 4000000 | tf_op jit(solution)/shard_map/far/pallas_call | solution.py:97
  7.8 0.7 %collective-permute-start.2 = (bf16[2176,128]{1,0:T(8,128)(2,1)}, bf16[2176,128]{1,0:T(8,128)(2,1)S(1)}, u32[]{:S(2)}, u32[]{:S(2)}) collective-permute-start(bf16[2176,128]{1,0:T(8,128)(2,1)} %get-tuple-element.17), channel_id=1, source_target_pairs={{4,8},{12,16},{20,24},{8,4},{16,12},{24,20},{5,9},{13,17},{21,25},... | collective-permute-start | bytes 1671176 | tf_op jit(solution)/shard_map/ppermute | solution.py:426
  8.5 1.5 %collective-permute-start = (bf16[8,544]{1,0:T(8,128)(2,1)S(1)}, bf16[8,544]{1,0:T(8,128)(2,1)S(1)}, u32[]{:S(2)}, u32[]{:S(2)}) collective-permute-start(bf16[8,544]{1,0:T(8,128)(2,1)S(1)} %get-tuple-element.13), channel_id=1, source_target_pairs={{0,1},{1,2},{2,3},{4,5},{5,6},{6,7},{8,9},{9,10},{10,11},{12,13},{... | collective-permute-start | bytes 26120 | tf_op jit(solution)/shard_map/ppermute | solution.py:428
  10.0 1.3 %collective-permute-start.1 = (bf16[8,544]{1,0:T(8,128)(2,1)S(1)}, bf16[8,544]{1,0:T(8,128)(2,1)S(1)}, u32[]{:S(2)}, u32[]{:S(2)}) collective-permute-start(bf16[8,544]{1,0:T(8,128)(2,1)S(1)} %get-tuple-element.14), channel_id=1, source_target_pairs={{1,0},{2,1},{3,2},{5,4},{6,5},{7,6},{9,8},{10,9},{11,10},{13,12},{... | collective-permute-start | bytes 26120 | tf_op jit(solution)/shard_map/ppermute | solution.py:429
  11.3 0.1 copy.13.triads_ref
  11.4 0.0 copy-start.7
  11.4 0.0 copy-start.8
  11.4 0.0 collective-permute-done.low_ref
  11.4 3.2 %collective-permute-done.1.high_ref = bf16[8,544]{1,0:T(8,128)(2,1)S(1)} collective-permute-done((bf16[8,544]{1,0:T(8,128)(2,1)S(1)}, bf16[8,544]{1,0:T(8,128)(2,1)S(1)}, u32[]{:S(2)}, u32[]{:S(2)}) %collective-permute-start.1) | collective-permute-done | bytes 8736 | tf_op jit(solution)/shard_map/ppermute | solution.py:429
  14.6 1.1 %local.1 = (f32[2,2176,128]{2,1,0:T(8,128)S(1)}, f32[2,8,128]{2,1,0:T(8,128)S(1)}) custom-call(s32[1]{0:T(128)} %bitcast.odd_ref, bf16[4352,128]{1,0:T(8,128)(2,1)S(1)} %bitcast.8, bf16[4352,128]{1,0:T(8,128)(2,1)S(1)} %bitcast.10, bf16[128,128]{1,0:T(8,128)(2,1)S(1)} %copy-done.9, bf16[8,544]{1,0:T(8,128)(2,1)S(1)} %collective-permute-done.low_ref, ...), custom_call_target="tpu_custom_call" | custom-call | flops 1000000000 | bytes 8000000 | tf_op jit(solution)/shard_map/local/pallas_call | solution.py:141
  15.8 13.2 %collective-permute-done.3.halo_ref = bf16[2176,128]{1,0:T(8,128)(2,1)} collective-permute-done((bf16[2176,128]{1,0:T(8,128)(2,1)S(1)}, bf16[2176,128]{1,0:T(8,128)(2,1)}, u32[]{:S(2)}, u32[]{:S(2)}) %collective-permute-start.3) | collective-permute-done | bytes 557088 | tf_op jit(solution)/shard_map/ppermute | solution.py:423
  29.0 3.1 %cross.2 = (f32[256,128]{1,0:T(8,128)S(1)}, bf16[2048,128]{1,0:T(8,128)(2,1)S(1)}) custom-call(s32[1]{0:T(128)} %bitcast.odd_ref, s32[16]{0:T(128)S(1)} %copy-done.6, s32[64,2]{1,0:T(8,128)S(1)} %copy.13.triads_ref, f32[2,2176,128]{2,1,0:T(8,128)S(1)} %get-tuple-element.15.z_ref, f32[2,8,128]{2,1,0:T(8,128)S(1)} %get-tuple-element.16.sum_ref, ...), custom_call_target="tpu_custom_call" | custom-call | flops 2000000000 | bytes 4000000 | tf_op jit(solution)/shard_map/cross/pallas_call | solution.py:272
  32.2 0.0 collective-permute-done.2.halo_ref
  32.2 3.1 %cross.3 = (f32[256,128]{1,0:T(8,128)S(1)}, bf16[2048,128]{1,0:T(8,128)(2,1)S(1)}) custom-call(s32[1]{0:T(128)} %bitcast.odd_ref, s32[16]{0:T(128)S(1)} %copy-done.6, s32[64,2]{1,0:T(8,128)S(1)} %copy.13.triads_ref, f32[2,2176,128]{2,1,0:T(8,128)S(1)} %get-tuple-element.15.z_ref, f32[2,8,128]{2,1,0:T(8,128)S(1)} %get-tuple-element.16.sum_ref, ...), custom_call_target="tpu_custom_call" | custom-call | flops 2000000000 | bytes 4000000 | tf_op jit(solution)/shard_map/cross/pallas_call | solution.py:272
  35.3 0.1 collective-permute-start.4
  35.4 1.2 %collective-permute-done.4 = f32[128,128]{1,0:T(8,128)S(1)} collective-permute-done((f32[128,128]{1,0:T(8,128)S(1)}, f32[128,128]{1,0:T(8,128)S(1)}, u32[]{:S(2)}, u32[]{:S(2)}) %collective-permute-start.4) | collective-permute-done | bytes 65568 | tf_op jit(solution)/shard_map/ppermute | solution.py:294
  36.7 1.6 %collective-permute-start.5 = (f32[128,128]{1,0:T(8,128)S(1)}, f32[128,128]{1,0:T(8,128)S(1)}, u32[]{:S(2)}, u32[]{:S(2)}) collective-permute-start(f32[128,128]{1,0:T(8,128)S(1)} %dynamic-slice_add_fusion), channel_id=1, source_target_pairs={{0,2},{1,3},{2,0},{3,1},{4,6},{5,7},{6,4},{7,5},{8,10},{9,11},{10,... | collective-permute-start | bytes 196616 | tf_op jit(solution)/shard_map/ppermute | solution.py:294
  38.2 2.7 %collective-permute-done.5 = f32[128,128]{1,0:T(8,128)S(1)} collective-permute-done((f32[128,128]{1,0:T(8,128)S(1)}, f32[128,128]{1,0:T(8,128)S(1)}, u32[]{:S(2)}, u32[]{:S(2)}) %collective-permute-start.5) | collective-permute-done | bytes 65568 | tf_op jit(solution)/shard_map/ppermute | solution.py:294
  41.0 2.7 %collective-permute-start.6 = (f32[128,128]{1,0:T(8,128)S(1)}, f32[128,128]{1,0:T(8,128)S(1)}, u32[]{:S(2)}, u32[]{:S(2)}) collective-permute-start(f32[128,128]{1,0:T(8,128)S(1)} %add.33), channel_id=1, source_target_pairs={{0,4},{4,0},{8,12},{12,8},{16,20},{20,16},{24,28},{28,24},{1,5},{5... | collective-permute-start | bytes 196616 | tf_op jit(solution)/shard_map/ppermute | solution.py:294
  43.7 2.2 %collective-permute-done.6 = f32[128,128]{1,0:T(8,128)S(1)} collective-permute-done((f32[128,128]{1,0:T(8,128)S(1)}, f32[128,128]{1,0:T(8,128)S(1)}, u32[]{:S(2)}, u32[]{:S(2)}) %collective-permute-start.6) | collective-permute-done | bytes 65568 | tf_op jit(solution)/shard_map/ppermute | solution.py:294
  45.9 2.2 %collective-permute-start.7 = (f32[128,128]{1,0:T(8,128)S(1)}, f32[128,128]{1,0:T(8,128)S(1)}, u32[]{:S(2)}, u32[]{:S(2)}) collective-permute-start(f32[128,128]{1,0:T(8,128)S(1)} %add.34), channel_id=1, source_target_pairs={{0,8},{4,12},{8,0},{12,4},{16,24},{20,28},{24,16},{28,20},{1,9},{5... | collective-permute-start | bytes 196616 | tf_op jit(solution)/shard_map/ppermute | solution.py:294
  48.1 2.2 %collective-permute-done.7 = f32[128,128]{1,0:T(8,128)S(1)} collective-permute-done((f32[128,128]{1,0:T(8,128)S(1)}, f32[128,128]{1,0:T(8,128)S(1)}, u32[]{:S(2)}, u32[]{:S(2)}) %collective-permute-start.7) | collective-permute-done | bytes 65568 | tf_op jit(solution)/shard_map/ppermute | solution.py:294
  50.3 3.8 %collective-permute-start.8 = (f32[128,128]{1,0:T(8,128)S(1)}, f32[128,128]{1,0:T(8,128)S(1)}, u32[]{:S(2)}, u32[]{:S(2)}) collective-permute-start(f32[128,128]{1,0:T(8,128)S(1)} %add.35), channel_id=1, source_target_pairs={{0,16},{4,20},{8,24},{12,28},{16,0},{20,4},{24,8},{28,12},{1,17},{... | collective-permute-start | bytes 196616 | tf_op jit(solution)/shard_map/ppermute | solution.py:294
  54.1 2.3 %collective-permute-done.8 = f32[128,128]{1,0:T(8,128)S(1)} collective-permute-done((f32[128,128]{1,0:T(8,128)S(1)}, f32[128,128]{1,0:T(8,128)S(1)}, u32[]{:S(2)}, u32[]{:S(2)}) %collective-permute-start.8) | collective-permute-done | bytes 65568 | tf_op jit(solution)/shard_map/ppermute | solution.py:294
  56.4 0.1 collective-permute-start.9
  56.5 1.2 %collective-permute-done.9.other_ref = f32[128,128]{1,0:T(8,128)S(1)} collective-permute-done((f32[128,128]{1,0:T(8,128)S(1)}, f32[128,128]{1,0:T(8,128)S(1)}, u32[]{:S(2)}, u32[]{:S(2)}) %collective-permute-start.9) | collective-permute-done | bytes 65568 | tf_op jit(solution)/shard_map/ppermute | solution.py:294
  57.7 2.8 %modes.1 = (f32[2,64]{1,0:T(2,128)}, f32[256,128]{1,0:T(8,128)}) custom-call(s32[1]{0:T(128)} %bitcast.odd_ref, s32[1]{0:T(128)} %bitcast.1.core_ref, f32[128,128]{1,0:T(8,128)S(1)} %add.36.mine_ref, f32[128,128]{1,0:T(8,128)S(1)} %collective-permute-done.9.other_ref, bf16[2048,128]{1,0:T(8,128)(2,1)S(1)} %get-tuple-element.20.near_ref, ...), custom_call_target="tpu_custom_call" | custom-call | tf_op jit(solution)/shard_map/modes/pallas_call | solution.py:393
  (25 shorter events, 0.1 us)
Async XLA Ops:
  0.6 4.6 %copy-start.4 = (bf16[8,16,128]{2,1,0:T(8,128)(2,1)S(1)}, bf16[8,16,128]{2,1,0:T(8,128)(2,1)}, u32[]{:S(2)}) copy-start(bf16[8,16,128]{2,1,0:T(8,128)(2,1)} %constant.42.clone.picks_ref) | copy-start | bytes 98308
  0.7 1.2 %copy-start = (bf16[2176,2,128]{2,1,0:T(2,128)(2,1)S(1)}, bf16[2176,2,128]{2,1,0:T(2,128)(2,1)}, u32[]{:S(2)}) copy-start(bf16[2176,2,128]{2,1,0:T(2,128)(2,1)} %param.11) | copy-start | bytes 3342340
  1.9 3.3 %copy-start.1 = (bf16[2176,2,128]{2,1,0:T(2,128)(2,1)S(1)}, bf16[2176,2,128]{2,1,0:T(2,128)(2,1)}, u32[]{:S(2)}) copy-start(bf16[2176,2,128]{2,1,0:T(2,128)(2,1)} %param.11) | copy-start | bytes 3342340
  2.2 26.9 %collective-permute-start.3 = (bf16[2176,128]{1,0:T(8,128)(2,1)S(1)}, bf16[2176,128]{1,0:T(8,128)(2,1)}, u32[]{:S(2)}, u32[]{:S(2)}) collective-permute-start(bf16[2176,128]{1,0:T(8,128)(2,1)S(1)} %near.1), channel_id=1, source_target_pairs={{0,4},{4,0},{8,12},{12,8},{16,20},{20,16},{24,28},{28,24},{1,5},{5... | collective-permute-start | bytes 1671176 | tf_op jit(solution)/shard_map/ppermute | solution.py:423
  5.2 1.2 %copy-start.2 = (bf16[2176,2,128]{2,1,0:T(2,128)(2,1)S(1)}, bf16[2176,2,128]{2,1,0:T(2,128)(2,1)}, u32[]{:S(2)}) copy-start(bf16[2176,2,128]{2,1,0:T(2,128)(2,1)} %param.10) | copy-start | bytes 3342340
  6.5 4.8 %copy-start.11 = (s32[64,2]{0,1:T(2,128)S(1)}, s32[64,2]{0,1:T(2,128)}, u32[]{:S(2)}) copy-start(s32[64,2]{0,1:T(2,128)} %param.14) | copy-start | bytes 1540
  6.5 8.2 %copy-start.3 = (bf16[2176,2,128]{2,1,0:T(2,128)(2,1)S(1)}, bf16[2176,2,128]{2,1,0:T(2,128)(2,1)}, u32[]{:S(2)}) copy-start(bf16[2176,2,128]{2,1,0:T(2,128)(2,1)} %param.10) | copy-start | bytes 3342340
  6.5 8.2 %copy-start.9 = (bf16[128,128]{1,0:T(8,128)(2,1)S(1)}, bf16[128,128]{1,0:T(8,128)(2,1)}, u32[]{:S(2)}) copy-start(bf16[128,128]{1,0:T(8,128)(2,1)} %constant.43.clone.shift_ref) | copy-start | bytes 98308
  6.5 8.2 %copy-start.10 = (bf16[8,16,128]{2,1,0:T(8,128)(2,1)S(1)}, bf16[8,16,128]{2,1,0:T(8,128)(2,1)}, u32[]{:S(2)}) copy-start(bf16[8,16,128]{2,1,0:T(8,128)(2,1)} %constant.44.clone.places_ref) | copy-start | bytes 98308
  7.8 24.4 %collective-permute-start.2 = (bf16[2176,128]{1,0:T(8,128)(2,1)}, bf16[2176,128]{1,0:T(8,128)(2,1)S(1)}, u32[]{:S(2)}, u32[]{:S(2)}) collective-permute-start(bf16[2176,128]{1,0:T(8,128)(2,1)} %get-tuple-element.17), channel_id=1, source_target_pairs={{4,8},{12,16},{20,24},{8,4},{16,12},{24,20},{5,9},{13,17},{21,25},... | collective-permute-start | bytes 1671176 | tf_op jit(solution)/shard_map/ppermute | solution.py:426
  8.5 2.9 %collective-permute-start = (bf16[8,544]{1,0:T(8,128)(2,1)S(1)}, bf16[8,544]{1,0:T(8,128)(2,1)S(1)}, u32[]{:S(2)}, u32[]{:S(2)}) collective-permute-start(bf16[8,544]{1,0:T(8,128)(2,1)S(1)} %get-tuple-element.13), channel_id=1, source_target_pairs={{0,1},{1,2},{2,3},{4,5},{5,6},{6,7},{8,9},{9,10},{10,11},{12,13},{... | collective-permute-start | bytes 26120 | tf_op jit(solution)/shard_map/ppermute | solution.py:428
  10.0 4.7 %collective-permute-start.1 = (bf16[8,544]{1,0:T(8,128)(2,1)S(1)}, bf16[8,544]{1,0:T(8,128)(2,1)S(1)}, u32[]{:S(2)}, u32[]{:S(2)}) collective-permute-start(bf16[8,544]{1,0:T(8,128)(2,1)S(1)} %get-tuple-element.14), channel_id=1, source_target_pairs={{1,0},{2,1},{3,2},{5,4},{6,5},{7,6},{9,8},{10,9},{11,10},{13,12},{... | collective-permute-start | bytes 26120 | tf_op jit(solution)/shard_map/ppermute | solution.py:429
  11.4 17.7 %copy-start.5 = (f32[2,128]{1,0:T(2,128)S(1)}, f32[2,128]{1,0:T(2,128)}, u32[]{:S(2)}) copy-start(f32[2,128]{1,0:T(2,128)} %weights_ref.3) | copy-start | bytes 3076
  11.4 17.7 %copy-start.6 = (s32[16]{0:T(128)S(1)}, s32[16]{0:T(128)}, u32[]{:S(2)}) copy-start(s32[16]{0:T(128)} %offsets_ref.3) | copy-start | bytes 196
  11.4 17.7 %copy-start.7 = (f32[256,128]{1,0:T(8,128)S(1)}, f32[256,128]{1,0:T(8,128)}, u32[]{:S(2)}) copy-start(f32[256,128]{1,0:T(8,128)} %constant.45.clone.window_ref) | copy-start | bytes 393220
  11.4 17.6 %copy-start.8 = (bf16[256,256]{1,0:T(8,128)(2,1)S(1)}, bf16[256,256]{1,0:T(8,128)(2,1)}, u32[]{:S(2)}) copy-start(bf16[256,256]{1,0:T(8,128)(2,1)} %constant.46.clone.transform_ref) | copy-start | bytes 393220
  35.3 1.3 %collective-permute-start.4 = (f32[128,128]{1,0:T(8,128)S(1)}, f32[128,128]{1,0:T(8,128)S(1)}, u32[]{:S(2)}, u32[]{:S(2)}) collective-permute-start(f32[128,128]{1,0:T(8,128)S(1)} %constant_dynamic-slice_fusion), channel_id=1, source_target_pairs={{0,1},{1,0},{2,3},{3,2},{4,5},{5,4},{6,7},{7,6},{8,9},{9,8},{10,11... | collective-permute-start | bytes 196616 | tf_op jit(solution)/shard_map/ppermute | solution.py:294
  36.7 4.3 %collective-permute-start.5 = (f32[128,128]{1,0:T(8,128)S(1)}, f32[128,128]{1,0:T(8,128)S(1)}, u32[]{:S(2)}, u32[]{:S(2)}) collective-permute-start(f32[128,128]{1,0:T(8,128)S(1)} %dynamic-slice_add_fusion), channel_id=1, source_target_pairs={{0,2},{1,3},{2,0},{3,1},{4,6},{5,7},{6,4},{7,5},{8,10},{9,11},{10,... | collective-permute-start | bytes 196616 | tf_op jit(solution)/shard_map/ppermute | solution.py:294
  41.0 4.9 %collective-permute-start.6 = (f32[128,128]{1,0:T(8,128)S(1)}, f32[128,128]{1,0:T(8,128)S(1)}, u32[]{:S(2)}, u32[]{:S(2)}) collective-permute-start(f32[128,128]{1,0:T(8,128)S(1)} %add.33), channel_id=1, source_target_pairs={{0,4},{4,0},{8,12},{12,8},{16,20},{20,16},{24,28},{28,24},{1,5},{5... | collective-permute-start | bytes 196616 | tf_op jit(solution)/shard_map/ppermute | solution.py:294
  45.9 4.4 %collective-permute-start.7 = (f32[128,128]{1,0:T(8,128)S(1)}, f32[128,128]{1,0:T(8,128)S(1)}, u32[]{:S(2)}, u32[]{:S(2)}) collective-permute-start(f32[128,128]{1,0:T(8,128)S(1)} %add.34), channel_id=1, source_target_pairs={{0,8},{4,12},{8,0},{12,4},{16,24},{20,28},{24,16},{28,20},{1,9},{5... | collective-permute-start | bytes 196616 | tf_op jit(solution)/shard_map/ppermute | solution.py:294
  50.3 6.0 %collective-permute-start.8 = (f32[128,128]{1,0:T(8,128)S(1)}, f32[128,128]{1,0:T(8,128)S(1)}, u32[]{:S(2)}, u32[]{:S(2)}) collective-permute-start(f32[128,128]{1,0:T(8,128)S(1)} %add.35), channel_id=1, source_target_pairs={{0,16},{4,20},{8,24},{12,28},{16,0},{20,4},{24,8},{28,12},{1,17},{... | collective-permute-start | bytes 196616 | tf_op jit(solution)/shard_map/ppermute | solution.py:294
  56.4 1.3 %collective-permute-start.9 = (f32[128,128]{1,0:T(8,128)S(1)}, f32[128,128]{1,0:T(8,128)S(1)}, u32[]{:S(2)}, u32[]{:S(2)}) collective-permute-start(f32[128,128]{1,0:T(8,128)S(1)} %add.36.mine_ref), channel_id=1, source_target_pairs={{0,1},{1,0},{2,3},{3,2},{4,5},{5,4},{6,7},{7,6},{8,9},{9,8},{10,11... | collective-permute-start | bytes 196616 | tf_op jit(solution)/shard_map/ppermute | solution.py:294

commit v3 on v2

--- a/solution.py
+++ b/solution.py
@@ -9,9 +9,9 @@
 from jax.experimental.pallas import tpu as pltpu
 from jax.sharding import PartitionSpec as P
 
+
 NFFT = 256
 POW = 4
-NEAR_STEPS = 2
 LANES = 128
 F32 = jnp.float32
 BF16 = jnp.bfloat16
@@ -31,7 +31,7 @@
     return window.astype(np.float32), transform.astype(np.float32)
 
 
-def edge_columns(rows, pieces):
+def edge_columns(pieces):
     picks = np.zeros((pieces, 2 * pieces, LANES), np.float32)
     places = np.zeros((pieces, 2 * pieces, LANES), np.float32)
     for m in range(pieces):
@@ -54,32 +54,52 @@
     return pltpu.CompilerParams(vmem_limit_bytes=mib * MIB)
 
 
-def near_kernel(sx, odd_ref, v_ref, near_ref, plain):
-    times = near_ref.shape[0]
+def near_kernel(sx, odd_ref, v_ref, early_ref, late_ref, plain):
     plain[...] = v_ref[...].astype(F32)
-    near_ref[...] = plain[pl.ds(row_at(0, sx, odd_ref[0]), times, stride=sx), :].astype(BF16)
+    row = row_at(0, sx, odd_ref[0])
+    early, late = early_ref.shape[0], late_ref.shape[0]
+    early_ref[...] = plain[pl.ds(row, early, stride=sx), :].astype(BF16)
+    late_ref[...] = plain[pl.ds(early * sx + row, late, stride=sx), :].astype(BF16)
 
 
 def near_edge(odd, v, sx):
     rows = v.shape[0]
-    steps = NEAR_STEPS
+    early = rows // sx // 32 * 16
     return pl.pallas_call(
         functools.partial(near_kernel, sx),
-        grid=(steps,),
-        out_shape=jax.ShapeDtypeStruct((rows // sx, LANES), BF16),
-        in_specs=[SMEM, pl.BlockSpec((rows // steps, LANES), lambda i: (i, 0))],
-        out_specs=pl.BlockSpec((rows // sx // steps, LANES), lambda i: (i, 0)),
-        scratch_shapes=[pltpu.VMEM((rows // steps, LANES), F32)],
+        out_shape=(
+            jax.ShapeDtypeStruct((early, LANES), BF16),
+            jax.ShapeDtypeStruct((rows // sx - early, LANES), BF16),
+        ),
+        in_specs=[SMEM, VMEM],
+        out_specs=(VMEM,) * 2,
+        scratch_shapes=[pltpu.VMEM((rows, LANES), F32)],
         compiler_params=limit(8),
         name="near",
     )(odd, v)
 
 
-def far_kernel(sx, pieces, odd_ref, v_ref, u_ref, picks_ref, far_ref, low_ref, high_ref, plain):
-    rows = v_ref.shape[0]
-    times = rows // sx
+def far_kernel(sx, odd_ref, v_ref, after_ref, far_ref, plain):
+    times = far_ref.shape[0]
     plain[...] = v_ref[...].astype(F32)
     far_ref[...] = plain[pl.ds(row_at(sx - 1, sx, odd_ref[0]), times, stride=sx), :].astype(BF16)
+
+
+def far_edge(odd, v, after, sx):
+    rows = v.shape[0]
+    return pl.pallas_call(
+        functools.partial(far_kernel, sx),
+        out_shape=jax.ShapeDtypeStruct((rows // sx, LANES), BF16),
+        in_specs=[SMEM, VMEM, pl.BlockSpec(memory_space=pl.ANY)],
+        out_specs=VMEM,
+        scratch_shapes=[pltpu.VMEM((rows, LANES), F32)],
+        compiler_params=limit(8),
+        name="far",
+    )(odd, v, after)
+
+
+def columns_kernel(pieces, u_ref, picks_ref, low_ref, high_ref):
+    rows = u_ref.shape[0]
     part = rows // pieces
     cols = jnp.zeros((2 * pieces, part), F32)
     for m in range(pieces):
@@ -90,24 +110,20 @@
     high_ref[...] = cols[pieces:].astype(BF16)
 
 
-def far_edge(odd, v, u, picks, sx):
-    rows = v.shape[0]
+def columns_edge(u, picks):
+    rows = u.shape[0]
     pieces = picks.shape[0]
-    times = rows // sx
-    return pl.pallas_call(
-        functools.partial(far_kernel, sx, pieces),
+    return pl.pallas_call(
+        functools.partial(columns_kernel, pieces),
         out_shape=(
-            jax.ShapeDtypeStruct((times, LANES), BF16),
             jax.ShapeDtypeStruct((pieces, rows // pieces), BF16),
             jax.ShapeDtypeStruct((pieces, rows // pieces), BF16),
         ),
-        in_specs=[SMEM] + [VMEM] * 3,
-        out_specs=(VMEM,) * 3,
-        scratch_shapes=[pltpu.VMEM((rows, LANES), F32)],
-        compiler_params=limit(12),
-        cost_estimate=pl.CostEstimate(flops=200000000, bytes_accessed=4000000, transcendentals=0),
-        name="far",
-    )(odd, v, u, picks)
+        in_specs=[VMEM] * 2,
+        out_specs=(VMEM,) * 2,
+        compiler_params=limit(8),
+        name="columns",
+    )(u, picks)
 
 
 def local_kernel(
@@ -154,14 +170,13 @@
 
 
 def cross_kernel(
-    sx, begin, odd_ref, offsets_ref, triads_ref, z_ref, sum_ref, halo_ref, weights_ref, window_ref, transform_ref,
-    *rest,
+    sx, begin, pieces, odd_ref, offsets_ref, triads_ref, z_ref, sum_ref, weights_ref, window_ref, transform_ref, *rest
 ):
     far = begin > 0
+    halo_refs, rest = rest[:pieces], rest[pieces:]
     if far:
-        before_ref, cross_ref, target_ref, full, spec, prod, packed = rest
-    else:
-        cross_ref, target_ref, full, spec, prod, packed = rest
+        before_ref, *rest = rest
+    cross_ref, target_ref, full, spec, prod, packed = rest
     count, times, _ = full.shape
     blocks = offsets_ref.shape[0]
     ntri = triads_ref.shape[0]
@@ -176,17 +191,23 @@
         sign = -sign
     touched = count - 1 if far else 0
 
-    chunk = times // 8
-
-    def add_halo(step, carry):
-        at = pl.ds(pl.multiple_of(step * chunk, 8), chunk)
-        halo = sign * halo_ref[at, :].astype(F32)
-        for row in range(count):
-            z = z_ref[begin + row, at, :]
-            full[row, at, :] = z + halo if row == touched else z
-        return carry + jnp.sum(halo.reshape(chunk // 8, 8, LANES), axis=0)
-
-    halo_sum = lax.fori_loop(0, 8, add_halo, jnp.zeros((8, LANES), F32))
+    halo_sum = jnp.zeros((8, LANES), F32)
+    base = 0
+    for halo_ref in halo_refs:
+        steps = 8 // pieces
+        chunk = halo_ref.shape[0] // steps
+
+        def add_halo(step, carry):
+            at = pl.ds(pl.multiple_of(step * chunk, 8), chunk)
+            to = pl.ds(pl.multiple_of(base + step * chunk, 8), chunk)
+            halo = sign * halo_ref[at, :].astype(F32)
+            for row in range(count):
+                z = z_ref[begin + row, to, :]
+                full[row, to, :] = z + halo if row == touched else z
+            return carry + jnp.sum(halo.reshape(chunk // 8, 8, LANES), axis=0)
+
+        halo_sum = lax.fori_loop(0, steps, add_halo, halo_sum)
+        base += halo_ref.shape[0]
     means = []
     for row in range(count):
         total = sum_ref[begin + row]
@@ -261,21 +282,21 @@
     cross_ref[...] = share
 
 
-def cross_part(begin, count, odd, offsets, triads, z, sums, halo, weights, window, transform, before=None):
+def cross_part(begin, count, odd, offsets, triads, z, sums, halos, weights, window, transform, before=None):
     sx, times, _ = z.shape
     blocks = offsets.shape[0]
     ntri = triads.shape[0]
     groups = LANES // blocks
     wide = 2 * blocks
     tall = ntri // groups * wide
-    more = [] if before is None else [before]
-    return pl.pallas_call(
-        functools.partial(cross_kernel, sx, begin),
+    more = list(halos) + ([] if before is None else [before])
+    return pl.pallas_call(
+        functools.partial(cross_kernel, sx, begin, len(halos)),
         out_shape=(
             jax.ShapeDtypeStruct((tall, LANES), F32),
             jax.ShapeDtypeStruct((ntri * wide, count * LANES), BF16),
         ),
-        in_specs=[SMEM] * 3 + [VMEM] * (6 + len(more)),
+        in_specs=[SMEM] * 3 + [VMEM] * (5 + len(more)),
         out_specs=(VMEM,) * 2,
         scratch_shapes=[
             pltpu.VMEM((count, times, LANES), F32),
@@ -285,8 +306,8 @@
         ],
         compiler_params=limit(26),
         cost_estimate=pl.CostEstimate(flops=2000000000, bytes_accessed=4000000, transcendentals=0),
-        name="cross",
-    )(odd, offsets, triads, z, sums, halo, weights, window, transform, *more)
+        name="cross_far" if begin else "cross_near",
+    )(odd, offsets, triads, z, sums, weights, window, transform, *more)
 
 
 def swap(x, axis, bit):
@@ -294,12 +315,20 @@
     return lax.ppermute(x, axis, [(i, i ^ bit) for i in range(count)])
 
 
-def sum_over(x, axis, bit):
-    count = lax.axis_size(axis)
-    while bit < count:
-        x = x + swap(x, axis, bit)
-        bit *= 2
+def sum_over_rest(x):
+    slabs, parts = lax.axis_size("space"), lax.axis_size("freq")
+    hops = [bit * parts for bit in bits_of(slabs)]
+    across = [bit for bit in bits_of(parts)[1:]]
+    first = hops[:1] + across + hops[1:]
+    second = across + hops[:1] + hops[:0:-1]
+    for one, other in zip(first, second, strict=True):
+        pairs = [(i, i ^ (other if i % 2 else one)) for i in range(slabs * parts)]
+        x = x + lax.ppermute(x, ("space", "freq"), pairs)
     return x
+
+
+def bits_of(count):
+    return [1 << n for n in range(count.bit_length() - 1)]
 
 
 def modes_kernel(sx, blocks, scaling, odd_ref, core_ref, mine_ref, other_ref, near_ref, far_ref, values_ref, modes_ref, cross):
@@ -413,15 +442,18 @@
     scaling = 1.0 / (blocks * math.sqrt(cells))
     pieces = 8
     window, transform = make_table(NFFT)
-    picks, places = edge_columns(times * sx, pieces)
+    picks, places = edge_columns(pieces)
     shift = 0.5 * (np.eye(LANES, k=1, dtype=np.float32) - np.eye(LANES, k=-1, dtype=np.float32))
     v = v_velocity.reshape(times * sx, columns)
     u = u_velocity.reshape(times * sx, columns)
     odd = is_odd()[None]
     core = (lax.axis_index("freq") % 2)[None]
 
-    near = lax.ppermute(near_edge(odd, v, sx), "space", [(i, i ^ 1) for i in range(slabs)])
-    far, low, high = far_edge(odd, v, u, jnp.asarray(picks, BF16), sx)
+    early, late = near_edge(odd, v, sx)
+    early = swap(early, "space", 1)
+    late = swap(late, "space", 1)
+    low, high = columns_edge(u, jnp.asarray(picks, BF16))
+    far = far_edge(odd, v, early, sx)
     inner = [(i, i + 1) for i in range(1, slabs - 1, 2)]
     far = lax.ppermute(far, "space", inner + [(b, a) for a, b in inner])
     ends = lax.axis_size("freq") - 1
@@ -431,16 +463,16 @@
     window = jnp.asarray(np.ascontiguousarray(np.broadcast_to(window[:, None], (NFFT, LANES))))
     transform = jnp.asarray(transform, BF16)
     share, near_target = cross_part(
-        0, sx - 1, odd, block_offsets, triads, z, sums, near, cell_weights, window, transform
+        0, sx - 1, odd, block_offsets, triads, z, sums, [early, late], cell_weights, window, transform
     )
     share, far_target = cross_part(
-        sx - 1, 1, odd, block_offsets, triads, z, sums, far, cell_weights, window, transform, share
+        sx - 1, 1, odd, block_offsets, triads, z, sums, [far], cell_weights, window, transform, share
     )
     half = share.shape[0] // 2
     mine = lax.dynamic_slice_in_dim(share, core[0] * half, half, 0)
     other = lax.dynamic_slice_in_dim(share, (1 - core[0]) * half, half, 0)
     mine = mine + swap(other, "freq", 1)
-    mine = sum_over(sum_over(mine, "freq", 2), "space", 1)
+    mine = sum_over_rest(mine)
     other = swap(mine, "freq", 1)
     values, modes = modes_part(odd, core, mine, other, near_target, far_target, blocks, ntri, sx, scaling)
     return (values.T, modes.reshape(ntri, 2, sx, columns))

time: 60.8 us -> 64.7 us (1.064)
  starting transfers between devices: 16.8 us -> 20.6 us
  waiting for transfers between devices: 28.4 us -> 30.5 us
  local copies, waits for them, and re-layouts: 2.65 us -> 1.41 us
  Pallas kernels: 11.8 us -> 11.1 us
    ppermute x1 -> x4, starting transfers between devices: 3.03 us -> 9.52 us  [sum_over_rest(): x = x + lax.ppermute(x, ('space', 'freq'), pairs)]
    ppermute x6 -> x4, waiting for transfers between devices: 12 us -> 17.7 us  [swap(): return lax.ppermute(x, axis, [(i, i ^ bit) for i in range(count)])]
    ppermute x1 -> x4, waiting for transfers between devices: 13.2 us -> 9.48 us  [sum_over_rest(): x = x + lax.ppermute(x, ('space', 'freq'), pairs)]
    ppermute x6 -> x4, starting transfers between devices: 10.3 us -> 6.96 us  [swap(): return lax.ppermute(x, axis, [(i, i ^ bit) for i in range(count)])]
    unnamed x25 -> x23, local copies, waits for them, and re-layouts: 2.63 us -> 1.4 us
    ppermute x1, starting transfers between devices: 0.68 us -> 1.5 us  [on_device(): far = lax.ppermute(far, 'space', inner + [(b, a) for a, b in inner])]
    pallas_call x4 -> x5, Pallas kernels: 7.83 us -> 7.12 us  [the longest x2 6.26 us: cross_part(): pl.pallas_call(functools.partial(cross_kernel, sx, begin, len(halos)), ou...]
  transfers between devices with their start and end apart: 10 -> 11, of which waited for: 8 -> 9; matrix products, arithmetic and copies ran while one was open for 0% -> 0% of each run, Pallas kernels for 9% -> 7%
where the time goes in v3:
time: 64.7 us; the launch traced here: 64.5 us
  waiting for transfers between devices  30.5 us (47%)
  starting transfers between devices  20.6 us (32%)
  Pallas kernels  11.1 us (17%)
  local copies, waits for them, and re-layouts  1.41 us (2%)
  between operations  0.84 us (1%)
    ppermute x4, waiting for transfers between devices, swap(): return lax.ppermute(x, axis, [(i, i ^ bit) for i in range(count)])  17.7 us
    ppermute x4, starting transfers between devices, sum_over_rest(): x = x + lax.ppermute(x, ('space', 'freq'), pairs)  9.52 us
    ppermute x4, waiting for transfers between devices, sum_over_rest(): x = x + lax.ppermute(x, ('space', 'freq'), pairs)  9.48 us
    ppermute x4, starting transfers between devices, swap(): return lax.ppermute(x, axis, [(i, i ^ bit) for i in range(count)])  6.96 us
    pallas_call x2, Pallas kernels, cross_part(): pl.pallas_call(functools.partial(cross_kernel, sx, begin, len(halos)), ou...  6.26 us
    ppermute x1, waiting for transfers between devices, on_device(): col_high = lax.ppermute(low, 'freq', [(i + 1, i) for i in range(ends)])  3.36 us
    pallas_call x1, Pallas kernels, modes_part(): pl.pallas_call(functools.partial(modes_kernel, sx, blocks, scaling), out_...  2.82 us
    ppermute x1, starting transfers between devices, on_device(): far = lax.ppermute(far, 'space', inner + [(b, a) for a, b in inner])  1.5 us
  transfers between devices with their start and end apart: 11, of which 9 were waited for; matrix products, arithmetic and copies ran while one was open for 0% of the time, Pallas kernels for 7%

profile of v3, /device:TPU:0, one launch (start us, length us, event | category | flops | bytes accessed | tf_op | source)
XLA Modules:
  0.0 64.5 jit_solution(5850039282600294219)
XLA Ops:
  0.7 1.2 %copy-done = bf16[2176,2,128]{2,1,0:T(2,128)(2,1)S(1)} copy-done((bf16[2176,2,128]{2,1,0:T(2,128)(2,1)S(1)}, bf16[2176,2,128]{2,1,0:T(2,128)(2,1)}, u32[]{:S(2)}) %copy-start) | copy-done | bytes 1114136
  1.9 0.2 near.1
  2.1 0.0 copy-start.3
  2.2 0.0 copy-start.8
  2.2 0.0 copy-start.9
  2.2 3.0 %collective-permute-start.2 = (bf16[1088,128]{1,0:T(8,128)(2,1)S(1)}, bf16[1088,128]{1,0:T(8,128)(2,1)S(1)}, u32[]{:S(2)}, u32[]{:S(2)}) collective-permute-start(bf16[1088,128]{1,0:T(8,128)(2,1)S(1)} %get-tuple-element.18), channel_id=1, source_target_pairs={{0,4},{4,0},{8,12},{12,8},{16,20},{20,16},{24,28},{28,24},{1,5},{5... | collective-permute-start | bytes 835592 | tf_op jit(solution)/shard_map/ppermute | solution.py:315
  5.2 6.7 %collective-permute-done.2.after_ref.rest_0_ = bf16[1088,128]{1,0:T(8,128)(2,1)S(1)} collective-permute-done((bf16[1088,128]{1,0:T(8,128)(2,1)S(1)}, bf16[1088,128]{1,0:T(8,128)(2,1)S(1)}, u32[]{:S(2)}, u32[]{:S(2)}) %collective-permute-start.2) | collective-permute-done | bytes 278560 | tf_op jit(solution)/shard_map/ppermute | solution.py:315
  11.9 0.2 far.1
  12.1 1.5 %collective-permute-start.3 = (bf16[2176,128]{1,0:T(8,128)(2,1)S(1)}, bf16[2176,128]{1,0:T(8,128)(2,1)}, u32[]{:S(2)}, u32[]{:S(2)}) collective-permute-start(bf16[2176,128]{1,0:T(8,128)(2,1)S(1)} %far.1), channel_id=1, source_target_pairs={{4,8},{12,16},{20,24},{8,4},{16,12},{24,20},{5,9},{13,17},{21,25},... | collective-permute-start | bytes 1671176 | tf_op jit(solution)/shard_map/ppermute | solution.py:458
  13.6 3.8 %collective-permute-start.4 = (bf16[1088,128]{1,0:T(8,128)(2,1)S(1)}, bf16[1088,128]{1,0:T(8,128)(2,1)}, u32[]{:S(2)}, u32[]{:S(2)}) collective-permute-start(bf16[1088,128]{1,0:T(8,128)(2,1)S(1)} %get-tuple-element.19), channel_id=1, source_target_pairs={{0,4},{4,0},{8,12},{12,8},{16,20},{20,16},{24,28},{28,24},{1,5},{5... | collective-permute-start | bytes 835592 | tf_op jit(solution)/shard_map/ppermute | solution.py:315
  17.4 0.4 columns.1
  17.8 1.3 %collective-permute-start = (bf16[8,544]{1,0:T(8,128)(2,1)S(1)}, bf16[8,544]{1,0:T(8,128)(2,1)S(1)}, u32[]{:S(2)}, u32[]{:S(2)}) collective-permute-start(bf16[8,544]{1,0:T(8,128)(2,1)S(1)} %get-tuple-element.14), channel_id=1, source_target_pairs={{0,1},{1,2},{2,3},{4,5},{5,6},{6,7},{8,9},{9,10},{10,11},{12,13},{... | collective-permute-start | bytes 26120 | tf_op jit(solution)/shard_map/ppermute | solution.py:460
  19.1 1.3 %collective-permute-start.1 = (bf16[8,544]{1,0:T(8,128)(2,1)S(1)}, bf16[8,544]{1,0:T(8,128)(2,1)S(1)}, u32[]{:S(2)}, u32[]{:S(2)}) collective-permute-start(bf16[8,544]{1,0:T(8,128)(2,1)S(1)} %get-tuple-element.15), channel_id=1, source_target_pairs={{1,0},{2,1},{3,2},{5,4},{6,5},{7,6},{9,8},{10,9},{11,10},{13,12},{... | collective-permute-start | bytes 26120 | tf_op jit(solution)/shard_map/ppermute | solution.py:461
  20.4 0.1 copy.13.triads_ref
  20.6 3.4 %collective-permute-done.1.high_ref = bf16[8,544]{1,0:T(8,128)(2,1)S(1)} collective-permute-done((bf16[8,544]{1,0:T(8,128)(2,1)S(1)}, bf16[8,544]{1,0:T(8,128)(2,1)S(1)}, u32[]{:S(2)}, u32[]{:S(2)}) %collective-permute-start.1) | collective-permute-done | bytes 8736 | tf_op jit(solution)/shard_map/ppermute | solution.py:461
  23.9 1.1 %local.1 = (f32[2,2176,128]{2,1,0:T(8,128)S(1)}, f32[2,8,128]{2,1,0:T(8,128)S(1)}) custom-call(s32[1]{0:T(128)} %bitcast.odd_ref, bf16[4352,128]{1,0:T(8,128)(2,1)S(1)} %bitcast.8, bf16[4352,128]{1,0:T(8,128)(2,1)S(1)} %bitcast.10, bf16[128,128]{1,0:T(8,128)(2,1)S(1)} %copy-done.8, bf16[8,544]{1,0:T(8,128)(2,1)S(1)} %collective-permute-done.low_ref, ...), custom_call_target="tpu_custom_call" | custom-call | flops 1000000000 | bytes 8000000 | tf_op jit(solution)/shard_map/local/pallas_call | solution.py:157
  25.1 8.6 %collective-permute-done.4.rest_1_ = bf16[1088,128]{1,0:T(8,128)(2,1)} collective-permute-done((bf16[1088,128]{1,0:T(8,128)(2,1)S(1)}, bf16[1088,128]{1,0:T(8,128)(2,1)}, u32[]{:S(2)}, u32[]{:S(2)}) %collective-permute-start.4) | collective-permute-done | bytes 278560 | tf_op jit(solution)/shard_map/ppermute | solution.py:315
  33.7 3.1 %cross_near.1 = (f32[256,128]{1,0:T(8,128)S(1)}, bf16[2048,128]{1,0:T(8,128)(2,1)S(1)}) custom-call(s32[1]{0:T(128)} %bitcast.odd_ref, s32[16]{0:T(128)S(1)} %copy-done.5, s32[64,2]{1,0:T(8,128)S(1)} %copy.13.triads_ref, f32[2,2176,128]{2,1,0:T(8,128)S(1)} %get-tuple-element.16.z_ref, f32[2,8,128]{2,1,0:T(8,128)S(1)} %get-tuple-element.17.sum_ref, ...), custom_call_target="tpu_custom_call" | custom-call | flops 2000000000 | bytes 4000000 | tf_op jit(solution)/shard_map/cross_near/pallas_call | solution.py:293
  36.8 3.1 %cross_far.1 = (f32[256,128]{1,0:T(8,128)S(1)}, bf16[2048,128]{1,0:T(8,128)(2,1)S(1)}) custom-call(s32[1]{0:T(128)} %bitcast.odd_ref, s32[16]{0:T(128)S(1)} %copy-done.5, s32[64,2]{1,0:T(8,128)S(1)} %copy.13.triads_ref, f32[2,2176,128]{2,1,0:T(8,128)S(1)} %get-tuple-element.16.z_ref, f32[2,8,128]{2,1,0:T(8,128)S(1)} %get-tuple-element.17.sum_ref, ...), custom_call_target="tpu_custom_call" | custom-call | flops 2000000000 | bytes 4000000 | tf_op jit(solution)/shard_map/cross_far/pallas_call | solution.py:293
  40.0 0.1 collective-permute-start.5
  40.0 1.2 %collective-permute-done.5 = f32[128,128]{1,0:T(8,128)S(1)} collective-permute-done((f32[128,128]{1,0:T(8,128)S(1)}, f32[128,128]{1,0:T(8,128)S(1)}, u32[]{:S(2)}, u32[]{:S(2)}) %collective-permute-start.5) | collective-permute-done | bytes 65568 | tf_op jit(solution)/shard_map/ppermute | solution.py:315
  41.3 2.7 %collective-permute-start.6 = (f32[128,128]{1,0:T(8,128)S(1)}, f32[128,128]{1,0:T(8,128)S(1)}, u32[]{:S(2)}, u32[]{:S(2)}) collective-permute-start(f32[128,128]{1,0:T(8,128)S(1)} %dynamic-slice_add_fusion), channel_id=1, source_target_pairs={{0,4},{1,3},{2,6},{3,1},{4,0},{5,7},{6,2},{7,5},{8,12},{9,11},{10,... | collective-permute-start | bytes 196616 | tf_op jit(solution)/shard_map/ppermute | solution.py:326
  44.0 2.2 %collective-permute-done.6 = f32[128,128]{1,0:T(8,128)S(1)} collective-permute-done((f32[128,128]{1,0:T(8,128)S(1)}, f32[128,128]{1,0:T(8,128)S(1)}, u32[]{:S(2)}, u32[]{:S(2)}) %collective-permute-start.6) | collective-permute-done | bytes 65568 | tf_op jit(solution)/shard_map/ppermute | solution.py:326
  46.2 1.6 %collective-permute-start.7 = (f32[128,128]{1,0:T(8,128)S(1)}, f32[128,128]{1,0:T(8,128)S(1)}, u32[]{:S(2)}, u32[]{:S(2)}) collective-permute-start(f32[128,128]{1,0:T(8,128)S(1)} %add.33), channel_id=1, source_target_pairs={{0,2},{1,5},{2,0},{3,7},{4,6},{5,1},{6,4},{7,3},{8,10},{9,13},{10,... | collective-permute-start | bytes 196616 | tf_op jit(solution)/shard_map/ppermute | solution.py:326
  47.8 2.7 %collective-permute-done.7 = f32[128,128]{1,0:T(8,128)S(1)} collective-permute-done((f32[128,128]{1,0:T(8,128)S(1)}, f32[128,128]{1,0:T(8,128)S(1)}, u32[]{:S(2)}, u32[]{:S(2)}) %collective-permute-start.7) | collective-permute-done | bytes 65568 | tf_op jit(solution)/shard_map/ppermute | solution.py:326
  50.6 2.2 %collective-permute-start.8 = (f32[128,128]{1,0:T(8,128)S(1)}, f32[128,128]{1,0:T(8,128)S(1)}, u32[]{:S(2)}, u32[]{:S(2)}) collective-permute-start(f32[128,128]{1,0:T(8,128)S(1)} %add.34), channel_id=1, source_target_pairs={{0,8},{1,17},{2,10},{3,19},{4,12},{5,21},{6,14},{7,23},{8,0},{9,25... | collective-permute-start | bytes 196616 | tf_op jit(solution)/shard_map/ppermute | solution.py:326
  52.7 2.2 %collective-permute-done.8 = f32[128,128]{1,0:T(8,128)S(1)} collective-permute-done((f32[128,128]{1,0:T(8,128)S(1)}, f32[128,128]{1,0:T(8,128)S(1)}, u32[]{:S(2)}, u32[]{:S(2)}) %collective-permute-start.8) | collective-permute-done | bytes 65568 | tf_op jit(solution)/shard_map/ppermute | solution.py:326
  55.0 3.1 %collective-permute-start.9 = (f32[128,128]{1,0:T(8,128)S(1)}, f32[128,128]{1,0:T(8,128)S(1)}, u32[]{:S(2)}, u32[]{:S(2)}) collective-permute-start(f32[128,128]{1,0:T(8,128)S(1)} %add.35), channel_id=1, source_target_pairs={{0,16},{1,9},{2,18},{3,11},{4,20},{5,13},{6,22},{7,15},{8,24},{9,1... | collective-permute-start | bytes 196616 | tf_op jit(solution)/shard_map/ppermute | solution.py:326
  58.1 2.2 %collective-permute-done.9 = f32[128,128]{1,0:T(8,128)S(1)} collective-permute-done((f32[128,128]{1,0:T(8,128)S(1)}, f32[128,128]{1,0:T(8,128)S(1)}, u32[]{:S(2)}, u32[]{:S(2)}) %collective-permute-start.9) | collective-permute-done | bytes 65568 | tf_op jit(solution)/shard_map/ppermute | solution.py:326
  60.3 0.1 collective-permute-start.10
  60.4 1.2 %collective-permute-done.10.other_ref = f32[128,128]{1,0:T(8,128)S(1)} collective-permute-done((f32[128,128]{1,0:T(8,128)S(1)}, f32[128,128]{1,0:T(8,128)S(1)}, u32[]{:S(2)}, u32[]{:S(2)}) %collective-permute-start.10) | collective-permute-done | bytes 65568 | tf_op jit(solution)/shard_map/ppermute | solution.py:315
  61.7 2.8 %modes.1 = (f32[2,64]{1,0:T(2,128)}, f32[256,128]{1,0:T(8,128)}) custom-call(s32[1]{0:T(128)} %bitcast.odd_ref, s32[1]{0:T(128)} %bitcast.1.core_ref, f32[128,128]{1,0:T(8,128)S(1)} %add.36.mine_ref, f32[128,128]{1,0:T(8,128)S(1)} %collective-permute-done.10.other_ref, bf16[2048,128]{1,0:T(8,128)(2,1)S(1)} %get-tuple-element.22.near_ref, ...), custom_call_target="tpu_custom_call" | custom-call | tf_op jit(solution)/shard_map/modes/pallas_call | solution.py:422
  (26 shorter events, 0.1 us)
Async XLA Ops:
  0.6 1.3 %copy-start = (bf16[2176,2,128]{2,1,0:T(2,128)(2,1)S(1)}, bf16[2176,2,128]{2,1,0:T(2,128)(2,1)}, u32[]{:S(2)}) copy-start(bf16[2176,2,128]{2,1,0:T(2,128)(2,1)} %param.11) | copy-start | bytes 3342340
  2.1 15.3 %copy-start.2 = (bf16[2176,2,128]{2,1,0:T(2,128)(2,1)S(1)}, bf16[2176,2,128]{2,1,0:T(2,128)(2,1)}, u32[]{:S(2)}) copy-start(bf16[2176,2,128]{2,1,0:T(2,128)(2,1)} %param.10) | copy-start | bytes 3342340
  2.1 15.3 %copy-start.3 = (bf16[8,16,128]{2,1,0:T(8,128)(2,1)S(1)}, bf16[8,16,128]{2,1,0:T(8,128)(2,1)}, u32[]{:S(2)}) copy-start(bf16[8,16,128]{2,1,0:T(8,128)(2,1)} %constant.42.clone.picks_ref) | copy-start | bytes 98308
  2.1 18.3 %copy-start.10 = (s32[64,2]{0,1:T(2,128)S(1)}, s32[64,2]{0,1:T(2,128)}, u32[]{:S(2)}) copy-start(s32[64,2]{0,1:T(2,128)} %param.14) | copy-start | bytes 1540
  2.2 21.8 %copy-start.1 = (bf16[2176,2,128]{2,1,0:T(2,128)(2,1)S(1)}, bf16[2176,2,128]{2,1,0:T(2,128)(2,1)}, u32[]{:S(2)}) copy-start(bf16[2176,2,128]{2,1,0:T(2,128)(2,1)} %param.11) | copy-start | bytes 3342340
  2.2 21.8 %copy-start.8 = (bf16[128,128]{1,0:T(8,128)(2,1)S(1)}, bf16[128,128]{1,0:T(8,128)(2,1)}, u32[]{:S(2)}) copy-start(bf16[128,128]{1,0:T(8,128)(2,1)} %constant.43.clone.shift_ref) | copy-start | bytes 98308
  2.2 21.8 %copy-start.9 = (bf16[8,16,128]{2,1,0:T(8,128)(2,1)S(1)}, bf16[8,16,128]{2,1,0:T(8,128)(2,1)}, u32[]{:S(2)}) copy-start(bf16[8,16,128]{2,1,0:T(8,128)(2,1)} %constant.44.clone.places_ref) | copy-start | bytes 98308
  2.2 9.7 %collective-permute-start.2 = (bf16[1088,128]{1,0:T(8,128)(2,1)S(1)}, bf16[1088,128]{1,0:T(8,128)(2,1)S(1)}, u32[]{:S(2)}, u32[]{:S(2)}) collective-permute-start(bf16[1088,128]{1,0:T(8,128)(2,1)S(1)} %get-tuple-element.18), channel_id=1, source_target_pairs={{0,4},{4,0},{8,12},{12,8},{16,20},{20,16},{24,28},{28,24},{1,5},{5... | collective-permute-start | bytes 835592 | tf_op jit(solution)/shard_map/ppermute | solution.py:315
  12.1 24.7 %collective-permute-start.3 = (bf16[2176,128]{1,0:T(8,128)(2,1)S(1)}, bf16[2176,128]{1,0:T(8,128)(2,1)}, u32[]{:S(2)}, u32[]{:S(2)}) collective-permute-start(bf16[2176,128]{1,0:T(8,128)(2,1)S(1)} %far.1), channel_id=1, source_target_pairs={{4,8},{12,16},{20,24},{8,4},{16,12},{24,20},{5,9},{13,17},{21,25},... | collective-permute-start | bytes 1671176 | tf_op jit(solution)/shard_map/ppermute | solution.py:458
  13.6 20.0 %collective-permute-start.4 = (bf16[1088,128]{1,0:T(8,128)(2,1)S(1)}, bf16[1088,128]{1,0:T(8,128)(2,1)}, u32[]{:S(2)}, u32[]{:S(2)}) collective-permute-start(bf16[1088,128]{1,0:T(8,128)(2,1)S(1)} %get-tuple-element.19), channel_id=1, source_target_pairs={{0,4},{4,0},{8,12},{12,8},{16,20},{20,16},{24,28},{28,24},{1,5},{5... | collective-permute-start | bytes 835592 | tf_op jit(solution)/shard_map/ppermute | solution.py:315
  17.8 2.8 %collective-permute-start = (bf16[8,544]{1,0:T(8,128)(2,1)S(1)}, bf16[8,544]{1,0:T(8,128)(2,1)S(1)}, u32[]{:S(2)}, u32[]{:S(2)}) collective-permute-start(bf16[8,544]{1,0:T(8,128)(2,1)S(1)} %get-tuple-element.14), channel_id=1, source_target_pairs={{0,1},{1,2},{2,3},{4,5},{5,6},{6,7},{8,9},{9,10},{10,11},{12,13},{... | collective-permute-start | bytes 26120 | tf_op jit(solution)/shard_map/ppermute | solution.py:460
  19.1 4.8 %collective-permute-start.1 = (bf16[8,544]{1,0:T(8,128)(2,1)S(1)}, bf16[8,544]{1,0:T(8,128)(2,1)S(1)}, u32[]{:S(2)}, u32[]{:S(2)}) collective-permute-start(bf16[8,544]{1,0:T(8,128)(2,1)S(1)} %get-tuple-element.15), channel_id=1, source_target_pairs={{1,0},{2,1},{3,2},{5,4},{6,5},{7,6},{9,8},{10,9},{11,10},{13,12},{... | collective-permute-start | bytes 26120 | tf_op jit(solution)/shard_map/ppermute | solution.py:461
  20.5 13.1 %copy-start.4 = (f32[2,128]{1,0:T(2,128)S(1)}, f32[2,128]{1,0:T(2,128)}, u32[]{:S(2)}) copy-start(f32[2,128]{1,0:T(2,128)} %weights_ref.3) | copy-start | bytes 3076
  20.5 13.1 %copy-start.5 = (s32[16]{0:T(128)S(1)}, s32[16]{0:T(128)}, u32[]{:S(2)}) copy-start(s32[16]{0:T(128)} %offsets_ref.3) | copy-start | bytes 196
  20.5 13.1 %copy-start.6 = (f32[256,128]{1,0:T(8,128)S(1)}, f32[256,128]{1,0:T(8,128)}, u32[]{:S(2)}) copy-start(f32[256,128]{1,0:T(8,128)} %constant.45.clone.window_ref) | copy-start | bytes 393220
  20.5 13.1 %copy-start.7 = (bf16[256,256]{1,0:T(8,128)(2,1)S(1)}, bf16[256,256]{1,0:T(8,128)(2,1)}, u32[]{:S(2)}) copy-start(bf16[256,256]{1,0:T(8,128)(2,1)} %constant.46.clone.transform_ref) | copy-start | bytes 393220
  40.0 1.3 %collective-permute-start.5 = (f32[128,128]{1,0:T(8,128)S(1)}, f32[128,128]{1,0:T(8,128)S(1)}, u32[]{:S(2)}, u32[]{:S(2)}) collective-permute-start(f32[128,128]{1,0:T(8,128)S(1)} %constant_dynamic-slice_fusion), channel_id=1, source_target_pairs={{0,1},{1,0},{2,3},{3,2},{4,5},{5,4},{6,7},{7,6},{8,9},{9,8},{10,11... | collective-permute-start | bytes 196616 | tf_op jit(solution)/shard_map/ppermute | solution.py:315
  41.3 4.9 %collective-permute-start.6 = (f32[128,128]{1,0:T(8,128)S(1)}, f32[128,128]{1,0:T(8,128)S(1)}, u32[]{:S(2)}, u32[]{:S(2)}) collective-permute-start(f32[128,128]{1,0:T(8,128)S(1)} %dynamic-slice_add_fusion), channel_id=1, source_target_pairs={{0,4},{1,3},{2,6},{3,1},{4,0},{5,7},{6,2},{7,5},{8,12},{9,11},{10,... | collective-permute-start | bytes 196616 | tf_op jit(solution)/shard_map/ppermute | solution.py:326
  46.2 4.3 %collective-permute-start.7 = (f32[128,128]{1,0:T(8,128)S(1)}, f32[128,128]{1,0:T(8,128)S(1)}, u32[]{:S(2)}, u32[]{:S(2)}) collective-permute-start(f32[128,128]{1,0:T(8,128)S(1)} %add.33), channel_id=1, source_target_pairs={{0,2},{1,5},{2,0},{3,7},{4,6},{5,1},{6,4},{7,3},{8,10},{9,13},{10,... | collective-permute-start | bytes 196616 | tf_op jit(solution)/shard_map/ppermute | solution.py:326
  50.6 4.4 %collective-permute-start.8 = (f32[128,128]{1,0:T(8,128)S(1)}, f32[128,128]{1,0:T(8,128)S(1)}, u32[]{:S(2)}, u32[]{:S(2)}) collective-permute-start(f32[128,128]{1,0:T(8,128)S(1)} %add.34), channel_id=1, source_target_pairs={{0,8},{1,17},{2,10},{3,19},{4,12},{5,21},{6,14},{7,23},{8,0},{9,25... | collective-permute-start | bytes 196616 | tf_op jit(solution)/shard_map/ppermute | solution.py:326
  55.0 5.3 %collective-permute-start.9 = (f32[128,128]{1,0:T(8,128)S(1)}, f32[128,128]{1,0:T(8,128)S(1)}, u32[]{:S(2)}, u32[]{:S(2)}) collective-permute-start(f32[128,128]{1,0:T(8,128)S(1)} %add.35), channel_id=1, source_target_pairs={{0,16},{1,9},{2,18},{3,11},{4,20},{5,13},{6,22},{7,15},{8,24},{9,1... | collective-permute-start | bytes 196616 | tf_op jit(solution)/shard_map/ppermute | solution.py:326
  60.3 1.3 %collective-permute-start.10 = (f32[128,128]{1,0:T(8,128)S(1)}, f32[128,128]{1,0:T(8,128)S(1)}, u32[]{:S(2)}, u32[]{:S(2)}) collective-permute-start(f32[128,128]{1,0:T(8,128)S(1)} %add.36.mine_ref), channel_id=1, source_target_pairs={{0,1},{1,0},{2,3},{3,2},{4,5},{5,4},{6,7},{7,6},{8,9},{9,8},{10,11... | collective-permute-start | bytes 196616 | tf_op jit(solution)/shard_map/ppermute | solution.py:315

commit v4 on v3

--- a/solution.py
+++ b/solution.py
@@ -64,7 +64,7 @@
 
 def near_edge(odd, v, sx):
     rows = v.shape[0]
-    early = rows // sx // 32 * 16
+    early = rows // sx * 3 // 4
     return pl.pallas_call(
         functools.partial(near_kernel, sx),
         out_shape=(
@@ -194,8 +194,8 @@
     halo_sum = jnp.zeros((8, LANES), F32)
     base = 0
     for halo_ref in halo_refs:
-        steps = 8 // pieces
-        chunk = halo_ref.shape[0] // steps
+        chunk = times // 8
+        steps = halo_ref.shape[0] // chunk
 
         def add_halo(step, carry):
             at = pl.ds(pl.multiple_of(step * chunk, 8), chunk)

time: 64.7 us -> 64.9 us (level)
  waiting for transfers between devices: 30.5 us -> 28.4 us
  local copies, waits for them, and re-layouts: 1.41 us -> 2.92 us
    ppermute x4, waiting for transfers between devices: 17.7 us -> 15.6 us  [swap(): return lax.ppermute(x, axis, [(i, i ^ bit) for i in range(count)])]
    unnamed x23, local copies, waits for them, and re-layouts: 1.4 us -> 2.9 us
  transfers between devices with their start and end apart: 11 -> 11, of which waited for: 9 -> 9; matrix products, arithmetic and copies ran while one was open for 0% -> 0% of each run, Pallas kernels for 7% -> 8%
where the time goes in v4:
time: 64.9 us; the launch traced here: 64.5 us
  waiting for transfers between devices  28.4 us (44%)
  starting transfers between devices  20.6 us (32%)
  Pallas kernels  11.7 us (18%)
  local copies, waits for them, and re-layouts  2.92 us (4%)
  between operations  0.83 us (1%)
    ppermute x4, waiting for transfers between devices, swap(): return lax.ppermute(x, axis, [(i, i ^ bit) for i in range(count)])  15.6 us
    ppermute x4, waiting for transfers between devices, sum_over_rest(): x = x + lax.ppermute(x, ('space', 'freq'), pairs)  9.48 us
    ppermute x4, starting transfers between devices, sum_over_rest(): x = x + lax.ppermute(x, ('space', 'freq'), pairs)  9.41 us
    ppermute x4, starting transfers between devices, swap(): return lax.ppermute(x, axis, [(i, i ^ bit) for i in range(count)])  6.95 us
    pallas_call x2, Pallas kernels, cross_part(): pl.pallas_call(functools.partial(cross_kernel, sx, begin, len(halos)), ou...  6.26 us
    ppermute x1, waiting for transfers between devices, on_device(): col_high = lax.ppermute(low, 'freq', [(i + 1, i) for i in range(ends)])  3.36 us
    unnamed x23, local copies, waits for them, and re-layouts  2.9 us
    pallas_call x1, Pallas kernels, modes_part(): pl.pallas_call(functools.partial(modes_kernel, sx, blocks, scaling), out_...  2.82 us
  transfers between devices with their start and end apart: 11, of which 9 were waited for; matrix products, arithmetic and copies ran while one was open for 0% of the time, Pallas kernels for 8%

profile of v4, /device:TPU:0, one launch (start us, length us, event | category | flops | bytes accessed | tf_op | source)
XLA Modules:
  0.0 64.5 jit_solution(14628216506503174630)
XLA Ops:
  0.7 1.2 %copy-done = bf16[2176,2,128]{2,1,0:T(2,128)(2,1)S(1)} copy-done((bf16[2176,2,128]{2,1,0:T(2,128)(2,1)S(1)}, bf16[2176,2,128]{2,1,0:T(2,128)(2,1)}, u32[]{:S(2)}) %copy-start) | copy-done | bytes 1114136
  1.9 0.2 near.1
  2.1 0.0 copy-start.3
  2.2 3.0 %collective-permute-start.2 = (bf16[1632,128]{1,0:T(8,128)(2,1)S(1)}, bf16[1632,128]{1,0:T(8,128)(2,1)S(1)}, u32[]{:S(2)}, u32[]{:S(2)}) collective-permute-start(bf16[1632,128]{1,0:T(8,128)(2,1)S(1)} %get-tuple-element.18), channel_id=1, source_target_pairs={{0,4},{4,0},{8,12},{12,8},{16,20},{20,16},{24,28},{28,24},{1,5},{5... | collective-permute-start | bytes 1253384 | tf_op jit(solution)/shard_map/ppermute | solution.py:315
  5.2 9.6 %collective-permute-done.2.after_ref.rest_0_ = bf16[1632,128]{1,0:T(8,128)(2,1)S(1)} collective-permute-done((bf16[1632,128]{1,0:T(8,128)(2,1)S(1)}, bf16[1632,128]{1,0:T(8,128)(2,1)S(1)}, u32[]{:S(2)}, u32[]{:S(2)}) %collective-permute-start.2) | collective-permute-done | bytes 417824 | tf_op jit(solution)/shard_map/ppermute | solution.py:315
  14.8 0.2 far.1
  15.1 1.6 %collective-permute-start.3 = (bf16[2176,128]{1,0:T(8,128)(2,1)S(1)}, bf16[2176,128]{1,0:T(8,128)(2,1)}, u32[]{:S(2)}, u32[]{:S(2)}) collective-permute-start(bf16[2176,128]{1,0:T(8,128)(2,1)S(1)} %far.1), channel_id=1, source_target_pairs={{4,8},{12,16},{20,24},{8,4},{16,12},{24,20},{5,9},{13,17},{21,25},... | collective-permute-start | bytes 1671176 | tf_op jit(solution)/shard_map/ppermute | solution.py:458
  16.7 3.8 %collective-permute-start.4 = (bf16[544,128]{1,0:T(8,128)(2,1)S(1)}, bf16[544,128]{1,0:T(8,128)(2,1)S(1)}, u32[]{:S(2)}, u32[]{:S(2)}) collective-permute-start(bf16[544,128]{1,0:T(8,128)(2,1)S(1)} %get-tuple-element.19), channel_id=1, source_target_pairs={{0,4},{4,0},{8,12},{12,8},{16,20},{20,16},{24,28},{28,24},{1,5},{5... | collective-permute-start | bytes 417800 | tf_op jit(solution)/shard_map/ppermute | solution.py:315
  20.5 1.0 %columns.1 = (bf16[8,544]{1,0:T(8,128)(2,1)S(1)}, bf16[8,544]{1,0:T(8,128)(2,1)}) custom-call(bf16[4352,128]{1,0:T(8,128)(2,1)S(1)} %bitcast.9, bf16[8,16,128]{2,1,0:T(8,128)(2,1)S(1)} %copy-done.3), custom_call_target="tpu_custom_call" | custom-call | tf_op jit(solution)/shard_map/columns/pallas_call | solution.py:116
  21.5 1.3 %collective-permute-start = (bf16[8,544]{1,0:T(8,128)(2,1)}, bf16[8,544]{1,0:T(8,128)(2,1)S(1)}, u32[]{:S(2)}, u32[]{:S(2)}) collective-permute-start(bf16[8,544]{1,0:T(8,128)(2,1)} %get-tuple-element.14), channel_id=1, source_target_pairs={{0,1},{1,2},{2,3},{4,5},{5,6},{6,7},{8,9},{9,10},{10,11},{12,13},{... | collective-permute-start | bytes 26120 | tf_op jit(solution)/shard_map/ppermute | solution.py:460
  22.8 1.3 %collective-permute-start.1 = (bf16[8,544]{1,0:T(8,128)(2,1)S(1)}, bf16[8,544]{1,0:T(8,128)(2,1)S(1)}, u32[]{:S(2)}, u32[]{:S(2)}) collective-permute-start(bf16[8,544]{1,0:T(8,128)(2,1)S(1)} %get-tuple-element.15), channel_id=1, source_target_pairs={{1,0},{2,1},{3,2},{5,4},{6,5},{7,6},{9,8},{10,9},{11,10},{13,12},{... | collective-permute-start | bytes 26120 | tf_op jit(solution)/shard_map/ppermute | solution.py:461
  24.1 0.1 copy.13.triads_ref
  24.2 3.4 %collective-permute-done.1.high_ref = bf16[8,544]{1,0:T(8,128)(2,1)S(1)} collective-permute-done((bf16[8,544]{1,0:T(8,128)(2,1)S(1)}, bf16[8,544]{1,0:T(8,128)(2,1)S(1)}, u32[]{:S(2)}, u32[]{:S(2)}) %collective-permute-start.1) | collective-permute-done | bytes 8736 | tf_op jit(solution)/shard_map/ppermute | solution.py:461
  27.6 0.8 %copy-done.8 = bf16[128,128]{1,0:T(8,128)(2,1)S(1)} copy-done((bf16[128,128]{1,0:T(8,128)(2,1)S(1)}, bf16[128,128]{1,0:T(8,128)(2,1)}, u32[]{:S(2)}) %copy-start.8) | copy-done | bytes 32792
  28.4 0.8 %copy-done.9 = bf16[8,16,128]{2,1,0:T(8,128)(2,1)S(1)} copy-done((bf16[8,16,128]{2,1,0:T(8,128)(2,1)S(1)}, bf16[8,16,128]{2,1,0:T(8,128)(2,1)}, u32[]{:S(2)}) %copy-start.9) | copy-done | bytes 32792
  29.1 1.1 %local.1 = (f32[2,2176,128]{2,1,0:T(8,128)S(1)}, f32[2,8,128]{2,1,0:T(8,128)S(1)}) custom-call(s32[1]{0:T(128)} %bitcast.odd_ref, bf16[4352,128]{1,0:T(8,128)(2,1)S(1)} %bitcast.8, bf16[4352,128]{1,0:T(8,128)(2,1)S(1)} %bitcast.10, bf16[128,128]{1,0:T(8,128)(2,1)S(1)} %copy-done.8, bf16[8,544]{1,0:T(8,128)(2,1)S(1)} %collective-permute-done.low_ref, ...), custom_call_target="tpu_custom_call" | custom-call | flops 1000000000 | bytes 8000000 | tf_op jit(solution)/shard_map/local/pallas_call | solution.py:157
  30.3 3.5 %collective-permute-done.4.rest_1_ = bf16[544,128]{1,0:T(8,128)(2,1)S(1)} collective-permute-done((bf16[544,128]{1,0:T(8,128)(2,1)S(1)}, bf16[544,128]{1,0:T(8,128)(2,1)S(1)}, u32[]{:S(2)}, u32[]{:S(2)}) %collective-permute-start.4) | collective-permute-done | bytes 139296 | tf_op jit(solution)/shard_map/ppermute | solution.py:315
  33.8 3.1 %cross_near.1 = (f32[256,128]{1,0:T(8,128)S(1)}, bf16[2048,128]{1,0:T(8,128)(2,1)S(1)}) custom-call(s32[1]{0:T(128)} %bitcast.odd_ref, s32[16]{0:T(128)S(1)} %copy-done.5, s32[64,2]{1,0:T(8,128)S(1)} %copy.13.triads_ref, f32[2,2176,128]{2,1,0:T(8,128)S(1)} %get-tuple-element.16.z_ref, f32[2,8,128]{2,1,0:T(8,128)S(1)} %get-tuple-element.17.sum_ref, ...), custom_call_target="tpu_custom_call" | custom-call | flops 2000000000 | bytes 4000000 | tf_op jit(solution)/shard_map/cross_near/pallas_call | solution.py:293
  36.9 3.1 %cross_far.1 = (f32[256,128]{1,0:T(8,128)S(1)}, bf16[2048,128]{1,0:T(8,128)(2,1)S(1)}) custom-call(s32[1]{0:T(128)} %bitcast.odd_ref, s32[16]{0:T(128)S(1)} %copy-done.5, s32[64,2]{1,0:T(8,128)S(1)} %copy.13.triads_ref, f32[2,2176,128]{2,1,0:T(8,128)S(1)} %get-tuple-element.16.z_ref, f32[2,8,128]{2,1,0:T(8,128)S(1)} %get-tuple-element.17.sum_ref, ...), custom_call_target="tpu_custom_call" | custom-call | flops 2000000000 | bytes 4000000 | tf_op jit(solution)/shard_map/cross_far/pallas_call | solution.py:293
  40.1 0.1 collective-permute-start.5
  40.2 1.2 %collective-permute-done.5 = f32[128,128]{1,0:T(8,128)S(1)} collective-permute-done((f32[128,128]{1,0:T(8,128)S(1)}, f32[128,128]{1,0:T(8,128)S(1)}, u32[]{:S(2)}, u32[]{:S(2)}) %collective-permute-start.5) | collective-permute-done | bytes 65568 | tf_op jit(solution)/shard_map/ppermute | solution.py:315
  41.4 2.5 %collective-permute-start.6 = (f32[128,128]{1,0:T(8,128)S(1)}, f32[128,128]{1,0:T(8,128)S(1)}, u32[]{:S(2)}, u32[]{:S(2)}) collective-permute-start(f32[128,128]{1,0:T(8,128)S(1)} %dynamic-slice_add_fusion), channel_id=1, source_target_pairs={{0,4},{1,3},{2,6},{3,1},{4,0},{5,7},{6,2},{7,5},{8,12},{9,11},{10,... | collective-permute-start | bytes 196616 | tf_op jit(solution)/shard_map/ppermute | solution.py:326
  43.9 2.2 %collective-permute-done.6 = f32[128,128]{1,0:T(8,128)S(1)} collective-permute-done((f32[128,128]{1,0:T(8,128)S(1)}, f32[128,128]{1,0:T(8,128)S(1)}, u32[]{:S(2)}, u32[]{:S(2)}) %collective-permute-start.6) | collective-permute-done | bytes 65568 | tf_op jit(solution)/shard_map/ppermute | solution.py:326
  46.2 1.6 %collective-permute-start.7 = (f32[128,128]{1,0:T(8,128)S(1)}, f32[128,128]{1,0:T(8,128)S(1)}, u32[]{:S(2)}, u32[]{:S(2)}) collective-permute-start(f32[128,128]{1,0:T(8,128)S(1)} %add.33), channel_id=1, source_target_pairs={{0,2},{1,5},{2,0},{3,7},{4,6},{5,1},{6,4},{7,3},{8,10},{9,13},{10,... | collective-permute-start | bytes 196616 | tf_op jit(solution)/shard_map/ppermute | solution.py:326
  47.8 2.7 %collective-permute-done.7 = f32[128,128]{1,0:T(8,128)S(1)} collective-permute-done((f32[128,128]{1,0:T(8,128)S(1)}, f32[128,128]{1,0:T(8,128)S(1)}, u32[]{:S(2)}, u32[]{:S(2)}) %collective-permute-start.7) | collective-permute-done | bytes 65568 | tf_op jit(solution)/shard_map/ppermute | solution.py:326
  50.6 2.2 %collective-permute-start.8 = (f32[128,128]{1,0:T(8,128)S(1)}, f32[128,128]{1,0:T(8,128)S(1)}, u32[]{:S(2)}, u32[]{:S(2)}) collective-permute-start(f32[128,128]{1,0:T(8,128)S(1)} %add.34), channel_id=1, source_target_pairs={{0,8},{1,17},{2,10},{3,19},{4,12},{5,21},{6,14},{7,23},{8,0},{9,25... | collective-permute-start | bytes 196616 | tf_op jit(solution)/shard_map/ppermute | solution.py:326
  52.7 2.2 %collective-permute-done.8 = f32[128,128]{1,0:T(8,128)S(1)} collective-permute-done((f32[128,128]{1,0:T(8,128)S(1)}, f32[128,128]{1,0:T(8,128)S(1)}, u32[]{:S(2)}, u32[]{:S(2)}) %collective-permute-start.8) | collective-permute-done | bytes 65568 | tf_op jit(solution)/shard_map/ppermute | solution.py:326
  55.0 3.1 %collective-permute-start.9 = (f32[128,128]{1,0:T(8,128)S(1)}, f32[128,128]{1,0:T(8,128)S(1)}, u32[]{:S(2)}, u32[]{:S(2)}) collective-permute-start(f32[128,128]{1,0:T(8,128)S(1)} %add.35), channel_id=1, source_target_pairs={{0,16},{1,9},{2,18},{3,11},{4,20},{5,13},{6,22},{7,15},{8,24},{9,1... | collective-permute-start | bytes 196616 | tf_op jit(solution)/shard_map/ppermute | solution.py:326
  58.1 2.2 %collective-permute-done.9 = f32[128,128]{1,0:T(8,128)S(1)} collective-permute-done((f32[128,128]{1,0:T(8,128)S(1)}, f32[128,128]{1,0:T(8,128)S(1)}, u32[]{:S(2)}, u32[]{:S(2)}) %collective-permute-start.9) | collective-permute-done | bytes 65568 | tf_op jit(solution)/shard_map/ppermute | solution.py:326
  60.3 0.1 collective-permute-start.10
  60.4 1.2 %collective-permute-done.10.other_ref = f32[128,128]{1,0:T(8,128)S(1)} collective-permute-done((f32[128,128]{1,0:T(8,128)S(1)}, f32[128,128]{1,0:T(8,128)S(1)}, u32[]{:S(2)}, u32[]{:S(2)}) %collective-permute-start.10) | collective-permute-done | bytes 65568 | tf_op jit(solution)/shard_map/ppermute | solution.py:315
  61.7 2.8 %modes.1 = (f32[2,64]{1,0:T(2,128)}, f32[256,128]{1,0:T(8,128)}) custom-call(s32[1]{0:T(128)} %bitcast.odd_ref, s32[1]{0:T(128)} %bitcast.1.core_ref, f32[128,128]{1,0:T(8,128)S(1)} %add.36.mine_ref, f32[128,128]{1,0:T(8,128)S(1)} %collective-permute-done.10.other_ref, bf16[2048,128]{1,0:T(8,128)(2,1)S(1)} %get-tuple-element.22.near_ref, ...), custom_call_target="tpu_custom_call" | custom-call | tf_op jit(solution)/shard_map/modes/pallas_call | solution.py:422
  (26 shorter events, 0.1 us)
Async XLA Ops:
  0.6 1.3 %copy-start = (bf16[2176,2,128]{2,1,0:T(2,128)(2,1)S(1)}, bf16[2176,2,128]{2,1,0:T(2,128)(2,1)}, u32[]{:S(2)}) copy-start(bf16[2176,2,128]{2,1,0:T(2,128)(2,1)} %param.11) | copy-start | bytes 3342340
  2.1 18.4 %copy-start.2 = (bf16[2176,2,128]{2,1,0:T(2,128)(2,1)S(1)}, bf16[2176,2,128]{2,1,0:T(2,128)(2,1)}, u32[]{:S(2)}) copy-start(bf16[2176,2,128]{2,1,0:T(2,128)(2,1)} %param.10) | copy-start | bytes 3342340
  2.1 18.3 %copy-start.3 = (bf16[8,16,128]{2,1,0:T(8,128)(2,1)S(1)}, bf16[8,16,128]{2,1,0:T(8,128)(2,1)}, u32[]{:S(2)}) copy-start(bf16[8,16,128]{2,1,0:T(8,128)(2,1)} %constant.42.clone.picks_ref) | copy-start | bytes 98308
  2.1 22.0 %copy-start.10 = (s32[64,2]{0,1:T(2,128)S(1)}, s32[64,2]{0,1:T(2,128)}, u32[]{:S(2)}) copy-start(s32[64,2]{0,1:T(2,128)} %param.14) | copy-start | bytes 1540
  2.2 12.7 %collective-permute-start.2 = (bf16[1632,128]{1,0:T(8,128)(2,1)S(1)}, bf16[1632,128]{1,0:T(8,128)(2,1)S(1)}, u32[]{:S(2)}, u32[]{:S(2)}) collective-permute-start(bf16[1632,128]{1,0:T(8,128)(2,1)S(1)} %get-tuple-element.18), channel_id=1, source_target_pairs={{0,4},{4,0},{8,12},{12,8},{16,20},{20,16},{24,28},{28,24},{1,5},{5... | collective-permute-start | bytes 1253384 | tf_op jit(solution)/shard_map/ppermute | solution.py:315
  15.1 12.6 %copy-start.1 = (bf16[2176,2,128]{2,1,0:T(2,128)(2,1)S(1)}, bf16[2176,2,128]{2,1,0:T(2,128)(2,1)}, u32[]{:S(2)}) copy-start(bf16[2176,2,128]{2,1,0:T(2,128)(2,1)} %param.11) | copy-start | bytes 3342340
  15.1 21.8 %collective-permute-start.3 = (bf16[2176,128]{1,0:T(8,128)(2,1)S(1)}, bf16[2176,128]{1,0:T(8,128)(2,1)}, u32[]{:S(2)}, u32[]{:S(2)}) collective-permute-start(bf16[2176,128]{1,0:T(8,128)(2,1)S(1)} %far.1), channel_id=1, source_target_pairs={{4,8},{12,16},{20,24},{8,4},{16,12},{24,20},{5,9},{13,17},{21,25},... | collective-permute-start | bytes 1671176 | tf_op jit(solution)/shard_map/ppermute | solution.py:458
  16.7 17.0 %collective-permute-start.4 = (bf16[544,128]{1,0:T(8,128)(2,1)S(1)}, bf16[544,128]{1,0:T(8,128)(2,1)S(1)}, u32[]{:S(2)}, u32[]{:S(2)}) collective-permute-start(bf16[544,128]{1,0:T(8,128)(2,1)S(1)} %get-tuple-element.19), channel_id=1, source_target_pairs={{0,4},{4,0},{8,12},{12,8},{16,20},{20,16},{24,28},{28,24},{1,5},{5... | collective-permute-start | bytes 417800 | tf_op jit(solution)/shard_map/ppermute | solution.py:315
  21.5 2.7 %collective-permute-start = (bf16[8,544]{1,0:T(8,128)(2,1)}, bf16[8,544]{1,0:T(8,128)(2,1)S(1)}, u32[]{:S(2)}, u32[]{:S(2)}) collective-permute-start(bf16[8,544]{1,0:T(8,128)(2,1)} %get-tuple-element.14), channel_id=1, source_target_pairs={{0,1},{1,2},{2,3},{4,5},{5,6},{6,7},{8,9},{9,10},{10,11},{12,13},{... | collective-permute-start | bytes 26120 | tf_op jit(solution)/shard_map/ppermute | solution.py:460
  22.8 4.8 %collective-permute-start.1 = (bf16[8,544]{1,0:T(8,128)(2,1)S(1)}, bf16[8,544]{1,0:T(8,128)(2,1)S(1)}, u32[]{:S(2)}, u32[]{:S(2)}) collective-permute-start(bf16[8,544]{1,0:T(8,128)(2,1)S(1)} %get-tuple-element.15), channel_id=1, source_target_pairs={{1,0},{2,1},{3,2},{5,4},{6,5},{7,6},{9,8},{10,9},{11,10},{13,12},{... | collective-permute-start | bytes 26120 | tf_op jit(solution)/shard_map/ppermute | solution.py:461
  24.2 9.6 %copy-start.4 = (f32[2,128]{1,0:T(2,128)S(1)}, f32[2,128]{1,0:T(2,128)}, u32[]{:S(2)}) copy-start(f32[2,128]{1,0:T(2,128)} %weights_ref.3) | copy-start | bytes 3076
  24.2 9.6 %copy-start.5 = (s32[16]{0:T(128)S(1)}, s32[16]{0:T(128)}, u32[]{:S(2)}) copy-start(s32[16]{0:T(128)} %offsets_ref.3) | copy-start | bytes 196
  24.2 9.5 %copy-start.6 = (f32[256,128]{1,0:T(8,128)S(1)}, f32[256,128]{1,0:T(8,128)}, u32[]{:S(2)}) copy-start(f32[256,128]{1,0:T(8,128)} %constant.45.clone.window_ref) | copy-start | bytes 393220
  24.2 9.5 %copy-start.7 = (bf16[256,256]{1,0:T(8,128)(2,1)S(1)}, bf16[256,256]{1,0:T(8,128)(2,1)}, u32[]{:S(2)}) copy-start(bf16[256,256]{1,0:T(8,128)(2,1)} %constant.46.clone.transform_ref) | copy-start | bytes 393220
  27.6 0.8 %copy-start.8 = (bf16[128,128]{1,0:T(8,128)(2,1)S(1)}, bf16[128,128]{1,0:T(8,128)(2,1)}, u32[]{:S(2)}) copy-start(bf16[128,128]{1,0:T(8,128)(2,1)} %constant.43.clone.shift_ref) | copy-start | bytes 98308
  28.4 0.8 %copy-start.9 = (bf16[8,16,128]{2,1,0:T(8,128)(2,1)S(1)}, bf16[8,16,128]{2,1,0:T(8,128)(2,1)}, u32[]{:S(2)}) copy-start(bf16[8,16,128]{2,1,0:T(8,128)(2,1)} %constant.44.clone.places_ref) | copy-start | bytes 98308
  40.1 1.3 %collective-permute-start.5 = (f32[128,128]{1,0:T(8,128)S(1)}, f32[128,128]{1,0:T(8,128)S(1)}, u32[]{:S(2)}, u32[]{:S(2)}) collective-permute-start(f32[128,128]{1,0:T(8,128)S(1)} %constant_dynamic-slice_fusion), channel_id=1, source_target_pairs={{0,1},{1,0},{2,3},{3,2},{4,5},{5,4},{6,7},{7,6},{8,9},{9,8},{10,11... | collective-permute-start | bytes 196616 | tf_op jit(solution)/shard_map/ppermute | solution.py:315
  41.4 4.8 %collective-permute-start.6 = (f32[128,128]{1,0:T(8,128)S(1)}, f32[128,128]{1,0:T(8,128)S(1)}, u32[]{:S(2)}, u32[]{:S(2)}) collective-permute-start(f32[128,128]{1,0:T(8,128)S(1)} %dynamic-slice_add_fusion), channel_id=1, source_target_pairs={{0,4},{1,3},{2,6},{3,1},{4,0},{5,7},{6,2},{7,5},{8,12},{9,11},{10,... | collective-permute-start | bytes 196616 | tf_op jit(solution)/shard_map/ppermute | solution.py:326
  46.2 4.3 %collective-permute-start.7 = (f32[128,128]{1,0:T(8,128)S(1)}, f32[128,128]{1,0:T(8,128)S(1)}, u32[]{:S(2)}, u32[]{:S(2)}) collective-permute-start(f32[128,128]{1,0:T(8,128)S(1)} %add.33), channel_id=1, source_target_pairs={{0,2},{1,5},{2,0},{3,7},{4,6},{5,1},{6,4},{7,3},{8,10},{9,13},{10,... | collective-permute-start | bytes 196616 | tf_op jit(solution)/shard_map/ppermute | solution.py:326
  50.6 4.4 %collective-permute-start.8 = (f32[128,128]{1,0:T(8,128)S(1)}, f32[128,128]{1,0:T(8,128)S(1)}, u32[]{:S(2)}, u32[]{:S(2)}) collective-permute-start(f32[128,128]{1,0:T(8,128)S(1)} %add.34), channel_id=1, source_target_pairs={{0,8},{1,17},{2,10},{3,19},{4,12},{5,21},{6,14},{7,23},{8,0},{9,25... | collective-permute-start | bytes 196616 | tf_op jit(solution)/shard_map/ppermute | solution.py:326
  55.0 5.3 %collective-permute-start.9 = (f32[128,128]{1,0:T(8,128)S(1)}, f32[128,128]{1,0:T(8,128)S(1)}, u32[]{:S(2)}, u32[]{:S(2)}) collective-permute-start(f32[128,128]{1,0:T(8,128)S(1)} %add.35), channel_id=1, source_target_pairs={{0,16},{1,9},{2,18},{3,11},{4,20},{5,13},{6,22},{7,15},{8,24},{9,1... | collective-permute-start | bytes 196616 | tf_op jit(solution)/shard_map/ppermute | solution.py:326
  60.3 1.3 %collective-permute-start.10 = (f32[128,128]{1,0:T(8,128)S(1)}, f32[128,128]{1,0:T(8,128)S(1)}, u32[]{:S(2)}, u32[]{:S(2)}) collective-permute-start(f32[128,128]{1,0:T(8,128)S(1)} %add.36.mine_ref), channel_id=1, source_target_pairs={{0,1},{1,0},{2,3},{3,2},{4,5},{5,4},{6,7},{7,6},{8,9},{9,8},{10,11... | collective-permute-start | bytes 196616 | tf_op jit(solution)/shard_map/ppermute | solution.py:315

commit v5 on v4

--- a/solution.py
+++ b/solution.py
@@ -13,6 +13,7 @@
 NFFT = 256
 POW = 4
 LANES = 128
+PIECES = 4
 F32 = jnp.float32
 BF16 = jnp.bfloat16
 MIB = 2**20
@@ -54,51 +55,47 @@
     return pltpu.CompilerParams(vmem_limit_bytes=mib * MIB)
 
 
-def near_kernel(sx, odd_ref, v_ref, early_ref, late_ref, plain):
+def near_kernel(sx, odd_ref, v_ref, near_ref, plain):
     plain[...] = v_ref[...].astype(F32)
-    row = row_at(0, sx, odd_ref[0])
-    early, late = early_ref.shape[0], late_ref.shape[0]
-    early_ref[...] = plain[pl.ds(row, early, stride=sx), :].astype(BF16)
-    late_ref[...] = plain[pl.ds(early * sx + row, late, stride=sx), :].astype(BF16)
+    near_ref[...] = plain[pl.ds(row_at(0, sx, odd_ref[0]), near_ref.shape[0], stride=sx), :].astype(BF16)
 
 
 def near_edge(odd, v, sx):
     rows = v.shape[0]
-    early = rows // sx * 3 // 4
     return pl.pallas_call(
         functools.partial(near_kernel, sx),
-        out_shape=(
-            jax.ShapeDtypeStruct((early, LANES), BF16),
-            jax.ShapeDtypeStruct((rows // sx - early, LANES), BF16),
-        ),
+        out_shape=jax.ShapeDtypeStruct((rows // sx, LANES), BF16),
         in_specs=[SMEM, VMEM],
-        out_specs=(VMEM,) * 2,
+        out_specs=VMEM,
         scratch_shapes=[pltpu.VMEM((rows, LANES), F32)],
         compiler_params=limit(8),
         name="near",
     )(odd, v)
 
 
-def far_kernel(sx, odd_ref, v_ref, after_ref, far_ref, plain):
-    times = far_ref.shape[0]
+def far_kernel(sx, odd_ref, v_ref, *rest):
+    far_refs, plain = rest[:-1], rest[-1]
     plain[...] = v_ref[...].astype(F32)
-    far_ref[...] = plain[pl.ds(row_at(sx - 1, sx, odd_ref[0]), times, stride=sx), :].astype(BF16)
-
-
-def far_edge(odd, v, after, sx):
+    row = row_at(sx - 1, sx, odd_ref[0])
+    for k, far_ref in enumerate(far_refs):
+        times = far_ref.shape[0]
+        far_ref[...] = plain[pl.ds(k * times * sx + row, times, stride=sx), :].astype(BF16)
+
+
+def far_edge(odd, v, sx):
     rows = v.shape[0]
     return pl.pallas_call(
         functools.partial(far_kernel, sx),
-        out_shape=jax.ShapeDtypeStruct((rows // sx, LANES), BF16),
-        in_specs=[SMEM, VMEM, pl.BlockSpec(memory_space=pl.ANY)],
-        out_specs=VMEM,
+        out_shape=(jax.ShapeDtypeStruct((rows // sx // PIECES, LANES), BF16),) * PIECES,
+        in_specs=[SMEM, VMEM],
+        out_specs=(VMEM,) * PIECES,
         scratch_shapes=[pltpu.VMEM((rows, LANES), F32)],
         compiler_params=limit(8),
         name="far",
-    )(odd, v, after)
-
-
-def columns_kernel(pieces, u_ref, picks_ref, low_ref, high_ref):
+    )(odd, v)
+
+
+def columns_kernel(pieces, side_ref, u_ref, picks_ref, near_ref, far_ref):
     rows = u_ref.shape[0]
     part = rows // pieces
     cols = jnp.zeros((2 * pieces, part), F32)
@@ -106,28 +103,27 @@
         cols += lax.dot_general(
             picks_ref[m], u_ref[m * part : (m + 1) * part, :], (((1,), (1,)), ((), ())), preferred_element_type=F32
         )
-    low_ref[...] = cols[:pieces].astype(BF16)
-    high_ref[...] = cols[pieces:].astype(BF16)
-
-
-def columns_edge(u, picks):
+    low, high = cols[:pieces], cols[pieces:]
+    odd = side_ref[0] == 1
+    near_ref[...] = jnp.where(odd, low, high).astype(BF16)
+    far_ref[...] = jnp.where(odd, high, low).astype(BF16)
+
+
+def columns_edge(side, u, picks):
     rows = u.shape[0]
     pieces = picks.shape[0]
     return pl.pallas_call(
         functools.partial(columns_kernel, pieces),
-        out_shape=(
-            jax.ShapeDtypeStruct((pieces, rows // pieces), BF16),
-            jax.ShapeDtypeStruct((pieces, rows // pieces), BF16),
-        ),
-        in_specs=[VMEM] * 2,
+        out_shape=(jax.ShapeDtypeStruct((pieces, rows // pieces), BF16),) * 2,
+        in_specs=[SMEM] + [VMEM] * 2,
         out_specs=(VMEM,) * 2,
         compiler_params=limit(8),
         name="columns",
-    )(u, picks)
+    )(side, u, picks)
 
 
 def local_kernel(
-    sx, pieces, odd_ref, v_ref, u_ref, shift_ref, low_ref, high_ref, places_ref, z_ref, sum_ref, plain, slope
+    sx, pieces, odd_ref, side_ref, v_ref, u_ref, shift_ref, near_ref, far_ref, places_ref, z_ref, sum_ref, plain, slope
 ):
     rows = v_ref.shape[0]
     times = rows // sx
@@ -135,7 +131,9 @@
     odd = odd_ref[0]
     sign = jnp.where(odd == 1, 0.5, -0.5)
     plain[...] = sign * v_ref[...].astype(F32)
-    cols = jnp.concatenate([low_ref[...], high_ref[...]], axis=0)
+    near, far = near_ref[...].astype(F32), far_ref[...].astype(F32)
+    side = side_ref[0] == 1
+    cols = jnp.concatenate([jnp.where(side, near, far), jnp.where(side, far, near)], axis=0).astype(BF16)
     for m in range(pieces):
         inner = jnp.dot(u_ref[m * part : (m + 1) * part, :], shift_ref[...], preferred_element_type=F32)
         outer = lax.dot_general(cols, places_ref[m], (((0,), (0,)), ((), ())), preferred_element_type=F32)
@@ -150,7 +148,7 @@
         sum_ref[position] = jnp.sum(z.reshape(times // 8, 8, LANES), axis=0)
 
 
-def local_part(odd, v, u, shift, low, high, places, sx):
+def local_part(odd, side, v, u, shift, near, far, places, sx):
     rows = v.shape[0]
     pieces = places.shape[0]
     times = rows // sx
@@ -160,17 +158,17 @@
             jax.ShapeDtypeStruct((sx, times, LANES), F32),
             jax.ShapeDtypeStruct((sx, 8, LANES), F32),
         ),
-        in_specs=[SMEM] + [VMEM] * 6,
+        in_specs=[SMEM] * 2 + [VMEM] * 6,
         out_specs=(VMEM,) * 2,
         scratch_shapes=[pltpu.VMEM((rows, LANES), F32), pltpu.VMEM((rows, LANES), F32)],
         compiler_params=limit(20),
         cost_estimate=pl.CostEstimate(flops=1000000000, bytes_accessed=8000000, transcendentals=0),
         name="local",
-    )(odd, v, u, shift, low, high, places)
+    )(odd, side, v, u, shift, near, far, places)
 
 
 def cross_kernel(
-    sx, begin, pieces, odd_ref, offsets_ref, triads_ref, z_ref, sum_ref, weights_ref, window_ref, transform_ref, *rest
+    sx, begin, pieces, blocks, ntri, scalars_ref, z_ref, sum_ref, weights_ref, window_ref, transform_ref, *rest
 ):
     far = begin > 0
     halo_refs, rest = rest[:pieces], rest[pieces:]
@@ -178,14 +176,12 @@
         before_ref, *rest = rest
     cross_ref, target_ref, full, spec, prod, packed = rest
     count, times, _ = full.shape
-    blocks = offsets_ref.shape[0]
-    ntri = triads_ref.shape[0]
     half = NFFT // 2
     groups = LANES // blocks
     per = ntri // groups
     wide = 2 * blocks
     pitch = blocks + 1
-    odd = odd_ref[0]
+    odd = scalars_ref[0]
     sign = jnp.where(odd == 1, 0.5, -0.5)
     if not far:
         sign = -sign
@@ -216,7 +212,7 @@
         means.append(jnp.sum(total, axis=0, keepdims=True) * (1.0 / times))
 
     def one_block(b, carry):
-        at = pl.ds(offsets_ref[b], NFFT)
+        at = pl.ds(scalars_ref[1 + b], NFFT)
         window = window_ref[...]
         for row in range(count):
             windowed = ((full[row, at, :] - means[row]) * window).astype(BF16)
@@ -228,8 +224,8 @@
     weights = [weights_ref[pl.ds(row_at(begin + row, sx, odd), 1), :] for row in range(count)]
 
     def one_triad(j, carry):
-        k = triads_ref[j, 0]
-        l = triads_ref[j, 1]
+        k = scalars_ref[1 + blocks + 2 * j]
+        l = scalars_ref[2 + blocks + 2 * j]
 
         def take(f, row):
             re = spec[row, pl.ds(f * pitch, blocks), :]
@@ -282,21 +278,19 @@
     cross_ref[...] = share
 
 
-def cross_part(begin, count, odd, offsets, triads, z, sums, halos, weights, window, transform, before=None):
+def cross_part(begin, count, blocks, ntri, scalars, z, sums, halos, weights, window, transform, before=None):
     sx, times, _ = z.shape
-    blocks = offsets.shape[0]
-    ntri = triads.shape[0]
     groups = LANES // blocks
     wide = 2 * blocks
     tall = ntri // groups * wide
     more = list(halos) + ([] if before is None else [before])
     return pl.pallas_call(
-        functools.partial(cross_kernel, sx, begin, len(halos)),
+        functools.partial(cross_kernel, sx, begin, len(halos), blocks, ntri),
         out_shape=(
             jax.ShapeDtypeStruct((tall, LANES), F32),
             jax.ShapeDtypeStruct((ntri * wide, count * LANES), BF16),
         ),
-        in_specs=[SMEM] * 3 + [VMEM] * (5 + len(more)),
+        in_specs=[SMEM] + [VMEM] * (5 + len(more)),
         out_specs=(VMEM,) * 2,
         scratch_shapes=[
             pltpu.VMEM((count, times, LANES), F32),
@@ -307,7 +301,7 @@
         compiler_params=limit(26),
         cost_estimate=pl.CostEstimate(flops=2000000000, bytes_accessed=4000000, transcendentals=0),
         name="cross_far" if begin else "cross_near",
-    )(odd, offsets, triads, z, sums, weights, window, transform, *more)
+    )(scalars, z, sums, weights, window, transform, *more)
 
 
 def swap(x, axis, bit):
@@ -352,34 +346,40 @@
 
     spots = [start + c for c in range(blocks)]
 
+    def tree(terms):
+        while len(terms) > 1:
+            terms = [sum(terms[n : n + 2]) for n in range(0, len(terms), 2)]
+        return terms[0]
+
     def apply(part_re, part_im):
-        sums = []
-        for parity in range(2):
-            out_re = jnp.zeros((per, LANES), F32)
-            out_im = jnp.zeros((per, LANES), F32)
-            for c in range(parity, blocks, 2):
-                re = pick(part_re, spots[c])
-                im = pick(part_im, spots[c])
-                out_re += mat_re[c] * re - mat_im[c] * im
-                out_im += mat_re[c] * im + mat_im[c] * re
-            sums.append((out_re, out_im))
-        return sums[0][0] + sums[1][0], sums[0][1] + sums[1][1]
+        re = [pick(part_re, spot) for spot in spots]
+        im = [pick(part_im, spot) for spot in spots]
+        every = range(blocks)
+        out_re = tree([mat_re[c] * re[c] - mat_im[c] * im[c] for c in every])
+        out_im = tree([mat_re[c] * im[c] + mat_im[c] * re[c] for c in every])
+        return out_re, out_im
 
     def over_blocks(x):
         bit = 1
         while bit < blocks:
-            x = x + pick(x, lane ^ bit)
-            bit *= 2
+            if 4 * bit <= blocks:
+                x = (x + pick(x, lane ^ bit)) + (pick(x, lane ^ (2 * bit)) + pick(x, lane ^ (3 * bit)))
+                bit *= 4
+            else:
+                x = x + pick(x, lane ^ bit)
+                bit *= 2
         return x
 
     vec_re = jnp.full((per, LANES), 1.0 / math.sqrt(blocks), F32)
     vec_im = jnp.zeros((per, LANES), F32)
+    out_re, out_im = apply(vec_re, vec_im)
     for _ in range(POW):
-        out_re, out_im = apply(vec_re, vec_im)
         length = jnp.sqrt(over_blocks(out_re * out_re + out_im * out_im))
         vec_re = out_re / length
         vec_im = out_im / length
-    out_re, out_im = apply(vec_re, vec_im)
+        out_re, out_im = apply(out_re, out_im)
+        out_re = out_re / length
+        out_im = out_im / length
     value_re = over_blocks(vec_re * out_re + vec_im * out_im)
     value_im = over_blocks(vec_re * out_im - vec_im * out_re)
 
@@ -433,6 +433,48 @@
     )(odd, core, mine, other, near, far)
 
 
+def between_pairs(count):
+    inner = [(i, i + 1) for i in range(1, count - 1, 2)]
+    return inner + [(b, a) for a, b in inner]
+
+
+def start_of(k, pairs):
+    return k * pairs // PIECES
+
+
+def stage_far(far):
+    pairs = lax.axis_size("space") // 2
+    index = lax.axis_index("space")
+    place = jnp.where(index % 2 == 1, index // 2, pairs - 1 - index // 2)
+    staged = []
+    for k, piece in enumerate(far):
+        start = start_of(k, pairs)
+        hops = [(2 * b + 1, 2 * b + 3) for b in range(start, pairs - 1)]
+        hops += [(2 * (pairs - 1 - b), 2 * (pairs - 2 - b)) for b in range(start, pairs - 1)]
+        if hops:
+            passed = lax.ppermute(piece, "space", hops)
+            piece = jnp.where(place > start, passed, piece)
+        staged.append(piece)
+    return staged
+
+
+def cross_far_edge(staged):
+    pairs = lax.axis_size("space") // 2
+    far = []
+    for k, piece in enumerate(staged):
+        start = start_of(k, pairs)
+        hops = []
+        for b in range(pairs - 1):
+            if b < start:
+                hops.append((2 * b + 1, 2 * b + 2))
+                hops.append((2 * (pairs - 1 - b), 2 * (pairs - 1 - b) - 1))
+            else:
+                hops.append((2 * b + 3, 2 * b + 2))
+                hops.append((2 * (pairs - 2 - b), 2 * (pairs - 2 - b) + 1))
+        far.append(lax.ppermute(piece, "space", hops))
+    return far
+
+
 def on_device(u_velocity, v_velocity, cell_weights, block_offsets, triads):
     times, sx, columns = u_velocity.shape
     blocks = block_offsets.shape[0]
@@ -448,25 +490,22 @@
     u = u_velocity.reshape(times * sx, columns)
     odd = is_odd()[None]
     core = (lax.axis_index("freq") % 2)[None]
-
-    early, late = near_edge(odd, v, sx)
-    early = swap(early, "space", 1)
-    late = swap(late, "space", 1)
-    low, high = columns_edge(u, jnp.asarray(picks, BF16))
-    far = far_edge(odd, v, early, sx)
-    inner = [(i, i + 1) for i in range(1, slabs - 1, 2)]
-    far = lax.ppermute(far, "space", inner + [(b, a) for a, b in inner])
-    ends = lax.axis_size("freq") - 1
-    col_low = lax.ppermute(high, "freq", [(i, i + 1) for i in range(ends)])
-    col_high = lax.ppermute(low, "freq", [(i + 1, i) for i in range(ends)])
-    z, sums = local_part(odd, v, u, jnp.asarray(shift, BF16), col_low, col_high, jnp.asarray(places, BF16), sx)
+    scalars = jnp.concatenate([odd, block_offsets, triads.reshape(-1)])
+
+    near = near_edge(odd, v, sx)
+    near = swap(near, "space", 1)
+    far = far_edge(odd, v, sx)
+    staged = stage_far(far)
+    col_near, col_far = columns_edge(core, u, jnp.asarray(picks, BF16))
+    col_near = swap(col_near, "freq", 1)
+    col_far = lax.ppermute(col_far, "freq", between_pairs(lax.axis_size("freq")))
+    z, sums = local_part(odd, core, v, u, jnp.asarray(shift, BF16), col_near, col_far, jnp.asarray(places, BF16), sx)
+    far = cross_far_edge(staged)
     window = jnp.asarray(np.ascontiguousarray(np.broadcast_to(window[:, None], (NFFT, LANES))))
     transform = jnp.asarray(transform, BF16)
-    share, near_target = cross_part(
-        0, sx - 1, odd, block_offsets, triads, z, sums, [early, late], cell_weights, window, transform
-    )
+    share, near_target = cross_part(0, sx - 1, blocks, ntri, scalars, z, sums, [near], cell_weights, window, transform)
     share, far_target = cross_part(
-        sx - 1, 1, odd, block_offsets, triads, z, sums, [far], cell_weights, window, transform, share
+        sx - 1, 1, blocks, ntri, scalars, z, sums, far, cell_weights, window, transform, share
     )
     half = share.shape[0] // 2
     mine = lax.dynamic_slice_in_dim(share, core[0] * half, half, 0)

time: 64.9 us -> 61.2 us (0.943)
  waiting for transfers between devices: 28.4 us -> 13.1 us
  starting transfers between devices: 20.6 us -> 32.7 us
  Pallas kernels: 11.7 us -> 9.56 us
  other arithmetic: 0.05 us -> 2.01 us
    ppermute x3 -> x8, starting transfers between devices: 4.2 us -> 19.5 us  [the longest x4 15 us: cross_far_edge(): far.append(lax.ppermute(piece, 'space', hops))]
    ppermute x4, waiting for transfers between devices: 15.6 us -> 2.15 us  [swap(): return lax.ppermute(x, axis, [(i, i ^ bit) for i in range(count)])]
    ppermute x4, starting transfers between devices: 6.95 us -> 3.66 us  [swap(): return lax.ppermute(x, axis, [(i, i ^ bit) for i in range(count)])]
    select_n x0 -> x3, other arithmetic: none -> 1.89 us  [stage_far(): piece = jnp.where(place > start, passed, piece)]
    ppermute x3 -> x8, waiting for transfers between devices: 3.37 us -> 1.5 us  [the longest x3 0.93 us: stage_far(): passed = lax.ppermute(piece, 'space', hops)]
    pallas_call x1, Pallas kernels: 2.82 us -> 1.82 us  [modes_part(): pl.pallas_call(functools.partial(modes_kernel, sx, blocks, scaling), out_...]
    unnamed x23, local copies, waits for them, and re-layouts: 2.9 us -> 2.24 us
  transfers between devices with their start and end apart: 11 -> 16, of which waited for: 9 -> 8; matrix products, arithmetic and copies ran while one was open for 0% -> 4% of each run, Pallas kernels for 8% -> 8%
where the time goes in v5:
time: 61.2 us; the launch traced here: 60.8 us
  starting transfers between devices  32.7 us (53%)
  waiting for transfers between devices  13.1 us (21%)
  Pallas kernels  9.56 us (16%)
  local copies, waits for them, and re-layouts  2.39 us (4%)
  other arithmetic  2.01 us (3%)
  between operations  1 us (2%)
    ppermute x4, starting transfers between devices, cross_far_edge(): far.append(lax.ppermute(piece, 'space', hops))  15 us
    ppermute x4, starting transfers between devices, sum_over_rest(): x = x + lax.ppermute(x, ('space', 'freq'), pairs)  9.5 us
    ppermute x4, waiting for transfers between devices, sum_over_rest(): x = x + lax.ppermute(x, ('space', 'freq'), pairs)  9.45 us
    pallas_call x2, Pallas kernels, cross_part(): pl.pallas_call(functools.partial(cross_kernel, sx, begin, len(halos), blo...  5.74 us
    ppermute x3, starting transfers between devices, stage_far(): passed = lax.ppermute(piece, 'space', hops)  3.87 us
    ppermute x4, starting transfers between devices, swap(): return lax.ppermute(x, axis, [(i, i ^ bit) for i in range(count)])  3.66 us
    unnamed x23, local copies, waits for them, and re-layouts  2.24 us
    ppermute x4, waiting for transfers between devices, swap(): return lax.ppermute(x, axis, [(i, i ^ bit) for i in range(count)])  2.15 us
  transfers between devices with their start and end apart: 16, of which 8 were waited for; matrix products, arithmetic and copies ran while one was open for 4% of the time, Pallas kernels for 8%

profile of v5, /device:TPU:0, one launch (start us, length us, event | category | flops | bytes accessed | tf_op | source)
XLA Modules:
  0.0 60.8 jit_solution(11882327761763196654)
XLA Ops:
  0.7 1.3 %copy-done.1 = bf16[2176,2,128]{2,1,0:T(2,128)(2,1)S(1)} copy-done((bf16[2176,2,128]{2,1,0:T(2,128)(2,1)S(1)}, bf16[2176,2,128]{2,1,0:T(2,128)(2,1)}, u32[]{:S(2)}) %copy-start.1) | copy-done | bytes 1114136
  2.0 0.8 %copy-done.3 = bf16[8,16,128]{2,1,0:T(8,128)(2,1)S(1)} copy-done((bf16[8,16,128]{2,1,0:T(8,128)(2,1)S(1)}, bf16[8,16,128]{2,1,0:T(8,128)(2,1)}, u32[]{:S(2)}) %copy-start.3) | copy-done | bytes 32792
  2.7 0.4 columns.1
  3.1 0.5 collective-permute-start
  3.7 0.7 %collective-permute-start.1 = (bf16[8,544]{1,0:T(8,128)(2,1)S(1)}, bf16[8,544]{1,0:T(8,128)(2,1)S(1)}, u32[]{:S(2)}, u32[]{:S(2)}) collective-permute-start(bf16[8,544]{1,0:T(8,128)(2,1)S(1)} %get-tuple-element.17), channel_id=1, source_target_pairs={{1,2},{2,1},{5,6},{6,5},{9,10},{10,9},{13,14},{14,13},{17,18},{18,... | collective-permute-start | bytes 26120 | tf_op jit(solution)/shard_map/ppermute | solution.py:501
  4.7 2.6 %collective-permute-start.9 = (bf16[2176,128]{1,0:T(8,128)(2,1)S(1)}, bf16[2176,128]{1,0:T(8,128)(2,1)}, u32[]{:S(2)}, u32[]{:S(2)}) collective-permute-start(bf16[2176,128]{1,0:T(8,128)(2,1)S(1)} %near.1), channel_id=1, source_target_pairs={{0,4},{4,0},{8,12},{12,8},{16,20},{20,16},{24,28},{28,24},{1,5},{5... | collective-permute-start | bytes 1671176 | tf_op jit(solution)/shard_map/ppermute | solution.py:309
  7.5 1.3 %collective-permute-start.2 = (bf16[544,128]{1,0:T(8,128)(2,1)S(1)}, bf16[544,128]{1,0:T(8,128)(2,1)}, u32[]{:S(2)}, u32[]{:S(2)}) collective-permute-start(bf16[544,128]{1,0:T(8,128)(2,1)S(1)} %get-tuple-element.20), channel_id=1, source_target_pairs={{4,12},{12,20},{20,28},{24,16},{16,8},{8,0},{5,13},{13,21},{21,29}... | collective-permute-start | bytes 417800 | tf_op jit(solution)/shard_map/ppermute | solution.py:455
  8.8 1.3 %collective-permute-start.4 = (bf16[544,128]{1,0:T(8,128)(2,1)S(1)}, bf16[544,128]{1,0:T(8,128)(2,1)}, u32[]{:S(2)}, u32[]{:S(2)}) collective-permute-start(bf16[544,128]{1,0:T(8,128)(2,1)S(1)} %get-tuple-element.21), channel_id=1, source_target_pairs={{12,20},{20,28},{16,8},{8,0},{13,21},{21,29},{17,9},{9,1},{14,22},... | collective-permute-start | bytes 417800 | tf_op jit(solution)/shard_map/ppermute | solution.py:455
  10.4 1.3 %collective-permute-start.6 = (bf16[544,128]{1,0:T(8,128)(2,1)S(1)}, bf16[544,128]{1,0:T(8,128)(2,1)S(1)}, u32[]{:S(2)}, u32[]{:S(2)}) collective-permute-start(bf16[544,128]{1,0:T(8,128)(2,1)S(1)} %get-tuple-element.22), channel_id=1, source_target_pairs={{20,28},{8,0},{21,29},{9,1},{22,30},{10,2},{23,31},{11,3}} | collective-permute-start | bytes 417800 | tf_op jit(solution)/shard_map/ppermute | solution.py:455
  11.7 0.7 %collective-permute-start.8 = (bf16[544,128]{1,0:T(8,128)(2,1)S(1)}, bf16[544,128]{1,0:T(8,128)(2,1)S(1)}, u32[]{:S(2)}, u32[]{:S(2)}) collective-permute-start(bf16[544,128]{1,0:T(8,128)(2,1)S(1)} %get-tuple-element.23), channel_id=1, source_target_pairs={{4,8},{24,20},{12,16},{16,12},{20,24},{8,4},{5,9},{25,21},{13,17},... | collective-permute-start | bytes 417800 | tf_op jit(solution)/shard_map/ppermute | solution.py:474
  12.4 1.1 %local.1 = (f32[2,2176,128]{2,1,0:T(8,128)S(1)}, f32[2,8,128]{2,1,0:T(8,128)S(1)}) custom-call(s32[1]{0:T(128)} %bitcast.odd_ref, s32[1]{0:T(128)} %bitcast.1.side_ref.core_ref, bf16[4352,128]{1,0:T(8,128)(2,1)S(1)} %bitcast.8, bf16[4352,128]{1,0:T(8,128)(2,1)S(1)} %bitcast.10, bf16[128,128]{1,0:T(8,128)(2,1)S(1)} %copy-done.7, ...), custom_call_target="tpu_custom_call" | custom-call | flops 1000000000 | bytes 8000000 | tf_op jit(solution)/shard_map/local/pallas_call | solution.py:155
  13.6 0.9 %collective-permute-done.2 = bf16[544,128]{1,0:T(8,128)(2,1)} collective-permute-done((bf16[544,128]{1,0:T(8,128)(2,1)S(1)}, bf16[544,128]{1,0:T(8,128)(2,1)}, u32[]{:S(2)}, u32[]{:S(2)}) %collective-permute-start.2) | collective-permute-done | bytes 139296 | tf_op jit(solution)/shard_map/ppermute | solution.py:455
  14.5 0.9 %broadcast_select_fusion.2 = bf16[544,128]{1,0:T(8,128)(2,1)S(1)} fusion(bf16[544,128]{1,0:T(8,128)(2,1)} %collective-permute-done.2, bf16[544,128]{1,0:T(8,128)(2,1)S(1)} %get-tuple-element.20, pred[]{:T(512)S(6)} %gt.9), kind=kLoop, calls=%fused_computation.2 | loop fusion | flops 69632 | bytes 417793 | tf_op jit(solution)/shard_map/jit(_where)/select_n | solution.py:456
  15.5 6.2 %collective-permute-start.3 = (bf16[544,128]{1,0:T(8,128)(2,1)S(1)}, bf16[544,128]{1,0:T(8,128)(2,1)S(1)}, u32[]{:S(2)}, u32[]{:S(2)}) collective-permute-start(bf16[544,128]{1,0:T(8,128)(2,1)S(1)} %broadcast_select_fusion.2), channel_id=1, source_target_pairs={{12,8},{16,20},{20,16},{8,12},{28,24},{0,4},{13,9},{17,21},{21,17}... | collective-permute-start | bytes 417800 | tf_op jit(solution)/shard_map/ppermute | solution.py:474
  21.7 0.9 %broadcast_select_fusion.1 = bf16[544,128]{1,0:T(8,128)(2,1)S(1)} fusion(bf16[544,128]{1,0:T(8,128)(2,1)} %collective-permute-done.4, bf16[544,128]{1,0:T(8,128)(2,1)S(1)} %get-tuple-element.21, pred[]{:T(512)S(6)} %gt.10), kind=kLoop, calls=%fused_computation.1 | loop fusion | flops 69632 | bytes 417793 | tf_op jit(solution)/shard_map/jit(_where)/select_n | solution.py:456
  22.6 1.3 %collective-permute-start.5 = (bf16[544,128]{1,0:T(8,128)(2,1)S(1)}, bf16[544,128]{1,0:T(8,128)(2,1)S(1)}, u32[]{:S(2)}, u32[]{:S(2)}) collective-permute-start(bf16[544,128]{1,0:T(8,128)(2,1)S(1)} %broadcast_select_fusion.1), channel_id=1, source_target_pairs={{4,8},{24,20},{20,16},{8,12},{28,24},{0,4},{5,9},{25,21},{21,17},{... | collective-permute-start | bytes 417800 | tf_op jit(solution)/shard_map/ppermute | solution.py:474
  24.0 6.8 %collective-permute-start.7 = (bf16[544,128]{1,0:T(8,128)(2,1)S(1)}, bf16[544,128]{1,0:T(8,128)(2,1)S(1)}, u32[]{:S(2)}, u32[]{:S(2)}) collective-permute-start(bf16[544,128]{1,0:T(8,128)(2,1)S(1)} %broadcast_select_fusion), channel_id=1, source_target_pairs={{4,8},{24,20},{12,16},{16,12},{28,24},{0,4},{5,9},{25,21},{13,17},... | collective-permute-start | bytes 417800 | tf_op jit(solution)/shard_map/ppermute | solution.py:474
  30.9 3.1 %cross_near.1 = (f32[256,128]{1,0:T(8,128)S(1)}, bf16[2048,128]{1,0:T(8,128)(2,1)S(1)}) custom-call(s32[145]{0:T(256)S(1)} %pad_add_fusion.scalars_ref, f32[2,2176,128]{2,1,0:T(8,128)S(1)} %get-tuple-element.18.z_ref, f32[2,8,128]{2,1,0:T(8,128)S(1)} %get-tuple-element.19.sum_ref, f32[2,128]{1,0:T(2,128)S(1)} %copy-done.4, f32[256,128]{1,0:T(8,128)S(1)} %copy-done.5, ...), custom_call_target="tpu_custom_call" | custom-call | flops 2000000000 | bytes 4000000 | tf_op jit(solution)/shard_map/cross_near/pallas_call | solution.py:287
  34.0 0.6 collective-permute-done.7.rest_2_
  34.6 2.6 %cross_far.1 = (f32[256,128]{1,0:T(8,128)S(1)}, bf16[2048,128]{1,0:T(8,128)(2,1)S(1)}) custom-call(s32[145]{0:T(256)S(1)} %pad_add_fusion.scalars_ref, f32[2,2176,128]{2,1,0:T(8,128)S(1)} %get-tuple-element.18.z_ref, f32[2,8,128]{2,1,0:T(8,128)S(1)} %get-tuple-element.19.sum_ref, f32[2,128]{1,0:T(2,128)S(1)} %copy-done.4, f32[256,128]{1,0:T(8,128)S(1)} %copy-done.5, ...), custom_call_target="tpu_custom_call" | custom-call | flops 2000000000 | bytes 4000000 | tf_op jit(solution)/shard_map/cross_far/pallas_call | solution.py:287
  37.2 0.5 collective-permute-start.10
  37.7 0.9 %collective-permute-done.10 = f32[128,128]{1,0:T(8,128)S(1)} collective-permute-done((f32[128,128]{1,0:T(8,128)S(1)}, f32[128,128]{1,0:T(8,128)S(1)}, u32[]{:S(2)}, u32[]{:S(2)}) %collective-permute-start.10) | collective-permute-done | bytes 65568 | tf_op jit(solution)/shard_map/ppermute | solution.py:309
  38.6 2.5 %collective-permute-start.11 = (f32[128,128]{1,0:T(8,128)S(1)}, f32[128,128]{1,0:T(8,128)S(1)}, u32[]{:S(2)}, u32[]{:S(2)}) collective-permute-start(f32[128,128]{1,0:T(8,128)S(1)} %dynamic-slice_add_fusion), channel_id=1, source_target_pairs={{0,4},{1,3},{2,6},{3,1},{4,0},{5,7},{6,2},{7,5},{8,12},{9,11},{10,... | collective-permute-start | bytes 196616 | tf_op jit(solution)/shard_map/ppermute | solution.py:320
  41.1 2.2 %collective-permute-done.11 = f32[128,128]{1,0:T(8,128)S(1)} collective-permute-done((f32[128,128]{1,0:T(8,128)S(1)}, f32[128,128]{1,0:T(8,128)S(1)}, u32[]{:S(2)}, u32[]{:S(2)}) %collective-permute-start.11) | collective-permute-done | bytes 65568 | tf_op jit(solution)/shard_map/ppermute | solution.py:320
  43.4 2.4 %collective-permute-start.12 = (f32[128,128]{1,0:T(8,128)S(1)}, f32[128,128]{1,0:T(8,128)S(1)}, u32[]{:S(2)}, u32[]{:S(2)}) collective-permute-start(f32[128,128]{1,0:T(8,128)S(1)} %add.35), channel_id=1, source_target_pairs={{0,2},{1,5},{2,0},{3,7},{4,6},{5,1},{6,4},{7,3},{8,10},{9,13},{10,... | collective-permute-start | bytes 196616 | tf_op jit(solution)/shard_map/ppermute | solution.py:320
  45.8 2.2 %collective-permute-done.12 = f32[128,128]{1,0:T(8,128)S(1)} collective-permute-done((f32[128,128]{1,0:T(8,128)S(1)}, f32[128,128]{1,0:T(8,128)S(1)}, u32[]{:S(2)}, u32[]{:S(2)}) %collective-permute-start.12) | collective-permute-done | bytes 65568 | tf_op jit(solution)/shard_map/ppermute | solution.py:320
  48.0 2.0 %collective-permute-start.13 = (f32[128,128]{1,0:T(8,128)S(1)}, f32[128,128]{1,0:T(8,128)S(1)}, u32[]{:S(2)}, u32[]{:S(2)}) collective-permute-start(f32[128,128]{1,0:T(8,128)S(1)} %add.36), channel_id=1, source_target_pairs={{0,8},{1,17},{2,10},{3,19},{4,12},{5,21},{6,14},{7,23},{8,0},{9,25... | collective-permute-start | bytes 196616 | tf_op jit(solution)/shard_map/ppermute | solution.py:320
  50.0 2.4 %collective-permute-done.13 = f32[128,128]{1,0:T(8,128)S(1)} collective-permute-done((f32[128,128]{1,0:T(8,128)S(1)}, f32[128,128]{1,0:T(8,128)S(1)}, u32[]{:S(2)}, u32[]{:S(2)}) %collective-permute-start.13) | collective-permute-done | bytes 65568 | tf_op jit(solution)/shard_map/ppermute | solution.py:320
  52.4 2.6 %collective-permute-start.14 = (f32[128,128]{1,0:T(8,128)S(1)}, f32[128,128]{1,0:T(8,128)S(1)}, u32[]{:S(2)}, u32[]{:S(2)}) collective-permute-start(f32[128,128]{1,0:T(8,128)S(1)} %add.37), channel_id=1, source_target_pairs={{0,16},{1,9},{2,18},{3,11},{4,20},{5,13},{6,22},{7,15},{8,24},{9,1... | collective-permute-start | bytes 196616 | tf_op jit(solution)/shard_map/ppermute | solution.py:320
  55.0 2.6 %collective-permute-done.14 = f32[128,128]{1,0:T(8,128)S(1)} collective-permute-done((f32[128,128]{1,0:T(8,128)S(1)}, f32[128,128]{1,0:T(8,128)S(1)}, u32[]{:S(2)}, u32[]{:S(2)}) %collective-permute-start.14) | collective-permute-done | bytes 65568 | tf_op jit(solution)/shard_map/ppermute | solution.py:320
  57.7 1.2 %collective-permute-done.15.other_ref = f32[128,128]{1,0:T(8,128)S(1)} collective-permute-done((f32[128,128]{1,0:T(8,128)S(1)}, f32[128,128]{1,0:T(8,128)S(1)}, u32[]{:S(2)}, u32[]{:S(2)}) %collective-permute-start.15) | collective-permute-done | bytes 65568 | tf_op jit(solution)/shard_map/ppermute | solution.py:309
  58.9 1.8 %modes.1 = (f32[2,64]{1,0:T(2,128)}, f32[256,128]{1,0:T(8,128)}) custom-call(s32[1]{0:T(128)} %bitcast.odd_ref, s32[1]{0:T(128)} %bitcast.1.side_ref.core_ref, f32[128,128]{1,0:T(8,128)S(1)} %add.38.mine_ref, f32[128,128]{1,0:T(8,128)S(1)} %collective-permute-done.15.other_ref, bf16[2048,128]{1,0:T(8,128)(2,1)S(1)} %get-tuple-element.26.near_ref, ...), custom_call_target="tpu_custom_call" | custom-call | tf_op jit(solution)/shard_map/modes/pallas_call | solution.py:422
  (41 shorter events, 1.0 us)
Async XLA Ops:
  0.6 3.7 %copy-start = (bf16[2176,2,128]{2,1,0:T(2,128)(2,1)S(1)}, bf16[2176,2,128]{2,1,0:T(2,128)(2,1)}, u32[]{:S(2)}) copy-start(bf16[2176,2,128]{2,1,0:T(2,128)(2,1)} %param.11) | copy-start | bytes 3342340
  0.7 1.3 %copy-start.1 = (bf16[2176,2,128]{2,1,0:T(2,128)(2,1)S(1)}, bf16[2176,2,128]{2,1,0:T(2,128)(2,1)}, u32[]{:S(2)}) copy-start(bf16[2176,2,128]{2,1,0:T(2,128)(2,1)} %param.10) | copy-start | bytes 3342340
  2.0 0.8 %copy-start.3 = (bf16[8,16,128]{2,1,0:T(8,128)(2,1)S(1)}, bf16[8,16,128]{2,1,0:T(8,128)(2,1)}, u32[]{:S(2)}) copy-start(bf16[8,16,128]{2,1,0:T(8,128)(2,1)} %constant.59.clone.picks_ref) | copy-start | bytes 98308
  3.1 7.3 %collective-permute-start = (bf16[8,544]{1,0:T(8,128)(2,1)S(1)}, bf16[8,544]{1,0:T(8,128)(2,1)S(1)}, u32[]{:S(2)}, u32[]{:S(2)}) collective-permute-start(bf16[8,544]{1,0:T(8,128)(2,1)S(1)} %get-tuple-element.16), channel_id=1, source_target_pairs={{0,1},{1,0},{2,3},{3,2},{4,5},{5,4},{6,7},{7,6},{8,9},{9,8},{10,11... | collective-permute-start | bytes 26120 | tf_op jit(solution)/shard_map/ppermute | solution.py:309
  3.7 8.0 %collective-permute-start.1 = (bf16[8,544]{1,0:T(8,128)(2,1)S(1)}, bf16[8,544]{1,0:T(8,128)(2,1)S(1)}, u32[]{:S(2)}, u32[]{:S(2)}) collective-permute-start(bf16[8,544]{1,0:T(8,128)(2,1)S(1)} %get-tuple-element.17), channel_id=1, source_target_pairs={{1,2},{2,1},{5,6},{6,5},{9,10},{10,9},{13,14},{14,13},{17,18},{18,... | collective-permute-start | bytes 26120 | tf_op jit(solution)/shard_map/ppermute | solution.py:501
  4.4 5.7 %copy-start.9 = (s32[64,2]{0,1:T(2,128)S(1)}, s32[64,2]{0,1:T(2,128)}, u32[]{:S(2)}) copy-start(s32[64,2]{0,1:T(2,128)} %param.14) | copy-start | bytes 1540
  4.4 5.9 %copy-start.10 = (s32[16]{0:T(128)S(1)}, s32[16]{0:T(128)}, u32[]{:S(2)}) copy-start(s32[16]{0:T(128)} %param.13) | copy-start | bytes 196
  4.4 8.0 %copy-start.2 = (bf16[2176,2,128]{2,1,0:T(2,128)(2,1)S(1)}, bf16[2176,2,128]{2,1,0:T(2,128)(2,1)}, u32[]{:S(2)}) copy-start(bf16[2176,2,128]{2,1,0:T(2,128)(2,1)} %param.10) | copy-start | bytes 3342340
  4.4 8.0 %copy-start.7 = (bf16[128,128]{1,0:T(8,128)(2,1)S(1)}, bf16[128,128]{1,0:T(8,128)(2,1)}, u32[]{:S(2)}) copy-start(bf16[128,128]{1,0:T(8,128)(2,1)} %constant.60.clone.shift_ref) | copy-start | bytes 98308
  4.4 8.0 %copy-start.8 = (bf16[8,16,128]{2,1,0:T(8,128)(2,1)S(1)}, bf16[8,16,128]{2,1,0:T(8,128)(2,1)}, u32[]{:S(2)}) copy-start(bf16[8,16,128]{2,1,0:T(8,128)(2,1)} %constant.61.clone.places_ref) | copy-start | bytes 98308
  4.7 26.1 %collective-permute-start.9 = (bf16[2176,128]{1,0:T(8,128)(2,1)S(1)}, bf16[2176,128]{1,0:T(8,128)(2,1)}, u32[]{:S(2)}, u32[]{:S(2)}) collective-permute-start(bf16[2176,128]{1,0:T(8,128)(2,1)S(1)} %near.1), channel_id=1, source_target_pairs={{0,4},{4,0},{8,12},{12,8},{16,20},{20,16},{24,28},{28,24},{1,5},{5... | collective-permute-start | bytes 1671176 | tf_op jit(solution)/shard_map/ppermute | solution.py:309
  7.5 7.1 %collective-permute-start.2 = (bf16[544,128]{1,0:T(8,128)(2,1)S(1)}, bf16[544,128]{1,0:T(8,128)(2,1)}, u32[]{:S(2)}, u32[]{:S(2)}) collective-permute-start(bf16[544,128]{1,0:T(8,128)(2,1)S(1)} %get-tuple-element.20), channel_id=1, source_target_pairs={{4,12},{12,20},{20,28},{24,16},{16,8},{8,0},{5,13},{13,21},{21,29}... | collective-permute-start | bytes 417800 | tf_op jit(solution)/shard_map/ppermute | solution.py:455
  8.8 12.9 %collective-permute-start.4 = (bf16[544,128]{1,0:T(8,128)(2,1)S(1)}, bf16[544,128]{1,0:T(8,128)(2,1)}, u32[]{:S(2)}, u32[]{:S(2)}) collective-permute-start(bf16[544,128]{1,0:T(8,128)(2,1)S(1)} %get-tuple-element.21), channel_id=1, source_target_pairs={{12,20},{20,28},{16,8},{8,0},{13,21},{21,29},{17,9},{9,1},{14,22},... | collective-permute-start | bytes 417800 | tf_op jit(solution)/shard_map/ppermute | solution.py:455
  10.4 13.5 %collective-permute-start.6 = (bf16[544,128]{1,0:T(8,128)(2,1)S(1)}, bf16[544,128]{1,0:T(8,128)(2,1)S(1)}, u32[]{:S(2)}, u32[]{:S(2)}) collective-permute-start(bf16[544,128]{1,0:T(8,128)(2,1)S(1)} %get-tuple-element.22), channel_id=1, source_target_pairs={{20,28},{8,0},{21,29},{9,1},{22,30},{10,2},{23,31},{11,3}} | collective-permute-start | bytes 417800 | tf_op jit(solution)/shard_map/ppermute | solution.py:455
  11.7 22.3 %collective-permute-start.8 = (bf16[544,128]{1,0:T(8,128)(2,1)S(1)}, bf16[544,128]{1,0:T(8,128)(2,1)S(1)}, u32[]{:S(2)}, u32[]{:S(2)}) collective-permute-start(bf16[544,128]{1,0:T(8,128)(2,1)S(1)} %get-tuple-element.23), channel_id=1, source_target_pairs={{4,8},{24,20},{12,16},{16,12},{20,24},{8,4},{5,9},{25,21},{13,17},... | collective-permute-start | bytes 417800 | tf_op jit(solution)/shard_map/ppermute | solution.py:474
  13.6 17.3 %copy-start.4 = (f32[2,128]{1,0:T(2,128)S(1)}, f32[2,128]{1,0:T(2,128)}, u32[]{:S(2)}) copy-start(f32[2,128]{1,0:T(2,128)} %weights_ref.3) | copy-start | bytes 3076
  13.6 17.3 %copy-start.5 = (f32[256,128]{1,0:T(8,128)S(1)}, f32[256,128]{1,0:T(8,128)}, u32[]{:S(2)}) copy-start(f32[256,128]{1,0:T(8,128)} %constant.62.clone.window_ref) | copy-start | bytes 393220
  13.6 17.3 %copy-start.6 = (bf16[256,256]{1,0:T(8,128)(2,1)S(1)}, bf16[256,256]{1,0:T(8,128)(2,1)}, u32[]{:S(2)}) copy-start(bf16[256,256]{1,0:T(8,128)(2,1)} %constant.63.clone.transform_ref) | copy-start | bytes 393220
  15.5 18.5 %collective-permute-start.3 = (bf16[544,128]{1,0:T(8,128)(2,1)S(1)}, bf16[544,128]{1,0:T(8,128)(2,1)S(1)}, u32[]{:S(2)}, u32[]{:S(2)}) collective-permute-start(bf16[544,128]{1,0:T(8,128)(2,1)S(1)} %broadcast_select_fusion.2), channel_id=1, source_target_pairs={{12,8},{16,20},{20,16},{8,12},{28,24},{0,4},{13,9},{17,21},{21,17}... | collective-permute-start | bytes 417800 | tf_op jit(solution)/shard_map/ppermute | solution.py:474
  22.6 11.4 %collective-permute-start.5 = (bf16[544,128]{1,0:T(8,128)(2,1)S(1)}, bf16[544,128]{1,0:T(8,128)(2,1)S(1)}, u32[]{:S(2)}, u32[]{:S(2)}) collective-permute-start(bf16[544,128]{1,0:T(8,128)(2,1)S(1)} %broadcast_select_fusion.1), channel_id=1, source_target_pairs={{4,8},{24,20},{20,16},{8,12},{28,24},{0,4},{5,9},{25,21},{21,17},{... | collective-permute-start | bytes 417800 | tf_op jit(solution)/shard_map/ppermute | solution.py:474
  24.0 10.6 %collective-permute-start.7 = (bf16[544,128]{1,0:T(8,128)(2,1)S(1)}, bf16[544,128]{1,0:T(8,128)(2,1)S(1)}, u32[]{:S(2)}, u32[]{:S(2)}) collective-permute-start(bf16[544,128]{1,0:T(8,128)(2,1)S(1)} %broadcast_select_fusion), channel_id=1, source_target_pairs={{4,8},{24,20},{12,16},{16,12},{28,24},{0,4},{5,9},{25,21},{13,17},... | collective-permute-start | bytes 417800 | tf_op jit(solution)/shard_map/ppermute | solution.py:474
  37.2 1.4 %collective-permute-start.10 = (f32[128,128]{1,0:T(8,128)S(1)}, f32[128,128]{1,0:T(8,128)S(1)}, u32[]{:S(2)}, u32[]{:S(2)}) collective-permute-start(f32[128,128]{1,0:T(8,128)S(1)} %constant_dynamic-slice_fusion), channel_id=1, source_target_pairs={{0,1},{1,0},{2,3},{3,2},{4,5},{5,4},{6,7},{7,6},{8,9},{9,8},{10,11... | collective-permute-start | bytes 196616 | tf_op jit(solution)/shard_map/ppermute | solution.py:309
  38.6 4.7 %collective-permute-start.11 = (f32[128,128]{1,0:T(8,128)S(1)}, f32[128,128]{1,0:T(8,128)S(1)}, u32[]{:S(2)}, u32[]{:S(2)}) collective-permute-start(f32[128,128]{1,0:T(8,128)S(1)} %dynamic-slice_add_fusion), channel_id=1, source_target_pairs={{0,4},{1,3},{2,6},{3,1},{4,0},{5,7},{6,2},{7,5},{8,12},{9,11},{10,... | collective-permute-start | bytes 196616 | tf_op jit(solution)/shard_map/ppermute | solution.py:320
  43.4 4.7 %collective-permute-start.12 = (f32[128,128]{1,0:T(8,128)S(1)}, f32[128,128]{1,0:T(8,128)S(1)}, u32[]{:S(2)}, u32[]{:S(2)}) collective-permute-start(f32[128,128]{1,0:T(8,128)S(1)} %add.35), channel_id=1, source_target_pairs={{0,2},{1,5},{2,0},{3,7},{4,6},{5,1},{6,4},{7,3},{8,10},{9,13},{10,... | collective-permute-start | bytes 196616 | tf_op jit(solution)/shard_map/ppermute | solution.py:320
  48.0 4.3 %collective-permute-start.13 = (f32[128,128]{1,0:T(8,128)S(1)}, f32[128,128]{1,0:T(8,128)S(1)}, u32[]{:S(2)}, u32[]{:S(2)}) collective-permute-start(f32[128,128]{1,0:T(8,128)S(1)} %add.36), channel_id=1, source_target_pairs={{0,8},{1,17},{2,10},{3,19},{4,12},{5,21},{6,14},{7,23},{8,0},{9,25... | collective-permute-start | bytes 196616 | tf_op jit(solution)/shard_map/ppermute | solution.py:320
  52.4 5.2 %collective-permute-start.14 = (f32[128,128]{1,0:T(8,128)S(1)}, f32[128,128]{1,0:T(8,128)S(1)}, u32[]{:S(2)}, u32[]{:S(2)}) collective-permute-start(f32[128,128]{1,0:T(8,128)S(1)} %add.37), channel_id=1, source_target_pairs={{0,16},{1,9},{2,18},{3,11},{4,20},{5,13},{6,22},{7,15},{8,24},{9,1... | collective-permute-start | bytes 196616 | tf_op jit(solution)/shard_map/ppermute | solution.py:320
  57.6 1.3 %collective-permute-start.15 = (f32[128,128]{1,0:T(8,128)S(1)}, f32[128,128]{1,0:T(8,128)S(1)}, u32[]{:S(2)}, u32[]{:S(2)}) collective-permute-start(f32[128,128]{1,0:T(8,128)S(1)} %add.38.mine_ref), channel_id=1, source_target_pairs={{0,1},{1,0},{2,3},{3,2},{4,5},{5,4},{6,7},{7,6},{8,9},{9,8},{10,11... | collective-permute-start | bytes 196616 | tf_op jit(solution)/shard_map/ppermute | solution.py:309

commit v6 on v5

--- a/solution.py
+++ b/solution.py
@@ -13,7 +13,7 @@
 NFFT = 256
 POW = 4
 LANES = 128
-PIECES = 4
+AHEAD = 5
 F32 = jnp.float32
 BF16 = jnp.bfloat16
 MIB = 2**20
@@ -55,44 +55,48 @@
     return pltpu.CompilerParams(vmem_limit_bytes=mib * MIB)
 
 
-def near_kernel(sx, odd_ref, v_ref, near_ref, plain):
+def near_kernel(sx, odd_ref, v_ref, early_ref, late_ref, plain):
     plain[...] = v_ref[...].astype(F32)
-    near_ref[...] = plain[pl.ds(row_at(0, sx, odd_ref[0]), near_ref.shape[0], stride=sx), :].astype(BF16)
+    row = row_at(0, sx, odd_ref[0])
+    early, late = early_ref.shape[0], late_ref.shape[0]
+    early_ref[...] = plain[pl.ds(row, early, stride=sx), :].astype(BF16)
+    late_ref[...] = plain[pl.ds(early * sx + row, late, stride=sx), :].astype(BF16)
 
 
 def near_edge(odd, v, sx):
     rows = v.shape[0]
+    early = rows // sx * AHEAD // 8
     return pl.pallas_call(
         functools.partial(near_kernel, sx),
-        out_shape=jax.ShapeDtypeStruct((rows // sx, LANES), BF16),
+        out_shape=(
+            jax.ShapeDtypeStruct((early, LANES), BF16),
+            jax.ShapeDtypeStruct((rows // sx - early, LANES), BF16),
+        ),
         in_specs=[SMEM, VMEM],
-        out_specs=VMEM,
+        out_specs=(VMEM,) * 2,
         scratch_shapes=[pltpu.VMEM((rows, LANES), F32)],
         compiler_params=limit(8),
         name="near",
     )(odd, v)
 
 
-def far_kernel(sx, odd_ref, v_ref, *rest):
-    far_refs, plain = rest[:-1], rest[-1]
+def far_kernel(sx, odd_ref, v_ref, after_ref, far_ref, plain):
+    times = far_ref.shape[0]
     plain[...] = v_ref[...].astype(F32)
-    row = row_at(sx - 1, sx, odd_ref[0])
-    for k, far_ref in enumerate(far_refs):
-        times = far_ref.shape[0]
-        far_ref[...] = plain[pl.ds(k * times * sx + row, times, stride=sx), :].astype(BF16)
-
-
-def far_edge(odd, v, sx):
+    far_ref[...] = plain[pl.ds(row_at(sx - 1, sx, odd_ref[0]), times, stride=sx), :].astype(BF16)
+
+
+def far_edge(odd, v, after, sx):
     rows = v.shape[0]
     return pl.pallas_call(
         functools.partial(far_kernel, sx),
-        out_shape=(jax.ShapeDtypeStruct((rows // sx // PIECES, LANES), BF16),) * PIECES,
-        in_specs=[SMEM, VMEM],
-        out_specs=(VMEM,) * PIECES,
+        out_shape=jax.ShapeDtypeStruct((rows // sx, LANES), BF16),
+        in_specs=[SMEM, VMEM, pl.BlockSpec(memory_space=pl.ANY)],
+        out_specs=VMEM,
         scratch_shapes=[pltpu.VMEM((rows, LANES), F32)],
         compiler_params=limit(8),
         name="far",
-    )(odd, v)
+    )(odd, v, after)
 
 
 def columns_kernel(pieces, side_ref, u_ref, picks_ref, near_ref, far_ref):
@@ -438,43 +442,6 @@
     return inner + [(b, a) for a, b in inner]
 
 
-def start_of(k, pairs):
-    return k * pairs // PIECES
-
-
-def stage_far(far):
-    pairs = lax.axis_size("space") // 2
-    index = lax.axis_index("space")
-    place = jnp.where(index % 2 == 1, index // 2, pairs - 1 - index // 2)
-    staged = []
-    for k, piece in enumerate(far):
-        start = start_of(k, pairs)
-        hops = [(2 * b + 1, 2 * b + 3) for b in range(start, pairs - 1)]
-        hops += [(2 * (pairs - 1 - b), 2 * (pairs - 2 - b)) for b in range(start, pairs - 1)]
-        if hops:
-            passed = lax.ppermute(piece, "space", hops)
-            piece = jnp.where(place > start, passed, piece)
-        staged.append(piece)
-    return staged
-
-
-def cross_far_edge(staged):
-    pairs = lax.axis_size("space") // 2
-    far = []
-    for k, piece in enumerate(staged):
-        start = start_of(k, pairs)
-        hops = []
-        for b in range(pairs - 1):
-            if b < start:
-                hops.append((2 * b + 1, 2 * b + 2))
-                hops.append((2 * (pairs - 1 - b), 2 * (pairs - 1 - b) - 1))
-            else:
-                hops.append((2 * b + 3, 2 * b + 2))
-                hops.append((2 * (pairs - 2 - b), 2 * (pairs - 2 - b) + 1))
-        far.append(lax.ppermute(piece, "space", hops))
-    return far
-
-
 def on_device(u_velocity, v_velocity, cell_weights, block_offsets, triads):
     times, sx, columns = u_velocity.shape
     blocks = block_offsets.shape[0]
@@ -492,20 +459,22 @@
     core = (lax.axis_index("freq") % 2)[None]
     scalars = jnp.concatenate([odd, block_offsets, triads.reshape(-1)])
 
-    near = near_edge(odd, v, sx)
-    near = swap(near, "space", 1)
-    far = far_edge(odd, v, sx)
-    staged = stage_far(far)
+    early, late = near_edge(odd, v, sx)
+    early = swap(early, "space", 1)
+    late = swap(late, "space", 1)
     col_near, col_far = columns_edge(core, u, jnp.asarray(picks, BF16))
     col_near = swap(col_near, "freq", 1)
     col_far = lax.ppermute(col_far, "freq", between_pairs(lax.axis_size("freq")))
     z, sums = local_part(odd, core, v, u, jnp.asarray(shift, BF16), col_near, col_far, jnp.asarray(places, BF16), sx)
-    far = cross_far_edge(staged)
+    far = far_edge(odd, v, early, sx)
+    far = lax.ppermute(far, "space", between_pairs(slabs))
     window = jnp.asarray(np.ascontiguousarray(np.broadcast_to(window[:, None], (NFFT, LANES))))
     transform = jnp.asarray(transform, BF16)
-    share, near_target = cross_part(0, sx - 1, blocks, ntri, scalars, z, sums, [near], cell_weights, window, transform)
+    share, near_target = cross_part(
+        0, sx - 1, blocks, ntri, scalars, z, sums, [early, late], cell_weights, window, transform
+    )
     share, far_target = cross_part(
-        sx - 1, 1, blocks, ntri, scalars, z, sums, far, cell_weights, window, transform, share
+        sx - 1, 1, blocks, ntri, scalars, z, sums, [far], cell_weights, window, transform, share
     )
     half = share.shape[0] // 2
     mine = lax.dynamic_slice_in_dim(share, core[0] * half, half, 0)

time: 61.2 us -> 63.7 us (1.041)
  waiting for transfers between devices: 13.1 us -> 32.2 us
  starting transfers between devices: 32.7 us -> 18.8 us
  other arithmetic: 2.01 us -> 0.12 us
  local copies, waits for them, and re-layouts: 2.39 us -> 1.55 us
    ppermute x4 -> x5, waiting for transfers between devices: 2.15 us -> 22.7 us  [swap(): return lax.ppermute(x, axis, [(i, i ^ bit) for i in range(count)])]
    ppermute x7 -> x1, starting transfers between devices: 18.9 us -> 1.63 us  [on_device(): far = lax.ppermute(far, 'space', between_pairs(slabs))]
    ppermute x4 -> x5, starting transfers between devices: 3.66 us -> 7.02 us  [swap(): return lax.ppermute(x, axis, [(i, i ^ bit) for i in range(count)])]
    select_n x3 -> x0, other arithmetic: 1.89 us -> none  [stage_far(): piece = jnp.where(place > start, passed, piece)]
    ppermute x7 -> x1, waiting for transfers between devices: 1.5 us -> 0.01 us  [on_device(): far = lax.ppermute(far, 'space', between_pairs(slabs))]
    unnamed x23, local copies, waits for them, and re-layouts: 2.24 us -> 1.4 us
  transfers between devices with their start and end apart: 16 -> 11, of which waited for: 8 -> 9; matrix products, arithmetic and copies ran while one was open for 4% -> 0% of each run, Pallas kernels for 8% -> 7%
where the time goes in v6:
time: 63.7 us; the launch traced here: 63.5 us
  waiting for transfers between devices  32.2 us (51%)
  starting transfers between devices  18.8 us (30%)
  Pallas kernels  9.94 us (16%)
  local copies, waits for them, and re-layouts  1.55 us (2%)
  between operations  0.83 us (1%)
    ppermute x5, waiting for transfers between devices, swap(): return lax.ppermute(x, axis, [(i, i ^ bit) for i in range(count)])  22.7 us
    ppermute x4, starting transfers between devices, sum_over_rest(): x = x + lax.ppermute(x, ('space', 'freq'), pairs)  9.51 us
    ppermute x4, waiting for transfers between devices, sum_over_rest(): x = x + lax.ppermute(x, ('space', 'freq'), pairs)  9.48 us
    ppermute x5, starting transfers between devices, swap(): return lax.ppermute(x, axis, [(i, i ^ bit) for i in range(count)])  7.02 us
    pallas_call x2, Pallas kernels, cross_part(): pl.pallas_call(functools.partial(cross_kernel, sx, begin, len(halos), blo...  6.13 us
    pallas_call x1, Pallas kernels, modes_part(): pl.pallas_call(functools.partial(modes_kernel, sx, blocks, scaling), out_...  1.82 us
    ppermute x1, starting transfers between devices, on_device(): far = lax.ppermute(far, 'space', between_pairs(slabs))  1.63 us
    unnamed x23, local copies, waits for them, and re-layouts  1.4 us
  transfers between devices with their start and end apart: 11, of which 9 were waited for; matrix products, arithmetic and copies ran while one was open for 0% of the time, Pallas kernels for 7%

profile of v6, /device:TPU:0, one launch (start us, length us, event | category | flops | bytes accessed | tf_op | source)
XLA Modules:
  0.0 63.5 jit_solution(13134200995467992487)
XLA Ops:
  0.7 1.2 %copy-done = bf16[2176,2,128]{2,1,0:T(2,128)(2,1)S(1)} copy-done((bf16[2176,2,128]{2,1,0:T(2,128)(2,1)S(1)}, bf16[2176,2,128]{2,1,0:T(2,128)(2,1)}, u32[]{:S(2)}) %copy-start) | copy-done | bytes 1114136
  1.9 0.2 near.1
  2.1 0.0 copy-start.3
  2.2 3.0 %collective-permute-start.2 = (bf16[1360,128]{1,0:T(8,128)(2,1)S(1)}, bf16[1360,128]{1,0:T(8,128)(2,1)S(1)}, u32[]{:S(2)}, u32[]{:S(2)}) collective-permute-start(bf16[1360,128]{1,0:T(8,128)(2,1)S(1)} %get-tuple-element.18), channel_id=1, source_target_pairs={{0,4},{4,0},{8,12},{12,8},{16,20},{20,16},{24,28},{28,24},{1,5},{5... | collective-permute-start | bytes 1044488 | tf_op jit(solution)/shard_map/ppermute | solution.py:313
  5.2 8.1 %collective-permute-done.2.after_ref.rest_0_ = bf16[1360,128]{1,0:T(8,128)(2,1)S(1)} collective-permute-done((bf16[1360,128]{1,0:T(8,128)(2,1)S(1)}, bf16[1360,128]{1,0:T(8,128)(2,1)S(1)}, u32[]{:S(2)}, u32[]{:S(2)}) %collective-permute-start.2) | collective-permute-done | bytes 348192 | tf_op jit(solution)/shard_map/ppermute | solution.py:313
  13.3 0.2 far.1
  13.6 1.6 %collective-permute-start.3 = (bf16[2176,128]{1,0:T(8,128)(2,1)S(1)}, bf16[2176,128]{1,0:T(8,128)(2,1)}, u32[]{:S(2)}, u32[]{:S(2)}) collective-permute-start(bf16[2176,128]{1,0:T(8,128)(2,1)S(1)} %far.1), channel_id=1, source_target_pairs={{4,8},{12,16},{20,24},{8,4},{16,12},{24,20},{5,9},{13,17},{21,25},... | collective-permute-start | bytes 1671176 | tf_op jit(solution)/shard_map/ppermute | solution.py:470
  15.2 3.8 %collective-permute-start.4 = (bf16[816,128]{1,0:T(8,128)(2,1)S(1)}, bf16[816,128]{1,0:T(8,128)(2,1)}, u32[]{:S(2)}, u32[]{:S(2)}) collective-permute-start(bf16[816,128]{1,0:T(8,128)(2,1)S(1)} %get-tuple-element.19), channel_id=1, source_target_pairs={{0,4},{4,0},{8,12},{12,8},{16,20},{20,16},{24,28},{28,24},{1,5},{5... | collective-permute-start | bytes 626696 | tf_op jit(solution)/shard_map/ppermute | solution.py:313
  19.0 0.4 columns.1
  19.4 0.1 collective-permute-start
  19.5 0.7 %collective-permute-start.1 = (bf16[8,544]{1,0:T(8,128)(2,1)S(1)}, bf16[8,544]{1,0:T(8,128)(2,1)S(1)}, u32[]{:S(2)}, u32[]{:S(2)}) collective-permute-start(bf16[8,544]{1,0:T(8,128)(2,1)S(1)} %get-tuple-element.15), channel_id=1, source_target_pairs={{1,2},{2,1},{5,6},{6,5},{9,10},{10,9},{13,14},{14,13},{17,18},{18,... | collective-permute-start | bytes 26120 | tf_op jit(solution)/shard_map/ppermute | solution.py:467
  20.2 0.1 copy.13
  20.3 0.1 reshape.16
  20.4 0.1 pad_add_fusion.scalars_ref
  20.5 0.2 collective-permute-done.near_ref
  20.7 1.1 %local.1 = (f32[2,2176,128]{2,1,0:T(8,128)S(1)}, f32[2,8,128]{2,1,0:T(8,128)S(1)}) custom-call(s32[1]{0:T(128)} %bitcast.odd_ref, s32[1]{0:T(128)} %bitcast.1.side_ref.core_ref, bf16[4352,128]{1,0:T(8,128)(2,1)S(1)} %bitcast.8, bf16[4352,128]{1,0:T(8,128)(2,1)S(1)} %bitcast.10, bf16[128,128]{1,0:T(8,128)(2,1)S(1)} %copy-done.7, ...), custom_call_target="tpu_custom_call" | custom-call | flops 1000000000 | bytes 8000000 | tf_op jit(solution)/shard_map/local/pallas_call | solution.py:159
  21.8 12.0 %collective-permute-done.4.rest_1_ = bf16[816,128]{1,0:T(8,128)(2,1)} collective-permute-done((bf16[816,128]{1,0:T(8,128)(2,1)S(1)}, bf16[816,128]{1,0:T(8,128)(2,1)}, u32[]{:S(2)}, u32[]{:S(2)}) %collective-permute-start.4) | collective-permute-done | bytes 208928 | tf_op jit(solution)/shard_map/ppermute | solution.py:313
  33.8 3.0 %cross_near.1 = (f32[256,128]{1,0:T(8,128)S(1)}, bf16[2048,128]{1,0:T(8,128)(2,1)S(1)}) custom-call(s32[145]{0:T(256)S(1)} %pad_add_fusion.scalars_ref, f32[2,2176,128]{2,1,0:T(8,128)S(1)} %get-tuple-element.16.z_ref, f32[2,8,128]{2,1,0:T(8,128)S(1)} %get-tuple-element.17.sum_ref, f32[2,128]{1,0:T(2,128)S(1)} %copy-done.4, f32[256,128]{1,0:T(8,128)S(1)} %copy-done.5, ...), custom_call_target="tpu_custom_call" | custom-call | flops 2000000000 | bytes 4000000 | tf_op jit(solution)/shard_map/cross_near/pallas_call | solution.py:291
  36.8 3.1 %cross_far.1 = (f32[256,128]{1,0:T(8,128)S(1)}, bf16[2048,128]{1,0:T(8,128)(2,1)S(1)}) custom-call(s32[145]{0:T(256)S(1)} %pad_add_fusion.scalars_ref, f32[2,2176,128]{2,1,0:T(8,128)S(1)} %get-tuple-element.16.z_ref, f32[2,8,128]{2,1,0:T(8,128)S(1)} %get-tuple-element.17.sum_ref, f32[2,128]{1,0:T(2,128)S(1)} %copy-done.4, f32[256,128]{1,0:T(8,128)S(1)} %copy-done.5, ...), custom_call_target="tpu_custom_call" | custom-call | flops 2000000000 | bytes 4000000 | tf_op jit(solution)/shard_map/cross_far/pallas_call | solution.py:291
  40.0 0.1 collective-permute-start.5
  40.0 1.2 %collective-permute-done.5 = f32[128,128]{1,0:T(8,128)S(1)} collective-permute-done((f32[128,128]{1,0:T(8,128)S(1)}, f32[128,128]{1,0:T(8,128)S(1)}, u32[]{:S(2)}, u32[]{:S(2)}) %collective-permute-start.5) | collective-permute-done | bytes 65568 | tf_op jit(solution)/shard_map/ppermute | solution.py:313
  41.3 2.7 %collective-permute-start.6 = (f32[128,128]{1,0:T(8,128)S(1)}, f32[128,128]{1,0:T(8,128)S(1)}, u32[]{:S(2)}, u32[]{:S(2)}) collective-permute-start(f32[128,128]{1,0:T(8,128)S(1)} %dynamic-slice_add_fusion), channel_id=1, source_target_pairs={{0,4},{1,3},{2,6},{3,1},{4,0},{5,7},{6,2},{7,5},{8,12},{9,11},{10,... | collective-permute-start | bytes 196616 | tf_op jit(solution)/shard_map/ppermute | solution.py:324
  44.0 2.2 %collective-permute-done.6 = f32[128,128]{1,0:T(8,128)S(1)} collective-permute-done((f32[128,128]{1,0:T(8,128)S(1)}, f32[128,128]{1,0:T(8,128)S(1)}, u32[]{:S(2)}, u32[]{:S(2)}) %collective-permute-start.6) | collective-permute-done | bytes 65568 | tf_op jit(solution)/shard_map/ppermute | solution.py:324
  46.2 1.6 %collective-permute-start.7 = (f32[128,128]{1,0:T(8,128)S(1)}, f32[128,128]{1,0:T(8,128)S(1)}, u32[]{:S(2)}, u32[]{:S(2)}) collective-permute-start(f32[128,128]{1,0:T(8,128)S(1)} %add.33), channel_id=1, source_target_pairs={{0,2},{1,5},{2,0},{3,7},{4,6},{5,1},{6,4},{7,3},{8,10},{9,13},{10,... | collective-permute-start | bytes 196616 | tf_op jit(solution)/shard_map/ppermute | solution.py:324
  47.8 2.7 %collective-permute-done.7 = f32[128,128]{1,0:T(8,128)S(1)} collective-permute-done((f32[128,128]{1,0:T(8,128)S(1)}, f32[128,128]{1,0:T(8,128)S(1)}, u32[]{:S(2)}, u32[]{:S(2)}) %collective-permute-start.7) | collective-permute-done | bytes 65568 | tf_op jit(solution)/shard_map/ppermute | solution.py:324
  50.6 2.2 %collective-permute-start.8 = (f32[128,128]{1,0:T(8,128)S(1)}, f32[128,128]{1,0:T(8,128)S(1)}, u32[]{:S(2)}, u32[]{:S(2)}) collective-permute-start(f32[128,128]{1,0:T(8,128)S(1)} %add.34), channel_id=1, source_target_pairs={{0,8},{1,17},{2,10},{3,19},{4,12},{5,21},{6,14},{7,23},{8,0},{9,25... | collective-permute-start | bytes 196616 | tf_op jit(solution)/shard_map/ppermute | solution.py:324
  52.7 2.2 %collective-permute-done.8 = f32[128,128]{1,0:T(8,128)S(1)} collective-permute-done((f32[128,128]{1,0:T(8,128)S(1)}, f32[128,128]{1,0:T(8,128)S(1)}, u32[]{:S(2)}, u32[]{:S(2)}) %collective-permute-start.8) | collective-permute-done | bytes 65568 | tf_op jit(solution)/shard_map/ppermute | solution.py:324
  55.0 3.1 %collective-permute-start.9 = (f32[128,128]{1,0:T(8,128)S(1)}, f32[128,128]{1,0:T(8,128)S(1)}, u32[]{:S(2)}, u32[]{:S(2)}) collective-permute-start(f32[128,128]{1,0:T(8,128)S(1)} %add.35), channel_id=1, source_target_pairs={{0,16},{1,9},{2,18},{3,11},{4,20},{5,13},{6,22},{7,15},{8,24},{9,1... | collective-permute-start | bytes 196616 | tf_op jit(solution)/shard_map/ppermute | solution.py:324
  58.1 2.2 %collective-permute-done.9 = f32[128,128]{1,0:T(8,128)S(1)} collective-permute-done((f32[128,128]{1,0:T(8,128)S(1)}, f32[128,128]{1,0:T(8,128)S(1)}, u32[]{:S(2)}, u32[]{:S(2)}) %collective-permute-start.9) | collective-permute-done | bytes 65568 | tf_op jit(solution)/shard_map/ppermute | solution.py:324
  60.3 0.1 collective-permute-start.10
  60.4 1.2 %collective-permute-done.10.other_ref = f32[128,128]{1,0:T(8,128)S(1)} collective-permute-done((f32[128,128]{1,0:T(8,128)S(1)}, f32[128,128]{1,0:T(8,128)S(1)}, u32[]{:S(2)}, u32[]{:S(2)}) %collective-permute-start.10) | collective-permute-done | bytes 65568 | tf_op jit(solution)/shard_map/ppermute | solution.py:313
  61.7 1.8 %modes.1 = (f32[2,64]{1,0:T(2,128)}, f32[256,128]{1,0:T(8,128)}) custom-call(s32[1]{0:T(128)} %bitcast.odd_ref, s32[1]{0:T(128)} %bitcast.1.side_ref.core_ref, f32[128,128]{1,0:T(8,128)S(1)} %add.36.mine_ref, f32[128,128]{1,0:T(8,128)S(1)} %collective-permute-done.10.other_ref, bf16[2048,128]{1,0:T(8,128)(2,1)S(1)} %get-tuple-element.22.near_ref, ...), custom_call_target="tpu_custom_call" | custom-call | tf_op jit(solution)/shard_map/modes/pallas_call | solution.py:426
  (28 shorter events, 0.1 us)
Async XLA Ops:
  0.6 1.3 %copy-start = (bf16[2176,2,128]{2,1,0:T(2,128)(2,1)S(1)}, bf16[2176,2,128]{2,1,0:T(2,128)(2,1)}, u32[]{:S(2)}) copy-start(bf16[2176,2,128]{2,1,0:T(2,128)(2,1)} %param.11) | copy-start | bytes 3342340
  2.1 16.9 %copy-start.2 = (bf16[2176,2,128]{2,1,0:T(2,128)(2,1)S(1)}, bf16[2176,2,128]{2,1,0:T(2,128)(2,1)}, u32[]{:S(2)}) copy-start(bf16[2176,2,128]{2,1,0:T(2,128)(2,1)} %param.10) | copy-start | bytes 3342340
  2.1 16.9 %copy-start.3 = (bf16[8,16,128]{2,1,0:T(8,128)(2,1)S(1)}, bf16[8,16,128]{2,1,0:T(8,128)(2,1)}, u32[]{:S(2)}) copy-start(bf16[8,16,128]{2,1,0:T(8,128)(2,1)} %constant.42.clone.picks_ref) | copy-start | bytes 98308
  2.1 18.0 %copy-start.9 = (s32[64,2]{0,1:T(2,128)S(1)}, s32[64,2]{0,1:T(2,128)}, u32[]{:S(2)}) copy-start(s32[64,2]{0,1:T(2,128)} %param.14) | copy-start | bytes 1540
  2.2 11.2 %collective-permute-start.2 = (bf16[1360,128]{1,0:T(8,128)(2,1)S(1)}, bf16[1360,128]{1,0:T(8,128)(2,1)S(1)}, u32[]{:S(2)}, u32[]{:S(2)}) collective-permute-start(bf16[1360,128]{1,0:T(8,128)(2,1)S(1)} %get-tuple-element.18), channel_id=1, source_target_pairs={{0,4},{4,0},{8,12},{12,8},{16,20},{20,16},{24,28},{28,24},{1,5},{5... | collective-permute-start | bytes 1044488 | tf_op jit(solution)/shard_map/ppermute | solution.py:313
  13.6 6.8 %copy-start.10 = (s32[16]{0:T(128)S(1)}, s32[16]{0:T(128)}, u32[]{:S(2)}) copy-start(s32[16]{0:T(128)} %param.13) | copy-start | bytes 196
  13.6 7.1 %copy-start.1 = (bf16[2176,2,128]{2,1,0:T(2,128)(2,1)S(1)}, bf16[2176,2,128]{2,1,0:T(2,128)(2,1)}, u32[]{:S(2)}) copy-start(bf16[2176,2,128]{2,1,0:T(2,128)(2,1)} %param.11) | copy-start | bytes 3342340
  13.6 7.1 %copy-start.7 = (bf16[128,128]{1,0:T(8,128)(2,1)S(1)}, bf16[128,128]{1,0:T(8,128)(2,1)}, u32[]{:S(2)}) copy-start(bf16[128,128]{1,0:T(8,128)(2,1)} %constant.43.clone.shift_ref) | copy-start | bytes 98308
  13.6 7.1 %copy-start.8 = (bf16[8,16,128]{2,1,0:T(8,128)(2,1)S(1)}, bf16[8,16,128]{2,1,0:T(8,128)(2,1)}, u32[]{:S(2)}) copy-start(bf16[8,16,128]{2,1,0:T(8,128)(2,1)} %constant.44.clone.places_ref) | copy-start | bytes 98308
  13.6 23.2 %collective-permute-start.3 = (bf16[2176,128]{1,0:T(8,128)(2,1)S(1)}, bf16[2176,128]{1,0:T(8,128)(2,1)}, u32[]{:S(2)}, u32[]{:S(2)}) collective-permute-start(bf16[2176,128]{1,0:T(8,128)(2,1)S(1)} %far.1), channel_id=1, source_target_pairs={{4,8},{12,16},{20,24},{8,4},{16,12},{24,20},{5,9},{13,17},{21,25},... | collective-permute-start | bytes 1671176 | tf_op jit(solution)/shard_map/ppermute | solution.py:470
  15.2 18.5 %collective-permute-start.4 = (bf16[816,128]{1,0:T(8,128)(2,1)S(1)}, bf16[816,128]{1,0:T(8,128)(2,1)}, u32[]{:S(2)}, u32[]{:S(2)}) collective-permute-start(bf16[816,128]{1,0:T(8,128)(2,1)S(1)} %get-tuple-element.19), channel_id=1, source_target_pairs={{0,4},{4,0},{8,12},{12,8},{16,20},{20,16},{24,28},{28,24},{1,5},{5... | collective-permute-start | bytes 626696 | tf_op jit(solution)/shard_map/ppermute | solution.py:313
  19.4 1.2 %collective-permute-start = (bf16[8,544]{1,0:T(8,128)(2,1)S(1)}, bf16[8,544]{1,0:T(8,128)(2,1)S(1)}, u32[]{:S(2)}, u32[]{:S(2)}) collective-permute-start(bf16[8,544]{1,0:T(8,128)(2,1)S(1)} %get-tuple-element.14), channel_id=1, source_target_pairs={{0,1},{1,0},{2,3},{3,2},{4,5},{5,4},{6,7},{7,6},{8,9},{9,8},{10,11... | collective-permute-start | bytes 26120 | tf_op jit(solution)/shard_map/ppermute | solution.py:313
  19.5 1.2 %collective-permute-start.1 = (bf16[8,544]{1,0:T(8,128)(2,1)S(1)}, bf16[8,544]{1,0:T(8,128)(2,1)S(1)}, u32[]{:S(2)}, u32[]{:S(2)}) collective-permute-start(bf16[8,544]{1,0:T(8,128)(2,1)S(1)} %get-tuple-element.15), channel_id=1, source_target_pairs={{1,2},{2,1},{5,6},{6,5},{9,10},{10,9},{13,14},{14,13},{17,18},{18,... | collective-permute-start | bytes 26120 | tf_op jit(solution)/shard_map/ppermute | solution.py:467
  20.5 13.3 %copy-start.4 = (f32[2,128]{1,0:T(2,128)S(1)}, f32[2,128]{1,0:T(2,128)}, u32[]{:S(2)}) copy-start(f32[2,128]{1,0:T(2,128)} %weights_ref.3) | copy-start | bytes 3076
  20.5 13.3 %copy-start.5 = (f32[256,128]{1,0:T(8,128)S(1)}, f32[256,128]{1,0:T(8,128)}, u32[]{:S(2)}) copy-start(f32[256,128]{1,0:T(8,128)} %constant.45.clone.window_ref) | copy-start | bytes 393220
  20.5 13.3 %copy-start.6 = (bf16[256,256]{1,0:T(8,128)(2,1)S(1)}, bf16[256,256]{1,0:T(8,128)(2,1)}, u32[]{:S(2)}) copy-start(bf16[256,256]{1,0:T(8,128)(2,1)} %constant.46.clone.transform_ref) | copy-start | bytes 393220
  40.0 1.3 %collective-permute-start.5 = (f32[128,128]{1,0:T(8,128)S(1)}, f32[128,128]{1,0:T(8,128)S(1)}, u32[]{:S(2)}, u32[]{:S(2)}) collective-permute-start(f32[128,128]{1,0:T(8,128)S(1)} %constant_dynamic-slice_fusion), channel_id=1, source_target_pairs={{0,1},{1,0},{2,3},{3,2},{4,5},{5,4},{6,7},{7,6},{8,9},{9,8},{10,11... | collective-permute-start | bytes 196616 | tf_op jit(solution)/shard_map/ppermute | solution.py:313
  41.3 4.9 %collective-permute-start.6 = (f32[128,128]{1,0:T(8,128)S(1)}, f32[128,128]{1,0:T(8,128)S(1)}, u32[]{:S(2)}, u32[]{:S(2)}) collective-permute-start(f32[128,128]{1,0:T(8,128)S(1)} %dynamic-slice_add_fusion), channel_id=1, source_target_pairs={{0,4},{1,3},{2,6},{3,1},{4,0},{5,7},{6,2},{7,5},{8,12},{9,11},{10,... | collective-permute-start | bytes 196616 | tf_op jit(solution)/shard_map/ppermute | solution.py:324
  46.2 4.3 %collective-permute-start.7 = (f32[128,128]{1,0:T(8,128)S(1)}, f32[128,128]{1,0:T(8,128)S(1)}, u32[]{:S(2)}, u32[]{:S(2)}) collective-permute-start(f32[128,128]{1,0:T(8,128)S(1)} %add.33), channel_id=1, source_target_pairs={{0,2},{1,5},{2,0},{3,7},{4,6},{5,1},{6,4},{7,3},{8,10},{9,13},{10,... | collective-permute-start | bytes 196616 | tf_op jit(solution)/shard_map/ppermute | solution.py:324
  50.6 4.4 %collective-permute-start.8 = (f32[128,128]{1,0:T(8,128)S(1)}, f32[128,128]{1,0:T(8,128)S(1)}, u32[]{:S(2)}, u32[]{:S(2)}) collective-permute-start(f32[128,128]{1,0:T(8,128)S(1)} %add.34), channel_id=1, source_target_pairs={{0,8},{1,17},{2,10},{3,19},{4,12},{5,21},{6,14},{7,23},{8,0},{9,25... | collective-permute-start | bytes 196616 | tf_op jit(solution)/shard_map/ppermute | solution.py:324
  55.0 5.3 %collective-permute-start.9 = (f32[128,128]{1,0:T(8,128)S(1)}, f32[128,128]{1,0:T(8,128)S(1)}, u32[]{:S(2)}, u32[]{:S(2)}) collective-permute-start(f32[128,128]{1,0:T(8,128)S(1)} %add.35), channel_id=1, source_target_pairs={{0,16},{1,9},{2,18},{3,11},{4,20},{5,13},{6,22},{7,15},{8,24},{9,1... | collective-permute-start | bytes 196616 | tf_op jit(solution)/shard_map/ppermute | solution.py:324
  60.3 1.3 %collective-permute-start.10 = (f32[128,128]{1,0:T(8,128)S(1)}, f32[128,128]{1,0:T(8,128)S(1)}, u32[]{:S(2)}, u32[]{:S(2)}) collective-permute-start(f32[128,128]{1,0:T(8,128)S(1)} %add.36.mine_ref), channel_id=1, source_target_pairs={{0,1},{1,0},{2,3},{3,2},{4,5},{5,4},{6,7},{7,6},{8,9},{9,8},{10,11... | collective-permute-start | bytes 196616 | tf_op jit(solution)/shard_map/ppermute | solution.py:313

commit v7 on v6

--- a/solution.py
+++ b/solution.py
@@ -80,23 +80,22 @@
     )(odd, v)
 
 
-def far_kernel(sx, odd_ref, v_ref, after_ref, far_ref, plain):
-    times = far_ref.shape[0]
+def far_kernel(sx, odd_ref, v_ref, far_ref, plain):
     plain[...] = v_ref[...].astype(F32)
-    far_ref[...] = plain[pl.ds(row_at(sx - 1, sx, odd_ref[0]), times, stride=sx), :].astype(BF16)
-
-
-def far_edge(odd, v, after, sx):
+    far_ref[...] = plain[pl.ds(row_at(sx - 1, sx, odd_ref[0]), far_ref.shape[0], stride=sx), :].astype(BF16)
+
+
+def far_edge(odd, v, sx):
     rows = v.shape[0]
     return pl.pallas_call(
         functools.partial(far_kernel, sx),
         out_shape=jax.ShapeDtypeStruct((rows // sx, LANES), BF16),
-        in_specs=[SMEM, VMEM, pl.BlockSpec(memory_space=pl.ANY)],
+        in_specs=[SMEM, VMEM],
         out_specs=VMEM,
         scratch_shapes=[pltpu.VMEM((rows, LANES), F32)],
         compiler_params=limit(8),
         name="far",
-    )(odd, v, after)
+    )(odd, v)
 
 
 def columns_kernel(pieces, side_ref, u_ref, picks_ref, near_ref, far_ref):
@@ -172,20 +171,23 @@
 
 
 def cross_kernel(
-    sx, begin, pieces, blocks, ntri, scalars_ref, z_ref, sum_ref, weights_ref, window_ref, transform_ref, *rest
+    sx, begin, pieces, odd_ref, core_ref, offsets_ref, triads_ref, z_ref, sum_ref, weights_ref, window_ref, transform_ref,
+    *rest,
 ):
     far = begin > 0
     halo_refs, rest = rest[:pieces], rest[pieces:]
     if far:
         before_ref, *rest = rest
-    cross_ref, target_ref, full, spec, prod, packed = rest
+    *cross_refs, target_ref, full, spec, prod, packed = rest
     count, times, _ = full.shape
+    blocks = offsets_ref.shape[0]
+    ntri = triads_ref.shape[1]
     half = NFFT // 2
     groups = LANES // blocks
     per = ntri // groups
     wide = 2 * blocks
     pitch = blocks + 1
-    odd = scalars_ref[0]
+    odd = odd_ref[0]
     sign = jnp.where(odd == 1, 0.5, -0.5)
     if not far:
         sign = -sign
@@ -215,21 +217,24 @@
             total = total + halo_sum
         means.append(jnp.sum(total, axis=0, keepdims=True) * (1.0 / times))
 
-    def one_block(b, carry):
-        at = pl.ds(scalars_ref[1 + b], NFFT)
+    def two_blocks(h, carry):
         window = window_ref[...]
+        pair = (2 * h, 2 * h + 1)
         for row in range(count):
-            windowed = ((full[row, at, :] - means[row]) * window).astype(BF16)
-            out = jnp.dot(transform_ref[...], windowed, preferred_element_type=F32)
-            spec[row, pl.ds(b, NFFT, stride=pitch), :] = out
+            windowed = [
+                ((full[row, pl.ds(offsets_ref[b], NFFT), :] - means[row]) * window).astype(BF16) for b in pair
+            ]
+            out = jnp.dot(transform_ref[...], jnp.concatenate(windowed, axis=1), preferred_element_type=F32)
+            for n, b in enumerate(pair):
+                spec[row, pl.ds(b, NFFT, stride=pitch), :] = out[:, n * LANES : (n + 1) * LANES]
         return carry
 
-    lax.fori_loop(0, blocks, one_block, 0, unroll=True)
+    lax.fori_loop(0, blocks // 2, two_blocks, 0, unroll=True)
     weights = [weights_ref[pl.ds(row_at(begin + row, sx, odd), 1), :] for row in range(count)]
 
     def one_triad(j, carry):
-        k = scalars_ref[1 + blocks + 2 * j]
-        l = scalars_ref[2 + blocks + 2 * j]
+        k = triads_ref[0, j]
+        l = triads_ref[1, j]
 
         def take(f, row):
             re = spec[row, pl.ds(f * pitch, blocks), :]
@@ -277,25 +282,31 @@
 
     lax.fori_loop(0, groups, one_group, 0, unroll=True)
     share = packed[...].T
-    if far:
-        share = share + before_ref[...]
-    cross_ref[...] = share
-
-
-def cross_part(begin, count, blocks, ntri, scalars, z, sums, halos, weights, window, transform, before=None):
+    if not far:
+        cross_refs[0][...] = share
+        return
+    share = share + before_ref[...]
+    lower, upper = share[: tall // 2], share[tall // 2 :]
+    second = core_ref[0] == 1
+    cross_refs[0][...] = jnp.where(second, upper, lower)
+    cross_refs[1][...] = jnp.where(second, lower, upper)
+
+
+def cross_part(begin, count, odd, core, offsets, triads, z, sums, halos, weights, window, transform, before=None):
     sx, times, _ = z.shape
+    blocks = offsets.shape[0]
+    ntri = triads.shape[1]
     groups = LANES // blocks
     wide = 2 * blocks
     tall = ntri // groups * wide
     more = list(halos) + ([] if before is None else [before])
+    parts = 1 if before is None else 2
     return pl.pallas_call(
-        functools.partial(cross_kernel, sx, begin, len(halos), blocks, ntri),
-        out_shape=(
-            jax.ShapeDtypeStruct((tall, LANES), F32),
-            jax.ShapeDtypeStruct((ntri * wide, count * LANES), BF16),
-        ),
-        in_specs=[SMEM] + [VMEM] * (5 + len(more)),
-        out_specs=(VMEM,) * 2,
+        functools.partial(cross_kernel, sx, begin, len(halos)),
+        out_shape=(jax.ShapeDtypeStruct((tall // parts, LANES), F32),) * parts
+        + (jax.ShapeDtypeStruct((ntri * wide, count * LANES), BF16),),
+        in_specs=[SMEM] * 4 + [VMEM] * (5 + len(more)),
+        out_specs=(VMEM,) * (parts + 1),
         scratch_shapes=[
             pltpu.VMEM((count, times, LANES), F32),
             pltpu.VMEM((count, NFFT * (blocks + 1), LANES), F32),
@@ -305,7 +316,7 @@
         compiler_params=limit(26),
         cost_estimate=pl.CostEstimate(flops=2000000000, bytes_accessed=4000000, transcendentals=0),
         name="cross_far" if begin else "cross_near",
-    )(scalars, z, sums, weights, window, transform, *more)
+    )(odd, core, offsets, triads, z, sums, weights, window, transform, *more)
 
 
 def swap(x, axis, bit):
@@ -457,7 +468,7 @@
     u = u_velocity.reshape(times * sx, columns)
     odd = is_odd()[None]
     core = (lax.axis_index("freq") % 2)[None]
-    scalars = jnp.concatenate([odd, block_offsets, triads.reshape(-1)])
+    pairs = triads.T
 
     early, late = near_edge(odd, v, sx)
     early = swap(early, "space", 1)
@@ -466,19 +477,16 @@
     col_near = swap(col_near, "freq", 1)
     col_far = lax.ppermute(col_far, "freq", between_pairs(lax.axis_size("freq")))
     z, sums = local_part(odd, core, v, u, jnp.asarray(shift, BF16), col_near, col_far, jnp.asarray(places, BF16), sx)
-    far = far_edge(odd, v, early, sx)
+    far = far_edge(odd, v, sx)
     far = lax.ppermute(far, "space", between_pairs(slabs))
     window = jnp.asarray(np.ascontiguousarray(np.broadcast_to(window[:, None], (NFFT, LANES))))
     transform = jnp.asarray(transform, BF16)
     share, near_target = cross_part(
-        0, sx - 1, blocks, ntri, scalars, z, sums, [early, late], cell_weights, window, transform
+        0, sx - 1, odd, core, block_offsets, pairs, z, sums, [early, late], cell_weights, window, transform
     )
-    share, far_target = cross_part(
-        sx - 1, 1, blocks, ntri, scalars, z, sums, [far], cell_weights, window, transform, share
+    mine, other, far_target = cross_part(
+        sx - 1, 1, odd, core, block_offsets, pairs, z, sums, [far], cell_weights, window, transform, share
     )
-    half = share.shape[0] // 2
-    mine = lax.dynamic_slice_in_dim(share, core[0] * half, half, 0)
-    other = lax.dynamic_slice_in_dim(share, (1 - core[0]) * half, half, 0)
     mine = mine + swap(other, "freq", 1)
     mine = sum_over_rest(mine)
     other = swap(mine, "freq", 1)

time: 63.7 us -> 61 us (0.958)
  starting transfers between devices: 18.8 us -> 17 us
    ppermute x5, starting transfers between devices: 7.02 us -> 5.96 us  [swap(): return lax.ppermute(x, axis, [(i, i ^ bit) for i in range(count)])]
    pallas_call x1, Pallas kernels: 0.23 us -> 1.05 us  [near_edge(): pl.pallas_call(functools.partial(near_kernel, sx), out_shape=(jax.ShapeDt...]
    ppermute x1, starting transfers between devices: 1.63 us -> 0.83 us  [on_device(): far = lax.ppermute(far, 'space', between_pairs(slabs))]
    pallas_call x2, Pallas kernels: 6.13 us -> 5.35 us  [cross_part(): pl.pallas_call(functools.partial(cross_kernel, sx, begin, len(halos)), ou...]
    unnamed x23 -> x22, local copies, waits for them, and re-layouts: 1.4 us -> 1.3 us
  transfers between devices with their start and end apart: 11 -> 11, of which waited for: 9 -> 8; matrix products, arithmetic and copies ran while one was open for 0% -> 0% of each run, Pallas kernels for 7% -> 9%
where the time goes in v7:
time: 61 us; the launch traced here: 60.8 us
  waiting for transfers between devices  31.6 us (52%)
  starting transfers between devices  17 us (28%)
  Pallas kernels  10 us (16%)
  local copies, waits for them, and re-layouts  1.3 us (2%)
  between operations  0.83 us (1%)
    ppermute x5, waiting for transfers between devices, swap(): return lax.ppermute(x, axis, [(i, i ^ bit) for i in range(count)])  22.1 us
    ppermute x4, waiting for transfers between devices, sum_over_rest(): x = x + lax.ppermute(x, ('space', 'freq'), pairs)  9.48 us
    ppermute x4, starting transfers between devices, sum_over_rest(): x = x + lax.ppermute(x, ('space', 'freq'), pairs)  9.4 us
    ppermute x5, starting transfers between devices, swap(): return lax.ppermute(x, axis, [(i, i ^ bit) for i in range(count)])  5.96 us
    pallas_call x2, Pallas kernels, cross_part(): pl.pallas_call(functools.partial(cross_kernel, sx, begin, len(halos)), ou...  5.35 us
    pallas_call x1, Pallas kernels, modes_part(): pl.pallas_call(functools.partial(modes_kernel, sx, blocks, scaling), out_...  1.82 us
    unnamed x22, local copies, waits for them, and re-layouts  1.3 us
  transfers between devices with their start and end apart: 11, of which 8 were waited for; matrix products, arithmetic and copies ran while one was open for 0% of the time, Pallas kernels for 9%

profile of v7, /device:TPU:0, one launch (start us, length us, event | category | flops | bytes accessed | tf_op | source)
XLA Modules:
  0.0 60.8 jit_solution(7553751570994212610)
XLA Ops:
  0.6 0.0 copy-start
  0.7 1.2 %copy-done = bf16[2176,2,128]{2,1,0:T(2,128)(2,1)S(1)} copy-done((bf16[2176,2,128]{2,1,0:T(2,128)(2,1)S(1)}, bf16[2176,2,128]{2,1,0:T(2,128)(2,1)}, u32[]{:S(2)}) %copy-start) | copy-done | bytes 1114136
  1.9 0.2 far.1
  2.1 0.0 copy-start.9
  2.1 0.0 copy-start.10
  2.2 0.8 %collective-permute-start.2 = (bf16[2176,128]{1,0:T(8,128)(2,1)S(1)}, bf16[2176,128]{1,0:T(8,128)(2,1)S(1)}, u32[]{:S(2)}, u32[]{:S(2)}) collective-permute-start(bf16[2176,128]{1,0:T(8,128)(2,1)S(1)} %far.1), channel_id=1, source_target_pairs={{4,8},{12,16},{20,24},{8,4},{16,12},{24,20},{5,9},{13,17},{21,25},... | collective-permute-start | bytes 1671176 | tf_op jit(solution)/shard_map/ppermute | solution.py:481
  3.0 1.0 %near.1 = (bf16[1360,128]{1,0:T(8,128)(2,1)}, bf16[816,128]{1,0:T(8,128)(2,1)}) custom-call(s32[1]{0:T(128)} %bitcast.odd_ref, bf16[4352,128]{1,0:T(8,128)(2,1)S(1)} %bitcast.8), custom_call_target="tpu_custom_call" | custom-call | tf_op jit(solution)/shard_map/near/pallas_call | solution.py:69
  4.0 5.7 %collective-permute-start.3 = (bf16[1360,128]{1,0:T(8,128)(2,1)}, bf16[1360,128]{1,0:T(8,128)(2,1)}, u32[]{:S(2)}, u32[]{:S(2)}) collective-permute-start(bf16[1360,128]{1,0:T(8,128)(2,1)} %get-tuple-element.19), channel_id=1, source_target_pairs={{0,4},{4,0},{8,12},{12,8},{16,20},{20,16},{24,28},{28,24},{1,5},{5... | collective-permute-start | bytes 1044488 | tf_op jit(solution)/shard_map/ppermute | solution.py:324
  9.8 0.0 collective-permute-start.4
  9.8 0.4 columns.1
  10.2 0.1 collective-permute-start
  10.3 0.0 copy-start.7
  10.3 0.0 copy-start.8
  10.3 0.8 %collective-permute-start.1 = (bf16[8,544]{1,0:T(8,128)(2,1)S(1)}, bf16[8,544]{1,0:T(8,128)(2,1)S(1)}, u32[]{:S(2)}, u32[]{:S(2)}) collective-permute-start(bf16[8,544]{1,0:T(8,128)(2,1)S(1)} %get-tuple-element.16), channel_id=1, source_target_pairs={{1,2},{2,1},{5,6},{6,5},{9,10},{10,9},{13,14},{14,13},{17,18},{18,... | collective-permute-start | bytes 26120 | tf_op jit(solution)/shard_map/ppermute | solution.py:478
  11.1 0.3 collective-permute-done.near_ref
  11.5 1.2 %local.1 = (f32[2,2176,128]{2,1,0:T(8,128)S(1)}, f32[2,8,128]{2,1,0:T(8,128)S(1)}) custom-call(s32[1]{0:T(128)} %bitcast.odd_ref, s32[1]{0:T(128)} %bitcast.1.side_ref.core_ref, bf16[4352,128]{1,0:T(8,128)(2,1)S(1)} %bitcast.9, bf16[4352,128]{1,0:T(8,128)(2,1)S(1)} %bitcast.11, bf16[128,128]{1,0:T(8,128)(2,1)S(1)} %copy-done.10, ...), custom_call_target="tpu_custom_call" | custom-call | flops 1000000000 | bytes 8000000 | tf_op jit(solution)/shard_map/local/pallas_call | solution.py:158
  12.6 19.4 %collective-permute-done.4.rest_1_ = bf16[816,128]{1,0:T(8,128)(2,1)} collective-permute-done((bf16[816,128]{1,0:T(8,128)(2,1)}, bf16[816,128]{1,0:T(8,128)(2,1)}, u32[]{:S(2)}, u32[]{:S(2)}) %collective-permute-start.4) | collective-permute-done | bytes 208928 | tf_op jit(solution)/shard_map/ppermute | solution.py:324
  32.0 2.9 %cross_near.1 = (f32[256,128]{1,0:T(8,128)S(1)}, bf16[2048,128]{1,0:T(8,128)(2,1)S(1)}) custom-call(s32[1]{0:T(128)} %bitcast.odd_ref, s32[1]{0:T(128)} %bitcast.1.side_ref.core_ref, s32[16]{0:T(128)S(1)} %copy-done.6, s32[2,64]{1,0:T(2,128)S(1)} %bitcast.12, f32[2,2176,128]{2,1,0:T(8,128)S(1)} %get-tuple-element.17.z_ref, ...), custom_call_target="tpu_custom_call" | custom-call | flops 2000000000 | bytes 4000000 | tf_op jit(solution)/shard_map/cross_near/pallas_call | solution.py:304
  35.0 2.4 %cross_far.1 = (f32[128,128]{1,0:T(8,128)S(1)}, f32[128,128]{1,0:T(8,128)S(1)}, bf16[2048,128]{1,0:T(8,128)(2,1)S(1)}) custom-call(s32[1]{0:T(128)} %bitcast.odd_ref, s32[1]{0:T(128)} %bitcast.1.side_ref.core_ref, s32[16]{0:T(128)S(1)} %copy-done.6, s32[2,64]{1,0:T(2,128)S(1)} %bitcast.13, f32[2,2176,128]{2,1,0:T(8,128)S(1)} %get-tuple-element.17.z_ref, ...), custom_call_target="tpu_custom_call" | custom-call | flops 2000000000 | bytes 4000000 | tf_op jit(solution)/shard_map/cross_far/pallas_call | solution.py:304
  37.4 0.1 collective-permute-start.5
  37.5 1.2 %collective-permute-done.5 = f32[128,128]{1,0:T(8,128)S(1)} collective-permute-done((f32[128,128]{1,0:T(8,128)S(1)}, f32[128,128]{1,0:T(8,128)S(1)}, u32[]{:S(2)}, u32[]{:S(2)}) %collective-permute-start.5) | collective-permute-done | bytes 65568 | tf_op jit(solution)/shard_map/ppermute | solution.py:324
  38.7 2.5 %collective-permute-start.6 = (f32[128,128]{1,0:T(8,128)S(1)}, f32[128,128]{1,0:T(8,128)S(1)}, u32[]{:S(2)}, u32[]{:S(2)}) collective-permute-start(f32[128,128]{1,0:T(8,128)S(1)} %add.24), channel_id=1, source_target_pairs={{0,4},{1,3},{2,6},{3,1},{4,0},{5,7},{6,2},{7,5},{8,12},{9,11},{10,... | collective-permute-start | bytes 196616 | tf_op jit(solution)/shard_map/ppermute | solution.py:335
  41.3 2.2 %collective-permute-done.6 = f32[128,128]{1,0:T(8,128)S(1)} collective-permute-done((f32[128,128]{1,0:T(8,128)S(1)}, f32[128,128]{1,0:T(8,128)S(1)}, u32[]{:S(2)}, u32[]{:S(2)}) %collective-permute-start.6) | collective-permute-done | bytes 65568 | tf_op jit(solution)/shard_map/ppermute | solution.py:335
  43.5 1.6 %collective-permute-start.7 = (f32[128,128]{1,0:T(8,128)S(1)}, f32[128,128]{1,0:T(8,128)S(1)}, u32[]{:S(2)}, u32[]{:S(2)}) collective-permute-start(f32[128,128]{1,0:T(8,128)S(1)} %add.25), channel_id=1, source_target_pairs={{0,2},{1,5},{2,0},{3,7},{4,6},{5,1},{6,4},{7,3},{8,10},{9,13},{10,... | collective-permute-start | bytes 196616 | tf_op jit(solution)/shard_map/ppermute | solution.py:335
  45.1 2.7 %collective-permute-done.7 = f32[128,128]{1,0:T(8,128)S(1)} collective-permute-done((f32[128,128]{1,0:T(8,128)S(1)}, f32[128,128]{1,0:T(8,128)S(1)}, u32[]{:S(2)}, u32[]{:S(2)}) %collective-permute-start.7) | collective-permute-done | bytes 65568 | tf_op jit(solution)/shard_map/ppermute | solution.py:335
  47.9 2.2 %collective-permute-start.8 = (f32[128,128]{1,0:T(8,128)S(1)}, f32[128,128]{1,0:T(8,128)S(1)}, u32[]{:S(2)}, u32[]{:S(2)}) collective-permute-start(f32[128,128]{1,0:T(8,128)S(1)} %add.26), channel_id=1, source_target_pairs={{0,8},{1,17},{2,10},{3,19},{4,12},{5,21},{6,14},{7,23},{8,0},{9,25... | collective-permute-start | bytes 196616 | tf_op jit(solution)/shard_map/ppermute | solution.py:335
  50.0 2.2 %collective-permute-done.8 = f32[128,128]{1,0:T(8,128)S(1)} collective-permute-done((f32[128,128]{1,0:T(8,128)S(1)}, f32[128,128]{1,0:T(8,128)S(1)}, u32[]{:S(2)}, u32[]{:S(2)}) %collective-permute-start.8) | collective-permute-done | bytes 65568 | tf_op jit(solution)/shard_map/ppermute | solution.py:335
  52.3 3.1 %collective-permute-start.9 = (f32[128,128]{1,0:T(8,128)S(1)}, f32[128,128]{1,0:T(8,128)S(1)}, u32[]{:S(2)}, u32[]{:S(2)}) collective-permute-start(f32[128,128]{1,0:T(8,128)S(1)} %add.27), channel_id=1, source_target_pairs={{0,16},{1,9},{2,18},{3,11},{4,20},{5,13},{6,22},{7,15},{8,24},{9,1... | collective-permute-start | bytes 196616 | tf_op jit(solution)/shard_map/ppermute | solution.py:335
  55.4 2.2 %collective-permute-done.9 = f32[128,128]{1,0:T(8,128)S(1)} collective-permute-done((f32[128,128]{1,0:T(8,128)S(1)}, f32[128,128]{1,0:T(8,128)S(1)}, u32[]{:S(2)}, u32[]{:S(2)}) %collective-permute-start.9) | collective-permute-done | bytes 65568 | tf_op jit(solution)/shard_map/ppermute | solution.py:335
  57.7 0.1 collective-permute-start.10
  57.7 1.2 %collective-permute-done.10.other_ref = f32[128,128]{1,0:T(8,128)S(1)} collective-permute-done((f32[128,128]{1,0:T(8,128)S(1)}, f32[128,128]{1,0:T(8,128)S(1)}, u32[]{:S(2)}, u32[]{:S(2)}) %collective-permute-start.10) | collective-permute-done | bytes 65568 | tf_op jit(solution)/shard_map/ppermute | solution.py:324
  59.0 1.8 %modes.1 = (f32[2,64]{1,0:T(2,128)}, f32[256,128]{1,0:T(8,128)}) custom-call(s32[1]{0:T(128)} %bitcast.odd_ref, s32[1]{0:T(128)} %bitcast.1.side_ref.core_ref, f32[128,128]{1,0:T(8,128)S(1)} %add.28.mine_ref, f32[128,128]{1,0:T(8,128)S(1)} %collective-permute-done.10.other_ref, bf16[2048,128]{1,0:T(8,128)(2,1)S(1)} %get-tuple-element.24.near_ref, ...), custom_call_target="tpu_custom_call" | custom-call | tf_op jit(solution)/shard_map/modes/pallas_call | solution.py:437
  (24 shorter events, 0.1 us)
Async XLA Ops:
  0.6 1.3 %copy-start = (bf16[2176,2,128]{2,1,0:T(2,128)(2,1)S(1)}, bf16[2176,2,128]{2,1,0:T(2,128)(2,1)}, u32[]{:S(2)}) copy-start(bf16[2176,2,128]{2,1,0:T(2,128)(2,1)} %param.11) | copy-start | bytes 3342340
  1.9 7.9 %copy-start.2 = (bf16[2176,2,128]{2,1,0:T(2,128)(2,1)S(1)}, bf16[2176,2,128]{2,1,0:T(2,128)(2,1)}, u32[]{:S(2)}) copy-start(bf16[2176,2,128]{2,1,0:T(2,128)(2,1)} %param.10) | copy-start | bytes 3342340
  1.9 7.9 %copy-start.3 = (bf16[8,16,128]{2,1,0:T(8,128)(2,1)S(1)}, bf16[8,16,128]{2,1,0:T(8,128)(2,1)}, u32[]{:S(2)}) copy-start(bf16[8,16,128]{2,1,0:T(8,128)(2,1)} %constant.36.clone.picks_ref) | copy-start | bytes 98308
  2.1 9.3 %copy-start.1 = (bf16[2176,2,128]{2,1,0:T(2,128)(2,1)S(1)}, bf16[2176,2,128]{2,1,0:T(2,128)(2,1)}, u32[]{:S(2)}) copy-start(bf16[2176,2,128]{2,1,0:T(2,128)(2,1)} %param.11) | copy-start | bytes 3342340
  2.1 9.3 %copy-start.9 = (bf16[8,16,128]{2,1,0:T(8,128)(2,1)S(1)}, bf16[8,16,128]{2,1,0:T(8,128)(2,1)}, u32[]{:S(2)}) copy-start(bf16[8,16,128]{2,1,0:T(8,128)(2,1)} %constant.38.clone.places_ref) | copy-start | bytes 98308
  2.1 9.3 %copy-start.10 = (bf16[128,128]{1,0:T(8,128)(2,1)S(1)}, bf16[128,128]{1,0:T(8,128)(2,1)}, u32[]{:S(2)}) copy-start(bf16[128,128]{1,0:T(8,128)(2,1)} %constant.37.clone.shift_ref) | copy-start | bytes 98308
  2.2 32.8 %collective-permute-start.2 = (bf16[2176,128]{1,0:T(8,128)(2,1)S(1)}, bf16[2176,128]{1,0:T(8,128)(2,1)S(1)}, u32[]{:S(2)}, u32[]{:S(2)}) collective-permute-start(bf16[2176,128]{1,0:T(8,128)(2,1)S(1)} %far.1), channel_id=1, source_target_pairs={{4,8},{12,16},{20,24},{8,4},{16,12},{24,20},{5,9},{13,17},{21,25},... | collective-permute-start | bytes 1671176 | tf_op jit(solution)/shard_map/ppermute | solution.py:481
  4.0 27.9 %collective-permute-start.3 = (bf16[1360,128]{1,0:T(8,128)(2,1)}, bf16[1360,128]{1,0:T(8,128)(2,1)}, u32[]{:S(2)}, u32[]{:S(2)}) collective-permute-start(bf16[1360,128]{1,0:T(8,128)(2,1)} %get-tuple-element.19), channel_id=1, source_target_pairs={{0,4},{4,0},{8,12},{12,8},{16,20},{20,16},{24,28},{28,24},{1,5},{5... | collective-permute-start | bytes 1044488 | tf_op jit(solution)/shard_map/ppermute | solution.py:324
  9.8 22.2 %collective-permute-start.4 = (bf16[816,128]{1,0:T(8,128)(2,1)}, bf16[816,128]{1,0:T(8,128)(2,1)}, u32[]{:S(2)}, u32[]{:S(2)}) collective-permute-start(bf16[816,128]{1,0:T(8,128)(2,1)} %get-tuple-element.20), channel_id=1, source_target_pairs={{0,4},{4,0},{8,12},{12,8},{16,20},{20,16},{24,28},{28,24},{1,5},{5... | collective-permute-start | bytes 626696 | tf_op jit(solution)/shard_map/ppermute | solution.py:324
  10.2 1.2 %collective-permute-start = (bf16[8,544]{1,0:T(8,128)(2,1)S(1)}, bf16[8,544]{1,0:T(8,128)(2,1)S(1)}, u32[]{:S(2)}, u32[]{:S(2)}) collective-permute-start(bf16[8,544]{1,0:T(8,128)(2,1)S(1)} %get-tuple-element.15), channel_id=1, source_target_pairs={{0,1},{1,0},{2,3},{3,2},{4,5},{5,4},{6,7},{7,6},{8,9},{9,8},{10,11... | collective-permute-start | bytes 26120 | tf_op jit(solution)/shard_map/ppermute | solution.py:324
  10.3 21.7 %copy-start.4 = (s32[64,2]{0,1:T(2,128)S(1)}, s32[64,2]{0,1:T(2,128)}, u32[]{:S(2)}) copy-start(s32[64,2]{0,1:T(2,128)} %param.14) | copy-start | bytes 1540
  10.3 21.7 %copy-start.5 = (f32[2,128]{1,0:T(2,128)S(1)}, f32[2,128]{1,0:T(2,128)}, u32[]{:S(2)}) copy-start(f32[2,128]{1,0:T(2,128)} %weights_ref.3) | copy-start | bytes 3076
  10.3 21.7 %copy-start.6 = (s32[16]{0:T(128)S(1)}, s32[16]{0:T(128)}, u32[]{:S(2)}) copy-start(s32[16]{0:T(128)} %offsets_ref.3) | copy-start | bytes 196
  10.3 21.7 %copy-start.7 = (bf16[256,256]{1,0:T(8,128)(2,1)S(1)}, bf16[256,256]{1,0:T(8,128)(2,1)}, u32[]{:S(2)}) copy-start(bf16[256,256]{1,0:T(8,128)(2,1)} %constant.40.clone.transform_ref) | copy-start | bytes 393220
  10.3 21.7 %copy-start.8 = (f32[256,128]{1,0:T(8,128)S(1)}, f32[256,128]{1,0:T(8,128)}, u32[]{:S(2)}) copy-start(f32[256,128]{1,0:T(8,128)} %constant.39.clone.window_ref) | copy-start | bytes 393220
  10.3 1.1 %collective-permute-start.1 = (bf16[8,544]{1,0:T(8,128)(2,1)S(1)}, bf16[8,544]{1,0:T(8,128)(2,1)S(1)}, u32[]{:S(2)}, u32[]{:S(2)}) collective-permute-start(bf16[8,544]{1,0:T(8,128)(2,1)S(1)} %get-tuple-element.16), channel_id=1, source_target_pairs={{1,2},{2,1},{5,6},{6,5},{9,10},{10,9},{13,14},{14,13},{17,18},{18,... | collective-permute-start | bytes 26120 | tf_op jit(solution)/shard_map/ppermute | solution.py:478
  37.4 1.3 %collective-permute-start.5 = (f32[128,128]{1,0:T(8,128)S(1)}, f32[128,128]{1,0:T(8,128)S(1)}, u32[]{:S(2)}, u32[]{:S(2)}) collective-permute-start(f32[128,128]{1,0:T(8,128)S(1)} %get-tuple-element.23), channel_id=1, source_target_pairs={{0,1},{1,0},{2,3},{3,2},{4,5},{5,4},{6,7},{7,6},{8,9},{9,8},{10,11... | collective-permute-start | bytes 196616 | tf_op jit(solution)/shard_map/ppermute | solution.py:324
  38.7 4.8 %collective-permute-start.6 = (f32[128,128]{1,0:T(8,128)S(1)}, f32[128,128]{1,0:T(8,128)S(1)}, u32[]{:S(2)}, u32[]{:S(2)}) collective-permute-start(f32[128,128]{1,0:T(8,128)S(1)} %add.24), channel_id=1, source_target_pairs={{0,4},{1,3},{2,6},{3,1},{4,0},{5,7},{6,2},{7,5},{8,12},{9,11},{10,... | collective-permute-start | bytes 196616 | tf_op jit(solution)/shard_map/ppermute | solution.py:335
  43.5 4.3 %collective-permute-start.7 = (f32[128,128]{1,0:T(8,128)S(1)}, f32[128,128]{1,0:T(8,128)S(1)}, u32[]{:S(2)}, u32[]{:S(2)}) collective-permute-start(f32[128,128]{1,0:T(8,128)S(1)} %add.25), channel_id=1, source_target_pairs={{0,2},{1,5},{2,0},{3,7},{4,6},{5,1},{6,4},{7,3},{8,10},{9,13},{10,... | collective-permute-start | bytes 196616 | tf_op jit(solution)/shard_map/ppermute | solution.py:335
  47.9 4.4 %collective-permute-start.8 = (f32[128,128]{1,0:T(8,128)S(1)}, f32[128,128]{1,0:T(8,128)S(1)}, u32[]{:S(2)}, u32[]{:S(2)}) collective-permute-start(f32[128,128]{1,0:T(8,128)S(1)} %add.26), channel_id=1, source_target_pairs={{0,8},{1,17},{2,10},{3,19},{4,12},{5,21},{6,14},{7,23},{8,0},{9,25... | collective-permute-start | bytes 196616 | tf_op jit(solution)/shard_map/ppermute | solution.py:335
  52.3 5.3 %collective-permute-start.9 = (f32[128,128]{1,0:T(8,128)S(1)}, f32[128,128]{1,0:T(8,128)S(1)}, u32[]{:S(2)}, u32[]{:S(2)}) collective-permute-start(f32[128,128]{1,0:T(8,128)S(1)} %add.27), channel_id=1, source_target_pairs={{0,16},{1,9},{2,18},{3,11},{4,20},{5,13},{6,22},{7,15},{8,24},{9,1... | collective-permute-start | bytes 196616 | tf_op jit(solution)/shard_map/ppermute | solution.py:335
  57.7 1.3 %collective-permute-start.10 = (f32[128,128]{1,0:T(8,128)S(1)}, f32[128,128]{1,0:T(8,128)S(1)}, u32[]{:S(2)}, u32[]{:S(2)}) collective-permute-start(f32[128,128]{1,0:T(8,128)S(1)} %add.28.mine_ref), channel_id=1, source_target_pairs={{0,1},{1,0},{2,3},{3,2},{4,5},{5,4},{6,7},{7,6},{8,9},{9,8},{10,11... | collective-permute-start | bytes 196616 | tf_op jit(solution)/shard_map/ppermute | solution.py:324

commit v8 on v7

--- a/solution.py
+++ b/solution.py
@@ -13,7 +13,7 @@
 NFFT = 256
 POW = 4
 LANES = 128
-AHEAD = 5
+AHEAD = 11
 F32 = jnp.float32
 BF16 = jnp.bfloat16
 MIB = 2**20
@@ -65,7 +65,7 @@
 
 def near_edge(odd, v, sx):
     rows = v.shape[0]
-    early = rows // sx * AHEAD // 8
+    early = rows // sx * AHEAD // 1024 * 64
     return pl.pallas_call(
         functools.partial(near_kernel, sx),
         out_shape=(
@@ -196,8 +196,9 @@
     halo_sum = jnp.zeros((8, LANES), F32)
     base = 0
     for halo_ref in halo_refs:
-        chunk = times // 8
-        steps = halo_ref.shape[0] // chunk
+        length = halo_ref.shape[0]
+        steps = max(n for n in range(1, 9) if length % (16 * n) == 0)
+        chunk = length // steps
 
         def add_halo(step, carry):
             at = pl.ds(pl.multiple_of(step * chunk, 8), chunk)

time: 61 us -> 59 us (0.967)
  waiting for transfers between devices: 31.6 us -> 28.2 us
  starting transfers between devices: 17 us -> 18.5 us
    ppermute x5, waiting for transfers between devices: 22.1 us -> 18.7 us  [swap(): return lax.ppermute(x, axis, [(i, i ^ bit) for i in range(count)])]
    ppermute x5, starting transfers between devices: 5.96 us -> 7.48 us  [swap(): return lax.ppermute(x, axis, [(i, i ^ bit) for i in range(count)])]
  transfers between devices with their start and end apart: 11 -> 11, of which waited for: 8 -> 8; matrix products, arithmetic and copies ran while one was open for 0% -> 0% of each run, Pallas kernels for 9% -> 8%
where the time goes in v8:
time: 59 us; the launch traced here: 58.8 us
  waiting for transfers between devices  28.2 us (48%)
  starting transfers between devices  18.5 us (31%)
  Pallas kernels  9.92 us (17%)
  local copies, waits for them, and re-layouts  1.29 us (2%)
  between operations  0.82 us (1%)
    ppermute x5, waiting for transfers between devices, swap(): return lax.ppermute(x, axis, [(i, i ^ bit) for i in range(count)])  18.7 us
    ppermute x4, starting transfers between devices, sum_over_rest(): x = x + lax.ppermute(x, ('space', 'freq'), pairs)  9.52 us
    ppermute x4, waiting for transfers between devices, sum_over_rest(): x = x + lax.ppermute(x, ('space', 'freq'), pairs)  9.48 us
    ppermute x5, starting transfers between devices, swap(): return lax.ppermute(x, axis, [(i, i ^ bit) for i in range(count)])  7.48 us
    pallas_call x2, Pallas kernels, cross_part(): pl.pallas_call(functools.partial(cross_kernel, sx, begin, len(halos)), ou...  5.35 us
    pallas_call x1, Pallas kernels, modes_part(): pl.pallas_call(functools.partial(modes_kernel, sx, blocks, scaling), out_...  1.82 us
    unnamed x22, local copies, waits for them, and re-layouts  1.29 us
  transfers between devices with their start and end apart: 11, of which 8 were waited for; matrix products, arithmetic and copies ran while one was open for 0% of the time, Pallas kernels for 8%

profile of v8, /device:TPU:0, one launch (start us, length us, event | category | flops | bytes accessed | tf_op | source)
XLA Modules:
  0.0 58.8 jit_solution(11586248680611523625)
XLA Ops:
  0.6 0.0 copy-start
  0.7 1.2 %copy-done = bf16[2176,2,128]{2,1,0:T(2,128)(2,1)S(1)} copy-done((bf16[2176,2,128]{2,1,0:T(2,128)(2,1)S(1)}, bf16[2176,2,128]{2,1,0:T(2,128)(2,1)}, u32[]{:S(2)}) %copy-start) | copy-done | bytes 1114136
  1.9 1.0 %near.1 = (bf16[1472,128]{1,0:T(8,128)(2,1)}, bf16[704,128]{1,0:T(8,128)(2,1)S(1)}) custom-call(s32[1]{0:T(128)} %bitcast.odd_ref, bf16[4352,128]{1,0:T(8,128)(2,1)S(1)} %bitcast.7), custom_call_target="tpu_custom_call" | custom-call | tf_op jit(solution)/shard_map/near/pallas_call | solution.py:69
  2.9 3.0 %collective-permute-start.3 = (bf16[1472,128]{1,0:T(8,128)(2,1)}, bf16[1472,128]{1,0:T(8,128)(2,1)}, u32[]{:S(2)}, u32[]{:S(2)}) collective-permute-start(bf16[1472,128]{1,0:T(8,128)(2,1)} %get-tuple-element.19), channel_id=1, source_target_pairs={{0,4},{4,0},{8,12},{12,8},{16,20},{20,16},{24,28},{28,24},{1,5},{5... | collective-permute-start | bytes 1130504 | tf_op jit(solution)/shard_map/ppermute | solution.py:325
  5.8 0.2 far.1
  6.1 0.7 %collective-permute-start.2 = (bf16[2176,128]{1,0:T(8,128)(2,1)S(1)}, bf16[2176,128]{1,0:T(8,128)(2,1)S(1)}, u32[]{:S(2)}, u32[]{:S(2)}) collective-permute-start(bf16[2176,128]{1,0:T(8,128)(2,1)S(1)} %far.1), channel_id=1, source_target_pairs={{4,8},{12,16},{20,24},{8,4},{16,12},{24,20},{5,9},{13,17},{21,25},... | collective-permute-start | bytes 1671176 | tf_op jit(solution)/shard_map/ppermute | solution.py:482
  6.8 4.3 %collective-permute-start.4 = (bf16[704,128]{1,0:T(8,128)(2,1)S(1)}, bf16[704,128]{1,0:T(8,128)(2,1)}, u32[]{:S(2)}, u32[]{:S(2)}) collective-permute-start(bf16[704,128]{1,0:T(8,128)(2,1)S(1)} %get-tuple-element.20), channel_id=1, source_target_pairs={{0,4},{4,0},{8,12},{12,8},{16,20},{20,16},{24,28},{28,24},{1,5},{5... | collective-permute-start | bytes 540680 | tf_op jit(solution)/shard_map/ppermute | solution.py:325
  11.1 0.4 columns.1
  11.5 0.1 collective-permute-start
  11.6 0.0 copy-start.5
  11.6 0.0 copy-start.6
  11.6 0.0 copy-start.7
  11.6 0.0 copy-start.8
  11.6 0.8 %collective-permute-start.1 = (bf16[8,544]{1,0:T(8,128)(2,1)S(1)}, bf16[8,544]{1,0:T(8,128)(2,1)S(1)}, u32[]{:S(2)}, u32[]{:S(2)}) collective-permute-start(bf16[8,544]{1,0:T(8,128)(2,1)S(1)} %get-tuple-element.16), channel_id=1, source_target_pairs={{1,2},{2,1},{5,6},{6,5},{9,10},{10,9},{13,14},{14,13},{17,18},{18,... | collective-permute-start | bytes 26120 | tf_op jit(solution)/shard_map/ppermute | solution.py:479
  12.4 0.3 collective-permute-done.near_ref
  12.7 1.2 %local.1 = (f32[2,2176,128]{2,1,0:T(8,128)S(1)}, f32[2,8,128]{2,1,0:T(8,128)S(1)}) custom-call(s32[1]{0:T(128)} %bitcast.odd_ref, s32[1]{0:T(128)} %bitcast.1.side_ref.core_ref, bf16[4352,128]{1,0:T(8,128)(2,1)S(1)} %bitcast.9, bf16[4352,128]{1,0:T(8,128)(2,1)S(1)} %bitcast.11, bf16[128,128]{1,0:T(8,128)(2,1)S(1)} %copy-done.10, ...), custom_call_target="tpu_custom_call" | custom-call | flops 1000000000 | bytes 8000000 | tf_op jit(solution)/shard_map/local/pallas_call | solution.py:158
  13.9 16.0 %collective-permute-done.4.rest_1_ = bf16[704,128]{1,0:T(8,128)(2,1)} collective-permute-done((bf16[704,128]{1,0:T(8,128)(2,1)S(1)}, bf16[704,128]{1,0:T(8,128)(2,1)}, u32[]{:S(2)}, u32[]{:S(2)}) %collective-permute-start.4) | collective-permute-done | bytes 180256 | tf_op jit(solution)/shard_map/ppermute | solution.py:325
  29.9 2.9 %cross_near.1 = (f32[256,128]{1,0:T(8,128)S(1)}, bf16[2048,128]{1,0:T(8,128)(2,1)S(1)}) custom-call(s32[1]{0:T(128)} %bitcast.odd_ref, s32[1]{0:T(128)} %bitcast.1.side_ref.core_ref, s32[16]{0:T(128)S(1)} %copy-done.6, s32[2,64]{1,0:T(2,128)S(1)} %bitcast.12, f32[2,2176,128]{2,1,0:T(8,128)S(1)} %get-tuple-element.17.z_ref, ...), custom_call_target="tpu_custom_call" | custom-call | flops 2000000000 | bytes 4000000 | tf_op jit(solution)/shard_map/cross_near/pallas_call | solution.py:305
  32.8 2.4 %cross_far.1 = (f32[128,128]{1,0:T(8,128)S(1)}, f32[128,128]{1,0:T(8,128)S(1)}, bf16[2048,128]{1,0:T(8,128)(2,1)S(1)}) custom-call(s32[1]{0:T(128)} %bitcast.odd_ref, s32[1]{0:T(128)} %bitcast.1.side_ref.core_ref, s32[16]{0:T(128)S(1)} %copy-done.6, s32[2,64]{1,0:T(2,128)S(1)} %bitcast.13, f32[2,2176,128]{2,1,0:T(8,128)S(1)} %get-tuple-element.17.z_ref, ...), custom_call_target="tpu_custom_call" | custom-call | flops 2000000000 | bytes 4000000 | tf_op jit(solution)/shard_map/cross_far/pallas_call | solution.py:305
  35.3 0.1 collective-permute-start.5
  35.3 1.2 %collective-permute-done.5 = f32[128,128]{1,0:T(8,128)S(1)} collective-permute-done((f32[128,128]{1,0:T(8,128)S(1)}, f32[128,128]{1,0:T(8,128)S(1)}, u32[]{:S(2)}, u32[]{:S(2)}) %collective-permute-start.5) | collective-permute-done | bytes 65568 | tf_op jit(solution)/shard_map/ppermute | solution.py:325
  36.6 2.7 %collective-permute-start.6 = (f32[128,128]{1,0:T(8,128)S(1)}, f32[128,128]{1,0:T(8,128)S(1)}, u32[]{:S(2)}, u32[]{:S(2)}) collective-permute-start(f32[128,128]{1,0:T(8,128)S(1)} %add.24), channel_id=1, source_target_pairs={{0,4},{1,3},{2,6},{3,1},{4,0},{5,7},{6,2},{7,5},{8,12},{9,11},{10,... | collective-permute-start | bytes 196616 | tf_op jit(solution)/shard_map/ppermute | solution.py:336
  39.3 2.2 %collective-permute-done.6 = f32[128,128]{1,0:T(8,128)S(1)} collective-permute-done((f32[128,128]{1,0:T(8,128)S(1)}, f32[128,128]{1,0:T(8,128)S(1)}, u32[]{:S(2)}, u32[]{:S(2)}) %collective-permute-start.6) | collective-permute-done | bytes 65568 | tf_op jit(solution)/shard_map/ppermute | solution.py:336
  41.5 1.6 %collective-permute-start.7 = (f32[128,128]{1,0:T(8,128)S(1)}, f32[128,128]{1,0:T(8,128)S(1)}, u32[]{:S(2)}, u32[]{:S(2)}) collective-permute-start(f32[128,128]{1,0:T(8,128)S(1)} %add.25), channel_id=1, source_target_pairs={{0,2},{1,5},{2,0},{3,7},{4,6},{5,1},{6,4},{7,3},{8,10},{9,13},{10,... | collective-permute-start | bytes 196616 | tf_op jit(solution)/shard_map/ppermute | solution.py:336
  43.1 2.7 %collective-permute-done.7 = f32[128,128]{1,0:T(8,128)S(1)} collective-permute-done((f32[128,128]{1,0:T(8,128)S(1)}, f32[128,128]{1,0:T(8,128)S(1)}, u32[]{:S(2)}, u32[]{:S(2)}) %collective-permute-start.7) | collective-permute-done | bytes 65568 | tf_op jit(solution)/shard_map/ppermute | solution.py:336
  45.9 2.2 %collective-permute-start.8 = (f32[128,128]{1,0:T(8,128)S(1)}, f32[128,128]{1,0:T(8,128)S(1)}, u32[]{:S(2)}, u32[]{:S(2)}) collective-permute-start(f32[128,128]{1,0:T(8,128)S(1)} %add.26), channel_id=1, source_target_pairs={{0,8},{1,17},{2,10},{3,19},{4,12},{5,21},{6,14},{7,23},{8,0},{9,25... | collective-permute-start | bytes 196616 | tf_op jit(solution)/shard_map/ppermute | solution.py:336
  48.0 2.2 %collective-permute-done.8 = f32[128,128]{1,0:T(8,128)S(1)} collective-permute-done((f32[128,128]{1,0:T(8,128)S(1)}, f32[128,128]{1,0:T(8,128)S(1)}, u32[]{:S(2)}, u32[]{:S(2)}) %collective-permute-start.8) | collective-permute-done | bytes 65568 | tf_op jit(solution)/shard_map/ppermute | solution.py:336
  50.3 3.1 %collective-permute-start.9 = (f32[128,128]{1,0:T(8,128)S(1)}, f32[128,128]{1,0:T(8,128)S(1)}, u32[]{:S(2)}, u32[]{:S(2)}) collective-permute-start(f32[128,128]{1,0:T(8,128)S(1)} %add.27), channel_id=1, source_target_pairs={{0,16},{1,9},{2,18},{3,11},{4,20},{5,13},{6,22},{7,15},{8,24},{9,1... | collective-permute-start | bytes 196616 | tf_op jit(solution)/shard_map/ppermute | solution.py:336
  53.4 2.2 %collective-permute-done.9 = f32[128,128]{1,0:T(8,128)S(1)} collective-permute-done((f32[128,128]{1,0:T(8,128)S(1)}, f32[128,128]{1,0:T(8,128)S(1)}, u32[]{:S(2)}, u32[]{:S(2)}) %collective-permute-start.9) | collective-permute-done | bytes 65568 | tf_op jit(solution)/shard_map/ppermute | solution.py:336
  55.6 0.1 collective-permute-start.10
  55.7 1.2 %collective-permute-done.10.other_ref = f32[128,128]{1,0:T(8,128)S(1)} collective-permute-done((f32[128,128]{1,0:T(8,128)S(1)}, f32[128,128]{1,0:T(8,128)S(1)}, u32[]{:S(2)}, u32[]{:S(2)}) %collective-permute-start.10) | collective-permute-done | bytes 65568 | tf_op jit(solution)/shard_map/ppermute | solution.py:325
  57.0 1.8 %modes.1 = (f32[2,64]{1,0:T(2,128)}, f32[256,128]{1,0:T(8,128)}) custom-call(s32[1]{0:T(128)} %bitcast.odd_ref, s32[1]{0:T(128)} %bitcast.1.side_ref.core_ref, f32[128,128]{1,0:T(8,128)S(1)} %add.28.mine_ref, f32[128,128]{1,0:T(8,128)S(1)} %collective-permute-done.10.other_ref, bf16[2048,128]{1,0:T(8,128)(2,1)S(1)} %get-tuple-element.24.near_ref, ...), custom_call_target="tpu_custom_call" | custom-call | tf_op jit(solution)/shard_map/modes/pallas_call | solution.py:438
  (24 shorter events, 0.1 us)
Async XLA Ops:
  0.6 1.3 %copy-start = (bf16[2176,2,128]{2,1,0:T(2,128)(2,1)S(1)}, bf16[2176,2,128]{2,1,0:T(2,128)(2,1)}, u32[]{:S(2)}) copy-start(bf16[2176,2,128]{2,1,0:T(2,128)(2,1)} %param.11) | copy-start | bytes 3342340
  2.9 8.2 %copy-start.2 = (bf16[2176,2,128]{2,1,0:T(2,128)(2,1)S(1)}, bf16[2176,2,128]{2,1,0:T(2,128)(2,1)}, u32[]{:S(2)}) copy-start(bf16[2176,2,128]{2,1,0:T(2,128)(2,1)} %param.10) | copy-start | bytes 3342340
  2.9 8.2 %copy-start.3 = (bf16[8,16,128]{2,1,0:T(8,128)(2,1)S(1)}, bf16[8,16,128]{2,1,0:T(8,128)(2,1)}, u32[]{:S(2)}) copy-start(bf16[8,16,128]{2,1,0:T(8,128)(2,1)} %constant.36.clone.picks_ref) | copy-start | bytes 98308
  2.9 9.9 %copy-start.1 = (bf16[2176,2,128]{2,1,0:T(2,128)(2,1)S(1)}, bf16[2176,2,128]{2,1,0:T(2,128)(2,1)}, u32[]{:S(2)}) copy-start(bf16[2176,2,128]{2,1,0:T(2,128)(2,1)} %param.11) | copy-start | bytes 3342340
  2.9 27.0 %collective-permute-start.3 = (bf16[1472,128]{1,0:T(8,128)(2,1)}, bf16[1472,128]{1,0:T(8,128)(2,1)}, u32[]{:S(2)}, u32[]{:S(2)}) collective-permute-start(bf16[1472,128]{1,0:T(8,128)(2,1)} %get-tuple-element.19), channel_id=1, source_target_pairs={{0,4},{4,0},{8,12},{12,8},{16,20},{20,16},{24,28},{28,24},{1,5},{5... | collective-permute-start | bytes 1130504 | tf_op jit(solution)/shard_map/ppermute | solution.py:325
  6.1 26.8 %collective-permute-start.2 = (bf16[2176,128]{1,0:T(8,128)(2,1)S(1)}, bf16[2176,128]{1,0:T(8,128)(2,1)S(1)}, u32[]{:S(2)}, u32[]{:S(2)}) collective-permute-start(bf16[2176,128]{1,0:T(8,128)(2,1)S(1)} %far.1), channel_id=1, source_target_pairs={{4,8},{12,16},{20,24},{8,4},{16,12},{24,20},{5,9},{13,17},{21,25},... | collective-permute-start | bytes 1671176 | tf_op jit(solution)/shard_map/ppermute | solution.py:482
  6.8 23.1 %collective-permute-start.4 = (bf16[704,128]{1,0:T(8,128)(2,1)S(1)}, bf16[704,128]{1,0:T(8,128)(2,1)}, u32[]{:S(2)}, u32[]{:S(2)}) collective-permute-start(bf16[704,128]{1,0:T(8,128)(2,1)S(1)} %get-tuple-element.20), channel_id=1, source_target_pairs={{0,4},{4,0},{8,12},{12,8},{16,20},{20,16},{24,28},{28,24},{1,5},{5... | collective-permute-start | bytes 540680 | tf_op jit(solution)/shard_map/ppermute | solution.py:325
  11.1 1.7 %copy-start.9 = (bf16[8,16,128]{2,1,0:T(8,128)(2,1)S(1)}, bf16[8,16,128]{2,1,0:T(8,128)(2,1)}, u32[]{:S(2)}) copy-start(bf16[8,16,128]{2,1,0:T(8,128)(2,1)} %constant.38.clone.places_ref) | copy-start | bytes 98308
  11.1 1.7 %copy-start.10 = (bf16[128,128]{1,0:T(8,128)(2,1)S(1)}, bf16[128,128]{1,0:T(8,128)(2,1)}, u32[]{:S(2)}) copy-start(bf16[128,128]{1,0:T(8,128)(2,1)} %constant.37.clone.shift_ref) | copy-start | bytes 98308
  11.5 1.2 %collective-permute-start = (bf16[8,544]{1,0:T(8,128)(2,1)S(1)}, bf16[8,544]{1,0:T(8,128)(2,1)S(1)}, u32[]{:S(2)}, u32[]{:S(2)}) collective-permute-start(bf16[8,544]{1,0:T(8,128)(2,1)S(1)} %get-tuple-element.15), channel_id=1, source_target_pairs={{0,1},{1,0},{2,3},{3,2},{4,5},{5,4},{6,7},{7,6},{8,9},{9,8},{10,11... | collective-permute-start | bytes 26120 | tf_op jit(solution)/shard_map/ppermute | solution.py:325
  11.6 18.3 %copy-start.4 = (s32[64,2]{0,1:T(2,128)S(1)}, s32[64,2]{0,1:T(2,128)}, u32[]{:S(2)}) copy-start(s32[64,2]{0,1:T(2,128)} %param.14) | copy-start | bytes 1540
  11.6 18.3 %copy-start.5 = (f32[2,128]{1,0:T(2,128)S(1)}, f32[2,128]{1,0:T(2,128)}, u32[]{:S(2)}) copy-start(f32[2,128]{1,0:T(2,128)} %weights_ref.3) | copy-start | bytes 3076
  11.6 18.3 %copy-start.6 = (s32[16]{0:T(128)S(1)}, s32[16]{0:T(128)}, u32[]{:S(2)}) copy-start(s32[16]{0:T(128)} %offsets_ref.3) | copy-start | bytes 196
  11.6 18.3 %copy-start.7 = (bf16[256,256]{1,0:T(8,128)(2,1)S(1)}, bf16[256,256]{1,0:T(8,128)(2,1)}, u32[]{:S(2)}) copy-start(bf16[256,256]{1,0:T(8,128)(2,1)} %constant.40.clone.transform_ref) | copy-start | bytes 393220
  11.6 18.3 %copy-start.8 = (f32[256,128]{1,0:T(8,128)S(1)}, f32[256,128]{1,0:T(8,128)}, u32[]{:S(2)}) copy-start(f32[256,128]{1,0:T(8,128)} %constant.39.clone.window_ref) | copy-start | bytes 393220
  11.6 1.1 %collective-permute-start.1 = (bf16[8,544]{1,0:T(8,128)(2,1)S(1)}, bf16[8,544]{1,0:T(8,128)(2,1)S(1)}, u32[]{:S(2)}, u32[]{:S(2)}) collective-permute-start(bf16[8,544]{1,0:T(8,128)(2,1)S(1)} %get-tuple-element.16), channel_id=1, source_target_pairs={{1,2},{2,1},{5,6},{6,5},{9,10},{10,9},{13,14},{14,13},{17,18},{18,... | collective-permute-start | bytes 26120 | tf_op jit(solution)/shard_map/ppermute | solution.py:479
  35.3 1.3 %collective-permute-start.5 = (f32[128,128]{1,0:T(8,128)S(1)}, f32[128,128]{1,0:T(8,128)S(1)}, u32[]{:S(2)}, u32[]{:S(2)}) collective-permute-start(f32[128,128]{1,0:T(8,128)S(1)} %get-tuple-element.23), channel_id=1, source_target_pairs={{0,1},{1,0},{2,3},{3,2},{4,5},{5,4},{6,7},{7,6},{8,9},{9,8},{10,11... | collective-permute-start | bytes 196616 | tf_op jit(solution)/shard_map/ppermute | solution.py:325
  36.6 4.9 %collective-permute-start.6 = (f32[128,128]{1,0:T(8,128)S(1)}, f32[128,128]{1,0:T(8,128)S(1)}, u32[]{:S(2)}, u32[]{:S(2)}) collective-permute-start(f32[128,128]{1,0:T(8,128)S(1)} %add.24), channel_id=1, source_target_pairs={{0,4},{1,3},{2,6},{3,1},{4,0},{5,7},{6,2},{7,5},{8,12},{9,11},{10,... | collective-permute-start | bytes 196616 | tf_op jit(solution)/shard_map/ppermute | solution.py:336
  41.5 4.3 %collective-permute-start.7 = (f32[128,128]{1,0:T(8,128)S(1)}, f32[128,128]{1,0:T(8,128)S(1)}, u32[]{:S(2)}, u32[]{:S(2)}) collective-permute-start(f32[128,128]{1,0:T(8,128)S(1)} %add.25), channel_id=1, source_target_pairs={{0,2},{1,5},{2,0},{3,7},{4,6},{5,1},{6,4},{7,3},{8,10},{9,13},{10,... | collective-permute-start | bytes 196616 | tf_op jit(solution)/shard_map/ppermute | solution.py:336
  45.9 4.4 %collective-permute-start.8 = (f32[128,128]{1,0:T(8,128)S(1)}, f32[128,128]{1,0:T(8,128)S(1)}, u32[]{:S(2)}, u32[]{:S(2)}) collective-permute-start(f32[128,128]{1,0:T(8,128)S(1)} %add.26), channel_id=1, source_target_pairs={{0,8},{1,17},{2,10},{3,19},{4,12},{5,21},{6,14},{7,23},{8,0},{9,25... | collective-permute-start | bytes 196616 | tf_op jit(solution)/shard_map/ppermute | solution.py:336
  50.3 5.3 %collective-permute-start.9 = (f32[128,128]{1,0:T(8,128)S(1)}, f32[128,128]{1,0:T(8,128)S(1)}, u32[]{:S(2)}, u32[]{:S(2)}) collective-permute-start(f32[128,128]{1,0:T(8,128)S(1)} %add.27), channel_id=1, source_target_pairs={{0,16},{1,9},{2,18},{3,11},{4,20},{5,13},{6,22},{7,15},{8,24},{9,1... | collective-permute-start | bytes 196616 | tf_op jit(solution)/shard_map/ppermute | solution.py:336
  55.6 1.3 %collective-permute-start.10 = (f32[128,128]{1,0:T(8,128)S(1)}, f32[128,128]{1,0:T(8,128)S(1)}, u32[]{:S(2)}, u32[]{:S(2)}) collective-permute-start(f32[128,128]{1,0:T(8,128)S(1)} %add.28.mine_ref), channel_id=1, source_target_pairs={{0,1},{1,0},{2,3},{3,2},{4,5},{5,4},{6,7},{7,6},{8,9},{9,8},{10,11... | collective-permute-start | bytes 196616 | tf_op jit(solution)/shard_map/ppermute | solution.py:325

commit v9 on v8

--- a/solution.py
+++ b/solution.py
@@ -233,7 +233,7 @@
     lax.fori_loop(0, blocks // 2, two_blocks, 0, unroll=True)
     weights = [weights_ref[pl.ds(row_at(begin + row, sx, odd), 1), :] for row in range(count)]
 
-    def one_triad(j, carry):
+    def one_triad(j):
         k = triads_ref[0, j]
         l = triads_ref[1, j]
 
@@ -257,9 +257,6 @@
                 axis=0,
             ).astype(BF16)
             target_ref[pl.ds(base, wide), lanes] = jnp.concatenate([target_re, target_im], axis=0).astype(BF16)
-        return carry
-
-    lax.fori_loop(0, ntri, one_triad, 0, unroll=4)
 
     tall = per * wide
     lane = lax.broadcasted_iota(jnp.int32, (wide, tall), 1)
@@ -267,6 +264,8 @@
     is_re = (lax.broadcasted_iota(jnp.int32, (blocks, tall), 1) % wide) < blocks
 
     def one_group(g, carry):
+        for i in range(per):
+            one_triad(g * per + i)
         at = pl.ds(pl.multiple_of(g * tall, 8), tall)
         every = lax.dot_general(
             prod[at, :], target_ref[at, :], (((1,), (1,)), ((), ())), preferred_element_type=F32
@@ -421,17 +420,15 @@
         high = rows.astype(BF16)
         both = jnp.concatenate([high, (rows - high.astype(F32)).astype(BF16)], axis=0)
         at = slice(g * tall, (g + 1) * tall)
+        target = jnp.concatenate([near_ref[at, :], far_ref[at, :]], axis=1)
+        out = jnp.dot(both, target, preferred_element_type=F32)
+        out = out[: 2 * per] + out[2 * per :]
         for position in range(sx):
-            if position + 1 < sx:
-                target = near_ref[at, position * LANES : (position + 1) * LANES]
-            else:
-                target = far_ref[at, :]
-            out = jnp.dot(both, target, preferred_element_type=F32)
-            out = out[: 2 * per] + out[2 * per :]
+            lanes = slice(position * LANES, (position + 1) * LANES)
             row = row_at(position, sx, odd)
             for part in range(2):
                 first = g * per * 2 * sx + part * sx
-                modes_ref[pl.ds(first + row, per, stride=2 * sx), :] = out[part * per : (part + 1) * per]
+                modes_ref[pl.ds(first + row, per, stride=2 * sx), :] = out[part * per : (part + 1) * per, lanes]
 
 
 def modes_part(odd, core, mine, other, near, far, blocks, ntri, sx, scaling):

time: 59 us -> 58.4 us (0.990)
  Pallas kernels: 9.92 us -> 9.32 us
where the time goes in v9:
time: 58.4 us; the launch traced here: 58.2 us
  waiting for transfers between devices  28.2 us (48%)
  starting transfers between devices  18.5 us (32%)
  Pallas kernels  9.32 us (16%)
  local copies, waits for them, and re-layouts  1.29 us (2%)
  between operations  0.82 us (1%)
    ppermute x5, waiting for transfers between devices, swap(): return lax.ppermute(x, axis, [(i, i ^ bit) for i in range(count)])  18.7 us
    ppermute x4, starting transfers between devices, sum_over_rest(): x = x + lax.ppermute(x, ('space', 'freq'), pairs)  9.51 us
    ppermute x4, waiting for transfers between devices, sum_over_rest(): x = x + lax.ppermute(x, ('space', 'freq'), pairs)  9.48 us
    ppermute x5, starting transfers between devices, swap(): return lax.ppermute(x, axis, [(i, i ^ bit) for i in range(count)])  7.48 us
    pallas_call x2, Pallas kernels, cross_part(): pl.pallas_call(functools.partial(cross_kernel, sx, begin, len(halos)), ou...  4.76 us
    pallas_call x1, Pallas kernels, modes_part(): pl.pallas_call(functools.partial(modes_kernel, sx, blocks, scaling), out_...  1.81 us
    unnamed x22, local copies, waits for them, and re-layouts  1.29 us
  transfers between devices with their start and end apart: 11, of which 8 were waited for; matrix products, arithmetic and copies ran while one was open for 0% of the time, Pallas kernels for 8%

profile of v9, /device:TPU:0, one launch (start us, length us, event | category | flops | bytes accessed | tf_op | source)
XLA Modules:
  0.0 58.2 jit_solution(18093552818263385123)
XLA Ops:
  0.6 0.0 copy-start
  0.7 1.2 %copy-done = bf16[2176,2,128]{2,1,0:T(2,128)(2,1)S(1)} copy-done((bf16[2176,2,128]{2,1,0:T(2,128)(2,1)S(1)}, bf16[2176,2,128]{2,1,0:T(2,128)(2,1)}, u32[]{:S(2)}) %copy-start) | copy-done | bytes 1114136
  1.9 1.0 %near.1 = (bf16[1472,128]{1,0:T(8,128)(2,1)}, bf16[704,128]{1,0:T(8,128)(2,1)S(1)}) custom-call(s32[1]{0:T(128)} %bitcast.odd_ref, bf16[4352,128]{1,0:T(8,128)(2,1)S(1)} %bitcast.7), custom_call_target="tpu_custom_call" | custom-call | tf_op jit(solution)/shard_map/near/pallas_call | solution.py:69
  2.9 3.0 %collective-permute-start.3 = (bf16[1472,128]{1,0:T(8,128)(2,1)}, bf16[1472,128]{1,0:T(8,128)(2,1)}, u32[]{:S(2)}, u32[]{:S(2)}) collective-permute-start(bf16[1472,128]{1,0:T(8,128)(2,1)} %get-tuple-element.19), channel_id=1, source_target_pairs={{0,4},{4,0},{8,12},{12,8},{16,20},{20,16},{24,28},{28,24},{1,5},{5... | collective-permute-start | bytes 1130504 | tf_op jit(solution)/shard_map/ppermute | solution.py:324
  5.8 0.2 far.1
  6.1 0.7 %collective-permute-start.2 = (bf16[2176,128]{1,0:T(8,128)(2,1)S(1)}, bf16[2176,128]{1,0:T(8,128)(2,1)S(1)}, u32[]{:S(2)}, u32[]{:S(2)}) collective-permute-start(bf16[2176,128]{1,0:T(8,128)(2,1)S(1)} %far.1), channel_id=1, source_target_pairs={{4,8},{12,16},{20,24},{8,4},{16,12},{24,20},{5,9},{13,17},{21,25},... | collective-permute-start | bytes 1671176 | tf_op jit(solution)/shard_map/ppermute | solution.py:479
  6.8 4.3 %collective-permute-start.4 = (bf16[704,128]{1,0:T(8,128)(2,1)S(1)}, bf16[704,128]{1,0:T(8,128)(2,1)}, u32[]{:S(2)}, u32[]{:S(2)}) collective-permute-start(bf16[704,128]{1,0:T(8,128)(2,1)S(1)} %get-tuple-element.20), channel_id=1, source_target_pairs={{0,4},{4,0},{8,12},{12,8},{16,20},{20,16},{24,28},{28,24},{1,5},{5... | collective-permute-start | bytes 540680 | tf_op jit(solution)/shard_map/ppermute | solution.py:324
  11.1 0.4 columns.1
  11.5 0.1 collective-permute-start
  11.6 0.0 copy-start.5
  11.6 0.0 copy-start.6
  11.6 0.0 copy-start.7
  11.6 0.0 copy-start.8
  11.6 0.8 %collective-permute-start.1 = (bf16[8,544]{1,0:T(8,128)(2,1)S(1)}, bf16[8,544]{1,0:T(8,128)(2,1)S(1)}, u32[]{:S(2)}, u32[]{:S(2)}) collective-permute-start(bf16[8,544]{1,0:T(8,128)(2,1)S(1)} %get-tuple-element.16), channel_id=1, source_target_pairs={{1,2},{2,1},{5,6},{6,5},{9,10},{10,9},{13,14},{14,13},{17,18},{18,... | collective-permute-start | bytes 26120 | tf_op jit(solution)/shard_map/ppermute | solution.py:476
  12.4 0.3 collective-permute-done.near_ref
  12.7 1.2 %local.1 = (f32[2,2176,128]{2,1,0:T(8,128)S(1)}, f32[2,8,128]{2,1,0:T(8,128)S(1)}) custom-call(s32[1]{0:T(128)} %bitcast.odd_ref, s32[1]{0:T(128)} %bitcast.1.side_ref.core_ref, bf16[4352,128]{1,0:T(8,128)(2,1)S(1)} %bitcast.9, bf16[4352,128]{1,0:T(8,128)(2,1)S(1)} %bitcast.11, bf16[128,128]{1,0:T(8,128)(2,1)S(1)} %copy-done.10, ...), custom_call_target="tpu_custom_call" | custom-call | flops 1000000000 | bytes 8000000 | tf_op jit(solution)/shard_map/local/pallas_call | solution.py:158
  13.9 16.0 %collective-permute-done.4.rest_1_ = bf16[704,128]{1,0:T(8,128)(2,1)} collective-permute-done((bf16[704,128]{1,0:T(8,128)(2,1)S(1)}, bf16[704,128]{1,0:T(8,128)(2,1)}, u32[]{:S(2)}, u32[]{:S(2)}) %collective-permute-start.4) | collective-permute-done | bytes 180256 | tf_op jit(solution)/shard_map/ppermute | solution.py:324
  29.9 2.6 %cross_near.1 = (f32[256,128]{1,0:T(8,128)S(1)}, bf16[2048,128]{1,0:T(8,128)(2,1)S(1)}) custom-call(s32[1]{0:T(128)} %bitcast.odd_ref, s32[1]{0:T(128)} %bitcast.1.side_ref.core_ref, s32[16]{0:T(128)S(1)} %copy-done.6, s32[2,64]{1,0:T(2,128)S(1)} %bitcast.12, f32[2,2176,128]{2,1,0:T(8,128)S(1)} %get-tuple-element.17.z_ref, ...), custom_call_target="tpu_custom_call" | custom-call | flops 2000000000 | bytes 4000000 | tf_op jit(solution)/shard_map/cross_near/pallas_call | solution.py:304
  32.5 2.1 %cross_far.1 = (f32[128,128]{1,0:T(8,128)S(1)}, f32[128,128]{1,0:T(8,128)S(1)}, bf16[2048,128]{1,0:T(8,128)(2,1)S(1)}) custom-call(s32[1]{0:T(128)} %bitcast.odd_ref, s32[1]{0:T(128)} %bitcast.1.side_ref.core_ref, s32[16]{0:T(128)S(1)} %copy-done.6, s32[2,64]{1,0:T(2,128)S(1)} %bitcast.13, f32[2,2176,128]{2,1,0:T(8,128)S(1)} %get-tuple-element.17.z_ref, ...), custom_call_target="tpu_custom_call" | custom-call | flops 2000000000 | bytes 4000000 | tf_op jit(solution)/shard_map/cross_far/pallas_call | solution.py:304
  34.7 0.1 collective-permute-start.5
  34.8 1.2 %collective-permute-done.5 = f32[128,128]{1,0:T(8,128)S(1)} collective-permute-done((f32[128,128]{1,0:T(8,128)S(1)}, f32[128,128]{1,0:T(8,128)S(1)}, u32[]{:S(2)}, u32[]{:S(2)}) %collective-permute-start.5) | collective-permute-done | bytes 65568 | tf_op jit(solution)/shard_map/ppermute | solution.py:324
  36.0 2.7 %collective-permute-start.6 = (f32[128,128]{1,0:T(8,128)S(1)}, f32[128,128]{1,0:T(8,128)S(1)}, u32[]{:S(2)}, u32[]{:S(2)}) collective-permute-start(f32[128,128]{1,0:T(8,128)S(1)} %add.24), channel_id=1, source_target_pairs={{0,4},{1,3},{2,6},{3,1},{4,0},{5,7},{6,2},{7,5},{8,12},{9,11},{10,... | collective-permute-start | bytes 196616 | tf_op jit(solution)/shard_map/ppermute | solution.py:335
  38.7 2.2 %collective-permute-done.6 = f32[128,128]{1,0:T(8,128)S(1)} collective-permute-done((f32[128,128]{1,0:T(8,128)S(1)}, f32[128,128]{1,0:T(8,128)S(1)}, u32[]{:S(2)}, u32[]{:S(2)}) %collective-permute-start.6) | collective-permute-done | bytes 65568 | tf_op jit(solution)/shard_map/ppermute | solution.py:335
  40.9 1.6 %collective-permute-start.7 = (f32[128,128]{1,0:T(8,128)S(1)}, f32[128,128]{1,0:T(8,128)S(1)}, u32[]{:S(2)}, u32[]{:S(2)}) collective-permute-start(f32[128,128]{1,0:T(8,128)S(1)} %add.25), channel_id=1, source_target_pairs={{0,2},{1,5},{2,0},{3,7},{4,6},{5,1},{6,4},{7,3},{8,10},{9,13},{10,... | collective-permute-start | bytes 196616 | tf_op jit(solution)/shard_map/ppermute | solution.py:335
  42.5 2.7 %collective-permute-done.7 = f32[128,128]{1,0:T(8,128)S(1)} collective-permute-done((f32[128,128]{1,0:T(8,128)S(1)}, f32[128,128]{1,0:T(8,128)S(1)}, u32[]{:S(2)}, u32[]{:S(2)}) %collective-permute-start.7) | collective-permute-done | bytes 65568 | tf_op jit(solution)/shard_map/ppermute | solution.py:335
  45.3 2.2 %collective-permute-start.8 = (f32[128,128]{1,0:T(8,128)S(1)}, f32[128,128]{1,0:T(8,128)S(1)}, u32[]{:S(2)}, u32[]{:S(2)}) collective-permute-start(f32[128,128]{1,0:T(8,128)S(1)} %add.26), channel_id=1, source_target_pairs={{0,8},{1,17},{2,10},{3,19},{4,12},{5,21},{6,14},{7,23},{8,0},{9,25... | collective-permute-start | bytes 196616 | tf_op jit(solution)/shard_map/ppermute | solution.py:335
  47.5 2.2 %collective-permute-done.8 = f32[128,128]{1,0:T(8,128)S(1)} collective-permute-done((f32[128,128]{1,0:T(8,128)S(1)}, f32[128,128]{1,0:T(8,128)S(1)}, u32[]{:S(2)}, u32[]{:S(2)}) %collective-permute-start.8) | collective-permute-done | bytes 65568 | tf_op jit(solution)/shard_map/ppermute | solution.py:335
  49.7 3.1 %collective-permute-start.9 = (f32[128,128]{1,0:T(8,128)S(1)}, f32[128,128]{1,0:T(8,128)S(1)}, u32[]{:S(2)}, u32[]{:S(2)}) collective-permute-start(f32[128,128]{1,0:T(8,128)S(1)} %add.27), channel_id=1, source_target_pairs={{0,16},{1,9},{2,18},{3,11},{4,20},{5,13},{6,22},{7,15},{8,24},{9,1... | collective-permute-start | bytes 196616 | tf_op jit(solution)/shard_map/ppermute | solution.py:335
  52.8 2.2 %collective-permute-done.9 = f32[128,128]{1,0:T(8,128)S(1)} collective-permute-done((f32[128,128]{1,0:T(8,128)S(1)}, f32[128,128]{1,0:T(8,128)S(1)}, u32[]{:S(2)}, u32[]{:S(2)}) %collective-permute-start.9) | collective-permute-done | bytes 65568 | tf_op jit(solution)/shard_map/ppermute | solution.py:335
  55.1 0.1 collective-permute-start.10
  55.1 1.2 %collective-permute-done.10.other_ref = f32[128,128]{1,0:T(8,128)S(1)} collective-permute-done((f32[128,128]{1,0:T(8,128)S(1)}, f32[128,128]{1,0:T(8,128)S(1)}, u32[]{:S(2)}, u32[]{:S(2)}) %collective-permute-start.10) | collective-permute-done | bytes 65568 | tf_op jit(solution)/shard_map/ppermute | solution.py:324
  56.4 1.8 %modes.1 = (f32[2,64]{1,0:T(2,128)}, f32[256,128]{1,0:T(8,128)}) custom-call(s32[1]{0:T(128)} %bitcast.odd_ref, s32[1]{0:T(128)} %bitcast.1.side_ref.core_ref, f32[128,128]{1,0:T(8,128)S(1)} %add.28.mine_ref, f32[128,128]{1,0:T(8,128)S(1)} %collective-permute-done.10.other_ref, bf16[2048,128]{1,0:T(8,128)(2,1)S(1)} %get-tuple-element.24.near_ref, ...), custom_call_target="tpu_custom_call" | custom-call | tf_op jit(solution)/shard_map/modes/pallas_call | solution.py:435
  (24 shorter events, 0.1 us)
Async XLA Ops:
  0.6 1.3 %copy-start = (bf16[2176,2,128]{2,1,0:T(2,128)(2,1)S(1)}, bf16[2176,2,128]{2,1,0:T(2,128)(2,1)}, u32[]{:S(2)}) copy-start(bf16[2176,2,128]{2,1,0:T(2,128)(2,1)} %param.11) | copy-start | bytes 3342340
  2.9 8.2 %copy-start.2 = (bf16[2176,2,128]{2,1,0:T(2,128)(2,1)S(1)}, bf16[2176,2,128]{2,1,0:T(2,128)(2,1)}, u32[]{:S(2)}) copy-start(bf16[2176,2,128]{2,1,0:T(2,128)(2,1)} %param.10) | copy-start | bytes 3342340
  2.9 8.2 %copy-start.3 = (bf16[8,16,128]{2,1,0:T(8,128)(2,1)S(1)}, bf16[8,16,128]{2,1,0:T(8,128)(2,1)}, u32[]{:S(2)}) copy-start(bf16[8,16,128]{2,1,0:T(8,128)(2,1)} %constant.36.clone.picks_ref) | copy-start | bytes 98308
  2.9 9.9 %copy-start.1 = (bf16[2176,2,128]{2,1,0:T(2,128)(2,1)S(1)}, bf16[2176,2,128]{2,1,0:T(2,128)(2,1)}, u32[]{:S(2)}) copy-start(bf16[2176,2,128]{2,1,0:T(2,128)(2,1)} %param.11) | copy-start | bytes 3342340
  2.9 27.0 %collective-permute-start.3 = (bf16[1472,128]{1,0:T(8,128)(2,1)}, bf16[1472,128]{1,0:T(8,128)(2,1)}, u32[]{:S(2)}, u32[]{:S(2)}) collective-permute-start(bf16[1472,128]{1,0:T(8,128)(2,1)} %get-tuple-element.19), channel_id=1, source_target_pairs={{0,4},{4,0},{8,12},{12,8},{16,20},{20,16},{24,28},{28,24},{1,5},{5... | collective-permute-start | bytes 1130504 | tf_op jit(solution)/shard_map/ppermute | solution.py:324
  6.1 26.5 %collective-permute-start.2 = (bf16[2176,128]{1,0:T(8,128)(2,1)S(1)}, bf16[2176,128]{1,0:T(8,128)(2,1)S(1)}, u32[]{:S(2)}, u32[]{:S(2)}) collective-permute-start(bf16[2176,128]{1,0:T(8,128)(2,1)S(1)} %far.1), channel_id=1, source_target_pairs={{4,8},{12,16},{20,24},{8,4},{16,12},{24,20},{5,9},{13,17},{21,25},... | collective-permute-start | bytes 1671176 | tf_op jit(solution)/shard_map/ppermute | solution.py:479
  6.8 23.1 %collective-permute-start.4 = (bf16[704,128]{1,0:T(8,128)(2,1)S(1)}, bf16[704,128]{1,0:T(8,128)(2,1)}, u32[]{:S(2)}, u32[]{:S(2)}) collective-permute-start(bf16[704,128]{1,0:T(8,128)(2,1)S(1)} %get-tuple-element.20), channel_id=1, source_target_pairs={{0,4},{4,0},{8,12},{12,8},{16,20},{20,16},{24,28},{28,24},{1,5},{5... | collective-permute-start | bytes 540680 | tf_op jit(solution)/shard_map/ppermute | solution.py:324
  11.1 1.7 %copy-start.9 = (bf16[8,16,128]{2,1,0:T(8,128)(2,1)S(1)}, bf16[8,16,128]{2,1,0:T(8,128)(2,1)}, u32[]{:S(2)}) copy-start(bf16[8,16,128]{2,1,0:T(8,128)(2,1)} %constant.38.clone.places_ref) | copy-start | bytes 98308
  11.1 1.7 %copy-start.10 = (bf16[128,128]{1,0:T(8,128)(2,1)S(1)}, bf16[128,128]{1,0:T(8,128)(2,1)}, u32[]{:S(2)}) copy-start(bf16[128,128]{1,0:T(8,128)(2,1)} %constant.37.clone.shift_ref) | copy-start | bytes 98308
  11.5 1.2 %collective-permute-start = (bf16[8,544]{1,0:T(8,128)(2,1)S(1)}, bf16[8,544]{1,0:T(8,128)(2,1)S(1)}, u32[]{:S(2)}, u32[]{:S(2)}) collective-permute-start(bf16[8,544]{1,0:T(8,128)(2,1)S(1)} %get-tuple-element.15), channel_id=1, source_target_pairs={{0,1},{1,0},{2,3},{3,2},{4,5},{5,4},{6,7},{7,6},{8,9},{9,8},{10,11... | collective-permute-start | bytes 26120 | tf_op jit(solution)/shard_map/ppermute | solution.py:324
  11.6 18.3 %copy-start.4 = (s32[64,2]{0,1:T(2,128)S(1)}, s32[64,2]{0,1:T(2,128)}, u32[]{:S(2)}) copy-start(s32[64,2]{0,1:T(2,128)} %param.14) | copy-start | bytes 1540
  11.6 18.3 %copy-start.5 = (f32[2,128]{1,0:T(2,128)S(1)}, f32[2,128]{1,0:T(2,128)}, u32[]{:S(2)}) copy-start(f32[2,128]{1,0:T(2,128)} %weights_ref.3) | copy-start | bytes 3076
  11.6 18.3 %copy-start.6 = (s32[16]{0:T(128)S(1)}, s32[16]{0:T(128)}, u32[]{:S(2)}) copy-start(s32[16]{0:T(128)} %offsets_ref.3) | copy-start | bytes 196
  11.6 18.3 %copy-start.7 = (bf16[256,256]{1,0:T(8,128)(2,1)S(1)}, bf16[256,256]{1,0:T(8,128)(2,1)}, u32[]{:S(2)}) copy-start(bf16[256,256]{1,0:T(8,128)(2,1)} %constant.40.clone.transform_ref) | copy-start | bytes 393220
  11.6 18.3 %copy-start.8 = (f32[256,128]{1,0:T(8,128)S(1)}, f32[256,128]{1,0:T(8,128)}, u32[]{:S(2)}) copy-start(f32[256,128]{1,0:T(8,128)} %constant.39.clone.window_ref) | copy-start | bytes 393220
  11.6 1.1 %collective-permute-start.1 = (bf16[8,544]{1,0:T(8,128)(2,1)S(1)}, bf16[8,544]{1,0:T(8,128)(2,1)S(1)}, u32[]{:S(2)}, u32[]{:S(2)}) collective-permute-start(bf16[8,544]{1,0:T(8,128)(2,1)S(1)} %get-tuple-element.16), channel_id=1, source_target_pairs={{1,2},{2,1},{5,6},{6,5},{9,10},{10,9},{13,14},{14,13},{17,18},{18,... | collective-permute-start | bytes 26120 | tf_op jit(solution)/shard_map/ppermute | solution.py:476
  34.7 1.3 %collective-permute-start.5 = (f32[128,128]{1,0:T(8,128)S(1)}, f32[128,128]{1,0:T(8,128)S(1)}, u32[]{:S(2)}, u32[]{:S(2)}) collective-permute-start(f32[128,128]{1,0:T(8,128)S(1)} %get-tuple-element.23), channel_id=1, source_target_pairs={{0,1},{1,0},{2,3},{3,2},{4,5},{5,4},{6,7},{7,6},{8,9},{9,8},{10,11... | collective-permute-start | bytes 196616 | tf_op jit(solution)/shard_map/ppermute | solution.py:324
  36.0 4.9 %collective-permute-start.6 = (f32[128,128]{1,0:T(8,128)S(1)}, f32[128,128]{1,0:T(8,128)S(1)}, u32[]{:S(2)}, u32[]{:S(2)}) collective-permute-start(f32[128,128]{1,0:T(8,128)S(1)} %add.24), channel_id=1, source_target_pairs={{0,4},{1,3},{2,6},{3,1},{4,0},{5,7},{6,2},{7,5},{8,12},{9,11},{10,... | collective-permute-start | bytes 196616 | tf_op jit(solution)/shard_map/ppermute | solution.py:335
  40.9 4.3 %collective-permute-start.7 = (f32[128,128]{1,0:T(8,128)S(1)}, f32[128,128]{1,0:T(8,128)S(1)}, u32[]{:S(2)}, u32[]{:S(2)}) collective-permute-start(f32[128,128]{1,0:T(8,128)S(1)} %add.25), channel_id=1, source_target_pairs={{0,2},{1,5},{2,0},{3,7},{4,6},{5,1},{6,4},{7,3},{8,10},{9,13},{10,... | collective-permute-start | bytes 196616 | tf_op jit(solution)/shard_map/ppermute | solution.py:335
  45.3 4.4 %collective-permute-start.8 = (f32[128,128]{1,0:T(8,128)S(1)}, f32[128,128]{1,0:T(8,128)S(1)}, u32[]{:S(2)}, u32[]{:S(2)}) collective-permute-start(f32[128,128]{1,0:T(8,128)S(1)} %add.26), channel_id=1, source_target_pairs={{0,8},{1,17},{2,10},{3,19},{4,12},{5,21},{6,14},{7,23},{8,0},{9,25... | collective-permute-start | bytes 196616 | tf_op jit(solution)/shard_map/ppermute | solution.py:335
  49.7 5.3 %collective-permute-start.9 = (f32[128,128]{1,0:T(8,128)S(1)}, f32[128,128]{1,0:T(8,128)S(1)}, u32[]{:S(2)}, u32[]{:S(2)}) collective-permute-start(f32[128,128]{1,0:T(8,128)S(1)} %add.27), channel_id=1, source_target_pairs={{0,16},{1,9},{2,18},{3,11},{4,20},{5,13},{6,22},{7,15},{8,24},{9,1... | collective-permute-start | bytes 196616 | tf_op jit(solution)/shard_map/ppermute | solution.py:335
  55.1 1.3 %collective-permute-start.10 = (f32[128,128]{1,0:T(8,128)S(1)}, f32[128,128]{1,0:T(8,128)S(1)}, u32[]{:S(2)}, u32[]{:S(2)}) collective-permute-start(f32[128,128]{1,0:T(8,128)S(1)} %add.28.mine_ref), channel_id=1, source_target_pairs={{0,1},{1,0},{2,3},{3,2},{4,5},{5,4},{6,7},{7,6},{8,9},{9,8},{10,11... | collective-permute-start | bytes 196616 | tf_op jit(solution)/shard_map/ppermute | solution.py:324

commit v10 on v9

--- a/solution.py
+++ b/solution.py
@@ -13,7 +13,7 @@
 NFFT = 256
 POW = 4
 LANES = 128
-AHEAD = 11
+PIECES = 4
 F32 = jnp.float32
 BF16 = jnp.bfloat16
 MIB = 2**20
@@ -55,47 +55,75 @@
     return pltpu.CompilerParams(vmem_limit_bytes=mib * MIB)
 
 
-def near_kernel(sx, odd_ref, v_ref, early_ref, late_ref, plain):
+def near_kernel(sx, odd_ref, v_ref, near_ref, plain):
     plain[...] = v_ref[...].astype(F32)
-    row = row_at(0, sx, odd_ref[0])
-    early, late = early_ref.shape[0], late_ref.shape[0]
-    early_ref[...] = plain[pl.ds(row, early, stride=sx), :].astype(BF16)
-    late_ref[...] = plain[pl.ds(early * sx + row, late, stride=sx), :].astype(BF16)
+    near_ref[...] = plain[pl.ds(row_at(0, sx, odd_ref[0]), near_ref.shape[0], stride=sx), :].astype(BF16)
 
 
 def near_edge(odd, v, sx):
     rows = v.shape[0]
-    early = rows // sx * AHEAD // 1024 * 64
     return pl.pallas_call(
         functools.partial(near_kernel, sx),
+        out_shape=jax.ShapeDtypeStruct((rows // sx, LANES), BF16),
+        in_specs=[SMEM, VMEM],
+        out_specs=VMEM,
+        scratch_shapes=[pltpu.VMEM((rows, LANES), F32)],
+        compiler_params=limit(8),
+        name="near",
+    )(odd, v)
+
+
+def far_kernel(sx, odd_ref, v_ref, moved_ref, direct_ref, plain):
+    plain[...] = v_ref[...].astype(F32)
+    row = row_at(sx - 1, sx, odd_ref[0])
+    moved, direct = moved_ref.shape[0], direct_ref.shape[0]
+    moved_ref[...] = plain[pl.ds(row, moved, stride=sx), :].astype(BF16)
+    direct_ref[...] = plain[pl.ds(moved * sx + row, direct, stride=sx), :].astype(BF16)
+
+
+def far_edge(odd, v, sx):
+    rows = v.shape[0]
+    piece = rows // sx // PIECES
+    return pl.pallas_call(
+        functools.partial(far_kernel, sx),
         out_shape=(
-            jax.ShapeDtypeStruct((early, LANES), BF16),
-            jax.ShapeDtypeStruct((rows // sx - early, LANES), BF16),
+            jax.ShapeDtypeStruct((piece * (PIECES - 1), LANES), BF16),
+            jax.ShapeDtypeStruct((piece, LANES), BF16),
         ),
         in_specs=[SMEM, VMEM],
         out_specs=(VMEM,) * 2,
         scratch_shapes=[pltpu.VMEM((rows, LANES), F32)],
         compiler_params=limit(8),
-        name="near",
-    )(odd, v)
-
-
-def far_kernel(sx, odd_ref, v_ref, far_ref, plain):
-    plain[...] = v_ref[...].astype(F32)
-    far_ref[...] = plain[pl.ds(row_at(sx - 1, sx, odd_ref[0]), far_ref.shape[0], stride=sx), :].astype(BF16)
-
-
-def far_edge(odd, v, sx):
-    rows = v.shape[0]
-    return pl.pallas_call(
-        functools.partial(far_kernel, sx),
-        out_shape=jax.ShapeDtypeStruct((rows // sx, LANES), BF16),
-        in_specs=[SMEM, VMEM],
-        out_specs=VMEM,
-        scratch_shapes=[pltpu.VMEM((rows, LANES), F32)],
-        compiler_params=limit(8),
         name="far",
     )(odd, v)
+
+
+def choose_kernel(starts, place_ref, own_ref, passed_ref, *out_refs):
+    for k, out_ref in enumerate(out_refs):
+        piece = out_ref.shape[0]
+        at = slice(k * piece, (k + 1) * piece)
+        relays = place_ref[0] > starts[k]
+
+        @pl.when(relays)
+        def _():
+            out_ref[...] = passed_ref[at, :]
+
+        @pl.when(jnp.logical_not(relays))
+        def _():
+            out_ref[...] = own_ref[at, :]
+
+
+def choose(place, own, passed, starts):
+    count = len(starts)
+    piece = own.shape[0] // count
+    return pl.pallas_call(
+        functools.partial(choose_kernel, starts),
+        out_shape=(jax.ShapeDtypeStruct((piece, LANES), BF16),) * count,
+        in_specs=[SMEM] + [VMEM] * 2,
+        out_specs=(VMEM,) * count,
+        compiler_params=limit(8),
+        name="choose",
+    )(place, own, passed)
 
 
 def columns_kernel(pieces, side_ref, u_ref, picks_ref, near_ref, far_ref):
@@ -451,6 +479,26 @@
     return inner + [(b, a) for a, b in inner]
 
 
+def start_of(k, pairs):
+    return k * pairs // PIECES
+
+
+def along_side(pairs):
+    hops = [(2 * b + 1, 2 * b + 3) for b in range(pairs - 1)]
+    return hops + [(2 * b + 2, 2 * b) for b in range(pairs - 1)]
+
+
+def across(k, pairs):
+    hops = []
+    last = pairs - 1
+    for b in range(last):
+        if b < start_of(k, pairs):
+            hops += [(2 * b + 1, 2 * b + 2), (2 * (last - b), 2 * (last - b) - 1)]
+        else:
+            hops += [(2 * b + 3, 2 * b + 2), (2 * (last - b) - 2, 2 * (last - b) - 1)]
+    return hops
+
+
 def on_device(u_velocity, v_velocity, cell_weights, block_offsets, triads):
     times, sx, columns = u_velocity.shape
     blocks = block_offsets.shape[0]
@@ -468,22 +516,28 @@
     core = (lax.axis_index("freq") % 2)[None]
     pairs = triads.T
 
-    early, late = near_edge(odd, v, sx)
-    early = swap(early, "space", 1)
-    late = swap(late, "space", 1)
+    near = near_edge(odd, v, sx)
+    near = swap(near, "space", 1)
+    moved, direct = far_edge(odd, v, sx)
+    passed = lax.ppermute(moved, "space", along_side(slabs // 2))
     col_near, col_far = columns_edge(core, u, jnp.asarray(picks, BF16))
     col_near = swap(col_near, "freq", 1)
     col_far = lax.ppermute(col_far, "freq", between_pairs(lax.axis_size("freq")))
     z, sums = local_part(odd, core, v, u, jnp.asarray(shift, BF16), col_near, col_far, jnp.asarray(places, BF16), sx)
-    far = far_edge(odd, v, sx)
-    far = lax.ppermute(far, "space", between_pairs(slabs))
+    count = slabs // 2
+    index = lax.axis_index("space") // 2
+    place = jnp.where(odd == 1, index, count - 1 - index)
+    far = choose(place, moved, passed, [start_of(k, count) for k in range(PIECES - 1)])
+    far = [*far, direct]
+    for k in reversed(range(PIECES)):
+        far[k] = lax.ppermute(far[k], "space", across(k, count))
     window = jnp.asarray(np.ascontiguousarray(np.broadcast_to(window[:, None], (NFFT, LANES))))
     transform = jnp.asarray(transform, BF16)
     share, near_target = cross_part(
-        0, sx - 1, odd, core, block_offsets, pairs, z, sums, [early, late], cell_weights, window, transform
+        0, sx - 1, odd, core, block_offsets, pairs, z, sums, [near], cell_weights, window, transform
     )
     mine, other, far_target = cross_part(
-        sx - 1, 1, odd, core, block_offsets, pairs, z, sums, [far], cell_weights, window, transform, share
+        sx - 1, 1, odd, core, block_offsets, pairs, z, sums, far, cell_weights, window, transform, share
     )
     mine = mine + swap(other, "freq", 1)
     mine = sum_over_rest(mine)

time: 58.4 us -> 59.1 us (1.012)
  waiting for transfers between devices: 28.2 us -> 19.7 us
  starting transfers between devices: 18.5 us -> 25.4 us
  local copies, waits for them, and re-layouts: 1.29 us -> 2.88 us
    ppermute x5 -> x4, waiting for transfers between devices: 18.7 us -> 2.49 us  [swap(): return lax.ppermute(x, axis, [(i, i ^ bit) for i in range(count)])]
    ppermute x1 -> x5, starting transfers between devices: 0.7 us -> 12.2 us  [the longest x4 10.9 us: on_device(): far[k] = lax.ppermute(far[k], 'space', across(k, count))]
    ppermute x1 -> x5, waiting for transfers between devices: 0.01 us -> 7.35 us  [the longest x1 7.34 us: on_device(): passed = lax.ppermute(moved, 'space', along_side(slabs // 2))]
    ppermute x5 -> x4, starting transfers between devices: 7.48 us -> 3.23 us  [swap(): return lax.ppermute(x, axis, [(i, i ^ bit) for i in range(count)])]
    unnamed x22, local copies, waits for them, and re-layouts: 1.29 us -> 2.88 us
    pallas_call x2 -> x3, Pallas kernels: 1.19 us -> 1.5 us  [the longest x1 1.05 us: choose(): pl.pallas_call(functools.partial(choose_kernel, starts), out_shape=(jax.S...]
  transfers between devices with their start and end apart: 11 -> 14, of which waited for: 8 -> 7; matrix products, arithmetic and copies ran while one was open for 0% -> 0% of each run, Pallas kernels for 8% -> 9%
where the time goes in v10:
time: 59.1 us; the launch traced here: 58.7 us
  starting transfers between devices  25.4 us (43%)
  waiting for transfers between devices  19.7 us (33%)
  Pallas kernels  9.65 us (16%)
  local copies, waits for them, and re-layouts  2.88 us (5%)
  between operations  0.98 us (2%)
    ppermute x4, starting transfers between devices, on_device(): far[k] = lax.ppermute(far[k], 'space', across(k, count))  10.9 us
    ppermute x4, waiting for transfers between devices, sum_over_rest(): x = x + lax.ppermute(x, ('space', 'freq'), pairs)  9.9 us
    ppermute x4, starting transfers between devices, sum_over_rest(): x = x + lax.ppermute(x, ('space', 'freq'), pairs)  9.33 us
    ppermute x1, waiting for transfers between devices, on_device(): passed = lax.ppermute(moved, 'space', along_side(slabs // 2))  7.34 us
    pallas_call x2, Pallas kernels, cross_part(): pl.pallas_call(functools.partial(cross_kernel, sx, begin, len(halos)), ou...  4.79 us
    ppermute x4, starting transfers between devices, swap(): return lax.ppermute(x, axis, [(i, i ^ bit) for i in range(count)])  3.23 us
    unnamed x22, local copies, waits for them, and re-layouts  2.88 us
    ppermute x4, waiting for transfers between devices, swap(): return lax.ppermute(x, axis, [(i, i ^ bit) for i in range(count)])  2.49 us
  transfers between devices with their start and end apart: 14, of which 7 were waited for; matrix products, arithmetic and copies ran while one was open for 0% of the time, Pallas kernels for 9%

profile of v10, /device:TPU:0, one launch (start us, length us, event | category | flops | bytes accessed | tf_op | source)
XLA Modules:
  0.0 58.7 jit_solution(4866723484820552663)
XLA Ops:
  0.7 1.2 %copy-done = bf16[2176,2,128]{2,1,0:T(2,128)(2,1)S(1)} copy-done((bf16[2176,2,128]{2,1,0:T(2,128)(2,1)S(1)}, bf16[2176,2,128]{2,1,0:T(2,128)(2,1)}, u32[]{:S(2)}) %copy-start) | copy-done | bytes 1114136
  1.9 0.2 near.1
  2.1 3.0 %collective-permute-start.7 = (bf16[2176,128]{1,0:T(8,128)(2,1)S(1)}, bf16[2176,128]{1,0:T(8,128)(2,1)}, u32[]{:S(2)}, u32[]{:S(2)}) collective-permute-start(bf16[2176,128]{1,0:T(8,128)(2,1)S(1)} %near.1), channel_id=1, source_target_pairs={{0,4},{4,0},{8,12},{12,8},{16,20},{20,16},{24,28},{28,24},{1,5},{5... | collective-permute-start | bytes 1671176 | tf_op jit(solution)/shard_map/ppermute | solution.py:352
  5.2 0.2 far.1
  5.4 1.3 %collective-permute-start.2 = (bf16[1632,128]{1,0:T(8,128)(2,1)S(1)}, bf16[1632,128]{1,0:T(8,128)(2,1)}, u32[]{:S(2)}, u32[]{:S(2)}) collective-permute-start(bf16[1632,128]{1,0:T(8,128)(2,1)S(1)} %get-tuple-element.22.own_ref), channel_id=1, source_target_pairs={{4,12},{12,20},{20,28},{8,0},{16,8},{24,16},{5,13},{13,21},{21,29}... | collective-permute-start | bytes 1253384 | tf_op jit(solution)/shard_map/ppermute | solution.py:522
  6.7 0.4 columns.1
  7.1 0.1 collective-permute-start
  7.2 0.7 %collective-permute-start.1 = (bf16[8,544]{1,0:T(8,128)(2,1)S(1)}, bf16[8,544]{1,0:T(8,128)(2,1)S(1)}, u32[]{:S(2)}, u32[]{:S(2)}) collective-permute-start(bf16[8,544]{1,0:T(8,128)(2,1)S(1)} %get-tuple-element.19), channel_id=1, source_target_pairs={{1,2},{2,1},{5,6},{6,5},{9,10},{10,9},{13,14},{14,13},{17,18},{18,... | collective-permute-start | bytes 26120 | tf_op jit(solution)/shard_map/ppermute | solution.py:525
  7.9 0.7 %collective-permute-start.6 = (bf16[544,128]{1,0:T(8,128)(2,1)S(1)}, bf16[544,128]{1,0:T(8,128)(2,1)S(1)}, u32[]{:S(2)}, u32[]{:S(2)}) collective-permute-start(bf16[544,128]{1,0:T(8,128)(2,1)S(1)} %get-tuple-element.26), channel_id=1, source_target_pairs={{4,8},{24,20},{12,16},{16,12},{20,24},{8,4},{5,9},{25,21},{13,17},... | collective-permute-start | bytes 417800 | tf_op jit(solution)/shard_map/ppermute | solution.py:533
  8.7 0.8 %copy-done.9 = bf16[8,16,128]{2,1,0:T(8,128)(2,1)S(1)} copy-done((bf16[8,16,128]{2,1,0:T(8,128)(2,1)S(1)}, bf16[8,16,128]{2,1,0:T(8,128)(2,1)}, u32[]{:S(2)}) %copy-start.9) | copy-done | bytes 32792
  9.5 0.8 %copy-done.10 = bf16[128,128]{1,0:T(8,128)(2,1)S(1)} copy-done((bf16[128,128]{1,0:T(8,128)(2,1)S(1)}, bf16[128,128]{1,0:T(8,128)(2,1)}, u32[]{:S(2)}) %copy-start.10) | copy-done | bytes 32792
  10.3 1.1 %local.1 = (f32[2,2176,128]{2,1,0:T(8,128)S(1)}, f32[2,8,128]{2,1,0:T(8,128)S(1)}) custom-call(s32[1]{0:T(128)} %bitcast.odd_ref, s32[1]{0:T(128)} %bitcast.1.side_ref.core_ref, bf16[4352,128]{1,0:T(8,128)(2,1)S(1)} %bitcast.11, bf16[4352,128]{1,0:T(8,128)(2,1)S(1)} %bitcast.13, bf16[128,128]{1,0:T(8,128)(2,1)S(1)} %copy-done.10, ...), custom_call_target="tpu_custom_call" | custom-call | flops 1000000000 | bytes 8000000 | tf_op jit(solution)/shard_map/local/pallas_call | solution.py:186
  11.4 7.3 %collective-permute-done.2.passed_ref = bf16[1632,128]{1,0:T(8,128)(2,1)} collective-permute-done((bf16[1632,128]{1,0:T(8,128)(2,1)S(1)}, bf16[1632,128]{1,0:T(8,128)(2,1)}, u32[]{:S(2)}, u32[]{:S(2)}) %collective-permute-start.2) | collective-permute-done | bytes 417824 | tf_op jit(solution)/shard_map/ppermute | solution.py:522
  18.8 1.1 %choose.1 = (bf16[544,128]{1,0:T(8,128)(2,1)S(1)}, bf16[544,128]{1,0:T(8,128)(2,1)S(1)}, bf16[544,128]{1,0:T(8,128)(2,1)S(1)}) custom-call(s32[1]{0:T(128)S(6)} %select_n.22.place_ref, bf16[1632,128]{1,0:T(8,128)(2,1)S(1)} %get-tuple-element.22.own_ref, bf16[1632,128]{1,0:T(8,128)(2,1)} %collective-permute-done.2.passed_ref), custom_call_target="tpu_custom_call" | custom-call | tf_op jit(solution)/shard_map/choose/pallas_call | solution.py:119
  19.8 2.3 %collective-permute-start.3 = (bf16[544,128]{1,0:T(8,128)(2,1)S(1)}, bf16[544,128]{1,0:T(8,128)(2,1)S(1)}, u32[]{:S(2)}, u32[]{:S(2)}) collective-permute-start(bf16[544,128]{1,0:T(8,128)(2,1)S(1)} %get-tuple-element.23), channel_id=1, source_target_pairs={{12,8},{16,20},{20,16},{8,12},{28,24},{0,4},{13,9},{17,21},{21,17}... | collective-permute-start | bytes 417800 | tf_op jit(solution)/shard_map/ppermute | solution.py:533
  22.2 1.3 %collective-permute-start.4 = (bf16[544,128]{1,0:T(8,128)(2,1)S(1)}, bf16[544,128]{1,0:T(8,128)(2,1)S(1)}, u32[]{:S(2)}, u32[]{:S(2)}) collective-permute-start(bf16[544,128]{1,0:T(8,128)(2,1)S(1)} %get-tuple-element.24), channel_id=1, source_target_pairs={{4,8},{24,20},{20,16},{8,12},{28,24},{0,4},{5,9},{25,21},{21,17},{... | collective-permute-start | bytes 417800 | tf_op jit(solution)/shard_map/ppermute | solution.py:533
  23.5 6.6 %collective-permute-start.5 = (bf16[544,128]{1,0:T(8,128)(2,1)S(1)}, bf16[544,128]{1,0:T(8,128)(2,1)S(1)}, u32[]{:S(2)}, u32[]{:S(2)}) collective-permute-start(bf16[544,128]{1,0:T(8,128)(2,1)S(1)} %get-tuple-element.25), channel_id=1, source_target_pairs={{4,8},{24,20},{12,16},{16,12},{28,24},{0,4},{5,9},{25,21},{13,17},... | collective-permute-start | bytes 417800 | tf_op jit(solution)/shard_map/ppermute | solution.py:533
  30.1 2.6 %cross_near.1 = (f32[256,128]{1,0:T(8,128)S(1)}, bf16[2048,128]{1,0:T(8,128)(2,1)S(1)}) custom-call(s32[1]{0:T(128)} %bitcast.odd_ref, s32[1]{0:T(128)} %bitcast.1.side_ref.core_ref, s32[16]{0:T(128)S(1)} %copy-done.6, s32[2,64]{1,0:T(2,128)S(1)} %bitcast.14, f32[2,2176,128]{2,1,0:T(8,128)S(1)} %get-tuple-element.20.z_ref, ...), custom_call_target="tpu_custom_call" | custom-call | flops 2000000000 | bytes 4000000 | tf_op jit(solution)/shard_map/cross_near/pallas_call | solution.py:332
  32.8 2.1 %cross_far.1 = (f32[128,128]{1,0:T(8,128)S(1)}, f32[128,128]{1,0:T(8,128)S(1)}, bf16[2048,128]{1,0:T(8,128)(2,1)S(1)}) custom-call(s32[1]{0:T(128)} %bitcast.odd_ref, s32[1]{0:T(128)} %bitcast.1.side_ref.core_ref, s32[16]{0:T(128)S(1)} %copy-done.6, s32[2,64]{1,0:T(2,128)S(1)} %bitcast.15, f32[2,2176,128]{2,1,0:T(8,128)S(1)} %get-tuple-element.20.z_ref, ...), custom_call_target="tpu_custom_call" | custom-call | flops 2000000000 | bytes 4000000 | tf_op jit(solution)/shard_map/cross_far/pallas_call | solution.py:332
  34.9 0.1 collective-permute-start.8
  35.0 1.2 %collective-permute-done.8 = f32[128,128]{1,0:T(8,128)S(1)} collective-permute-done((f32[128,128]{1,0:T(8,128)S(1)}, f32[128,128]{1,0:T(8,128)S(1)}, u32[]{:S(2)}, u32[]{:S(2)}) %collective-permute-start.8) | collective-permute-done | bytes 65568 | tf_op jit(solution)/shard_map/ppermute | solution.py:352
  36.3 2.3 %collective-permute-start.9 = (f32[128,128]{1,0:T(8,128)S(1)}, f32[128,128]{1,0:T(8,128)S(1)}, u32[]{:S(2)}, u32[]{:S(2)}) collective-permute-start(f32[128,128]{1,0:T(8,128)S(1)} %add.25), channel_id=1, source_target_pairs={{0,4},{1,3},{2,6},{3,1},{4,0},{5,7},{6,2},{7,5},{8,12},{9,11},{10,... | collective-permute-start | bytes 196616 | tf_op jit(solution)/shard_map/ppermute | solution.py:363
  38.6 2.2 %collective-permute-done.9 = f32[128,128]{1,0:T(8,128)S(1)} collective-permute-done((f32[128,128]{1,0:T(8,128)S(1)}, f32[128,128]{1,0:T(8,128)S(1)}, u32[]{:S(2)}, u32[]{:S(2)}) %collective-permute-start.9) | collective-permute-done | bytes 65568 | tf_op jit(solution)/shard_map/ppermute | solution.py:363
  40.9 1.8 %collective-permute-start.10 = (f32[128,128]{1,0:T(8,128)S(1)}, f32[128,128]{1,0:T(8,128)S(1)}, u32[]{:S(2)}, u32[]{:S(2)}) collective-permute-start(f32[128,128]{1,0:T(8,128)S(1)} %add.26), channel_id=1, source_target_pairs={{0,2},{1,5},{2,0},{3,7},{4,6},{5,1},{6,4},{7,3},{8,10},{9,13},{10,... | collective-permute-start | bytes 196616 | tf_op jit(solution)/shard_map/ppermute | solution.py:363
  42.7 2.5 %collective-permute-done.10 = f32[128,128]{1,0:T(8,128)S(1)} collective-permute-done((f32[128,128]{1,0:T(8,128)S(1)}, f32[128,128]{1,0:T(8,128)S(1)}, u32[]{:S(2)}, u32[]{:S(2)}) %collective-permute-start.10) | collective-permute-done | bytes 65568 | tf_op jit(solution)/shard_map/ppermute | solution.py:363
  45.2 2.8 %collective-permute-start.11 = (f32[128,128]{1,0:T(8,128)S(1)}, f32[128,128]{1,0:T(8,128)S(1)}, u32[]{:S(2)}, u32[]{:S(2)}) collective-permute-start(f32[128,128]{1,0:T(8,128)S(1)} %add.27), channel_id=1, source_target_pairs={{0,8},{1,17},{2,10},{3,19},{4,12},{5,21},{6,14},{7,23},{8,0},{9,25... | collective-permute-start | bytes 196616 | tf_op jit(solution)/shard_map/ppermute | solution.py:363
  48.1 2.2 %collective-permute-done.11 = f32[128,128]{1,0:T(8,128)S(1)} collective-permute-done((f32[128,128]{1,0:T(8,128)S(1)}, f32[128,128]{1,0:T(8,128)S(1)}, u32[]{:S(2)}, u32[]{:S(2)}) %collective-permute-start.11) | collective-permute-done | bytes 65568 | tf_op jit(solution)/shard_map/ppermute | solution.py:363
  50.3 2.3 %collective-permute-start.12 = (f32[128,128]{1,0:T(8,128)S(1)}, f32[128,128]{1,0:T(8,128)S(1)}, u32[]{:S(2)}, u32[]{:S(2)}) collective-permute-start(f32[128,128]{1,0:T(8,128)S(1)} %add.28), channel_id=1, source_target_pairs={{0,16},{1,9},{2,18},{3,11},{4,20},{5,13},{6,22},{7,15},{8,24},{9,1... | collective-permute-start | bytes 196616 | tf_op jit(solution)/shard_map/ppermute | solution.py:363
  52.6 2.9 %collective-permute-done.12 = f32[128,128]{1,0:T(8,128)S(1)} collective-permute-done((f32[128,128]{1,0:T(8,128)S(1)}, f32[128,128]{1,0:T(8,128)S(1)}, u32[]{:S(2)}, u32[]{:S(2)}) %collective-permute-start.12) | collective-permute-done | bytes 65568 | tf_op jit(solution)/shard_map/ppermute | solution.py:363
  55.6 0.1 collective-permute-start.13
  55.6 1.2 %collective-permute-done.13.other_ref = f32[128,128]{1,0:T(8,128)S(1)} collective-permute-done((f32[128,128]{1,0:T(8,128)S(1)}, f32[128,128]{1,0:T(8,128)S(1)}, u32[]{:S(2)}, u32[]{:S(2)}) %collective-permute-start.13) | collective-permute-done | bytes 65568 | tf_op jit(solution)/shard_map/ppermute | solution.py:352
  56.9 1.8 %modes.1 = (f32[2,64]{1,0:T(2,128)}, f32[256,128]{1,0:T(8,128)}) custom-call(s32[1]{0:T(128)} %bitcast.odd_ref, s32[1]{0:T(128)} %bitcast.1.side_ref.core_ref, f32[128,128]{1,0:T(8,128)S(1)} %add.29.mine_ref, f32[128,128]{1,0:T(8,128)S(1)} %collective-permute-done.13.other_ref, bf16[2048,128]{1,0:T(8,128)(2,1)S(1)} %get-tuple-element.30.near_ref, ...), custom_call_target="tpu_custom_call" | custom-call | tf_op jit(solution)/shard_map/modes/pallas_call | solution.py:463
  (31 shorter events, 0.1 us)
Async XLA Ops:
  0.6 1.3 %copy-start = (bf16[2176,2,128]{2,1,0:T(2,128)(2,1)S(1)}, bf16[2176,2,128]{2,1,0:T(2,128)(2,1)}, u32[]{:S(2)}) copy-start(bf16[2176,2,128]{2,1,0:T(2,128)(2,1)} %param.11) | copy-start | bytes 3342340
  1.9 4.8 %copy-start.2 = (bf16[2176,2,128]{2,1,0:T(2,128)(2,1)S(1)}, bf16[2176,2,128]{2,1,0:T(2,128)(2,1)}, u32[]{:S(2)}) copy-start(bf16[2176,2,128]{2,1,0:T(2,128)(2,1)} %param.10) | copy-start | bytes 3342340
  1.9 4.8 %copy-start.3 = (bf16[8,16,128]{2,1,0:T(8,128)(2,1)S(1)}, bf16[8,16,128]{2,1,0:T(8,128)(2,1)}, u32[]{:S(2)}) copy-start(bf16[8,16,128]{2,1,0:T(8,128)(2,1)} %constant.51.clone.picks_ref) | copy-start | bytes 98308
  2.1 6.5 %copy-start.1 = (bf16[2176,2,128]{2,1,0:T(2,128)(2,1)S(1)}, bf16[2176,2,128]{2,1,0:T(2,128)(2,1)}, u32[]{:S(2)}) copy-start(bf16[2176,2,128]{2,1,0:T(2,128)(2,1)} %param.11) | copy-start | bytes 3342340
  2.1 27.9 %collective-permute-start.7 = (bf16[2176,128]{1,0:T(8,128)(2,1)S(1)}, bf16[2176,128]{1,0:T(8,128)(2,1)}, u32[]{:S(2)}, u32[]{:S(2)}) collective-permute-start(bf16[2176,128]{1,0:T(8,128)(2,1)S(1)} %near.1), channel_id=1, source_target_pairs={{0,4},{4,0},{8,12},{12,8},{16,20},{20,16},{24,28},{28,24},{1,5},{5... | collective-permute-start | bytes 1671176 | tf_op jit(solution)/shard_map/ppermute | solution.py:352
  5.4 13.4 %collective-permute-start.2 = (bf16[1632,128]{1,0:T(8,128)(2,1)S(1)}, bf16[1632,128]{1,0:T(8,128)(2,1)}, u32[]{:S(2)}, u32[]{:S(2)}) collective-permute-start(bf16[1632,128]{1,0:T(8,128)(2,1)S(1)} %get-tuple-element.22.own_ref), channel_id=1, source_target_pairs={{4,12},{12,20},{20,28},{8,0},{16,8},{24,16},{5,13},{13,21},{21,29}... | collective-permute-start | bytes 1253384 | tf_op jit(solution)/shard_map/ppermute | solution.py:522
  7.1 1.5 %collective-permute-start = (bf16[8,544]{1,0:T(8,128)(2,1)S(1)}, bf16[8,544]{1,0:T(8,128)(2,1)S(1)}, u32[]{:S(2)}, u32[]{:S(2)}) collective-permute-start(bf16[8,544]{1,0:T(8,128)(2,1)S(1)} %get-tuple-element.18), channel_id=1, source_target_pairs={{0,1},{1,0},{2,3},{3,2},{4,5},{5,4},{6,7},{7,6},{8,9},{9,8},{10,11... | collective-permute-start | bytes 26120 | tf_op jit(solution)/shard_map/ppermute | solution.py:352
  7.2 1.4 %collective-permute-start.1 = (bf16[8,544]{1,0:T(8,128)(2,1)S(1)}, bf16[8,544]{1,0:T(8,128)(2,1)S(1)}, u32[]{:S(2)}, u32[]{:S(2)}) collective-permute-start(bf16[8,544]{1,0:T(8,128)(2,1)S(1)} %get-tuple-element.19), channel_id=1, source_target_pairs={{1,2},{2,1},{5,6},{6,5},{9,10},{10,9},{13,14},{14,13},{17,18},{18,... | collective-permute-start | bytes 26120 | tf_op jit(solution)/shard_map/ppermute | solution.py:525
  7.9 24.9 %collective-permute-start.6 = (bf16[544,128]{1,0:T(8,128)(2,1)S(1)}, bf16[544,128]{1,0:T(8,128)(2,1)S(1)}, u32[]{:S(2)}, u32[]{:S(2)}) collective-permute-start(bf16[544,128]{1,0:T(8,128)(2,1)S(1)} %get-tuple-element.26), channel_id=1, source_target_pairs={{4,8},{24,20},{12,16},{16,12},{20,24},{8,4},{5,9},{25,21},{13,17},... | collective-permute-start | bytes 417800 | tf_op jit(solution)/shard_map/ppermute | solution.py:533
  8.6 21.5 %copy-start.4 = (s32[64,2]{0,1:T(2,128)S(1)}, s32[64,2]{0,1:T(2,128)}, u32[]{:S(2)}) copy-start(s32[64,2]{0,1:T(2,128)} %param.14) | copy-start | bytes 1540
  8.6 21.5 %copy-start.5 = (f32[2,128]{1,0:T(2,128)S(1)}, f32[2,128]{1,0:T(2,128)}, u32[]{:S(2)}) copy-start(f32[2,128]{1,0:T(2,128)} %weights_ref.3) | copy-start | bytes 3076
  8.6 21.5 %copy-start.6 = (s32[16]{0:T(128)S(1)}, s32[16]{0:T(128)}, u32[]{:S(2)}) copy-start(s32[16]{0:T(128)} %offsets_ref.3) | copy-start | bytes 196
  8.6 21.5 %copy-start.7 = (bf16[256,256]{1,0:T(8,128)(2,1)S(1)}, bf16[256,256]{1,0:T(8,128)(2,1)}, u32[]{:S(2)}) copy-start(bf16[256,256]{1,0:T(8,128)(2,1)} %constant.55.clone.transform_ref) | copy-start | bytes 393220
  8.6 21.5 %copy-start.8 = (f32[256,128]{1,0:T(8,128)S(1)}, f32[256,128]{1,0:T(8,128)}, u32[]{:S(2)}) copy-start(f32[256,128]{1,0:T(8,128)} %constant.54.clone.window_ref) | copy-start | bytes 393220
  8.7 0.8 %copy-start.9 = (bf16[8,16,128]{2,1,0:T(8,128)(2,1)S(1)}, bf16[8,16,128]{2,1,0:T(8,128)(2,1)}, u32[]{:S(2)}) copy-start(bf16[8,16,128]{2,1,0:T(8,128)(2,1)} %constant.53.clone.places_ref) | copy-start | bytes 98308
  9.5 0.8 %copy-start.10 = (bf16[128,128]{1,0:T(8,128)(2,1)S(1)}, bf16[128,128]{1,0:T(8,128)(2,1)}, u32[]{:S(2)}) copy-start(bf16[128,128]{1,0:T(8,128)(2,1)} %constant.52.clone.shift_ref) | copy-start | bytes 98308
  19.8 12.9 %collective-permute-start.3 = (bf16[544,128]{1,0:T(8,128)(2,1)S(1)}, bf16[544,128]{1,0:T(8,128)(2,1)S(1)}, u32[]{:S(2)}, u32[]{:S(2)}) collective-permute-start(bf16[544,128]{1,0:T(8,128)(2,1)S(1)} %get-tuple-element.23), channel_id=1, source_target_pairs={{12,8},{16,20},{20,16},{8,12},{28,24},{0,4},{13,9},{17,21},{21,17}... | collective-permute-start | bytes 417800 | tf_op jit(solution)/shard_map/ppermute | solution.py:533
  22.2 10.6 %collective-permute-start.4 = (bf16[544,128]{1,0:T(8,128)(2,1)S(1)}, bf16[544,128]{1,0:T(8,128)(2,1)S(1)}, u32[]{:S(2)}, u32[]{:S(2)}) collective-permute-start(bf16[544,128]{1,0:T(8,128)(2,1)S(1)} %get-tuple-element.24), channel_id=1, source_target_pairs={{4,8},{24,20},{20,16},{8,12},{28,24},{0,4},{5,9},{25,21},{21,17},{... | collective-permute-start | bytes 417800 | tf_op jit(solution)/shard_map/ppermute | solution.py:533
  23.5 9.3 %collective-permute-start.5 = (bf16[544,128]{1,0:T(8,128)(2,1)S(1)}, bf16[544,128]{1,0:T(8,128)(2,1)S(1)}, u32[]{:S(2)}, u32[]{:S(2)}) collective-permute-start(bf16[544,128]{1,0:T(8,128)(2,1)S(1)} %get-tuple-element.25), channel_id=1, source_target_pairs={{4,8},{24,20},{12,16},{16,12},{28,24},{0,4},{5,9},{25,21},{13,17},... | collective-permute-start | bytes 417800 | tf_op jit(solution)/shard_map/ppermute | solution.py:533
  34.9 1.3 %collective-permute-start.8 = (f32[128,128]{1,0:T(8,128)S(1)}, f32[128,128]{1,0:T(8,128)S(1)}, u32[]{:S(2)}, u32[]{:S(2)}) collective-permute-start(f32[128,128]{1,0:T(8,128)S(1)} %get-tuple-element.29), channel_id=1, source_target_pairs={{0,1},{1,0},{2,3},{3,2},{4,5},{5,4},{6,7},{7,6},{8,9},{9,8},{10,11... | collective-permute-start | bytes 196616 | tf_op jit(solution)/shard_map/ppermute | solution.py:352
  36.3 4.6 %collective-permute-start.9 = (f32[128,128]{1,0:T(8,128)S(1)}, f32[128,128]{1,0:T(8,128)S(1)}, u32[]{:S(2)}, u32[]{:S(2)}) collective-permute-start(f32[128,128]{1,0:T(8,128)S(1)} %add.25), channel_id=1, source_target_pairs={{0,4},{1,3},{2,6},{3,1},{4,0},{5,7},{6,2},{7,5},{8,12},{9,11},{10,... | collective-permute-start | bytes 196616 | tf_op jit(solution)/shard_map/ppermute | solution.py:363
  40.9 4.3 %collective-permute-start.10 = (f32[128,128]{1,0:T(8,128)S(1)}, f32[128,128]{1,0:T(8,128)S(1)}, u32[]{:S(2)}, u32[]{:S(2)}) collective-permute-start(f32[128,128]{1,0:T(8,128)S(1)} %add.26), channel_id=1, source_target_pairs={{0,2},{1,5},{2,0},{3,7},{4,6},{5,1},{6,4},{7,3},{8,10},{9,13},{10,... | collective-permute-start | bytes 196616 | tf_op jit(solution)/shard_map/ppermute | solution.py:363
  45.2 5.1 %collective-permute-start.11 = (f32[128,128]{1,0:T(8,128)S(1)}, f32[128,128]{1,0:T(8,128)S(1)}, u32[]{:S(2)}, u32[]{:S(2)}) collective-permute-start(f32[128,128]{1,0:T(8,128)S(1)} %add.27), channel_id=1, source_target_pairs={{0,8},{1,17},{2,10},{3,19},{4,12},{5,21},{6,14},{7,23},{8,0},{9,25... | collective-permute-start | bytes 196616 | tf_op jit(solution)/shard_map/ppermute | solution.py:363
  50.3 5.2 %collective-permute-start.12 = (f32[128,128]{1,0:T(8,128)S(1)}, f32[128,128]{1,0:T(8,128)S(1)}, u32[]{:S(2)}, u32[]{:S(2)}) collective-permute-start(f32[128,128]{1,0:T(8,128)S(1)} %add.28), channel_id=1, source_target_pairs={{0,16},{1,9},{2,18},{3,11},{4,20},{5,13},{6,22},{7,15},{8,24},{9,1... | collective-permute-start | bytes 196616 | tf_op jit(solution)/shard_map/ppermute | solution.py:363
  55.6 1.3 %collective-permute-start.13 = (f32[128,128]{1,0:T(8,128)S(1)}, f32[128,128]{1,0:T(8,128)S(1)}, u32[]{:S(2)}, u32[]{:S(2)}) collective-permute-start(f32[128,128]{1,0:T(8,128)S(1)} %add.29.mine_ref), channel_id=1, source_target_pairs={{0,1},{1,0},{2,3},{3,2},{4,5},{5,4},{6,7},{7,6},{8,9},{9,8},{10,11... | collective-permute-start | bytes 196616 | tf_op jit(solution)/shard_map/ppermute | solution.py:352

commit v11 on v9

--- a/solution.py
+++ b/solution.py
@@ -13,7 +13,7 @@
 NFFT = 256
 POW = 4
 LANES = 128
-AHEAD = 11
+CUTS = (0, 4, 11, 16)
 F32 = jnp.float32
 BF16 = jnp.bfloat16
 MIB = 2**20
@@ -55,25 +55,18 @@
     return pltpu.CompilerParams(vmem_limit_bytes=mib * MIB)
 
 
-def near_kernel(sx, odd_ref, v_ref, early_ref, late_ref, plain):
+def near_kernel(sx, odd_ref, v_ref, near_ref, plain):
     plain[...] = v_ref[...].astype(F32)
-    row = row_at(0, sx, odd_ref[0])
-    early, late = early_ref.shape[0], late_ref.shape[0]
-    early_ref[...] = plain[pl.ds(row, early, stride=sx), :].astype(BF16)
-    late_ref[...] = plain[pl.ds(early * sx + row, late, stride=sx), :].astype(BF16)
+    near_ref[...] = plain[pl.ds(row_at(0, sx, odd_ref[0]), near_ref.shape[0], stride=sx), :].astype(BF16)
 
 
 def near_edge(odd, v, sx):
     rows = v.shape[0]
-    early = rows // sx * AHEAD // 1024 * 64
     return pl.pallas_call(
         functools.partial(near_kernel, sx),
-        out_shape=(
-            jax.ShapeDtypeStruct((early, LANES), BF16),
-            jax.ShapeDtypeStruct((rows // sx - early, LANES), BF16),
-        ),
+        out_shape=jax.ShapeDtypeStruct((rows // sx, LANES), BF16),
         in_specs=[SMEM, VMEM],
-        out_specs=(VMEM,) * 2,
+        out_specs=VMEM,
         scratch_shapes=[pltpu.VMEM((rows, LANES), F32)],
         compiler_params=limit(8),
         name="near",
@@ -468,9 +461,11 @@
     core = (lax.axis_index("freq") % 2)[None]
     pairs = triads.T
 
-    early, late = near_edge(odd, v, sx)
-    early = swap(early, "space", 1)
-    late = swap(late, "space", 1)
+    near = []
+    for begin, end in zip(CUTS[:-1], CUTS[1:]):
+        begin, end = (times * cut // 1024 * 64 if cut < 16 else times for cut in (begin, end))
+        edge = near_edge(odd, v[begin * sx : end * sx], sx)
+        near.append(swap(edge, "space", 1))
     col_near, col_far = columns_edge(core, u, jnp.asarray(picks, BF16))
     col_near = swap(col_near, "freq", 1)
     col_far = lax.ppermute(col_far, "freq", between_pairs(lax.axis_size("freq")))
@@ -480,7 +475,7 @@
     window = jnp.asarray(np.ascontiguousarray(np.broadcast_to(window[:, None], (NFFT, LANES))))
     transform = jnp.asarray(transform, BF16)
     share, near_target = cross_part(
-        0, sx - 1, odd, core, block_offsets, pairs, z, sums, [early, late], cell_weights, window, transform
+        0, sx - 1, odd, core, block_offsets, pairs, z, sums, near, cell_weights, window, transform
     )
     mine, other, far_target = cross_part(
         sx - 1, 1, odd, core, block_offsets, pairs, z, sums, [far], cell_weights, window, transform, share

time: 58.4 us -> 61 us (1.045)
  waiting for transfers between devices: 28.2 us -> 29.3 us
  starting transfers between devices: 18.5 us -> 19.3 us
  local copies, waits for them, and re-layouts: 1.29 us -> 2.06 us
    ppermute x5 -> x6, waiting for transfers between devices: 18.7 us -> 19.8 us  [swap(): return lax.ppermute(x, axis, [(i, i ^ bit) for i in range(count)])]
    ppermute x1, starting transfers between devices: 0.7 us -> 1.63 us  [on_device(): far = lax.ppermute(far, 'space', between_pairs(slabs))]
    slice x0 -> x3, local copies, waits for them, and re-layouts: none -> 0.77 us  [on_device(): edge = near_edge(odd, v[begin * sx:end * sx], sx)]
    pallas_call x1 -> x3, Pallas kernels: 0.97 us -> 0.26 us  [near_edge(): pl.pallas_call(functools.partial(near_kernel, sx), out_shape=jax.ShapeDty...]
    ppermute x5 -> x6, starting transfers between devices: 7.48 us -> 7.38 us  [swap(): return lax.ppermute(x, axis, [(i, i ^ bit) for i in range(count)])]
  transfers between devices with their start and end apart: 11 -> 12, of which waited for: 8 -> 8; matrix products, arithmetic and copies ran while one was open for 0% -> 1% of each run, Pallas kernels for 8% -> 7%
where the time goes in v11:
time: 61 us; the launch traced here: 60.7 us
  waiting for transfers between devices  29.3 us (48%)
  starting transfers between devices  19.3 us (32%)
  Pallas kernels  9.15 us (15%)
  local copies, waits for them, and re-layouts  2.06 us (3%)
  between operations  0.85 us (1%)
    ppermute x6, waiting for transfers between devices, swap(): return lax.ppermute(x, axis, [(i, i ^ bit) for i in range(count)])  19.8 us
    ppermute x4, starting transfers between devices, sum_over_rest(): x = x + lax.ppermute(x, ('space', 'freq'), pairs)  9.51 us
    ppermute x4, waiting for transfers between devices, sum_over_rest(): x = x + lax.ppermute(x, ('space', 'freq'), pairs)  9.48 us
    ppermute x6, starting transfers between devices, swap(): return lax.ppermute(x, axis, [(i, i ^ bit) for i in range(count)])  7.38 us
    pallas_call x2, Pallas kernels, cross_part(): pl.pallas_call(functools.partial(cross_kernel, sx, begin, len(halos)), ou...  5.31 us
    pallas_call x1, Pallas kernels, modes_part(): pl.pallas_call(functools.partial(modes_kernel, sx, blocks, scaling), out_...  1.81 us
    ppermute x1, starting transfers between devices, on_device(): far = lax.ppermute(far, 'space', between_pairs(slabs))  1.63 us
    unnamed x22, local copies, waits for them, and re-layouts  1.29 us
  transfers between devices with their start and end apart: 12, of which 8 were waited for; matrix products, arithmetic and copies ran while one was open for 1% of the time, Pallas kernels for 7%

profile of v11, /device:TPU:0, one launch (start us, length us, event | category | flops | bytes accessed | tf_op | source)
XLA Modules:
  0.0 60.7 jit_solution(10554562974419538288)
XLA Ops:
  0.7 1.2 %copy-done = bf16[2176,2,128]{2,1,0:T(2,128)(2,1)S(1)} copy-done((bf16[2176,2,128]{2,1,0:T(2,128)(2,1)S(1)}, bf16[2176,2,128]{2,1,0:T(2,128)(2,1)}, u32[]{:S(2)}) %copy-start) | copy-done | bytes 1114136
  1.9 0.2 far.1
  2.1 1.6 %collective-permute-start.2 = (bf16[2176,128]{1,0:T(8,128)(2,1)S(1)}, bf16[2176,128]{1,0:T(8,128)(2,1)}, u32[]{:S(2)}, u32[]{:S(2)}) collective-permute-start(bf16[2176,128]{1,0:T(8,128)(2,1)S(1)} %far.1), channel_id=1, source_target_pairs={{4,8},{12,16},{20,24},{8,4},{16,12},{24,20},{5,9},{13,17},{21,25},... | collective-permute-start | bytes 1671176 | tf_op jit(solution)/shard_map/ppermute | solution.py:474
  3.8 0.3 slice.20
  4.1 0.1 near.4
  4.2 5.0 %collective-permute-start.4 = (bf16[960,128]{1,0:T(8,128)(2,1)S(1)}, bf16[960,128]{1,0:T(8,128)(2,1)}, u32[]{:S(2)}, u32[]{:S(2)}) collective-permute-start(bf16[960,128]{1,0:T(8,128)(2,1)S(1)} %near.4), channel_id=1, source_target_pairs={{0,4},{4,0},{8,12},{12,8},{16,20},{20,16},{24,28},{28,24},{1,5},{5... | collective-permute-start | bytes 737288 | tf_op jit(solution)/shard_map/ppermute | solution.py:317
  9.2 0.2 slice.22
  9.5 0.1 near.5
  9.6 0.1 collective-permute-start.5
  9.7 0.2 slice.18
  9.9 0.1 near.3
  9.9 2.1 %collective-permute-start.3 = (bf16[512,128]{1,0:T(8,128)(2,1)S(1)}, bf16[512,128]{1,0:T(8,128)(2,1)}, u32[]{:S(2)}, u32[]{:S(2)}) collective-permute-start(bf16[512,128]{1,0:T(8,128)(2,1)S(1)} %near.3), channel_id=1, source_target_pairs={{0,4},{4,0},{8,12},{12,8},{16,20},{20,16},{24,28},{28,24},{1,5},{5... | collective-permute-start | bytes 393224 | tf_op jit(solution)/shard_map/ppermute | solution.py:317
  12.0 0.4 columns.1
  12.5 1.2 %collective-permute-done.near_ref = bf16[8,544]{1,0:T(8,128)(2,1)S(1)} collective-permute-done((bf16[8,544]{1,0:T(8,128)(2,1)S(1)}, bf16[8,544]{1,0:T(8,128)(2,1)S(1)}, u32[]{:S(2)}, u32[]{:S(2)}) %collective-permute-start) | collective-permute-done | bytes 8736 | tf_op jit(solution)/shard_map/ppermute | solution.py:317
  13.7 0.8 %collective-permute-start.1 = (bf16[8,544]{1,0:T(8,128)(2,1)S(1)}, bf16[8,544]{1,0:T(8,128)(2,1)S(1)}, u32[]{:S(2)}, u32[]{:S(2)}) collective-permute-start(bf16[8,544]{1,0:T(8,128)(2,1)S(1)} %get-tuple-element.14), channel_id=1, source_target_pairs={{1,2},{2,1},{5,6},{6,5},{9,10},{10,9},{13,14},{14,13},{17,18},{18,... | collective-permute-start | bytes 26120 | tf_op jit(solution)/shard_map/ppermute | solution.py:471
  14.5 1.2 %local.1 = (f32[2,2176,128]{2,1,0:T(8,128)S(1)}, f32[2,8,128]{2,1,0:T(8,128)S(1)}) custom-call(s32[1]{0:T(128)} %bitcast.odd_ref, s32[1]{0:T(128)} %bitcast.1.side_ref.core_ref, bf16[4352,128]{1,0:T(8,128)(2,1)S(1)} %bitcast.11, bf16[4352,128]{1,0:T(8,128)(2,1)S(1)} %bitcast.15, bf16[128,128]{1,0:T(8,128)(2,1)S(1)} %copy-done.10, ...), custom_call_target="tpu_custom_call" | custom-call | flops 1000000000 | bytes 8000000 | tf_op jit(solution)/shard_map/local/pallas_call | solution.py:151
  15.7 16.2 %collective-permute-done.3.rest_0_ = bf16[512,128]{1,0:T(8,128)(2,1)} collective-permute-done((bf16[512,128]{1,0:T(8,128)(2,1)S(1)}, bf16[512,128]{1,0:T(8,128)(2,1)}, u32[]{:S(2)}, u32[]{:S(2)}) %collective-permute-start.3) | collective-permute-done | bytes 131104 | tf_op jit(solution)/shard_map/ppermute | solution.py:317
  31.9 2.7 %cross_near.1 = (f32[256,128]{1,0:T(8,128)S(1)}, bf16[2048,128]{1,0:T(8,128)(2,1)S(1)}) custom-call(s32[1]{0:T(128)} %bitcast.odd_ref, s32[1]{0:T(128)} %bitcast.1.side_ref.core_ref, s32[16]{0:T(128)S(1)} %copy-done.6, s32[2,64]{1,0:T(2,128)S(1)} %bitcast.17, f32[2,2176,128]{2,1,0:T(8,128)S(1)} %get-tuple-element.15.z_ref, ...), custom_call_target="tpu_custom_call" | custom-call | flops 2000000000 | bytes 4000000 | tf_op jit(solution)/shard_map/cross_near/pallas_call | solution.py:297
  34.5 2.7 %cross_far.1 = (f32[128,128]{1,0:T(8,128)S(1)}, f32[128,128]{1,0:T(8,128)S(1)}, bf16[2048,128]{1,0:T(8,128)(2,1)S(1)}) custom-call(s32[1]{0:T(128)} %bitcast.odd_ref, s32[1]{0:T(128)} %bitcast.1.side_ref.core_ref, s32[16]{0:T(128)S(1)} %copy-done.6, s32[2,64]{1,0:T(2,128)S(1)} %bitcast.18, f32[2,2176,128]{2,1,0:T(8,128)S(1)} %get-tuple-element.15.z_ref, ...), custom_call_target="tpu_custom_call" | custom-call | flops 2000000000 | bytes 4000000 | tf_op jit(solution)/shard_map/cross_far/pallas_call | solution.py:297
  37.2 0.1 collective-permute-start.6
  37.3 1.2 %collective-permute-done.6 = f32[128,128]{1,0:T(8,128)S(1)} collective-permute-done((f32[128,128]{1,0:T(8,128)S(1)}, f32[128,128]{1,0:T(8,128)S(1)}, u32[]{:S(2)}, u32[]{:S(2)}) %collective-permute-start.6) | collective-permute-done | bytes 65568 | tf_op jit(solution)/shard_map/ppermute | solution.py:317
  38.5 2.7 %collective-permute-start.7 = (f32[128,128]{1,0:T(8,128)S(1)}, f32[128,128]{1,0:T(8,128)S(1)}, u32[]{:S(2)}, u32[]{:S(2)}) collective-permute-start(f32[128,128]{1,0:T(8,128)S(1)} %add.24), channel_id=1, source_target_pairs={{0,4},{1,3},{2,6},{3,1},{4,0},{5,7},{6,2},{7,5},{8,12},{9,11},{10,... | collective-permute-start | bytes 196616 | tf_op jit(solution)/shard_map/ppermute | solution.py:328
  41.2 2.2 %collective-permute-done.7 = f32[128,128]{1,0:T(8,128)S(1)} collective-permute-done((f32[128,128]{1,0:T(8,128)S(1)}, f32[128,128]{1,0:T(8,128)S(1)}, u32[]{:S(2)}, u32[]{:S(2)}) %collective-permute-start.7) | collective-permute-done | bytes 65568 | tf_op jit(solution)/shard_map/ppermute | solution.py:328
  43.5 1.6 %collective-permute-start.8 = (f32[128,128]{1,0:T(8,128)S(1)}, f32[128,128]{1,0:T(8,128)S(1)}, u32[]{:S(2)}, u32[]{:S(2)}) collective-permute-start(f32[128,128]{1,0:T(8,128)S(1)} %add.25), channel_id=1, source_target_pairs={{0,2},{1,5},{2,0},{3,7},{4,6},{5,1},{6,4},{7,3},{8,10},{9,13},{10,... | collective-permute-start | bytes 196616 | tf_op jit(solution)/shard_map/ppermute | solution.py:328
  45.0 2.7 %collective-permute-done.8 = f32[128,128]{1,0:T(8,128)S(1)} collective-permute-done((f32[128,128]{1,0:T(8,128)S(1)}, f32[128,128]{1,0:T(8,128)S(1)}, u32[]{:S(2)}, u32[]{:S(2)}) %collective-permute-start.8) | collective-permute-done | bytes 65568 | tf_op jit(solution)/shard_map/ppermute | solution.py:328
  47.8 2.2 %collective-permute-start.9 = (f32[128,128]{1,0:T(8,128)S(1)}, f32[128,128]{1,0:T(8,128)S(1)}, u32[]{:S(2)}, u32[]{:S(2)}) collective-permute-start(f32[128,128]{1,0:T(8,128)S(1)} %add.26), channel_id=1, source_target_pairs={{0,8},{1,17},{2,10},{3,19},{4,12},{5,21},{6,14},{7,23},{8,0},{9,25... | collective-permute-start | bytes 196616 | tf_op jit(solution)/shard_map/ppermute | solution.py:328
  50.0 2.2 %collective-permute-done.9 = f32[128,128]{1,0:T(8,128)S(1)} collective-permute-done((f32[128,128]{1,0:T(8,128)S(1)}, f32[128,128]{1,0:T(8,128)S(1)}, u32[]{:S(2)}, u32[]{:S(2)}) %collective-permute-start.9) | collective-permute-done | bytes 65568 | tf_op jit(solution)/shard_map/ppermute | solution.py:328
  52.2 3.1 %collective-permute-start.10 = (f32[128,128]{1,0:T(8,128)S(1)}, f32[128,128]{1,0:T(8,128)S(1)}, u32[]{:S(2)}, u32[]{:S(2)}) collective-permute-start(f32[128,128]{1,0:T(8,128)S(1)} %add.27), channel_id=1, source_target_pairs={{0,16},{1,9},{2,18},{3,11},{4,20},{5,13},{6,22},{7,15},{8,24},{9,1... | collective-permute-start | bytes 196616 | tf_op jit(solution)/shard_map/ppermute | solution.py:328
  55.3 2.2 %collective-permute-done.10 = f32[128,128]{1,0:T(8,128)S(1)} collective-permute-done((f32[128,128]{1,0:T(8,128)S(1)}, f32[128,128]{1,0:T(8,128)S(1)}, u32[]{:S(2)}, u32[]{:S(2)}) %collective-permute-start.10) | collective-permute-done | bytes 65568 | tf_op jit(solution)/shard_map/ppermute | solution.py:328
  57.6 0.1 collective-permute-start.11
  57.7 1.2 %collective-permute-done.11.other_ref = f32[128,128]{1,0:T(8,128)S(1)} collective-permute-done((f32[128,128]{1,0:T(8,128)S(1)}, f32[128,128]{1,0:T(8,128)S(1)}, u32[]{:S(2)}, u32[]{:S(2)}) %collective-permute-start.11) | collective-permute-done | bytes 65568 | tf_op jit(solution)/shard_map/ppermute | solution.py:317
  58.9 1.8 %modes.1 = (f32[2,64]{1,0:T(2,128)}, f32[256,128]{1,0:T(8,128)}) custom-call(s32[1]{0:T(128)} %bitcast.odd_ref, s32[1]{0:T(128)} %bitcast.1.side_ref.core_ref, f32[128,128]{1,0:T(8,128)S(1)} %add.28.mine_ref, f32[128,128]{1,0:T(8,128)S(1)} %collective-permute-done.11.other_ref, bf16[2048,128]{1,0:T(8,128)(2,1)S(1)} %get-tuple-element.20.near_ref, ...), custom_call_target="tpu_custom_call" | custom-call | tf_op jit(solution)/shard_map/modes/pallas_call | solution.py:428
  (31 shorter events, 0.2 us)
Async XLA Ops:
  0.6 1.2 %copy-start = (bf16[2176,2,128]{2,1,0:T(2,128)(2,1)S(1)}, bf16[2176,2,128]{2,1,0:T(2,128)(2,1)}, u32[]{:S(2)}) copy-start(bf16[2176,2,128]{2,1,0:T(2,128)(2,1)} %param.11) | copy-start | bytes 3342340
  1.9 1.9 %copy-start.1 = (bf16[2176,2,128]{2,1,0:T(2,128)(2,1)S(1)}, bf16[2176,2,128]{2,1,0:T(2,128)(2,1)}, u32[]{:S(2)}) copy-start(bf16[2176,2,128]{2,1,0:T(2,128)(2,1)} %param.11) | copy-start | bytes 3342340
  2.1 32.4 %collective-permute-start.2 = (bf16[2176,128]{1,0:T(8,128)(2,1)S(1)}, bf16[2176,128]{1,0:T(8,128)(2,1)}, u32[]{:S(2)}, u32[]{:S(2)}) collective-permute-start(bf16[2176,128]{1,0:T(8,128)(2,1)S(1)} %far.1), channel_id=1, source_target_pairs={{4,8},{12,16},{20,24},{8,4},{16,12},{24,20},{5,9},{13,17},{21,25},... | collective-permute-start | bytes 1671176 | tf_op jit(solution)/shard_map/ppermute | solution.py:474
  4.2 7.8 %copy-start.2 = (bf16[2176,2,128]{2,1,0:T(2,128)(2,1)S(1)}, bf16[2176,2,128]{2,1,0:T(2,128)(2,1)}, u32[]{:S(2)}) copy-start(bf16[2176,2,128]{2,1,0:T(2,128)(2,1)} %param.10) | copy-start | bytes 3342340
  4.2 7.8 %copy-start.3 = (bf16[8,16,128]{2,1,0:T(8,128)(2,1)S(1)}, bf16[8,16,128]{2,1,0:T(8,128)(2,1)}, u32[]{:S(2)}) copy-start(bf16[8,16,128]{2,1,0:T(8,128)(2,1)} %constant.36.clone.picks_ref) | copy-start | bytes 98308
  4.2 27.6 %collective-permute-start.4 = (bf16[960,128]{1,0:T(8,128)(2,1)S(1)}, bf16[960,128]{1,0:T(8,128)(2,1)}, u32[]{:S(2)}, u32[]{:S(2)}) collective-permute-start(bf16[960,128]{1,0:T(8,128)(2,1)S(1)} %near.4), channel_id=1, source_target_pairs={{0,4},{4,0},{8,12},{12,8},{16,20},{20,16},{24,28},{28,24},{1,5},{5... | collective-permute-start | bytes 737288 | tf_op jit(solution)/shard_map/ppermute | solution.py:317
  9.6 22.2 %collective-permute-start.5 = (bf16[704,128]{1,0:T(8,128)(2,1)S(1)}, bf16[704,128]{1,0:T(8,128)(2,1)S(1)}, u32[]{:S(2)}, u32[]{:S(2)}) collective-permute-start(bf16[704,128]{1,0:T(8,128)(2,1)S(1)} %near.5), channel_id=1, source_target_pairs={{0,4},{4,0},{8,12},{12,8},{16,20},{20,16},{24,28},{28,24},{1,5},{5... | collective-permute-start | bytes 540680 | tf_op jit(solution)/shard_map/ppermute | solution.py:317
  9.9 21.9 %collective-permute-start.3 = (bf16[512,128]{1,0:T(8,128)(2,1)S(1)}, bf16[512,128]{1,0:T(8,128)(2,1)}, u32[]{:S(2)}, u32[]{:S(2)}) collective-permute-start(bf16[512,128]{1,0:T(8,128)(2,1)S(1)} %near.3), channel_id=1, source_target_pairs={{0,4},{4,0},{8,12},{12,8},{16,20},{20,16},{24,28},{28,24},{1,5},{5... | collective-permute-start | bytes 393224 | tf_op jit(solution)/shard_map/ppermute | solution.py:317
  12.0 2.5 %copy-start.9 = (bf16[8,16,128]{2,1,0:T(8,128)(2,1)S(1)}, bf16[8,16,128]{2,1,0:T(8,128)(2,1)}, u32[]{:S(2)}) copy-start(bf16[8,16,128]{2,1,0:T(8,128)(2,1)} %constant.38.clone.places_ref) | copy-start | bytes 98308
  12.0 2.5 %copy-start.10 = (bf16[128,128]{1,0:T(8,128)(2,1)S(1)}, bf16[128,128]{1,0:T(8,128)(2,1)}, u32[]{:S(2)}) copy-start(bf16[128,128]{1,0:T(8,128)(2,1)} %constant.37.clone.shift_ref) | copy-start | bytes 98308
  12.4 1.2 %collective-permute-start = (bf16[8,544]{1,0:T(8,128)(2,1)S(1)}, bf16[8,544]{1,0:T(8,128)(2,1)S(1)}, u32[]{:S(2)}, u32[]{:S(2)}) collective-permute-start(bf16[8,544]{1,0:T(8,128)(2,1)S(1)} %get-tuple-element.13), channel_id=1, source_target_pairs={{0,1},{1,0},{2,3},{3,2},{4,5},{5,4},{6,7},{7,6},{8,9},{9,8},{10,11... | collective-permute-start | bytes 26120 | tf_op jit(solution)/shard_map/ppermute | solution.py:317
  13.7 18.2 %copy-start.4 = (s32[64,2]{0,1:T(2,128)S(1)}, s32[64,2]{0,1:T(2,128)}, u32[]{:S(2)}) copy-start(s32[64,2]{0,1:T(2,128)} %param.14) | copy-start | bytes 1540
  13.7 18.2 %copy-start.5 = (f32[2,128]{1,0:T(2,128)S(1)}, f32[2,128]{1,0:T(2,128)}, u32[]{:S(2)}) copy-start(f32[2,128]{1,0:T(2,128)} %weights_ref.3) | copy-start | bytes 3076
  13.7 18.2 %copy-start.6 = (s32[16]{0:T(128)S(1)}, s32[16]{0:T(128)}, u32[]{:S(2)}) copy-start(s32[16]{0:T(128)} %offsets_ref.3) | copy-start | bytes 196
  13.7 18.2 %copy-start.7 = (bf16[256,256]{1,0:T(8,128)(2,1)S(1)}, bf16[256,256]{1,0:T(8,128)(2,1)}, u32[]{:S(2)}) copy-start(bf16[256,256]{1,0:T(8,128)(2,1)} %constant.40.clone.transform_ref) | copy-start | bytes 393220
  13.7 18.2 %copy-start.8 = (f32[256,128]{1,0:T(8,128)S(1)}, f32[256,128]{1,0:T(8,128)}, u32[]{:S(2)}) copy-start(f32[256,128]{1,0:T(8,128)} %constant.39.clone.window_ref) | copy-start | bytes 393220
  13.7 0.8 %collective-permute-start.1 = (bf16[8,544]{1,0:T(8,128)(2,1)S(1)}, bf16[8,544]{1,0:T(8,128)(2,1)S(1)}, u32[]{:S(2)}, u32[]{:S(2)}) collective-permute-start(bf16[8,544]{1,0:T(8,128)(2,1)S(1)} %get-tuple-element.14), channel_id=1, source_target_pairs={{1,2},{2,1},{5,6},{6,5},{9,10},{10,9},{13,14},{14,13},{17,18},{18,... | collective-permute-start | bytes 26120 | tf_op jit(solution)/shard_map/ppermute | solution.py:471
  37.2 1.3 %collective-permute-start.6 = (f32[128,128]{1,0:T(8,128)S(1)}, f32[128,128]{1,0:T(8,128)S(1)}, u32[]{:S(2)}, u32[]{:S(2)}) collective-permute-start(f32[128,128]{1,0:T(8,128)S(1)} %get-tuple-element.19), channel_id=1, source_target_pairs={{0,1},{1,0},{2,3},{3,2},{4,5},{5,4},{6,7},{7,6},{8,9},{9,8},{10,11... | collective-permute-start | bytes 196616 | tf_op jit(solution)/shard_map/ppermute | solution.py:317
  38.5 4.9 %collective-permute-start.7 = (f32[128,128]{1,0:T(8,128)S(1)}, f32[128,128]{1,0:T(8,128)S(1)}, u32[]{:S(2)}, u32[]{:S(2)}) collective-permute-start(f32[128,128]{1,0:T(8,128)S(1)} %add.24), channel_id=1, source_target_pairs={{0,4},{1,3},{2,6},{3,1},{4,0},{5,7},{6,2},{7,5},{8,12},{9,11},{10,... | collective-permute-start | bytes 196616 | tf_op jit(solution)/shard_map/ppermute | solution.py:328
  43.5 4.3 %collective-permute-start.8 = (f32[128,128]{1,0:T(8,128)S(1)}, f32[128,128]{1,0:T(8,128)S(1)}, u32[]{:S(2)}, u32[]{:S(2)}) collective-permute-start(f32[128,128]{1,0:T(8,128)S(1)} %add.25), channel_id=1, source_target_pairs={{0,2},{1,5},{2,0},{3,7},{4,6},{5,1},{6,4},{7,3},{8,10},{9,13},{10,... | collective-permute-start | bytes 196616 | tf_op jit(solution)/shard_map/ppermute | solution.py:328
  47.8 4.4 %collective-permute-start.9 = (f32[128,128]{1,0:T(8,128)S(1)}, f32[128,128]{1,0:T(8,128)S(1)}, u32[]{:S(2)}, u32[]{:S(2)}) collective-permute-start(f32[128,128]{1,0:T(8,128)S(1)} %add.26), channel_id=1, source_target_pairs={{0,8},{1,17},{2,10},{3,19},{4,12},{5,21},{6,14},{7,23},{8,0},{9,25... | collective-permute-start | bytes 196616 | tf_op jit(solution)/shard_map/ppermute | solution.py:328
  52.2 5.3 %collective-permute-start.10 = (f32[128,128]{1,0:T(8,128)S(1)}, f32[128,128]{1,0:T(8,128)S(1)}, u32[]{:S(2)}, u32[]{:S(2)}) collective-permute-start(f32[128,128]{1,0:T(8,128)S(1)} %add.27), channel_id=1, source_target_pairs={{0,16},{1,9},{2,18},{3,11},{4,20},{5,13},{6,22},{7,15},{8,24},{9,1... | collective-permute-start | bytes 196616 | tf_op jit(solution)/shard_map/ppermute | solution.py:328
  57.6 1.3 %collective-permute-start.11 = (f32[128,128]{1,0:T(8,128)S(1)}, f32[128,128]{1,0:T(8,128)S(1)}, u32[]{:S(2)}, u32[]{:S(2)}) collective-permute-start(f32[128,128]{1,0:T(8,128)S(1)} %add.28.mine_ref), channel_id=1, source_target_pairs={{0,1},{1,0},{2,3},{3,2},{4,5},{5,4},{6,7},{7,6},{8,9},{9,8},{10,11... | collective-permute-start | bytes 196616 | tf_op jit(solution)/shard_map/ppermute | solution.py:317

commit v12 on v9

--- a/solution.py
+++ b/solution.py
@@ -327,12 +327,22 @@
 def sum_over_rest(x):
     slabs, parts = lax.axis_size("space"), lax.axis_size("freq")
     hops = [bit * parts for bit in bits_of(slabs)]
-    across = [bit for bit in bits_of(parts)[1:]]
-    first = hops[:1] + across + hops[1:]
-    second = across + hops[:1] + hops[:0:-1]
-    for one, other in zip(first, second, strict=True):
+    first = hops[:1] + bits_of(parts)[1:] + hops[1:]
+    second = first[2:] + first[:2]
+
+    def swapped(one, other):
         pairs = [(i, i ^ (other if i % 2 else one)) for i in range(slabs * parts)]
-        x = x + lax.ppermute(x, ("space", "freq"), pairs)
+        return lax.ppermute(sent, ("space", "freq"), pairs).astype(F32)
+
+    for n in range(0, len(first), 2):
+        one, other = first[n : n + 2], second[n : n + 2]
+        x = lax.reduce_precision(x, 8, 7)
+        sent = x.astype(BF16)
+        if len(one) == 1:
+            x = x + swapped(one[0], other[0])
+            continue
+        near, far, both = swapped(one[0], other[0]), swapped(one[1], other[1]), swapped(sum(one), sum(other))
+        x = (x + near) + (far + both)
     return x
 
 

time: 58.4 us -> 54.8 us (0.938)
  waiting for transfers between devices: 28.2 us -> 25.4 us
  starting transfers between devices: 18.5 us -> 17.7 us
    ppermute x4 -> x6, waiting for transfers between devices: 9.48 us -> 6.69 us  [swapped(): return lax.ppermute(sent, ('space', 'freq'), pairs).astype(F32)]
    ppermute x4 -> x6, starting transfers between devices: 9.51 us -> 8.71 us  [swapped(): return lax.ppermute(sent, ('space', 'freq'), pairs).astype(F32)]
  transfers between devices with their start and end apart: 11 -> 13, of which waited for: 8 -> 10; matrix products, arithmetic and copies ran while one was open for 0% -> 0% of each run, Pallas kernels for 8% -> 8%
where the time goes in v12:
time: 54.8 us; the launch traced here: 54.6 us
  waiting for transfers between devices  25.4 us (46%)
  starting transfers between devices  17.7 us (32%)
  Pallas kernels  9.32 us (17%)
  local copies, waits for them, and re-layouts  1.29 us (2%)
  between operations  0.81 us (1%)
    ppermute x5, waiting for transfers between devices, swap(): return lax.ppermute(x, axis, [(i, i ^ bit) for i in range(count)])  18.7 us
    ppermute x6, starting transfers between devices, swapped(): return lax.ppermute(sent, ('space', 'freq'), pairs).astype(F32)  8.71 us
    ppermute x5, starting transfers between devices, swap(): return lax.ppermute(x, axis, [(i, i ^ bit) for i in range(count)])  7.48 us
    ppermute x6, waiting for transfers between devices, swapped(): return lax.ppermute(sent, ('space', 'freq'), pairs).astype(F32)  6.69 us
    pallas_call x2, Pallas kernels, cross_part(): pl.pallas_call(functools.partial(cross_kernel, sx, begin, len(halos)), ou...  4.76 us
    pallas_call x1, Pallas kernels, modes_part(): pl.pallas_call(functools.partial(modes_kernel, sx, blocks, scaling), out_...  1.81 us
    unnamed x22, local copies, waits for them, and re-layouts  1.29 us
    pallas_call x1, Pallas kernels, local_part(): pl.pallas_call(functools.partial(local_kernel, sx, pieces), out_shape=(ja...  1.15 us
  transfers between devices with their start and end apart: 13, of which 10 were waited for; matrix products, arithmetic and copies ran while one was open for 0% of the time, Pallas kernels for 8%

profile of v12, /device:TPU:0, one launch (start us, length us, event | category | flops | bytes accessed | tf_op | source)
XLA Modules:
  0.0 54.6 jit_solution(7490130078251500678)
XLA Ops:
  0.7 1.2 %copy-done = bf16[2176,2,128]{2,1,0:T(2,128)(2,1)S(1)} copy-done((bf16[2176,2,128]{2,1,0:T(2,128)(2,1)S(1)}, bf16[2176,2,128]{2,1,0:T(2,128)(2,1)}, u32[]{:S(2)}) %copy-start) | copy-done | bytes 1114136
  1.9 1.0 %near.1 = (bf16[1472,128]{1,0:T(8,128)(2,1)}, bf16[704,128]{1,0:T(8,128)(2,1)S(1)}) custom-call(s32[1]{0:T(128)} %bitcast.odd_ref, bf16[4352,128]{1,0:T(8,128)(2,1)S(1)} %bitcast.7), custom_call_target="tpu_custom_call" | custom-call | tf_op jit(solution)/shard_map/near/pallas_call | solution.py:69
  2.9 3.0 %collective-permute-start.3 = (bf16[1472,128]{1,0:T(8,128)(2,1)}, bf16[1472,128]{1,0:T(8,128)(2,1)}, u32[]{:S(2)}, u32[]{:S(2)}) collective-permute-start(bf16[1472,128]{1,0:T(8,128)(2,1)} %get-tuple-element.19), channel_id=1, source_target_pairs={{0,4},{4,0},{8,12},{12,8},{16,20},{20,16},{24,28},{28,24},{1,5},{5... | collective-permute-start | bytes 1130504 | tf_op jit(solution)/shard_map/ppermute | solution.py:324
  5.8 0.2 far.1
  6.1 0.7 %collective-permute-start.2 = (bf16[2176,128]{1,0:T(8,128)(2,1)S(1)}, bf16[2176,128]{1,0:T(8,128)(2,1)S(1)}, u32[]{:S(2)}, u32[]{:S(2)}) collective-permute-start(bf16[2176,128]{1,0:T(8,128)(2,1)S(1)} %far.1), channel_id=1, source_target_pairs={{4,8},{12,16},{20,24},{8,4},{16,12},{24,20},{5,9},{13,17},{21,25},... | collective-permute-start | bytes 1671176 | tf_op jit(solution)/shard_map/ppermute | solution.py:489
  6.8 4.3 %collective-permute-start.4 = (bf16[704,128]{1,0:T(8,128)(2,1)S(1)}, bf16[704,128]{1,0:T(8,128)(2,1)}, u32[]{:S(2)}, u32[]{:S(2)}) collective-permute-start(bf16[704,128]{1,0:T(8,128)(2,1)S(1)} %get-tuple-element.20), channel_id=1, source_target_pairs={{0,4},{4,0},{8,12},{12,8},{16,20},{20,16},{24,28},{28,24},{1,5},{5... | collective-permute-start | bytes 540680 | tf_op jit(solution)/shard_map/ppermute | solution.py:324
  11.1 0.4 columns.1
  11.5 0.1 collective-permute-start
  11.6 0.0 copy-start.7
  11.6 0.8 %collective-permute-start.1 = (bf16[8,544]{1,0:T(8,128)(2,1)S(1)}, bf16[8,544]{1,0:T(8,128)(2,1)S(1)}, u32[]{:S(2)}, u32[]{:S(2)}) collective-permute-start(bf16[8,544]{1,0:T(8,128)(2,1)S(1)} %get-tuple-element.16), channel_id=1, source_target_pairs={{1,2},{2,1},{5,6},{6,5},{9,10},{10,9},{13,14},{14,13},{17,18},{18,... | collective-permute-start | bytes 26120 | tf_op jit(solution)/shard_map/ppermute | solution.py:486
  12.4 0.3 collective-permute-done.near_ref
  12.7 1.2 %local.1 = (f32[2,2176,128]{2,1,0:T(8,128)S(1)}, f32[2,8,128]{2,1,0:T(8,128)S(1)}) custom-call(s32[1]{0:T(128)} %bitcast.odd_ref, s32[1]{0:T(128)} %bitcast.1.side_ref.core_ref, bf16[4352,128]{1,0:T(8,128)(2,1)S(1)} %bitcast.9, bf16[4352,128]{1,0:T(8,128)(2,1)S(1)} %bitcast.11, bf16[128,128]{1,0:T(8,128)(2,1)S(1)} %copy-done.10, ...), custom_call_target="tpu_custom_call" | custom-call | flops 1000000000 | bytes 8000000 | tf_op jit(solution)/shard_map/local/pallas_call | solution.py:158
  13.9 16.0 %collective-permute-done.4.rest_1_ = bf16[704,128]{1,0:T(8,128)(2,1)} collective-permute-done((bf16[704,128]{1,0:T(8,128)(2,1)S(1)}, bf16[704,128]{1,0:T(8,128)(2,1)}, u32[]{:S(2)}, u32[]{:S(2)}) %collective-permute-start.4) | collective-permute-done | bytes 180256 | tf_op jit(solution)/shard_map/ppermute | solution.py:324
  29.9 2.6 %cross_near.1 = (f32[256,128]{1,0:T(8,128)S(1)}, bf16[2048,128]{1,0:T(8,128)(2,1)S(1)}) custom-call(s32[1]{0:T(128)} %bitcast.odd_ref, s32[1]{0:T(128)} %bitcast.1.side_ref.core_ref, s32[16]{0:T(128)S(1)} %copy-done.6, s32[2,64]{1,0:T(2,128)S(1)} %bitcast.12, f32[2,2176,128]{2,1,0:T(8,128)S(1)} %get-tuple-element.17.z_ref, ...), custom_call_target="tpu_custom_call" | custom-call | flops 2000000000 | bytes 4000000 | tf_op jit(solution)/shard_map/cross_near/pallas_call | solution.py:304
  32.5 2.1 %cross_far.1 = (f32[128,128]{1,0:T(8,128)S(1)}, f32[128,128]{1,0:T(8,128)S(1)}, bf16[2048,128]{1,0:T(8,128)(2,1)S(1)}) custom-call(s32[1]{0:T(128)} %bitcast.odd_ref, s32[1]{0:T(128)} %bitcast.1.side_ref.core_ref, s32[16]{0:T(128)S(1)} %copy-done.6, s32[2,64]{1,0:T(2,128)S(1)} %bitcast.13, f32[2,2176,128]{2,1,0:T(8,128)S(1)} %get-tuple-element.17.z_ref, ...), custom_call_target="tpu_custom_call" | custom-call | flops 2000000000 | bytes 4000000 | tf_op jit(solution)/shard_map/cross_far/pallas_call | solution.py:304
  34.7 0.1 collective-permute-start.5
  34.8 1.2 %collective-permute-done.5 = f32[128,128]{1,0:T(8,128)S(1)} collective-permute-done((f32[128,128]{1,0:T(8,128)S(1)}, f32[128,128]{1,0:T(8,128)S(1)}, u32[]{:S(2)}, u32[]{:S(2)}) %collective-permute-start.5) | collective-permute-done | bytes 65568 | tf_op jit(solution)/shard_map/ppermute | solution.py:324
  36.0 3.6 %collective-permute-start.8 = (bf16[128,128]{1,0:T(8,128)(2,1)S(1)}, bf16[128,128]{1,0:T(8,128)(2,1)S(1)}, u32[]{:S(2)}, u32[]{:S(2)}) collective-permute-start(bf16[128,128]{1,0:T(8,128)(2,1)S(1)} %fusion), channel_id=1, source_target_pairs={{0,6},{1,25},{2,4},{3,27},{4,2},{5,29},{6,0},{7,31},{8,14},{9,17},... | collective-permute-start | bytes 98312 | tf_op jit(solution)/shard_map/ppermute | solution.py:335
  39.6 0.5 collective-permute-start.7
  40.1 0.1 collective-permute-start.6
  40.3 1.3 %collective-permute-done.8 = bf16[128,128]{1,0:T(8,128)(2,1)S(1)} collective-permute-done((bf16[128,128]{1,0:T(8,128)(2,1)S(1)}, bf16[128,128]{1,0:T(8,128)(2,1)S(1)}, u32[]{:S(2)}, u32[]{:S(2)}) %collective-permute-start.8) | collective-permute-done | bytes 32800 | tf_op jit(solution)/shard_map/ppermute | solution.py:335
  41.5 2.0 %collective-permute-done.7 = bf16[128,128]{1,0:T(8,128)(2,1)S(1)} collective-permute-done((bf16[128,128]{1,0:T(8,128)(2,1)S(1)}, bf16[128,128]{1,0:T(8,128)(2,1)S(1)}, u32[]{:S(2)}, u32[]{:S(2)}) %collective-permute-start.7) | collective-permute-done | bytes 32800 | tf_op jit(solution)/shard_map/ppermute | solution.py:335
  43.5 0.5 collective-permute-done.6
  44.1 2.3 %collective-permute-start.11 = (bf16[128,128]{1,0:T(8,128)(2,1)S(1)}, bf16[128,128]{1,0:T(8,128)(2,1)S(1)}, u32[]{:S(2)}, u32[]{:S(2)}) collective-permute-start(bf16[128,128]{1,0:T(8,128)(2,1)S(1)} %get-tuple-element.28), channel_id=1, source_target_pairs={{0,24},{1,7},{2,26},{3,5},{4,28},{5,3},{6,30},{7,1},{8,16},{9,15},... | collective-permute-start | bytes 98312 | tf_op jit(solution)/shard_map/ppermute | solution.py:335
  46.4 0.8 %collective-permute-start.10 = (bf16[128,128]{1,0:T(8,128)(2,1)S(1)}, bf16[128,128]{1,0:T(8,128)(2,1)S(1)}, u32[]{:S(2)}, u32[]{:S(2)}) collective-permute-start(bf16[128,128]{1,0:T(8,128)(2,1)S(1)} %get-tuple-element.28), channel_id=1, source_target_pairs={{0,16},{1,3},{2,18},{3,1},{4,20},{5,7},{6,22},{7,5},{8,24},{9,11},... | collective-permute-start | bytes 98312 | tf_op jit(solution)/shard_map/ppermute | solution.py:335
  47.2 1.4 %collective-permute-start.9 = (bf16[128,128]{1,0:T(8,128)(2,1)S(1)}, bf16[128,128]{1,0:T(8,128)(2,1)S(1)}, u32[]{:S(2)}, u32[]{:S(2)}) collective-permute-start(bf16[128,128]{1,0:T(8,128)(2,1)S(1)} %get-tuple-element.28), channel_id=1, source_target_pairs={{0,8},{1,5},{2,10},{3,7},{4,12},{5,1},{6,14},{7,3},{8,0},{9,13},{1... | collective-permute-start | bytes 98312 | tf_op jit(solution)/shard_map/ppermute | solution.py:335
  48.5 1.3 %collective-permute-done.11 = bf16[128,128]{1,0:T(8,128)(2,1)S(1)} collective-permute-done((bf16[128,128]{1,0:T(8,128)(2,1)S(1)}, bf16[128,128]{1,0:T(8,128)(2,1)S(1)}, u32[]{:S(2)}, u32[]{:S(2)}) %collective-permute-start.11) | collective-permute-done | bytes 32800 | tf_op jit(solution)/shard_map/ppermute | solution.py:335
  49.9 1.4 %collective-permute-done.10 = bf16[128,128]{1,0:T(8,128)(2,1)S(1)} collective-permute-done((bf16[128,128]{1,0:T(8,128)(2,1)S(1)}, bf16[128,128]{1,0:T(8,128)(2,1)S(1)}, u32[]{:S(2)}, u32[]{:S(2)}) %collective-permute-start.10) | collective-permute-done | bytes 32800 | tf_op jit(solution)/shard_map/ppermute | solution.py:335
  51.3 0.1 collective-permute-done.9
  51.5 0.1 collective-permute-start.12
  51.6 1.2 %collective-permute-done.12.other_ref = f32[128,128]{1,0:T(8,128)S(1)} collective-permute-done((f32[128,128]{1,0:T(8,128)S(1)}, f32[128,128]{1,0:T(8,128)S(1)}, u32[]{:S(2)}, u32[]{:S(2)}) %collective-permute-start.12) | collective-permute-done | bytes 65568 | tf_op jit(solution)/shard_map/ppermute | solution.py:324
  52.8 1.8 %modes.1 = (f32[2,64]{1,0:T(2,128)}, f32[256,128]{1,0:T(8,128)}) custom-call(s32[1]{0:T(128)} %bitcast.odd_ref, s32[1]{0:T(128)} %bitcast.1.side_ref.core_ref, f32[128,128]{1,0:T(8,128)S(1)} %add_add_fusion.mine_ref, f32[128,128]{1,0:T(8,128)S(1)} %collective-permute-done.12.other_ref, bf16[2048,128]{1,0:T(8,128)(2,1)S(1)} %get-tuple-element.24.near_ref, ...), custom_call_target="tpu_custom_call" | custom-call | tf_op jit(solution)/shard_map/modes/pallas_call | solution.py:445
  (26 shorter events, 0.1 us)
Async XLA Ops:
  0.6 1.3 %copy-start = (bf16[2176,2,128]{2,1,0:T(2,128)(2,1)S(1)}, bf16[2176,2,128]{2,1,0:T(2,128)(2,1)}, u32[]{:S(2)}) copy-start(bf16[2176,2,128]{2,1,0:T(2,128)(2,1)} %param.11) | copy-start | bytes 3342340
  2.9 8.2 %copy-start.2 = (bf16[2176,2,128]{2,1,0:T(2,128)(2,1)S(1)}, bf16[2176,2,128]{2,1,0:T(2,128)(2,1)}, u32[]{:S(2)}) copy-start(bf16[2176,2,128]{2,1,0:T(2,128)(2,1)} %param.10) | copy-start | bytes 3342340
  2.9 8.2 %copy-start.3 = (bf16[8,16,128]{2,1,0:T(8,128)(2,1)S(1)}, bf16[8,16,128]{2,1,0:T(8,128)(2,1)}, u32[]{:S(2)}) copy-start(bf16[8,16,128]{2,1,0:T(8,128)(2,1)} %constant.36.clone.picks_ref) | copy-start | bytes 98308
  2.9 9.9 %copy-start.1 = (bf16[2176,2,128]{2,1,0:T(2,128)(2,1)S(1)}, bf16[2176,2,128]{2,1,0:T(2,128)(2,1)}, u32[]{:S(2)}) copy-start(bf16[2176,2,128]{2,1,0:T(2,128)(2,1)} %param.11) | copy-start | bytes 3342340
  2.9 27.0 %collective-permute-start.3 = (bf16[1472,128]{1,0:T(8,128)(2,1)}, bf16[1472,128]{1,0:T(8,128)(2,1)}, u32[]{:S(2)}, u32[]{:S(2)}) collective-permute-start(bf16[1472,128]{1,0:T(8,128)(2,1)} %get-tuple-element.19), channel_id=1, source_target_pairs={{0,4},{4,0},{8,12},{12,8},{16,20},{20,16},{24,28},{28,24},{1,5},{5... | collective-permute-start | bytes 1130504 | tf_op jit(solution)/shard_map/ppermute | solution.py:324
  6.1 26.5 %collective-permute-start.2 = (bf16[2176,128]{1,0:T(8,128)(2,1)S(1)}, bf16[2176,128]{1,0:T(8,128)(2,1)S(1)}, u32[]{:S(2)}, u32[]{:S(2)}) collective-permute-start(bf16[2176,128]{1,0:T(8,128)(2,1)S(1)} %far.1), channel_id=1, source_target_pairs={{4,8},{12,16},{20,24},{8,4},{16,12},{24,20},{5,9},{13,17},{21,25},... | collective-permute-start | bytes 1671176 | tf_op jit(solution)/shard_map/ppermute | solution.py:489
  6.8 23.1 %collective-permute-start.4 = (bf16[704,128]{1,0:T(8,128)(2,1)S(1)}, bf16[704,128]{1,0:T(8,128)(2,1)}, u32[]{:S(2)}, u32[]{:S(2)}) collective-permute-start(bf16[704,128]{1,0:T(8,128)(2,1)S(1)} %get-tuple-element.20), channel_id=1, source_target_pairs={{0,4},{4,0},{8,12},{12,8},{16,20},{20,16},{24,28},{28,24},{1,5},{5... | collective-permute-start | bytes 540680 | tf_op jit(solution)/shard_map/ppermute | solution.py:324
  11.1 1.7 %copy-start.9 = (bf16[8,16,128]{2,1,0:T(8,128)(2,1)S(1)}, bf16[8,16,128]{2,1,0:T(8,128)(2,1)}, u32[]{:S(2)}) copy-start(bf16[8,16,128]{2,1,0:T(8,128)(2,1)} %constant.38.clone.places_ref) | copy-start | bytes 98308
  11.1 1.7 %copy-start.10 = (bf16[128,128]{1,0:T(8,128)(2,1)S(1)}, bf16[128,128]{1,0:T(8,128)(2,1)}, u32[]{:S(2)}) copy-start(bf16[128,128]{1,0:T(8,128)(2,1)} %constant.37.clone.shift_ref) | copy-start | bytes 98308
  11.5 1.2 %collective-permute-start = (bf16[8,544]{1,0:T(8,128)(2,1)S(1)}, bf16[8,544]{1,0:T(8,128)(2,1)S(1)}, u32[]{:S(2)}, u32[]{:S(2)}) collective-permute-start(bf16[8,544]{1,0:T(8,128)(2,1)S(1)} %get-tuple-element.15), channel_id=1, source_target_pairs={{0,1},{1,0},{2,3},{3,2},{4,5},{5,4},{6,7},{7,6},{8,9},{9,8},{10,11... | collective-permute-start | bytes 26120 | tf_op jit(solution)/shard_map/ppermute | solution.py:324
  11.6 18.3 %copy-start.4 = (s32[64,2]{0,1:T(2,128)S(1)}, s32[64,2]{0,1:T(2,128)}, u32[]{:S(2)}) copy-start(s32[64,2]{0,1:T(2,128)} %param.14) | copy-start | bytes 1540
  11.6 18.3 %copy-start.5 = (f32[2,128]{1,0:T(2,128)S(1)}, f32[2,128]{1,0:T(2,128)}, u32[]{:S(2)}) copy-start(f32[2,128]{1,0:T(2,128)} %weights_ref.3) | copy-start | bytes 3076
  11.6 18.3 %copy-start.6 = (s32[16]{0:T(128)S(1)}, s32[16]{0:T(128)}, u32[]{:S(2)}) copy-start(s32[16]{0:T(128)} %offsets_ref.3) | copy-start | bytes 196
  11.6 18.3 %copy-start.7 = (bf16[256,256]{1,0:T(8,128)(2,1)S(1)}, bf16[256,256]{1,0:T(8,128)(2,1)}, u32[]{:S(2)}) copy-start(bf16[256,256]{1,0:T(8,128)(2,1)} %constant.40.clone.transform_ref) | copy-start | bytes 393220
  11.6 18.3 %copy-start.8 = (f32[256,128]{1,0:T(8,128)S(1)}, f32[256,128]{1,0:T(8,128)}, u32[]{:S(2)}) copy-start(f32[256,128]{1,0:T(8,128)} %constant.39.clone.window_ref) | copy-start | bytes 393220
  11.6 1.1 %collective-permute-start.1 = (bf16[8,544]{1,0:T(8,128)(2,1)S(1)}, bf16[8,544]{1,0:T(8,128)(2,1)S(1)}, u32[]{:S(2)}, u32[]{:S(2)}) collective-permute-start(bf16[8,544]{1,0:T(8,128)(2,1)S(1)} %get-tuple-element.16), channel_id=1, source_target_pairs={{1,2},{2,1},{5,6},{6,5},{9,10},{10,9},{13,14},{14,13},{17,18},{18,... | collective-permute-start | bytes 26120 | tf_op jit(solution)/shard_map/ppermute | solution.py:486
  34.7 1.3 %collective-permute-start.5 = (f32[128,128]{1,0:T(8,128)S(1)}, f32[128,128]{1,0:T(8,128)S(1)}, u32[]{:S(2)}, u32[]{:S(2)}) collective-permute-start(f32[128,128]{1,0:T(8,128)S(1)} %get-tuple-element.23), channel_id=1, source_target_pairs={{0,1},{1,0},{2,3},{3,2},{4,5},{5,4},{6,7},{7,6},{8,9},{9,8},{10,11... | collective-permute-start | bytes 196616 | tf_op jit(solution)/shard_map/ppermute | solution.py:324
  36.0 5.5 %collective-permute-start.8 = (bf16[128,128]{1,0:T(8,128)(2,1)S(1)}, bf16[128,128]{1,0:T(8,128)(2,1)S(1)}, u32[]{:S(2)}, u32[]{:S(2)}) collective-permute-start(bf16[128,128]{1,0:T(8,128)(2,1)S(1)} %fusion), channel_id=1, source_target_pairs={{0,6},{1,25},{2,4},{3,27},{4,2},{5,29},{6,0},{7,31},{8,14},{9,17},... | collective-permute-start | bytes 98312 | tf_op jit(solution)/shard_map/ppermute | solution.py:335
  39.6 3.9 %collective-permute-start.7 = (bf16[128,128]{1,0:T(8,128)(2,1)S(1)}, bf16[128,128]{1,0:T(8,128)(2,1)S(1)}, u32[]{:S(2)}, u32[]{:S(2)}) collective-permute-start(bf16[128,128]{1,0:T(8,128)(2,1)S(1)} %fusion), channel_id=1, source_target_pairs={{0,2},{1,17},{2,0},{3,19},{4,6},{5,21},{6,4},{7,23},{8,10},{9,25},... | collective-permute-start | bytes 98312 | tf_op jit(solution)/shard_map/ppermute | solution.py:335
  40.1 3.9 %collective-permute-start.6 = (bf16[128,128]{1,0:T(8,128)(2,1)S(1)}, bf16[128,128]{1,0:T(8,128)(2,1)S(1)}, u32[]{:S(2)}, u32[]{:S(2)}) collective-permute-start(bf16[128,128]{1,0:T(8,128)(2,1)S(1)} %fusion), channel_id=1, source_target_pairs={{0,4},{1,9},{2,6},{3,11},{4,0},{5,13},{6,2},{7,15},{8,12},{9,1},{1... | collective-permute-start | bytes 98312 | tf_op jit(solution)/shard_map/ppermute | solution.py:335
  44.1 5.8 %collective-permute-start.11 = (bf16[128,128]{1,0:T(8,128)(2,1)S(1)}, bf16[128,128]{1,0:T(8,128)(2,1)S(1)}, u32[]{:S(2)}, u32[]{:S(2)}) collective-permute-start(bf16[128,128]{1,0:T(8,128)(2,1)S(1)} %get-tuple-element.28), channel_id=1, source_target_pairs={{0,24},{1,7},{2,26},{3,5},{4,28},{5,3},{6,30},{7,1},{8,16},{9,15},... | collective-permute-start | bytes 98312 | tf_op jit(solution)/shard_map/ppermute | solution.py:335
  46.4 4.9 %collective-permute-start.10 = (bf16[128,128]{1,0:T(8,128)(2,1)S(1)}, bf16[128,128]{1,0:T(8,128)(2,1)S(1)}, u32[]{:S(2)}, u32[]{:S(2)}) collective-permute-start(bf16[128,128]{1,0:T(8,128)(2,1)S(1)} %get-tuple-element.28), channel_id=1, source_target_pairs={{0,16},{1,3},{2,18},{3,1},{4,20},{5,7},{6,22},{7,5},{8,24},{9,11},... | collective-permute-start | bytes 98312 | tf_op jit(solution)/shard_map/ppermute | solution.py:335
  47.2 4.3 %collective-permute-start.9 = (bf16[128,128]{1,0:T(8,128)(2,1)S(1)}, bf16[128,128]{1,0:T(8,128)(2,1)S(1)}, u32[]{:S(2)}, u32[]{:S(2)}) collective-permute-start(bf16[128,128]{1,0:T(8,128)(2,1)S(1)} %get-tuple-element.28), channel_id=1, source_target_pairs={{0,8},{1,5},{2,10},{3,7},{4,12},{5,1},{6,14},{7,3},{8,0},{9,13},{1... | collective-permute-start | bytes 98312 | tf_op jit(solution)/shard_map/ppermute | solution.py:335
  51.5 1.3 %collective-permute-start.12 = (f32[128,128]{1,0:T(8,128)S(1)}, f32[128,128]{1,0:T(8,128)S(1)}, u32[]{:S(2)}, u32[]{:S(2)}) collective-permute-start(f32[128,128]{1,0:T(8,128)S(1)} %add_add_fusion.mine_ref), channel_id=1, source_target_pairs={{0,1},{1,0},{2,3},{3,2},{4,5},{5,4},{6,7},{7,6},{8,9},{9,8},{10,11... | collective-permute-start | bytes 196616 | tf_op jit(solution)/shard_map/ppermute | solution.py:324

commit v13 on v12

--- a/solution.py
+++ b/solution.py
@@ -171,14 +171,14 @@
 
 
 def cross_kernel(
-    sx, begin, pieces, odd_ref, core_ref, offsets_ref, triads_ref, z_ref, sum_ref, weights_ref, window_ref, transform_ref,
+    sx, begin, pieces, odd_ref, offsets_ref, triads_ref, z_ref, sum_ref, weights_ref, window_ref, transform_ref,
     *rest,
 ):
     far = begin > 0
     halo_refs, rest = rest[:pieces], rest[pieces:]
     if far:
         before_ref, *rest = rest
-    *cross_refs, target_ref, full, spec, prod, packed = rest
+    cross_ref, target_ref, full, spec, prod, packed = rest
     count, times, _ = full.shape
     blocks = offsets_ref.shape[0]
     ntri = triads_ref.shape[1]
@@ -282,17 +282,12 @@
 
     lax.fori_loop(0, groups, one_group, 0, unroll=True)
     share = packed[...].T
-    if not far:
-        cross_refs[0][...] = share
-        return
-    share = share + before_ref[...]
-    lower, upper = share[: tall // 2], share[tall // 2 :]
-    second = core_ref[0] == 1
-    cross_refs[0][...] = jnp.where(second, upper, lower)
-    cross_refs[1][...] = jnp.where(second, lower, upper)
-
-
-def cross_part(begin, count, odd, core, offsets, triads, z, sums, halos, weights, window, transform, before=None):
+    if far:
+        share = share + before_ref[...]
+    cross_ref[...] = share
+
+
+def cross_part(begin, count, odd, offsets, triads, z, sums, halos, weights, window, transform, before=None):
     sx, times, _ = z.shape
     blocks = offsets.shape[0]
     ntri = triads.shape[1]
@@ -300,13 +295,14 @@
     wide = 2 * blocks
     tall = ntri // groups * wide
     more = list(halos) + ([] if before is None else [before])
-    parts = 1 if before is None else 2
     return pl.pallas_call(
         functools.partial(cross_kernel, sx, begin, len(halos)),
-        out_shape=(jax.ShapeDtypeStruct((tall // parts, LANES), F32),) * parts
-        + (jax.ShapeDtypeStruct((ntri * wide, count * LANES), BF16),),
-        in_specs=[SMEM] * 4 + [VMEM] * (5 + len(more)),
-        out_specs=(VMEM,) * (parts + 1),
+        out_shape=(
+            jax.ShapeDtypeStruct((tall, LANES), F32),
+            jax.ShapeDtypeStruct((ntri * wide, count * LANES), BF16),
+        ),
+        in_specs=[SMEM] * 3 + [VMEM] * (5 + len(more)),
+        out_specs=(VMEM,) * 2,
         scratch_shapes=[
             pltpu.VMEM((count, times, LANES), F32),
             pltpu.VMEM((count, NFFT * (blocks + 1), LANES), F32),
@@ -316,7 +312,7 @@
         compiler_params=limit(26),
         cost_estimate=pl.CostEstimate(flops=2000000000, bytes_accessed=4000000, transcendentals=0),
         name="cross_far" if begin else "cross_near",
-    )(odd, core, offsets, triads, z, sums, weights, window, transform, *more)
+    )(odd, offsets, triads, z, sums, weights, window, transform, *more)
 
 
 def swap(x, axis, bit):
@@ -350,16 +346,13 @@
     return [1 << n for n in range(count.bit_length() - 1)]
 
 
-def modes_kernel(sx, blocks, scaling, odd_ref, core_ref, mine_ref, other_ref, near_ref, far_ref, values_ref, modes_ref, cross):
+def modes_kernel(sx, blocks, scaling, odd_ref, mine_ref, other_ref, near_ref, far_ref, values_ref, modes_ref, cross):
     tall = cross.shape[0]
     wide = 2 * blocks
     per = tall // wide
     groups = LANES // blocks
     odd = odd_ref[0]
-    core = core_ref[0]
-    half = tall // 2
-    cross[pl.ds(pl.multiple_of(core * half, 8), half), :] = mine_ref[...] * scaling
-    cross[pl.ds(pl.multiple_of((1 - core) * half, 8), half), :] = other_ref[...] * scaling
+    cross[...] = (mine_ref[...] + other_ref[...]) * scaling
     lane = lax.broadcasted_iota(jnp.int32, (per, LANES), 1)
     start = lane - lane % blocks
 
@@ -441,19 +434,19 @@
                 modes_ref[pl.ds(first + row, per, stride=2 * sx), :] = out[part * per : (part + 1) * per, lanes]
 
 
-def modes_part(odd, core, mine, other, near, far, blocks, ntri, sx, scaling):
+def modes_part(odd, mine, other, near, far, blocks, ntri, sx, scaling):
     return pl.pallas_call(
         functools.partial(modes_kernel, sx, blocks, scaling),
         out_shape=(
             jax.ShapeDtypeStruct((2, ntri), F32),
             jax.ShapeDtypeStruct((ntri * 2 * sx, LANES), F32),
         ),
-        in_specs=[SMEM] * 2 + [VMEM] * 4,
+        in_specs=[SMEM] + [VMEM] * 4,
         out_specs=(VMEM,) * 2,
-        scratch_shapes=[pltpu.VMEM((2 * mine.shape[0], LANES), F32)],
+        scratch_shapes=[pltpu.VMEM(mine.shape, F32)],
         compiler_params=limit(12),
         name="modes",
-    )(odd, core, mine, other, near, far)
+    )(odd, mine, other, near, far)
 
 
 def between_pairs(count):
@@ -490,15 +483,14 @@
     window = jnp.asarray(np.ascontiguousarray(np.broadcast_to(window[:, None], (NFFT, LANES))))
     transform = jnp.asarray(transform, BF16)
     share, near_target = cross_part(
-        0, sx - 1, odd, core, block_offsets, pairs, z, sums, [early, late], cell_weights, window, transform
+        0, sx - 1, odd, block_offsets, pairs, z, sums, [early, late], cell_weights, window, transform
     )
-    mine, other, far_target = cross_part(
-        sx - 1, 1, odd, core, block_offsets, pairs, z, sums, [far], cell_weights, window, transform, share
+    share, far_target = cross_part(
+        sx - 1, 1, odd, block_offsets, pairs, z, sums, [far], cell_weights, window, transform, share
     )
-    mine = mine + swap(other, "freq", 1)
-    mine = sum_over_rest(mine)
+    mine = sum_over_rest(share)
     other = swap(mine, "freq", 1)
-    values, modes = modes_part(odd, core, mine, other, near_target, far_target, blocks, ntri, sx, scaling)
+    values, modes = modes_part(odd, mine, other, near_target, far_target, blocks, ntri, sx, scaling)
     return (values.T, modes.reshape(ntri, 2, sx, columns))
 
 

time: 54.8 us -> 54.9 us (level)
    ppermute x6, waiting for transfers between devices: 6.69 us -> 7.91 us  [swapped(): return lax.ppermute(sent, ('space', 'freq'), pairs).astype(F32)]
    ppermute x5 -> x4, waiting for transfers between devices: 18.7 us -> 17.6 us  [swap(): return lax.ppermute(x, axis, [(i, i ^ bit) for i in range(count)])]
    ppermute x5 -> x4, starting transfers between devices: 7.48 us -> 7.41 us  [swap(): return lax.ppermute(x, axis, [(i, i ^ bit) for i in range(count)])]
  transfers between devices with their start and end apart: 13 -> 12, of which waited for: 10 -> 8; matrix products, arithmetic and copies ran while one was open for 0% -> 0% of each run, Pallas kernels for 8% -> 8%
where the time goes in v13:
time: 54.9 us; the launch traced here: 54.7 us
  waiting for transfers between devices  25.5 us (46%)
  starting transfers between devices  17.6 us (32%)
  Pallas kernels  9.32 us (17%)
  local copies, waits for them, and re-layouts  1.29 us (2%)
  between operations  0.81 us (1%)
    ppermute x4, waiting for transfers between devices, swap(): return lax.ppermute(x, axis, [(i, i ^ bit) for i in range(count)])  17.6 us
    ppermute x6, starting transfers between devices, swapped(): return lax.ppermute(sent, ('space', 'freq'), pairs).astype(F32)  8.71 us
    ppermute x6, waiting for transfers between devices, swapped(): return lax.ppermute(sent, ('space', 'freq'), pairs).astype(F32)  7.91 us
    ppermute x4, starting transfers between devices, swap(): return lax.ppermute(x, axis, [(i, i ^ bit) for i in range(count)])  7.41 us
    pallas_call x2, Pallas kernels, cross_part(): pl.pallas_call(functools.partial(cross_kernel, sx, begin, len(halos)), ou...  4.76 us
    pallas_call x1, Pallas kernels, modes_part(): pl.pallas_call(functools.partial(modes_kernel, sx, blocks, scaling), out_...  1.81 us
    unnamed x22, local copies, waits for them, and re-layouts  1.29 us
    pallas_call x1, Pallas kernels, local_part(): pl.pallas_call(functools.partial(local_kernel, sx, pieces), out_shape=(ja...  1.15 us
  transfers between devices with their start and end apart: 12, of which 8 were waited for; matrix products, arithmetic and copies ran while one was open for 0% of the time, Pallas kernels for 8%

profile of v13, /device:TPU:0, one launch (start us, length us, event | category | flops | bytes accessed | tf_op | source)
XLA Modules:
  0.0 54.7 jit_solution(7324034374362698497)
XLA Ops:
  0.6 0.0 copy-start
  0.7 1.2 %copy-done = bf16[2176,2,128]{2,1,0:T(2,128)(2,1)S(1)} copy-done((bf16[2176,2,128]{2,1,0:T(2,128)(2,1)S(1)}, bf16[2176,2,128]{2,1,0:T(2,128)(2,1)}, u32[]{:S(2)}) %copy-start) | copy-done | bytes 1114136
  1.9 1.0 %near.1 = (bf16[1472,128]{1,0:T(8,128)(2,1)}, bf16[704,128]{1,0:T(8,128)(2,1)S(1)}) custom-call(s32[1]{0:T(128)} %bitcast.odd_ref, bf16[4352,128]{1,0:T(8,128)(2,1)S(1)} %bitcast.7), custom_call_target="tpu_custom_call" | custom-call | tf_op jit(solution)/shard_map/near/pallas_call | solution.py:69
  2.9 3.0 %collective-permute-start.3 = (bf16[1472,128]{1,0:T(8,128)(2,1)}, bf16[1472,128]{1,0:T(8,128)(2,1)}, u32[]{:S(2)}, u32[]{:S(2)}) collective-permute-start(bf16[1472,128]{1,0:T(8,128)(2,1)} %get-tuple-element.18), channel_id=1, source_target_pairs={{0,4},{4,0},{8,12},{12,8},{16,20},{20,16},{24,28},{28,24},{1,5},{5... | collective-permute-start | bytes 1130504 | tf_op jit(solution)/shard_map/ppermute | solution.py:320
  5.8 0.2 far.1
  6.1 0.7 %collective-permute-start.2 = (bf16[2176,128]{1,0:T(8,128)(2,1)S(1)}, bf16[2176,128]{1,0:T(8,128)(2,1)S(1)}, u32[]{:S(2)}, u32[]{:S(2)}) collective-permute-start(bf16[2176,128]{1,0:T(8,128)(2,1)S(1)} %far.1), channel_id=1, source_target_pairs={{4,8},{12,16},{20,24},{8,4},{16,12},{24,20},{5,9},{13,17},{21,25},... | collective-permute-start | bytes 1671176 | tf_op jit(solution)/shard_map/ppermute | solution.py:482
  6.8 4.3 %collective-permute-start.4 = (bf16[704,128]{1,0:T(8,128)(2,1)S(1)}, bf16[704,128]{1,0:T(8,128)(2,1)}, u32[]{:S(2)}, u32[]{:S(2)}) collective-permute-start(bf16[704,128]{1,0:T(8,128)(2,1)S(1)} %get-tuple-element.19), channel_id=1, source_target_pairs={{0,4},{4,0},{8,12},{12,8},{16,20},{20,16},{24,28},{28,24},{1,5},{5... | collective-permute-start | bytes 540680 | tf_op jit(solution)/shard_map/ppermute | solution.py:320
  11.1 0.4 columns.1
  11.5 0.1 collective-permute-start
  11.6 0.0 copy-start.7
  11.6 0.0 copy-start.8
  11.6 0.8 %collective-permute-start.1 = (bf16[8,544]{1,0:T(8,128)(2,1)S(1)}, bf16[8,544]{1,0:T(8,128)(2,1)S(1)}, u32[]{:S(2)}, u32[]{:S(2)}) collective-permute-start(bf16[8,544]{1,0:T(8,128)(2,1)S(1)} %get-tuple-element.15), channel_id=1, source_target_pairs={{1,2},{2,1},{5,6},{6,5},{9,10},{10,9},{13,14},{14,13},{17,18},{18,... | collective-permute-start | bytes 26120 | tf_op jit(solution)/shard_map/ppermute | solution.py:479
  12.4 0.3 collective-permute-done.near_ref
  12.8 1.1 %local.1 = (f32[2,2176,128]{2,1,0:T(8,128)S(1)}, f32[2,8,128]{2,1,0:T(8,128)S(1)}) custom-call(s32[1]{0:T(128)} %bitcast.odd_ref, s32[1]{0:T(128)} %bitcast.2.side_ref, bf16[4352,128]{1,0:T(8,128)(2,1)S(1)} %bitcast.9, bf16[4352,128]{1,0:T(8,128)(2,1)S(1)} %bitcast.11, bf16[128,128]{1,0:T(8,128)(2,1)S(1)} %copy-done.10, ...), custom_call_target="tpu_custom_call" | custom-call | flops 1000000000 | bytes 8000000 | tf_op jit(solution)/shard_map/local/pallas_call | solution.py:158
  13.9 16.0 %collective-permute-done.4.rest_1_ = bf16[704,128]{1,0:T(8,128)(2,1)} collective-permute-done((bf16[704,128]{1,0:T(8,128)(2,1)S(1)}, bf16[704,128]{1,0:T(8,128)(2,1)}, u32[]{:S(2)}, u32[]{:S(2)}) %collective-permute-start.4) | collective-permute-done | bytes 180256 | tf_op jit(solution)/shard_map/ppermute | solution.py:320
  29.9 2.6 %cross_near.1 = (f32[256,128]{1,0:T(8,128)S(1)}, bf16[2048,128]{1,0:T(8,128)(2,1)S(1)}) custom-call(s32[1]{0:T(128)} %bitcast.odd_ref, s32[16]{0:T(128)S(1)} %copy-done.6, s32[2,64]{1,0:T(2,128)S(1)} %bitcast.12, f32[2,2176,128]{2,1,0:T(8,128)S(1)} %get-tuple-element.16.z_ref, f32[2,8,128]{2,1,0:T(8,128)S(1)} %get-tuple-element.17.sum_ref, ...), custom_call_target="tpu_custom_call" | custom-call | flops 2000000000 | bytes 4000000 | tf_op jit(solution)/shard_map/cross_near/pallas_call | solution.py:298
  32.5 2.1 %cross_far.1 = (f32[256,128]{1,0:T(8,128)S(1)}, bf16[2048,128]{1,0:T(8,128)(2,1)S(1)}) custom-call(s32[1]{0:T(128)} %bitcast.odd_ref, s32[16]{0:T(128)S(1)} %copy-done.6, s32[2,64]{1,0:T(2,128)S(1)} %bitcast.13, f32[2,2176,128]{2,1,0:T(8,128)S(1)} %get-tuple-element.16.z_ref, f32[2,8,128]{2,1,0:T(8,128)S(1)} %get-tuple-element.17.sum_ref, ...), custom_call_target="tpu_custom_call" | custom-call | flops 2000000000 | bytes 4000000 | tf_op jit(solution)/shard_map/cross_far/pallas_call | solution.py:298
  34.7 3.6 %collective-permute-start.7 = (bf16[256,128]{1,0:T(8,128)(2,1)S(1)}, bf16[256,128]{1,0:T(8,128)(2,1)S(1)}, u32[]{:S(2)}, u32[]{:S(2)}) collective-permute-start(bf16[256,128]{1,0:T(8,128)(2,1)S(1)} %reduce-precision_convert_fusion), channel_id=1, source_target_pairs={{0,6},{1,25},{2,4},{3,27},{4,2},{5,29},{6,0},{7,31},{8,14},{9,17},... | collective-permute-start | bytes 196616 | tf_op jit(solution)/shard_map/ppermute | solution.py:331
  38.3 0.5 collective-permute-start.6
  38.8 0.1 collective-permute-start.5
  39.0 1.6 %collective-permute-done.7 = bf16[256,128]{1,0:T(8,128)(2,1)S(1)} collective-permute-done((bf16[256,128]{1,0:T(8,128)(2,1)S(1)}, bf16[256,128]{1,0:T(8,128)(2,1)S(1)}, u32[]{:S(2)}, u32[]{:S(2)}) %collective-permute-start.7) | collective-permute-done | bytes 65568 | tf_op jit(solution)/shard_map/ppermute | solution.py:331
  40.6 2.0 %collective-permute-done.6 = bf16[256,128]{1,0:T(8,128)(2,1)S(1)} collective-permute-done((bf16[256,128]{1,0:T(8,128)(2,1)S(1)}, bf16[256,128]{1,0:T(8,128)(2,1)S(1)}, u32[]{:S(2)}, u32[]{:S(2)}) %collective-permute-start.6) | collective-permute-done | bytes 65568 | tf_op jit(solution)/shard_map/ppermute | solution.py:331
  42.6 0.5 collective-permute-done.5
  43.1 2.4 %collective-permute-start.10 = (bf16[256,128]{1,0:T(8,128)(2,1)S(1)}, bf16[256,128]{1,0:T(8,128)(2,1)S(1)}, u32[]{:S(2)}, u32[]{:S(2)}) collective-permute-start(bf16[256,128]{1,0:T(8,128)(2,1)S(1)} %fusion), channel_id=1, source_target_pairs={{0,24},{1,7},{2,26},{3,5},{4,28},{5,3},{6,30},{7,1},{8,16},{9,15},... | collective-permute-start | bytes 196616 | tf_op jit(solution)/shard_map/ppermute | solution.py:331
  45.5 0.7 %collective-permute-start.9 = (bf16[256,128]{1,0:T(8,128)(2,1)S(1)}, bf16[256,128]{1,0:T(8,128)(2,1)S(1)}, u32[]{:S(2)}, u32[]{:S(2)}) collective-permute-start(bf16[256,128]{1,0:T(8,128)(2,1)S(1)} %fusion), channel_id=1, source_target_pairs={{0,16},{1,3},{2,18},{3,1},{4,20},{5,7},{6,22},{7,5},{8,24},{9,11},... | collective-permute-start | bytes 196616 | tf_op jit(solution)/shard_map/ppermute | solution.py:331
  46.2 1.3 %collective-permute-start.8 = (bf16[256,128]{1,0:T(8,128)(2,1)S(1)}, bf16[256,128]{1,0:T(8,128)(2,1)S(1)}, u32[]{:S(2)}, u32[]{:S(2)}) collective-permute-start(bf16[256,128]{1,0:T(8,128)(2,1)S(1)} %fusion), channel_id=1, source_target_pairs={{0,8},{1,5},{2,10},{3,7},{4,12},{5,1},{6,14},{7,3},{8,0},{9,13},{1... | collective-permute-start | bytes 196616 | tf_op jit(solution)/shard_map/ppermute | solution.py:331
  47.6 1.7 %collective-permute-done.10 = bf16[256,128]{1,0:T(8,128)(2,1)S(1)} collective-permute-done((bf16[256,128]{1,0:T(8,128)(2,1)S(1)}, bf16[256,128]{1,0:T(8,128)(2,1)S(1)}, u32[]{:S(2)}, u32[]{:S(2)}) %collective-permute-start.10) | collective-permute-done | bytes 65568 | tf_op jit(solution)/shard_map/ppermute | solution.py:331
  49.3 2.1 %collective-permute-done.9 = bf16[256,128]{1,0:T(8,128)(2,1)S(1)} collective-permute-done((bf16[256,128]{1,0:T(8,128)(2,1)S(1)}, bf16[256,128]{1,0:T(8,128)(2,1)S(1)}, u32[]{:S(2)}, u32[]{:S(2)}) %collective-permute-start.9) | collective-permute-done | bytes 65568 | tf_op jit(solution)/shard_map/ppermute | solution.py:331
  51.4 0.1 add_add_fusion.mine_ref
  51.4 0.1 collective-permute-start.11
  51.5 1.3 %collective-permute-done.11.other_ref = f32[256,128]{1,0:T(8,128)S(1)} collective-permute-done((f32[256,128]{1,0:T(8,128)S(1)}, f32[256,128]{1,0:T(8,128)S(1)}, u32[]{:S(2)}, u32[]{:S(2)}) %collective-permute-start.11) | collective-permute-done | bytes 131104 | tf_op jit(solution)/shard_map/ppermute | solution.py:320
  52.9 1.8 %modes.1 = (f32[2,64]{1,0:T(2,128)}, f32[256,128]{1,0:T(8,128)}) custom-call(s32[1]{0:T(128)} %bitcast.odd_ref, f32[256,128]{1,0:T(8,128)S(1)} %add_add_fusion.mine_ref, f32[256,128]{1,0:T(8,128)S(1)} %collective-permute-done.11.other_ref, bf16[2048,128]{1,0:T(8,128)(2,1)S(1)} %get-tuple-element.22.near_ref, bf16[2048,128]{1,0:T(8,128)(2,1)S(1)} %get-tuple-element.23.far_ref), custom_call_target="tpu_custom_call" | custom-call | tf_op jit(solution)/shard_map/modes/pallas_call | solution.py:438
  (24 shorter events, 0.1 us)
Async XLA Ops:
  0.6 1.3 %copy-start = (bf16[2176,2,128]{2,1,0:T(2,128)(2,1)S(1)}, bf16[2176,2,128]{2,1,0:T(2,128)(2,1)}, u32[]{:S(2)}) copy-start(bf16[2176,2,128]{2,1,0:T(2,128)(2,1)} %param.11) | copy-start | bytes 3342340
  2.9 8.2 %copy-start.2 = (bf16[2176,2,128]{2,1,0:T(2,128)(2,1)S(1)}, bf16[2176,2,128]{2,1,0:T(2,128)(2,1)}, u32[]{:S(2)}) copy-start(bf16[2176,2,128]{2,1,0:T(2,128)(2,1)} %param.10) | copy-start | bytes 3342340
  2.9 8.2 %copy-start.3 = (bf16[8,16,128]{2,1,0:T(8,128)(2,1)S(1)}, bf16[8,16,128]{2,1,0:T(8,128)(2,1)}, u32[]{:S(2)}) copy-start(bf16[8,16,128]{2,1,0:T(8,128)(2,1)} %constant.36.clone.picks_ref) | copy-start | bytes 98308
  2.9 9.9 %copy-start.1 = (bf16[2176,2,128]{2,1,0:T(2,128)(2,1)S(1)}, bf16[2176,2,128]{2,1,0:T(2,128)(2,1)}, u32[]{:S(2)}) copy-start(bf16[2176,2,128]{2,1,0:T(2,128)(2,1)} %param.11) | copy-start | bytes 3342340
  2.9 27.0 %collective-permute-start.3 = (bf16[1472,128]{1,0:T(8,128)(2,1)}, bf16[1472,128]{1,0:T(8,128)(2,1)}, u32[]{:S(2)}, u32[]{:S(2)}) collective-permute-start(bf16[1472,128]{1,0:T(8,128)(2,1)} %get-tuple-element.18), channel_id=1, source_target_pairs={{0,4},{4,0},{8,12},{12,8},{16,20},{20,16},{24,28},{28,24},{1,5},{5... | collective-permute-start | bytes 1130504 | tf_op jit(solution)/shard_map/ppermute | solution.py:320
  6.1 26.5 %collective-permute-start.2 = (bf16[2176,128]{1,0:T(8,128)(2,1)S(1)}, bf16[2176,128]{1,0:T(8,128)(2,1)S(1)}, u32[]{:S(2)}, u32[]{:S(2)}) collective-permute-start(bf16[2176,128]{1,0:T(8,128)(2,1)S(1)} %far.1), channel_id=1, source_target_pairs={{4,8},{12,16},{20,24},{8,4},{16,12},{24,20},{5,9},{13,17},{21,25},... | collective-permute-start | bytes 1671176 | tf_op jit(solution)/shard_map/ppermute | solution.py:482
  6.8 23.1 %collective-permute-start.4 = (bf16[704,128]{1,0:T(8,128)(2,1)S(1)}, bf16[704,128]{1,0:T(8,128)(2,1)}, u32[]{:S(2)}, u32[]{:S(2)}) collective-permute-start(bf16[704,128]{1,0:T(8,128)(2,1)S(1)} %get-tuple-element.19), channel_id=1, source_target_pairs={{0,4},{4,0},{8,12},{12,8},{16,20},{20,16},{24,28},{28,24},{1,5},{5... | collective-permute-start | bytes 540680 | tf_op jit(solution)/shard_map/ppermute | solution.py:320
  11.1 1.7 %copy-start.9 = (bf16[8,16,128]{2,1,0:T(8,128)(2,1)S(1)}, bf16[8,16,128]{2,1,0:T(8,128)(2,1)}, u32[]{:S(2)}) copy-start(bf16[8,16,128]{2,1,0:T(8,128)(2,1)} %constant.38.clone.places_ref) | copy-start | bytes 98308
  11.1 1.7 %copy-start.10 = (bf16[128,128]{1,0:T(8,128)(2,1)S(1)}, bf16[128,128]{1,0:T(8,128)(2,1)}, u32[]{:S(2)}) copy-start(bf16[128,128]{1,0:T(8,128)(2,1)} %constant.37.clone.shift_ref) | copy-start | bytes 98308
  11.5 1.2 %collective-permute-start = (bf16[8,544]{1,0:T(8,128)(2,1)S(1)}, bf16[8,544]{1,0:T(8,128)(2,1)S(1)}, u32[]{:S(2)}, u32[]{:S(2)}) collective-permute-start(bf16[8,544]{1,0:T(8,128)(2,1)S(1)} %get-tuple-element.14), channel_id=1, source_target_pairs={{0,1},{1,0},{2,3},{3,2},{4,5},{5,4},{6,7},{7,6},{8,9},{9,8},{10,11... | collective-permute-start | bytes 26120 | tf_op jit(solution)/shard_map/ppermute | solution.py:320
  11.6 18.3 %copy-start.4 = (s32[64,2]{0,1:T(2,128)S(1)}, s32[64,2]{0,1:T(2,128)}, u32[]{:S(2)}) copy-start(s32[64,2]{0,1:T(2,128)} %param.14) | copy-start | bytes 1540
  11.6 18.3 %copy-start.5 = (f32[2,128]{1,0:T(2,128)S(1)}, f32[2,128]{1,0:T(2,128)}, u32[]{:S(2)}) copy-start(f32[2,128]{1,0:T(2,128)} %weights_ref.3) | copy-start | bytes 3076
  11.6 18.3 %copy-start.6 = (s32[16]{0:T(128)S(1)}, s32[16]{0:T(128)}, u32[]{:S(2)}) copy-start(s32[16]{0:T(128)} %offsets_ref.3) | copy-start | bytes 196
  11.6 18.3 %copy-start.7 = (bf16[256,256]{1,0:T(8,128)(2,1)S(1)}, bf16[256,256]{1,0:T(8,128)(2,1)}, u32[]{:S(2)}) copy-start(bf16[256,256]{1,0:T(8,128)(2,1)} %constant.40.clone.transform_ref) | copy-start | bytes 393220
  11.6 18.3 %copy-start.8 = (f32[256,128]{1,0:T(8,128)S(1)}, f32[256,128]{1,0:T(8,128)}, u32[]{:S(2)}) copy-start(f32[256,128]{1,0:T(8,128)} %constant.39.clone.window_ref) | copy-start | bytes 393220
  11.6 1.1 %collective-permute-start.1 = (bf16[8,544]{1,0:T(8,128)(2,1)S(1)}, bf16[8,544]{1,0:T(8,128)(2,1)S(1)}, u32[]{:S(2)}, u32[]{:S(2)}) collective-permute-start(bf16[8,544]{1,0:T(8,128)(2,1)S(1)} %get-tuple-element.15), channel_id=1, source_target_pairs={{1,2},{2,1},{5,6},{6,5},{9,10},{10,9},{13,14},{14,13},{17,18},{18,... | collective-permute-start | bytes 26120 | tf_op jit(solution)/shard_map/ppermute | solution.py:479
  34.7 5.9 %collective-permute-start.7 = (bf16[256,128]{1,0:T(8,128)(2,1)S(1)}, bf16[256,128]{1,0:T(8,128)(2,1)S(1)}, u32[]{:S(2)}, u32[]{:S(2)}) collective-permute-start(bf16[256,128]{1,0:T(8,128)(2,1)S(1)} %reduce-precision_convert_fusion), channel_id=1, source_target_pairs={{0,6},{1,25},{2,4},{3,27},{4,2},{5,29},{6,0},{7,31},{8,14},{9,17},... | collective-permute-start | bytes 196616 | tf_op jit(solution)/shard_map/ppermute | solution.py:331
  38.3 4.3 %collective-permute-start.6 = (bf16[256,128]{1,0:T(8,128)(2,1)S(1)}, bf16[256,128]{1,0:T(8,128)(2,1)S(1)}, u32[]{:S(2)}, u32[]{:S(2)}) collective-permute-start(bf16[256,128]{1,0:T(8,128)(2,1)S(1)} %reduce-precision_convert_fusion), channel_id=1, source_target_pairs={{0,2},{1,17},{2,0},{3,19},{4,6},{5,21},{6,4},{7,23},{8,10},{9,25},... | collective-permute-start | bytes 196616 | tf_op jit(solution)/shard_map/ppermute | solution.py:331
  38.8 4.3 %collective-permute-start.5 = (bf16[256,128]{1,0:T(8,128)(2,1)S(1)}, bf16[256,128]{1,0:T(8,128)(2,1)S(1)}, u32[]{:S(2)}, u32[]{:S(2)}) collective-permute-start(bf16[256,128]{1,0:T(8,128)(2,1)S(1)} %reduce-precision_convert_fusion), channel_id=1, source_target_pairs={{0,4},{1,9},{2,6},{3,11},{4,0},{5,13},{6,2},{7,15},{8,12},{9,1},{1... | collective-permute-start | bytes 196616 | tf_op jit(solution)/shard_map/ppermute | solution.py:331
  43.1 6.1 %collective-permute-start.10 = (bf16[256,128]{1,0:T(8,128)(2,1)S(1)}, bf16[256,128]{1,0:T(8,128)(2,1)S(1)}, u32[]{:S(2)}, u32[]{:S(2)}) collective-permute-start(bf16[256,128]{1,0:T(8,128)(2,1)S(1)} %fusion), channel_id=1, source_target_pairs={{0,24},{1,7},{2,26},{3,5},{4,28},{5,3},{6,30},{7,1},{8,16},{9,15},... | collective-permute-start | bytes 196616 | tf_op jit(solution)/shard_map/ppermute | solution.py:331
  45.5 5.9 %collective-permute-start.9 = (bf16[256,128]{1,0:T(8,128)(2,1)S(1)}, bf16[256,128]{1,0:T(8,128)(2,1)S(1)}, u32[]{:S(2)}, u32[]{:S(2)}) collective-permute-start(bf16[256,128]{1,0:T(8,128)(2,1)S(1)} %fusion), channel_id=1, source_target_pairs={{0,16},{1,3},{2,18},{3,1},{4,20},{5,7},{6,22},{7,5},{8,24},{9,11},... | collective-permute-start | bytes 196616 | tf_op jit(solution)/shard_map/ppermute | solution.py:331
  46.2 5.1 %collective-permute-start.8 = (bf16[256,128]{1,0:T(8,128)(2,1)S(1)}, bf16[256,128]{1,0:T(8,128)(2,1)S(1)}, u32[]{:S(2)}, u32[]{:S(2)}) collective-permute-start(bf16[256,128]{1,0:T(8,128)(2,1)S(1)} %fusion), channel_id=1, source_target_pairs={{0,8},{1,5},{2,10},{3,7},{4,12},{5,1},{6,14},{7,3},{8,0},{9,13},{1... | collective-permute-start | bytes 196616 | tf_op jit(solution)/shard_map/ppermute | solution.py:331
  51.4 1.4 %collective-permute-start.11 = (f32[256,128]{1,0:T(8,128)S(1)}, f32[256,128]{1,0:T(8,128)S(1)}, u32[]{:S(2)}, u32[]{:S(2)}) collective-permute-start(f32[256,128]{1,0:T(8,128)S(1)} %add_add_fusion.mine_ref), channel_id=1, source_target_pairs={{0,1},{1,0},{2,3},{3,2},{4,5},{5,4},{6,7},{7,6},{8,9},{9,8},{10,11... | collective-permute-start | bytes 393224 | tf_op jit(solution)/shard_map/ppermute | solution.py:320

commit v14 on v13

--- a/solution.py
+++ b/solution.py
@@ -13,7 +13,7 @@
 NFFT = 256
 POW = 4
 LANES = 128
-AHEAD = 11
+AHEAD = 21
 F32 = jnp.float32
 BF16 = jnp.bfloat16
 MIB = 2**20
@@ -65,7 +65,7 @@
 
 def near_edge(odd, v, sx):
     rows = v.shape[0]
-    early = rows // sx * AHEAD // 1024 * 64
+    early = rows // sx * AHEAD // 2048 * 64
     return pl.pallas_call(
         functools.partial(near_kernel, sx),
         out_shape=(
@@ -324,7 +324,7 @@
     slabs, parts = lax.axis_size("space"), lax.axis_size("freq")
     hops = [bit * parts for bit in bits_of(slabs)]
     first = hops[:1] + bits_of(parts)[1:] + hops[1:]
-    second = first[2:] + first[:2]
+    second = first
 
     def swapped(one, other):
         pairs = [(i, i ^ (other if i % 2 else one)) for i in range(slabs * parts)]

time: 54.9 us -> 57.3 us (1.044)
  waiting for transfers between devices: 25.5 us -> 29.3 us
  starting transfers between devices: 17.6 us -> 16.1 us
    ppermute x4, waiting for transfers between devices: 17.6 us -> 21 us  [swap(): return lax.ppermute(x, axis, [(i, i ^ bit) for i in range(count)])]
    ppermute x4, starting transfers between devices: 7.41 us -> 5.88 us  [swap(): return lax.ppermute(x, axis, [(i, i ^ bit) for i in range(count)])]
  transfers between devices with their start and end apart: 12 -> 12, of which waited for: 8 -> 8; matrix products, arithmetic and copies ran while one was open for 0% -> 0% of each run, Pallas kernels for 8% -> 9%
where the time goes in v14:
time: 57.3 us; the launch traced here: 57.1 us
  waiting for transfers between devices  29.3 us (51%)
  starting transfers between devices  16.1 us (28%)
  Pallas kernels  9.42 us (16%)
  local copies, waits for them, and re-layouts  1.3 us (2%)
  between operations  0.83 us (1%)
    ppermute x4, waiting for transfers between devices, swap(): return lax.ppermute(x, axis, [(i, i ^ bit) for i in range(count)])  21 us
    ppermute x6, starting transfers between devices, swapped(): return lax.ppermute(sent, ('space', 'freq'), pairs).astype(F32)  8.61 us
    ppermute x6, waiting for transfers between devices, swapped(): return lax.ppermute(sent, ('space', 'freq'), pairs).astype(F32)  8.29 us
    ppermute x4, starting transfers between devices, swap(): return lax.ppermute(x, axis, [(i, i ^ bit) for i in range(count)])  5.88 us
    pallas_call x2, Pallas kernels, cross_part(): pl.pallas_call(functools.partial(cross_kernel, sx, begin, len(halos)), ou...  4.8 us
    pallas_call x1, Pallas kernels, modes_part(): pl.pallas_call(functools.partial(modes_kernel, sx, blocks, scaling), out_...  1.81 us
    unnamed x22, local copies, waits for them, and re-layouts  1.3 us
  transfers between devices with their start and end apart: 12, of which 8 were waited for; matrix products, arithmetic and copies ran while one was open for 0% of the time, Pallas kernels for 9%

profile of v14, /device:TPU:0, one launch (start us, length us, event | category | flops | bytes accessed | tf_op | source)
XLA Modules:
  0.0 57.1 jit_solution(8501894009052544050)
XLA Ops:
  0.7 1.2 %copy-done = bf16[2176,2,128]{2,1,0:T(2,128)(2,1)S(1)} copy-done((bf16[2176,2,128]{2,1,0:T(2,128)(2,1)S(1)}, bf16[2176,2,128]{2,1,0:T(2,128)(2,1)}, u32[]{:S(2)}) %copy-start) | copy-done | bytes 1114136
  1.9 0.2 far.1
  2.1 0.0 copy-start.9
  2.1 0.0 copy-start.10
  2.2 0.8 %collective-permute-start.2 = (bf16[2176,128]{1,0:T(8,128)(2,1)S(1)}, bf16[2176,128]{1,0:T(8,128)(2,1)S(1)}, u32[]{:S(2)}, u32[]{:S(2)}) collective-permute-start(bf16[2176,128]{1,0:T(8,128)(2,1)S(1)} %far.1), channel_id=1, source_target_pairs={{4,8},{12,16},{20,24},{8,4},{16,12},{24,20},{5,9},{13,17},{21,25},... | collective-permute-start | bytes 1671176 | tf_op jit(solution)/shard_map/ppermute | solution.py:482
  3.0 1.0 %near.1 = (bf16[1408,128]{1,0:T(8,128)(2,1)}, bf16[768,128]{1,0:T(8,128)(2,1)}) custom-call(s32[1]{0:T(128)} %bitcast.odd_ref, bf16[4352,128]{1,0:T(8,128)(2,1)S(1)} %bitcast.8), custom_call_target="tpu_custom_call" | custom-call | tf_op jit(solution)/shard_map/near/pallas_call | solution.py:69
  4.0 5.7 %collective-permute-start.3 = (bf16[1408,128]{1,0:T(8,128)(2,1)}, bf16[1408,128]{1,0:T(8,128)(2,1)}, u32[]{:S(2)}, u32[]{:S(2)}) collective-permute-start(bf16[1408,128]{1,0:T(8,128)(2,1)} %get-tuple-element.18), channel_id=1, source_target_pairs={{0,4},{4,0},{8,12},{12,8},{16,20},{20,16},{24,28},{28,24},{1,5},{5... | collective-permute-start | bytes 1081352 | tf_op jit(solution)/shard_map/ppermute | solution.py:320
  9.8 0.0 collective-permute-start.4
  9.8 0.4 columns.1
  10.2 0.1 collective-permute-start
  10.3 0.0 copy-start.7
  10.3 0.8 %collective-permute-start.1 = (bf16[8,544]{1,0:T(8,128)(2,1)S(1)}, bf16[8,544]{1,0:T(8,128)(2,1)S(1)}, u32[]{:S(2)}, u32[]{:S(2)}) collective-permute-start(bf16[8,544]{1,0:T(8,128)(2,1)S(1)} %get-tuple-element.15), channel_id=1, source_target_pairs={{1,2},{2,1},{5,6},{6,5},{9,10},{10,9},{13,14},{14,13},{17,18},{18,... | collective-permute-start | bytes 26120 | tf_op jit(solution)/shard_map/ppermute | solution.py:479
  11.1 0.3 collective-permute-done.near_ref
  11.4 1.1 %local.1 = (f32[2,2176,128]{2,1,0:T(8,128)S(1)}, f32[2,8,128]{2,1,0:T(8,128)S(1)}) custom-call(s32[1]{0:T(128)} %bitcast.odd_ref, s32[1]{0:T(128)} %bitcast.2.side_ref, bf16[4352,128]{1,0:T(8,128)(2,1)S(1)} %bitcast.9, bf16[4352,128]{1,0:T(8,128)(2,1)S(1)} %bitcast.11, bf16[128,128]{1,0:T(8,128)(2,1)S(1)} %copy-done.10, ...), custom_call_target="tpu_custom_call" | custom-call | flops 1000000000 | bytes 8000000 | tf_op jit(solution)/shard_map/local/pallas_call | solution.py:158
  12.6 19.4 %collective-permute-done.4.rest_1_ = bf16[768,128]{1,0:T(8,128)(2,1)} collective-permute-done((bf16[768,128]{1,0:T(8,128)(2,1)}, bf16[768,128]{1,0:T(8,128)(2,1)}, u32[]{:S(2)}, u32[]{:S(2)}) %collective-permute-start.4) | collective-permute-done | bytes 196640 | tf_op jit(solution)/shard_map/ppermute | solution.py:320
  32.0 2.7 %cross_near.1 = (f32[256,128]{1,0:T(8,128)S(1)}, bf16[2048,128]{1,0:T(8,128)(2,1)S(1)}) custom-call(s32[1]{0:T(128)} %bitcast.odd_ref, s32[16]{0:T(128)S(1)} %copy-done.6, s32[2,64]{1,0:T(2,128)S(1)} %bitcast.12, f32[2,2176,128]{2,1,0:T(8,128)S(1)} %get-tuple-element.16.z_ref, f32[2,8,128]{2,1,0:T(8,128)S(1)} %get-tuple-element.17.sum_ref, ...), custom_call_target="tpu_custom_call" | custom-call | flops 2000000000 | bytes 4000000 | tf_op jit(solution)/shard_map/cross_near/pallas_call | solution.py:298
  34.7 2.1 %cross_far.1 = (f32[256,128]{1,0:T(8,128)S(1)}, bf16[2048,128]{1,0:T(8,128)(2,1)S(1)}) custom-call(s32[1]{0:T(128)} %bitcast.odd_ref, s32[16]{0:T(128)S(1)} %copy-done.6, s32[2,64]{1,0:T(2,128)S(1)} %bitcast.13, f32[2,2176,128]{2,1,0:T(8,128)S(1)} %get-tuple-element.16.z_ref, f32[2,8,128]{2,1,0:T(8,128)S(1)} %get-tuple-element.17.sum_ref, ...), custom_call_target="tpu_custom_call" | custom-call | flops 2000000000 | bytes 4000000 | tf_op jit(solution)/shard_map/cross_far/pallas_call | solution.py:298
  36.8 3.5 %collective-permute-start.7 = (bf16[256,128]{1,0:T(8,128)(2,1)S(1)}, bf16[256,128]{1,0:T(8,128)(2,1)S(1)}, u32[]{:S(2)}, u32[]{:S(2)}) collective-permute-start(bf16[256,128]{1,0:T(8,128)(2,1)S(1)} %reduce-precision_convert_fusion), channel_id=1, source_target_pairs={{0,6},{1,7},{2,4},{3,5},{4,2},{5,3},{6,0},{7,1},{8,14},{9,15},{10,... | collective-permute-start | bytes 196616 | tf_op jit(solution)/shard_map/ppermute | solution.py:331
  40.4 0.5 collective-permute-start.6
  40.9 0.1 collective-permute-start.5
  41.0 1.6 %collective-permute-done.7 = bf16[256,128]{1,0:T(8,128)(2,1)S(1)} collective-permute-done((bf16[256,128]{1,0:T(8,128)(2,1)S(1)}, bf16[256,128]{1,0:T(8,128)(2,1)S(1)}, u32[]{:S(2)}, u32[]{:S(2)}) %collective-permute-start.7) | collective-permute-done | bytes 65568 | tf_op jit(solution)/shard_map/ppermute | solution.py:331
  42.6 2.0 %collective-permute-done.6 = bf16[256,128]{1,0:T(8,128)(2,1)S(1)} collective-permute-done((bf16[256,128]{1,0:T(8,128)(2,1)S(1)}, bf16[256,128]{1,0:T(8,128)(2,1)S(1)}, u32[]{:S(2)}, u32[]{:S(2)}) %collective-permute-start.6) | collective-permute-done | bytes 65568 | tf_op jit(solution)/shard_map/ppermute | solution.py:331
  44.6 0.5 collective-permute-done.5
  45.2 2.8 %collective-permute-start.10 = (bf16[256,128]{1,0:T(8,128)(2,1)S(1)}, bf16[256,128]{1,0:T(8,128)(2,1)S(1)}, u32[]{:S(2)}, u32[]{:S(2)}) collective-permute-start(bf16[256,128]{1,0:T(8,128)(2,1)S(1)} %fusion), channel_id=1, source_target_pairs={{0,24},{1,25},{2,26},{3,27},{4,28},{5,29},{6,30},{7,31},{8,16},{9,... | collective-permute-start | bytes 196616 | tf_op jit(solution)/shard_map/ppermute | solution.py:331
  48.0 0.3 collective-permute-start.9
  48.3 1.3 %collective-permute-start.8 = (bf16[256,128]{1,0:T(8,128)(2,1)S(1)}, bf16[256,128]{1,0:T(8,128)(2,1)S(1)}, u32[]{:S(2)}, u32[]{:S(2)}) collective-permute-start(bf16[256,128]{1,0:T(8,128)(2,1)S(1)} %fusion), channel_id=1, source_target_pairs={{0,8},{1,9},{2,10},{3,11},{4,12},{5,13},{6,14},{7,15},{8,0},{9,1},... | collective-permute-start | bytes 196616 | tf_op jit(solution)/shard_map/ppermute | solution.py:331
  49.6 1.7 %collective-permute-done.10 = bf16[256,128]{1,0:T(8,128)(2,1)S(1)} collective-permute-done((bf16[256,128]{1,0:T(8,128)(2,1)S(1)}, bf16[256,128]{1,0:T(8,128)(2,1)S(1)}, u32[]{:S(2)}, u32[]{:S(2)}) %collective-permute-start.10) | collective-permute-done | bytes 65568 | tf_op jit(solution)/shard_map/ppermute | solution.py:331
  51.3 2.5 %collective-permute-done.9 = bf16[256,128]{1,0:T(8,128)(2,1)S(1)} collective-permute-done((bf16[256,128]{1,0:T(8,128)(2,1)S(1)}, bf16[256,128]{1,0:T(8,128)(2,1)S(1)}, u32[]{:S(2)}, u32[]{:S(2)}) %collective-permute-start.9) | collective-permute-done | bytes 65568 | tf_op jit(solution)/shard_map/ppermute | solution.py:331
  53.8 0.1 add_add_fusion.mine_ref
  53.9 0.1 collective-permute-start.11
  53.9 1.3 %collective-permute-done.11.other_ref = f32[256,128]{1,0:T(8,128)S(1)} collective-permute-done((f32[256,128]{1,0:T(8,128)S(1)}, f32[256,128]{1,0:T(8,128)S(1)}, u32[]{:S(2)}, u32[]{:S(2)}) %collective-permute-start.11) | collective-permute-done | bytes 131104 | tf_op jit(solution)/shard_map/ppermute | solution.py:320
  55.3 1.8 %modes.1 = (f32[2,64]{1,0:T(2,128)}, f32[256,128]{1,0:T(8,128)}) custom-call(s32[1]{0:T(128)} %bitcast.odd_ref, f32[256,128]{1,0:T(8,128)S(1)} %add_add_fusion.mine_ref, f32[256,128]{1,0:T(8,128)S(1)} %collective-permute-done.11.other_ref, bf16[2048,128]{1,0:T(8,128)(2,1)S(1)} %get-tuple-element.22.near_ref, bf16[2048,128]{1,0:T(8,128)(2,1)S(1)} %get-tuple-element.23.far_ref), custom_call_target="tpu_custom_call" | custom-call | tf_op jit(solution)/shard_map/modes/pallas_call | solution.py:438
  (24 shorter events, 0.1 us)
Async XLA Ops:
  0.6 1.3 %copy-start = (bf16[2176,2,128]{2,1,0:T(2,128)(2,1)S(1)}, bf16[2176,2,128]{2,1,0:T(2,128)(2,1)}, u32[]{:S(2)}) copy-start(bf16[2176,2,128]{2,1,0:T(2,128)(2,1)} %param.11) | copy-start | bytes 3342340
  1.9 7.9 %copy-start.2 = (bf16[2176,2,128]{2,1,0:T(2,128)(2,1)S(1)}, bf16[2176,2,128]{2,1,0:T(2,128)(2,1)}, u32[]{:S(2)}) copy-start(bf16[2176,2,128]{2,1,0:T(2,128)(2,1)} %param.10) | copy-start | bytes 3342340
  1.9 7.9 %copy-start.3 = (bf16[8,16,128]{2,1,0:T(8,128)(2,1)S(1)}, bf16[8,16,128]{2,1,0:T(8,128)(2,1)}, u32[]{:S(2)}) copy-start(bf16[8,16,128]{2,1,0:T(8,128)(2,1)} %constant.36.clone.picks_ref) | copy-start | bytes 98308
  2.1 9.3 %copy-start.1 = (bf16[2176,2,128]{2,1,0:T(2,128)(2,1)S(1)}, bf16[2176,2,128]{2,1,0:T(2,128)(2,1)}, u32[]{:S(2)}) copy-start(bf16[2176,2,128]{2,1,0:T(2,128)(2,1)} %param.11) | copy-start | bytes 3342340
  2.1 9.3 %copy-start.9 = (bf16[8,16,128]{2,1,0:T(8,128)(2,1)S(1)}, bf16[8,16,128]{2,1,0:T(8,128)(2,1)}, u32[]{:S(2)}) copy-start(bf16[8,16,128]{2,1,0:T(8,128)(2,1)} %constant.38.clone.places_ref) | copy-start | bytes 98308
  2.1 9.3 %copy-start.10 = (bf16[128,128]{1,0:T(8,128)(2,1)S(1)}, bf16[128,128]{1,0:T(8,128)(2,1)}, u32[]{:S(2)}) copy-start(bf16[128,128]{1,0:T(8,128)(2,1)} %constant.37.clone.shift_ref) | copy-start | bytes 98308
  2.2 32.5 %collective-permute-start.2 = (bf16[2176,128]{1,0:T(8,128)(2,1)S(1)}, bf16[2176,128]{1,0:T(8,128)(2,1)S(1)}, u32[]{:S(2)}, u32[]{:S(2)}) collective-permute-start(bf16[2176,128]{1,0:T(8,128)(2,1)S(1)} %far.1), channel_id=1, source_target_pairs={{4,8},{12,16},{20,24},{8,4},{16,12},{24,20},{5,9},{13,17},{21,25},... | collective-permute-start | bytes 1671176 | tf_op jit(solution)/shard_map/ppermute | solution.py:482
  4.0 27.9 %collective-permute-start.3 = (bf16[1408,128]{1,0:T(8,128)(2,1)}, bf16[1408,128]{1,0:T(8,128)(2,1)}, u32[]{:S(2)}, u32[]{:S(2)}) collective-permute-start(bf16[1408,128]{1,0:T(8,128)(2,1)} %get-tuple-element.18), channel_id=1, source_target_pairs={{0,4},{4,0},{8,12},{12,8},{16,20},{20,16},{24,28},{28,24},{1,5},{5... | collective-permute-start | bytes 1081352 | tf_op jit(solution)/shard_map/ppermute | solution.py:320
  9.8 22.2 %collective-permute-start.4 = (bf16[768,128]{1,0:T(8,128)(2,1)}, bf16[768,128]{1,0:T(8,128)(2,1)}, u32[]{:S(2)}, u32[]{:S(2)}) collective-permute-start(bf16[768,128]{1,0:T(8,128)(2,1)} %get-tuple-element.19), channel_id=1, source_target_pairs={{0,4},{4,0},{8,12},{12,8},{16,20},{20,16},{24,28},{28,24},{1,5},{5... | collective-permute-start | bytes 589832 | tf_op jit(solution)/shard_map/ppermute | solution.py:320
  10.2 1.2 %collective-permute-start = (bf16[8,544]{1,0:T(8,128)(2,1)S(1)}, bf16[8,544]{1,0:T(8,128)(2,1)S(1)}, u32[]{:S(2)}, u32[]{:S(2)}) collective-permute-start(bf16[8,544]{1,0:T(8,128)(2,1)S(1)} %get-tuple-element.14), channel_id=1, source_target_pairs={{0,1},{1,0},{2,3},{3,2},{4,5},{5,4},{6,7},{7,6},{8,9},{9,8},{10,11... | collective-permute-start | bytes 26120 | tf_op jit(solution)/shard_map/ppermute | solution.py:320
  10.3 21.7 %copy-start.4 = (s32[64,2]{0,1:T(2,128)S(1)}, s32[64,2]{0,1:T(2,128)}, u32[]{:S(2)}) copy-start(s32[64,2]{0,1:T(2,128)} %param.14) | copy-start | bytes 1540
  10.3 21.7 %copy-start.5 = (f32[2,128]{1,0:T(2,128)S(1)}, f32[2,128]{1,0:T(2,128)}, u32[]{:S(2)}) copy-start(f32[2,128]{1,0:T(2,128)} %weights_ref.3) | copy-start | bytes 3076
  10.3 21.7 %copy-start.6 = (s32[16]{0:T(128)S(1)}, s32[16]{0:T(128)}, u32[]{:S(2)}) copy-start(s32[16]{0:T(128)} %offsets_ref.3) | copy-start | bytes 196
  10.3 21.7 %copy-start.7 = (bf16[256,256]{1,0:T(8,128)(2,1)S(1)}, bf16[256,256]{1,0:T(8,128)(2,1)}, u32[]{:S(2)}) copy-start(bf16[256,256]{1,0:T(8,128)(2,1)} %constant.40.clone.transform_ref) | copy-start | bytes 393220
  10.3 21.7 %copy-start.8 = (f32[256,128]{1,0:T(8,128)S(1)}, f32[256,128]{1,0:T(8,128)}, u32[]{:S(2)}) copy-start(f32[256,128]{1,0:T(8,128)} %constant.39.clone.window_ref) | copy-start | bytes 393220
  10.3 1.1 %collective-permute-start.1 = (bf16[8,544]{1,0:T(8,128)(2,1)S(1)}, bf16[8,544]{1,0:T(8,128)(2,1)S(1)}, u32[]{:S(2)}, u32[]{:S(2)}) collective-permute-start(bf16[8,544]{1,0:T(8,128)(2,1)S(1)} %get-tuple-element.15), channel_id=1, source_target_pairs={{1,2},{2,1},{5,6},{6,5},{9,10},{10,9},{13,14},{14,13},{17,18},{18,... | collective-permute-start | bytes 26120 | tf_op jit(solution)/shard_map/ppermute | solution.py:479
  36.8 5.8 %collective-permute-start.7 = (bf16[256,128]{1,0:T(8,128)(2,1)S(1)}, bf16[256,128]{1,0:T(8,128)(2,1)S(1)}, u32[]{:S(2)}, u32[]{:S(2)}) collective-permute-start(bf16[256,128]{1,0:T(8,128)(2,1)S(1)} %reduce-precision_convert_fusion), channel_id=1, source_target_pairs={{0,6},{1,7},{2,4},{3,5},{4,2},{5,3},{6,0},{7,1},{8,14},{9,15},{10,... | collective-permute-start | bytes 196616 | tf_op jit(solution)/shard_map/ppermute | solution.py:331
  40.4 4.3 %collective-permute-start.6 = (bf16[256,128]{1,0:T(8,128)(2,1)S(1)}, bf16[256,128]{1,0:T(8,128)(2,1)S(1)}, u32[]{:S(2)}, u32[]{:S(2)}) collective-permute-start(bf16[256,128]{1,0:T(8,128)(2,1)S(1)} %reduce-precision_convert_fusion), channel_id=1, source_target_pairs={{0,2},{1,3},{2,0},{3,1},{4,6},{5,7},{6,4},{7,5},{8,10},{9,11},{10,... | collective-permute-start | bytes 196616 | tf_op jit(solution)/shard_map/ppermute | solution.py:331
  40.9 4.3 %collective-permute-start.5 = (bf16[256,128]{1,0:T(8,128)(2,1)S(1)}, bf16[256,128]{1,0:T(8,128)(2,1)S(1)}, u32[]{:S(2)}, u32[]{:S(2)}) collective-permute-start(bf16[256,128]{1,0:T(8,128)(2,1)S(1)} %reduce-precision_convert_fusion), channel_id=1, source_target_pairs={{0,4},{1,5},{2,6},{3,7},{4,0},{5,1},{6,2},{7,3},{8,12},{9,13},{10,... | collective-permute-start | bytes 196616 | tf_op jit(solution)/shard_map/ppermute | solution.py:331
  45.2 6.1 %collective-permute-start.10 = (bf16[256,128]{1,0:T(8,128)(2,1)S(1)}, bf16[256,128]{1,0:T(8,128)(2,1)S(1)}, u32[]{:S(2)}, u32[]{:S(2)}) collective-permute-start(bf16[256,128]{1,0:T(8,128)(2,1)S(1)} %fusion), channel_id=1, source_target_pairs={{0,24},{1,25},{2,26},{3,27},{4,28},{5,29},{6,30},{7,31},{8,16},{9,... | collective-permute-start | bytes 196616 | tf_op jit(solution)/shard_map/ppermute | solution.py:331
  48.0 5.8 %collective-permute-start.9 = (bf16[256,128]{1,0:T(8,128)(2,1)S(1)}, bf16[256,128]{1,0:T(8,128)(2,1)S(1)}, u32[]{:S(2)}, u32[]{:S(2)}) collective-permute-start(bf16[256,128]{1,0:T(8,128)(2,1)S(1)} %fusion), channel_id=1, source_target_pairs={{0,16},{1,17},{2,18},{3,19},{4,20},{5,21},{6,22},{7,23},{8,24},{9,... | collective-permute-start | bytes 196616 | tf_op jit(solution)/shard_map/ppermute | solution.py:331
  48.3 5.5 %collective-permute-start.8 = (bf16[256,128]{1,0:T(8,128)(2,1)S(1)}, bf16[256,128]{1,0:T(8,128)(2,1)S(1)}, u32[]{:S(2)}, u32[]{:S(2)}) collective-permute-start(bf16[256,128]{1,0:T(8,128)(2,1)S(1)} %fusion), channel_id=1, source_target_pairs={{0,8},{1,9},{2,10},{3,11},{4,12},{5,13},{6,14},{7,15},{8,0},{9,1},... | collective-permute-start | bytes 196616 | tf_op jit(solution)/shard_map/ppermute | solution.py:331
  53.9 1.4 %collective-permute-start.11 = (f32[256,128]{1,0:T(8,128)S(1)}, f32[256,128]{1,0:T(8,128)S(1)}, u32[]{:S(2)}, u32[]{:S(2)}) collective-permute-start(f32[256,128]{1,0:T(8,128)S(1)} %add_add_fusion.mine_ref), channel_id=1, source_target_pairs={{0,1},{1,0},{2,3},{3,2},{4,5},{5,4},{6,7},{7,6},{8,9},{9,8},{10,11... | collective-permute-start | bytes 393224 | tf_op jit(solution)/shard_map/ppermute | solution.py:320
